TPU v7x, 32 devices: a whole 2x2x4 slice. The times are simulated.
32 devices in a mesh: seq: 4 (over x, core), fsdp: 8 (over z, y).
Axes of the slice: x: 2, y: 2, z: 4, core: 2. Of those that a mesh axis runs over, the one named last changes fastest.
Arguments:
- inputs: bfloat16 [8, 1536, 1152], P('fsdp', 'seq'), may hold values from -6 to 6
- image_ids: int32 [8, 1536], P('fsdp', 'seq'), may hold values from 0 to 2, never falling along the last dimension, each value on 1 to 729 neighbouring positions
- pad_mask: int32 [8, 1536], P('fsdp', 'seq'), may hold values 0 or 1
- cotangent: bfloat16 [8, 1536, 1152], P('fsdp', 'seq'), may hold values from -6 to 6
- w_qkv: bfloat16 [1152, 3456], P('fsdp'), may hold values from -0.1875 to 0.1875
- w_out: bfloat16 [1152, 1152], P('fsdp'), may hold values from -1.5 to 1.5
- w_up: bfloat16 [1152, 4304], P('fsdp'), may hold values from -0.1875 to 0.1875
- w_down: bfloat16 [4304, 1152], P('fsdp'), may hold values from -0.09375 to 0.09375
- ln1_gain: float32 [1152], replicated, may hold values from 0.5 to 1.5
- ln1_shift: float32 [1152], replicated, may hold values from -4 to 4
- q_bias: float32 [1152], replicated, may hold values from -4 to 4
- v_bias: float32 [1152], replicated, may hold values from -4 to 4
- out_bias: float32 [1152], replicated, may hold values from -4 to 4
- ln2_gain: float32 [1152], replicated, may hold values from 0.5 to 1.5
- ln2_shift: float32 [1152], replicated, may hold values from -4 to 4
- up_bias: float32 [4304], replicated, may hold values from -4 to 4
- down_bias: float32 [1152], replicated, may hold values from -4 to 4
Outputs:
- layer_out: bfloat16 [8, 1536, 1152], P('fsdp', 'seq')
- grad_inputs: bfloat16 [8, 1536, 1152], P('fsdp', 'seq')
- grad_w_qkv: float32 [1152, 3456], P('fsdp', 'seq')
- grad_w_out: float32 [1152, 1152], P('fsdp', 'seq')
- grad_w_up: float32 [1152, 4304], P('fsdp', 'seq')
- grad_w_down: float32 [4304, 1152], P('fsdp', 'seq')
- grad_ln1_gain: float32 [1152], replicated
- grad_ln1_shift: float32 [1152], replicated
- grad_q_bias: float32 [1152], replicated
- grad_v_bias: float32 [1152], replicated
- grad_out_bias: float32 [1152], replicated
- grad_ln2_gain: float32 [1152], replicated
- grad_ln2_shift: float32 [1152], replicated
- grad_up_bias: float32 [4304], replicated
- grad_down_bias: float32 [1152], replicated
Inputs may be any that keep to these rules, and one draw needn't show every extreme that they name: `image_ids`: within a group ids never fall; every image has 1 to 729 tokens, one of them exactly 729, and all 3 ids occur.
All inputs are finite; a program needn't handle non-finite values. No bound on the sum of `pad_mask` on one device may be relied on, other than what follows from the above.
Results may differ from a plain program's by a relative error of at most 0.015.
Values may be sent and summed in bfloat16 or wider, within the bound.
No kernel may reach another device: no remote copies, remote signals or barrier semaphores. Data moves between devices by JAX's collectives and lax.ppermute only.
A program may use at most 192 MiB of HBM per device.

v0:
```python
import jax
import jax.numpy as jnp
from jax import lax
from jax.sharding import PartitionSpec as P

HEADS = 16
HD = 72


EPSILON = 1e-06


def layer_norm(values, gain, shift):
    average = jnp.mean(values, axis=-1, keepdims=True)
    centred = values - average
    spread = jnp.mean(centred * centred, axis=-1, keepdims=True)
    return centred * lax.rsqrt(spread + EPSILON) * gain + shift


def gelu_tanh(value):
    return jax.nn.gelu(value, approximate=True)


def local(
    inputs,
    image_ids,
    pad_mask,
    cotangent,
    w_qkv,
    w_out,
    w_up,
    w_down,
    ln1_gain,
    ln1_shift,
    q_bias,
    v_bias,
    out_bias,
    ln2_gain,
    ln2_shift,
    up_bias,
    down_bias,
):
    tok_rows = inputs.shape[1]
    width = inputs.shape[2]
    head_dim = HD
    group_size = lax.axis_size("seq")
    local_heads = HEADS // group_size
    scaling = head_dim ** (-0.5)
    run_len = tok_rows * group_size
    block_rows = min(512, run_len)
    block_count = run_len // block_rows
    run_ids, run_pads = (
        lax.all_gather(image_ids, "seq", axis=1, tiled=True),
        lax.all_gather(pad_mask, "seq", axis=1, tiled=True),
    )
    run_ids = run_ids[0]
    key_valid = run_pads[0] == 0
    full_qkv, full_out, full_up, full_down = (
        lax.all_gather(w_qkv, "fsdp", axis=0, tiled=True),
        lax.all_gather(w_out, "fsdp", axis=0, tiled=True),
        lax.all_gather(w_up, "fsdp", axis=0, tiled=True),
        lax.all_gather(w_down, "fsdp", axis=0, tiled=True),
    )
    x_float = inputs.reshape(tok_rows, width).astype(jnp.float32)
    h_one = layer_norm(x_float, ln1_gain, ln1_shift).astype(jnp.bfloat16)
    projected = jnp.dot(h_one, full_qkv, preferred_element_type=jnp.float32)
    queries = (
        (projected[:, :width] + q_bias).astype(jnp.bfloat16).reshape(tok_rows, HEADS, head_dim)
    )
    keys = projected[:, width : 2 * width].astype(jnp.bfloat16).reshape(tok_rows, HEADS, head_dim)
    values = (
        (projected[:, 2 * width :] + v_bias).astype(jnp.bfloat16).reshape(tok_rows, HEADS, head_dim)
    )
    q_heads, k_heads, v_heads = (
        lax.all_to_all(queries, "seq", split_axis=1, concat_axis=0, tiled=True),
        lax.all_to_all(keys, "seq", split_axis=1, concat_axis=0, tiled=True),
        lax.all_to_all(values, "seq", split_axis=1, concat_axis=0, tiled=True),
    )
    key_pos = jnp.arange(run_len, dtype=jnp.int32)

    def block_scores(query_block, start):
        query_ids = lax.dynamic_slice_in_dim(run_ids, start, block_rows)
        query_pos = start + jnp.arange(block_rows, dtype=jnp.int32)
        allowed = (query_ids[:, None] == run_ids[None, :]) & (
            key_valid[None, :] | (query_pos[:, None] == key_pos[None, :])
        )
        raw_scores = (
            jnp.einsum("qhd,khd->hqk", query_block, k_heads, preferred_element_type=jnp.float32)
            * scaling
        )
        return jnp.where(allowed[None], raw_scores, -1e30)

    query_blocks = q_heads.reshape(block_count, block_rows, local_heads, head_dim)
    block_index = jnp.arange(block_count, dtype=jnp.int32)

    def forward_block(carry, item):
        query_block, index = item
        masked = block_scores(query_block, index * block_rows)
        top_score = jnp.max(masked, axis=-1, keepdims=True)
        expo = jnp.exp(masked - top_score)
        total = jnp.sum(expo, axis=-1, keepdims=True)
        probs = (expo / total).astype(jnp.bfloat16)
        attended = jnp.einsum("hqk,khd->qhd", probs, v_heads, preferred_element_type=jnp.float32)
        return (carry, (attended.astype(jnp.bfloat16), (top_score + jnp.log(total))[..., 0]))

    unused, (out_blocks, lse_blocks) = lax.scan(
        forward_block, jnp.zeros((), jnp.float32), (query_blocks, block_index)
    )
    o_heads = out_blocks.reshape(run_len, local_heads, head_dim)
    o_rows = lax.all_to_all(o_heads, "seq", split_axis=0, concat_axis=1, tiled=True).reshape(
        tok_rows, width
    )
    branch = jnp.dot(o_rows, full_out, preferred_element_type=jnp.float32) + out_bias
    x_one = x_float + branch
    h_two = layer_norm(x_one, ln2_gain, ln2_shift).astype(jnp.bfloat16)
    hidden = jnp.dot(h_two, full_up, preferred_element_type=jnp.float32) + up_bias
    active = gelu_tanh(hidden).astype(jnp.bfloat16)
    mixed = jnp.dot(active, full_down, preferred_element_type=jnp.float32) + down_bias
    layer_out = (x_one + mixed).astype(jnp.bfloat16).reshape(1, tok_rows, width)
    full_qkv, full_out, full_up, full_down = (
        lax.all_gather(w_qkv, "fsdp", axis=0, tiled=True),
        lax.all_gather(w_out, "fsdp", axis=0, tiled=True),
        lax.all_gather(w_up, "fsdp", axis=0, tiled=True),
        lax.all_gather(w_down, "fsdp", axis=0, tiled=True),
    )
    keep = (1 - pad_mask.reshape(tok_rows)).astype(jnp.float32)
    d_out = cotangent.reshape(tok_rows, width).astype(jnp.float32) * keep[:, None]
    grad_mixed = d_out.astype(jnp.bfloat16)
    grad_down = jnp.einsum("nf,nd->fd", active, grad_mixed, preferred_element_type=jnp.float32)
    sum_down_bias = jnp.sum(grad_mixed.astype(jnp.float32), axis=0)
    d_active = jnp.einsum("nd,fd->nf", grad_mixed, full_down, preferred_element_type=jnp.float32)
    unused_value, gelu_back = jax.vjp(gelu_tanh, hidden)
    grad_hidden = gelu_back(d_active)[0].astype(jnp.bfloat16)
    grad_up = jnp.einsum("nd,nf->df", h_two, grad_hidden, preferred_element_type=jnp.float32)
    sum_up_bias = jnp.sum(grad_hidden.astype(jnp.float32), axis=0)
    d_h_two = jnp.einsum("nf,df->nd", grad_hidden, full_up, preferred_element_type=jnp.float32)
    unused_norm, norm_two_back = jax.vjp(layer_norm, x_one, ln2_gain, ln2_shift)
    d_x_norm, sum_ln2_gain, sum_ln2_shift = norm_two_back(d_h_two)
    d_x_one = d_out + d_x_norm
    grad_branch = d_x_one.astype(jnp.bfloat16)
    grad_out = jnp.einsum("nc,nd->cd", o_rows, grad_branch, preferred_element_type=jnp.float32)
    sum_out_bias = jnp.sum(grad_branch.astype(jnp.float32), axis=0)
    d_attended = jnp.einsum("nd,cd->nc", grad_branch, full_out, preferred_element_type=jnp.float32)
    d_attended = d_attended.astype(jnp.bfloat16).reshape(tok_rows, HEADS, head_dim)
    do_heads = lax.all_to_all(d_attended, "seq", split_axis=1, concat_axis=0, tiled=True)
    grad_blocks = do_heads.reshape(block_count, block_rows, local_heads, head_dim)

    def backward_block(carry, item):
        key_sum, value_sum = carry
        query_block, grad_block, lse_block, index = item
        masked = block_scores(query_block, index * block_rows)
        probs = jnp.exp(masked - lse_block[..., None])
        probs_low = probs.astype(jnp.bfloat16)
        d_probs = jnp.einsum(
            "qhd,khd->hqk", grad_block, v_heads, preferred_element_type=jnp.float32
        )
        inner = jnp.sum(probs * d_probs, axis=-1, keepdims=True)
        d_scores = (probs * (d_probs - inner)).astype(jnp.bfloat16)
        query_grad = (
            jnp.einsum("hqk,khd->qhd", d_scores, k_heads, preferred_element_type=jnp.float32)
            * scaling
        )
        key_sum = (
            key_sum
            + jnp.einsum("hqk,qhd->khd", d_scores, query_block, preferred_element_type=jnp.float32)
            * scaling
        )
        value_sum = value_sum + jnp.einsum(
            "hqk,qhd->khd", probs_low, grad_block, preferred_element_type=jnp.float32
        )
        return ((key_sum, value_sum), query_grad)

    zero_heads = jnp.zeros((run_len, local_heads, head_dim), jnp.float32)
    (dk_heads, dv_heads), dq_blocks = lax.scan(
        backward_block,
        (zero_heads, zero_heads),
        (query_blocks, grad_blocks, lse_blocks, block_index),
    )
    dq_heads = dq_blocks.reshape(run_len, local_heads, head_dim).astype(jnp.bfloat16)
    dq_rows, dk_rows, dv_rows = (
        lax.all_to_all(dq_heads, "seq", split_axis=0, concat_axis=1, tiled=True),
        lax.all_to_all(
            dk_heads.astype(jnp.bfloat16), "seq", split_axis=0, concat_axis=1, tiled=True
        ),
        lax.all_to_all(
            dv_heads.astype(jnp.bfloat16), "seq", split_axis=0, concat_axis=1, tiled=True
        ),
    )
    dq_flat = dq_rows.reshape(tok_rows, width)
    dv_flat = dv_rows.reshape(tok_rows, width)
    grad_proj = jnp.concatenate([dq_flat, dk_rows.reshape(tok_rows, width), dv_flat], axis=1)
    grad_qkv = jnp.einsum("nc,nd->cd", h_one, grad_proj, preferred_element_type=jnp.float32)
    sum_q_bias = jnp.sum(dq_flat.astype(jnp.float32), axis=0)
    sum_v_bias = jnp.sum(dv_flat.astype(jnp.float32), axis=0)
    d_h_one = jnp.einsum("nd,cd->nc", grad_proj, full_qkv, preferred_element_type=jnp.float32)
    unused_first, norm_one_back = jax.vjp(layer_norm, x_float, ln1_gain, ln1_shift)
    d_x_first, sum_ln1_gain, sum_ln1_shift = norm_one_back(d_h_one)
    grad_inputs = (d_x_one + d_x_first).astype(jnp.bfloat16).reshape(1, tok_rows, width)
    seq_parts = (
        lax.psum_scatter(
            grad_qkv.astype(jnp.bfloat16), "seq", scatter_dimension=1, tiled=True
        ).astype(jnp.float32),
        lax.psum_scatter(
            grad_out.astype(jnp.bfloat16), "seq", scatter_dimension=1, tiled=True
        ).astype(jnp.float32),
        lax.psum_scatter(
            grad_up.astype(jnp.bfloat16), "seq", scatter_dimension=1, tiled=True
        ).astype(jnp.float32),
        lax.psum_scatter(
            grad_down.astype(jnp.bfloat16), "seq", scatter_dimension=1, tiled=True
        ).astype(jnp.float32),
    )
    col_parts = (
        lax.psum_scatter(
            seq_parts[0].astype(jnp.bfloat16), "fsdp", scatter_dimension=0, tiled=True
        ).astype(jnp.float32),
        lax.psum_scatter(
            seq_parts[1].astype(jnp.bfloat16), "fsdp", scatter_dimension=0, tiled=True
        ).astype(jnp.float32),
        lax.psum_scatter(
            seq_parts[2].astype(jnp.bfloat16), "fsdp", scatter_dimension=0, tiled=True
        ).astype(jnp.float32),
        lax.psum_scatter(
            seq_parts[3].astype(jnp.bfloat16), "fsdp", scatter_dimension=0, tiled=True
        ).astype(jnp.float32),
    )
    vector_sums = lax.psum(
        (
            sum_ln1_gain,
            sum_ln1_shift,
            sum_q_bias,
            sum_v_bias,
            sum_out_bias,
            sum_ln2_gain,
            sum_ln2_shift,
            sum_up_bias,
            sum_down_bias,
        ),
        ("seq", "fsdp"),
    )
    return (
        layer_out,
        grad_inputs,
        col_parts[0],
        col_parts[1],
        col_parts[2],
        col_parts[3],
        vector_sums[0],
        vector_sums[1],
        vector_sums[2],
        vector_sums[3],
        vector_sums[4],
        vector_sums[5],
        vector_sums[6],
        vector_sums[7],
        vector_sums[8],
    )


def solution(mesh):
    placed = (
        P("fsdp", "seq", None),
        P("fsdp", "seq"),
        P("fsdp", "seq"),
        P("fsdp", "seq", None),
        P("fsdp", None),
        P("fsdp", None),
        P("fsdp", None),
        P("fsdp", None),
        P(),
        P(),
        P(),
        P(),
        P(),
        P(),
        P(),
        P(),
        P(),
    )
    return jax.shard_map(
        local,
        mesh=mesh,
        in_specs=placed,
        out_specs=(
            P("fsdp", "seq", None),
            P("fsdp", "seq", None),
            P("fsdp", "seq"),
            P("fsdp", "seq"),
            P("fsdp", "seq"),
            P("fsdp", "seq"),
            P(),
            P(),
            P(),
            P(),
            P(),
            P(),
            P(),
            P(),
            P(),
        ),
        check_vma=False,
    )
```

profile of v0, /device:TPU:0, one launch (start us, length us, event | category | flops | bytes accessed | tf_op | source)
XLA Modules:
  0.0 1286.0 jit_solution(9758439323579876990)
XLA Ops:
  10.7 121.9 %all-gather.6.cloned.1.call-done = bf16[1152,3456]{1,0:T(8,128)(2,1)} async-done(((bf16[144,3456]{1,0:T(8,128)(2,1)}), bf16[1152,3456]{1,0:T(8,128)(2,1)}) %all-gather.6.cloned.1.call-update) | async-done | bytes 7962640 | tf_op jit(solution)/shard_map/all_gather | solution.py:59
  132.6 6.5 fusion.86
  142.9 3.5 all-to-all-start
  149.3 9.8 all-to-all-done
  159.1 3.6 all-to-all-start.1
  164.0 11.3 all-to-all-done.1
  175.4 4.2 all-to-all-start.2
  179.6 13.6 %all_gather.22 = s32[1,1536]{1,0:T(1,128)S(1)} all-gather(s32[1,384]{1,0:T(1,128)S(1)} %copy-done.60), channel_id=1, replica_groups=mesh['seq'=4,'fsdp'=8] {'seq'}, dimensions={1}, use_global_device_ids=true | all-gather | bytes 7680 | tf_op jit(solution)/shard_map/all_gather | solution.py:53
  193.8 5.7 all_gather.23
  203.7 50.4 %while.28 = (s32[]{:T(128)}, bf16[3,512,4,72]{1,3,2,0:T(8,128)(2,1)}, f32[3,4,512]{2,1,0:T(4,128)}, s32[3]{0:T(128)S(1)}, s32[1536]{0:T(1024)}, /*index=5*/s32[1...) while((s32[]{:T(128)}, ...), condition=%wide.region_5.6_spmd.clone, body=%wide.region_2.5_spmd.clone.sunk | while | flops 947010048 | bytes 43349876 | solution.py:106
  210.9 3.7 fusion.138
  214.6 5.3 fusion.139
  227.7 3.7 fusion.138
  231.4 5.3 fusion.139
  244.5 3.7 fusion.138
  248.2 5.3 fusion.139
  257.6 4.5 all-to-all-start.3
  262.2 20.1 %all-to-all-done.3 = bf16[1536,4,72]{2,1,0:T(4,128)(2,1)} async-done(((bf16[1536,4,72]{2,1,0:T(4,128)(2,1)}), bf16[1536,4,72]{2,1,0:T(4,128)(2,1)}, u32[]{:S(2)}, u32[]{:S(2)}) %all-to-all-start.3) | async-done | bytes 884768 | tf_op jit(solution)/shard_map/all_to_all | solution.py:110
  285.7 3.6 fusion.92
  291.5 42.6 %all-gather.12.cloned.1.call-done = bf16[8,538,1152]{2,1,0:T(8,128)(2,1)} async-done(((bf16[1,538,1152]{2,1,0:T(8,128)(2,1)}), bf16[8,538,1152]{2,1,0:T(8,128)(2,1)}) %all-gather.12.cloned.1.call-update) | async-done | bytes 9916432 | tf_op jit(solution)/shard_map/all_gather | solution.py:62
  334.0 12.4 reshape.364
  346.4 133.1 %all-gather.10.cloned.1.call-done = bf16[1152,4304]{1,0:T(8,128)(2,1)} async-done(((bf16[144,4304]{1,0:T(8,128)(2,1)}), bf16[1152,4304]{1,0:T(8,128)(2,1)}) %all-gather.10.cloned.1.call-update) | async-done | bytes 9916432 | tf_op jit(solution)/shard_map/all_gather | solution.py:61
  479.6 10.0 convolution_add_fusion
  489.6 12.3 convert_reduce_fusion
  502.0 10.5 multiply_reduce_fusion.1
  522.7 4.6 convolution_convert_fusion.3
  527.3 8.0 all-to-all-done.4
  536.7 4.0 reshape.357
  542.1 121.9 %while.29 = (s32[]{:T(128)}, f32[1536,4,72]{0,2,1:T(8,128)}, f32[1536,4,72]{0,2,1:T(8,128)}, bf16[3,512,4,72]{1,3,2,0:T(8,128)(2,1)}, bf16[3,512,4,72]{1,3,2,0:T...) while((s32[]{:T(128)}, f32[1536,4,72]{0,2,1:T(8,128)}, ...), condition=%wide.region_12.13_spmd.clone, body=%wide.region_10.12_spmd.clone.sunk | while | flops 2298739200 | bytes 264018192 | solution.py:174
  542.2 6.3 fusion.149
  553.3 8.1 multiply_reduce_fusion.5
  561.5 4.5 multiply_convert_fusion.5
  567.8 5.4 fusion.151
  573.3 6.2 fusion.152
  582.5 6.3 fusion.149
  593.7 8.0 multiply_reduce_fusion.5
  601.8 4.5 multiply_convert_fusion.5
  608.1 5.9 fusion.151
  614.1 6.2 fusion.152
  623.3 6.3 fusion.149
  634.4 8.0 multiply_reduce_fusion.5
  642.5 4.5 multiply_convert_fusion.5
  648.9 5.9 fusion.151
  654.9 6.2 fusion.152
  667.9 3.6 all-to-all-start.7
  676.0 15.6 %all-to-all-done.7 = bf16[1536,4,72]{2,1,0:T(4,128)(2,1)S(1)} async-done(((bf16[1536,4,72]{2,1,0:T(4,128)(2,1)}), bf16[1536,4,72]{2,1,0:T(4,128)(2,1)S(1)}, u32[]{:S(2)}, u32[]{:S(2)}) %all-to-all-start.7) | async-done | bytes 884768 | tf_op jit(solution)/shard_map/all_to_all | solution.py:185
  691.5 3.6 all-to-all-start.6
  698.5 16.6 %all-to-all-done.6 = bf16[1536,4,72]{2,1,0:T(4,128)(2,1)S(1)} async-done(((bf16[1536,4,72]{2,1,0:T(4,128)(2,1)}), bf16[1536,4,72]{2,1,0:T(4,128)(2,1)S(1)}, u32[]{:S(2)}, u32[]{:S(2)}) %all-to-all-start.6) | async-done | bytes 884768 | tf_op jit(solution)/shard_map/all_to_all | solution.py:182
  716.3 3.6 all-to-all-start.5
  725.5 14.4 %all-to-all-done.5 = bf16[1536,4,72]{2,1,0:T(4,128)(2,1)S(1)} async-done(((bf16[1536,4,72]{2,1,0:T(4,128)(2,1)}), bf16[1536,4,72]{2,1,0:T(4,128)(2,1)S(1)}, u32[]{:S(2)}, u32[]{:S(2)}) %all-to-all-start.5) | async-done | bytes 884768 | tf_op jit(solution)/shard_map/all_to_all | solution.py:181
  741.9 9.8 convolution_convert_fusion.2
  752.3 11.1 convolution_convert_fusion.1
  764.1 10.7 convolution_convert_fusion
  774.9 148.2 %fusion.4 = bf16[1152,1088]{0,1:T(8,128)(2,1)} fusion(bf16[1152,4304]{0,1:T(8,128)(2,1)} %convolution_convert_fusion), kind=kCustom, calls=%all-reduce-scatter | all-reduce-scatter fusion | flops 5013505 | bytes 12423680
  926.6 13.2 %concatenate.4 = bf16[1152,1124]{0,1:T(8,128)(2,1)} concatenate(bf16[1152,36]{0,1:T(8,128)(2,1)S(1)} %collective-permute-done, bf16[1152,1088]{0,1:T(8,128)(2,1)} %fusion.4), dimensions={1} | concatenate | bytes 5179392
  939.8 3.8 constant_dynamic-slice_fusion
  943.6 5.2 copy.231
  951.3 4.1 copy.227
  956.8 11.7 fusion.56
  976.2 8.2 fusion.89
  987.0 49.2 %all-reduce.3 = (f32[1152]{0:T(1024)}, f32[1152]{0:T(1024)}, f32[1152]{0:T(1024)}, f32[1152]{0:T(1024)}, f32[1152]{0:T(1024)}, /*index=5*/f32[1152]{0:T(1024)}, f32[1152]{0:T(1024)}, f32[4304]{0:T(1024)}, f32[1152]{0:T(1024)}) all-reduce(f32[1152]{0:T(1024)} %get-tuple-element.501, ...), channel_id=1, replica_groups=mesh['seq'=4,'fsdp'=8] {'seq','fsdp'}, use_global_device_ids=true, to_apply=%region_24.25 | all-reduce | flops 13520 | bytes 108160 | tf_op jit(solution)/shard_map/psum | solution.py:227
  1042.4 50.3 %reduce-scatter.24.cloned.1.call-done = bf16[144,288]{1,0:T(8,128)(2,1)} async-done(((bf16[1152,288]{1,0:T(8,128)(2,1)}), bf16[144,288]{1,0:T(8,128)(2,1)}) %reduce-scatter.24.cloned.1.call-update) | async-done | bytes 82960
  1094.4 67.3 %reduce-scatter.22.cloned.1.call-done = bf16[144,864]{1,0:T(8,128)(2,1)} async-done(((bf16[1152,864]{1,0:T(8,128)(2,1)}), bf16[144,864]{1,0:T(8,128)(2,1)}) %reduce-scatter.22.cloned.1.call-update) | async-done | bytes 248848
  1163.9 113.3 %all-reduce.6.cloned.1.call-done = bf16[4304,288]{0,1:T(8,128)(2,1)} async-done(((bf16[4304,288]{0,1:T(8,128)(2,1)}), bf16[4304,288]{0,1:T(8,128)(2,1)}) %all-reduce.6.cloned.1.call-update) | async-done | bytes 2479120
  (379 shorter events, 136.4 us)
Async XLA Ops:
  7.2 125.4 %copy-start.63 = (f32[1152]{0:T(1024)S(1)}, f32[1152]{0:T(1024)}, u32[]{:S(2)}) copy-start(f32[1152]{0:T(1024)} %param.30) | copy-start | bytes 13828
  7.2 125.4 %copy-start.33 = (f32[1152]{0:T(1024)S(1)}, f32[1152]{0:T(1024)}, u32[]{:S(2)}) copy-start(f32[1152]{0:T(1024)} %param.29) | copy-start | bytes 13828
  7.2 125.3 %all-gather.6.cloned.1.call-start = ((), (), s32[]{:S(2)}) async-start(), calls=%async_computation.14 | async-start | bytes 8957952 | tf_op jit(solution)/shard_map/all_gather | solution.py:59
  7.9 277.8 %all-gather.8.cloned.1.call-start = ((), (), s32[]{:S(2)}) async-start(), calls=%async_computation.15 | async-start | bytes 2985984 | tf_op jit(solution)/shard_map/all_gather | solution.py:60
  8.7 325.3 %all-gather.12.cloned.1.call-start = ((), (), s32[]{:S(2)}) async-start(), calls=%async_computation.20 | async-start | bytes 11280384 | tf_op jit(solution)/shard_map/all_gather | solution.py:62
  9.4 470.1 %all-gather.10.cloned.1.call-start = ((), (), s32[]{:S(2)}) async-start(), calls=%async_computation.16 | async-start | bytes 11280384 | tf_op jit(solution)/shard_map/all_gather | solution.py:61
  10.2 122.3 %copy-start.36 = (f32[384]{0:T(512)}, f32[384]{0:T(512)S(1)}, u32[]{:S(2)}) copy-start(f32[384]{0:T(512)S(1)} %broadcast_multiply_fusion.1) | copy-start | bytes 4612
  10.6 122.0 %copy-start.44 = (f32[384]{0:T(512)}, f32[384]{0:T(512)S(1)}, u32[]{:S(2)}) copy-start(f32[384]{0:T(512)S(1)} %fusion.67) | copy-start | bytes 4612
  10.6 121.9 %copy-start.49 = (f32[384]{0:T(512)}, f32[384]{0:T(512)S(1)}, u32[]{:S(2)}) copy-start(f32[384]{0:T(512)S(1)} %fusion.76) | copy-start | bytes 4612
  10.6 128.5 %copy-start.52 = (f32[1152]{0:T(1024)S(1)}, f32[1152]{0:T(1024)}, u32[]{:S(2)}) copy-start(f32[1152]{0:T(1024)} %param.32) | copy-start | bytes 13828
  10.6 128.5 %copy-start.53 = (f32[1152]{0:T(1024)S(1)}, f32[1152]{0:T(1024)}, u32[]{:S(2)}) copy-start(f32[1152]{0:T(1024)} %param.31) | copy-start | bytes 13828
  142.9 16.2 %all-to-all-start = ((bf16[384,16,72]{0,2,1:T(8,128)(2,1)}), bf16[384,16,72]{0,2,1:T(8,128)(2,1)S(1)}, u32[]{:S(2)}, u32[]{:S(2)}) async-start(bf16[384,16,72]{0,2,1:T(8,128)(2,1)} %bitcast.1), calls=%async_computation | async-start | bytes 1769472 | tf_op jit(solution)/shard_map/all_to_all | solution.py:75
  159.0 20.6 %copy-start.60 = (s32[1,384]{1,0:T(1,128)S(1)}, s32[1,384]{1,0:T(1,128)}, u32[]{:S(2)}) copy-start(s32[1,384]{1,0:T(1,128)} %param.22) | copy-start | bytes 4612
  159.0 34.8 %copy-start.58 = (s32[1,384]{1,0:T(1,128)S(1)}, s32[1,384]{1,0:T(1,128)}, u32[]{:S(2)}) copy-start(s32[1,384]{1,0:T(1,128)} %param.23) | copy-start | bytes 4612
  159.1 16.3 %all-to-all-start.1 = ((bf16[384,16,72]{0,2,1:T(8,128)(2,1)}), bf16[384,16,72]{0,2,1:T(8,128)(2,1)S(1)}, u32[]{:S(2)}, u32[]{:S(2)}) async-start(bf16[384,16,72]{0,2,1:T(8,128)(2,1)} %bitcast.4), calls=%async_computation.1 | async-start | bytes 1769472 | tf_op jit(solution)/shard_map/all_to_all | solution.py:76
  175.4 25.2 %copy-start.23 = (bf16[384,16,72]{0,2,1:T(8,128)(2,1)}, bf16[384,16,72]{0,2,1:T(8,128)(2,1)S(1)}, u32[]{:S(2)}) copy-start(bf16[384,16,72]{0,2,1:T(8,128)(2,1)S(1)} %all-to-all-done.1) | copy-start | bytes 2654212
  175.4 27.1 %all-to-all-start.2 = ((bf16[384,16,72]{0,2,1:T(8,128)(2,1)}), bf16[384,16,72]{0,2,1:T(8,128)(2,1)}, u32[]{:S(2)}, u32[]{:S(2)}) async-start(bf16[384,16,72]{0,2,1:T(8,128)(2,1)} %bitcast.7), calls=%async_computation.2 | async-start | bytes 1769472 | tf_op jit(solution)/shard_map/all_to_all | solution.py:77
  254.2 8.0 copy-start.59
  257.6 24.7 %all-to-all-start.3 = ((bf16[1536,4,72]{2,1,0:T(4,128)(2,1)}), bf16[1536,4,72]{2,1,0:T(4,128)(2,1)}, u32[]{:S(2)}, u32[]{:S(2)}) async-start(bf16[1536,4,72]{2,1,0:T(4,128)(2,1)} %bitcast.230), calls=%async_computation.3 | async-start | bytes 3145728 | tf_op jit(solution)/shard_map/all_to_all | solution.py:110
  262.2 250.9 %copy-start.39 = (f32[384]{0:T(512)}, f32[384]{0:T(512)S(1)}, u32[]{:S(2)}) copy-start(f32[384]{0:T(512)S(1)} %convert_reduce_fusion.6) | copy-start | bytes 4612
  289.3 223.1 %copy-start.42 = (f32[384]{0:T(512)}, f32[384]{0:T(512)S(1)}, u32[]{:S(2)}) copy-start(f32[384]{0:T(512)S(1)} %broadcast_multiply_fusion) | copy-start | bytes 4612
  290.9 43.2 %copy-start.46 = (f32[384]{0:T(512)}, f32[384]{0:T(512)S(1)}, u32[]{:S(2)}) copy-start(f32[384]{0:T(512)S(1)} %multiply_reduce_fusion.3) | copy-start | bytes 4612
  346.4 143.1 %copy-start.25 = (bf16[1,384,1152]{2,1,0:T(8,128)(2,1)S(1)}, bf16[1,384,1152]{2,1,0:T(8,128)(2,1)}, u32[]{:S(2)}) copy-start(bf16[1,384,1152]{2,1,0:T(8,128)(2,1)} %param.24) | copy-start | bytes 2654212
  479.6 10.0 copy-start.17
  489.6 12.4 copy-start.70
  489.6 12.4 copy-start.19
  489.6 12.4 copy-start.54
  489.6 12.3 copy-start.56
  502.0 10.5 copy-start.47
  519.1 16.2 %all-to-all-start.4 = ((bf16[384,16,72]{0,2,1:T(8,128)(2,1)}), bf16[384,16,72]{0,2,1:T(8,128)(2,1)S(1)}, u32[]{:S(2)}, u32[]{:S(2)}) async-start(bf16[384,16,72]{0,2,1:T(8,128)(2,1)} %bitcast.234), calls=%async_computation.4 | async-start | bytes 1769472 | tf_op jit(solution)/shard_map/all_to_all | solution.py:145
  522.6 426.2 %reduce-scatter.18.cloned.1.call-start = ((), (), s32[]{:S(2)}) async-start(), calls=%async_computation.18 | async-start | bytes 3317760 | tf_op jit(solution)/shard_map/reduce_scatter | solution.py:203
  551.3 10.1 slice-start
  553.3 8.1 slice-start.1
  553.3 8.1 slice-start.2
  567.8 11.7 slice-start.3
  591.6 10.1 slice-start
  593.6 8.1 slice-start.1
  593.6 8.1 slice-start.2
  608.1 12.2 slice-start.3
  632.4 10.1 slice-start
  634.4 8.1 slice-start.1
  634.4 8.1 slice-start.2
  648.9 12.2 slice-start.3
  667.9 23.6 %all-to-all-start.7 = ((bf16[1536,4,72]{2,1,0:T(4,128)(2,1)}), bf16[1536,4,72]{2,1,0:T(4,128)(2,1)S(1)}, u32[]{:S(2)}, u32[]{:S(2)}) async-start(bf16[1536,4,72]{2,1,0:T(4,128)(2,1)} %copy.209), calls=%async_computation.7 | async-start | bytes 3145728 | tf_op jit(solution)/shard_map/all_to_all | solution.py:185
  691.5 23.6 %all-to-all-start.6 = ((bf16[1536,4,72]{2,1,0:T(4,128)(2,1)}), bf16[1536,4,72]{2,1,0:T(4,128)(2,1)S(1)}, u32[]{:S(2)}, u32[]{:S(2)}) async-start(bf16[1536,4,72]{2,1,0:T(4,128)(2,1)} %copy.206), calls=%async_computation.6 | async-start | bytes 3145728 | tf_op jit(solution)/shard_map/all_to_all | solution.py:182
  716.3 23.6 %all-to-all-start.5 = ((bf16[1536,4,72]{2,1,0:T(4,128)(2,1)}), bf16[1536,4,72]{2,1,0:T(4,128)(2,1)S(1)}, u32[]{:S(2)}, u32[]{:S(2)}) async-start(bf16[1536,4,72]{2,1,0:T(4,128)(2,1)} %bitcast.229), calls=%async_computation.5 | async-start | bytes 3145728 | tf_op jit(solution)/shard_map/all_to_all | solution.py:181
  719.8 231.5 %reduce-scatter.16.cloned.1.call-start = ((), (), s32[]{:S(2)}) async-start(), calls=%async_computation.17 | async-start | bytes 9953280 | tf_op jit(solution)/shard_map/reduce_scatter | solution.py:200
  722.0 19.9 %copy-start.34 = (f32[1152]{0:T(1024)S(1)}, f32[1152]{0:T(1024)}, u32[]{:S(2)}) copy-start(f32[1152]{0:T(1024)} %param.29) | copy-start | bytes 13828
  722.0 19.9 %copy-start.37 = (f32[384]{0:T(512)S(1)}, f32[384]{0:T(512)}, u32[]{:S(2)}) copy-start(f32[384]{0:T(512)} %copy-done.36) | copy-start | bytes 4612
  722.0 19.9 %copy-start.50 = (f32[384]{0:T(512)S(1)}, f32[384]{0:T(512)}, u32[]{:S(2)}) copy-start(f32[384]{0:T(512)} %copy-done.49) | copy-start | bytes 4612
  722.0 19.9 %copy-start.64 = (f32[1152]{0:T(1024)S(1)}, f32[1152]{0:T(1024)}, u32[]{:S(2)}) copy-start(f32[1152]{0:T(1024)} %param.30) | copy-start | bytes 13828
  751.7 224.1 %reduce-scatter.20.cloned.1.call-start = ((), (), s32[]{:S(2)}) async-start(), calls=%async_computation.19 | async-start | bytes 12533760 | tf_op jit(solution)/shard_map/reduce_scatter | solution.py:209
  763.4 276.7 %reduce-scatter.26.cloned.1.call-start = ((), (), s32[]{:S(2)}) async-start(), calls=%async_computation.23 | async-start | bytes 2985984
  774.9 150.5 %copy-start.61 = (u32[32]{0:T(128)S(1)}, u32[32]{0:T(128)}, u32[]{:S(2)}) copy-start(u32[32]{0:T(128)} %constant.95) | copy-start | bytes 388
  924.0 2.6 collective-permute-start
  948.8 143.8 %reduce-scatter.24.cloned.1.call-start = ((), (), s32[]{:S(2)}) async-start(), calls=%async_computation.22 | async-start | bytes 995328
  951.2 210.5 %reduce-scatter.22.cloned.1.call-start = ((), (), s32[]{:S(2)}) async-start(), calls=%async_computation.21 | async-start | bytes 2322432
  955.5 321.7 %all-reduce.6.cloned.1.call-start = ((), (), s32[]{:S(2)}) async-start(), calls=%async_computation.24 | async-start | bytes 5013504
  976.2 8.2 copy-start.45
  976.2 9.4 copy-start.16
  976.2 9.4 copy-start.38
  976.2 9.4 copy-start.51
  984.4 52.5 %copy-start.13 = (f32[384,1152]{1,0:T(8,128)S(1)}, f32[384,1152]{1,0:T(8,128)}, u32[]{:S(2)}) copy-start(f32[384,1152]{1,0:T(8,128)} %copy-done.12) | copy-start | bytes 5308420
  984.4 52.5 %copy-start.26 = (bf16[1,384,1152]{2,1,0:T(8,128)(2,1)S(1)}, bf16[1,384,1152]{2,1,0:T(8,128)(2,1)}, u32[]{:S(2)}) copy-start(bf16[1,384,1152]{2,1,0:T(8,128)(2,1)} %param.24) | copy-start | bytes 2654212
  (72 other events, 290.7 us)
Sparse Core Ops, SparseCore 0:
  10.2 122.2 all-gather.5
  134.7 53.1 all-gather.7
  190.2 143.8 all-gather.11
  336.1 143.4 all-gather.9
  527.4 33.5 reduce-scatter.17
  751.8 101.4 reduce-scatter.15
  856.1 96.7 reduce-scatter.19
  957.0 71.6 reduce-scatter.25
  1032.2 60.4 reduce-scatter.23
  1096.0 65.6 reduce-scatter.21
  1165.4 111.7 all-reduce.5
where the time goes:
time: 1290 us
  waiting for transfers between devices  627 us (49%)
  blocking collectives  217 us (17%)
  matrix products  210 us (16%)
  local copies, waits for them, and re-layouts  124 us (10%)
  other arithmetic  56.4 us (4%)
  starting transfers between devices  31.8 us (2%)
  between operations  16.2 us (1%)
    unnamed x16, waiting for transfers between devices  234 us
    unnamed x1, blocking collectives  148 us
    all_gather x1, waiting for transfers between devices, local(): lax.all_gather(w_up, 'fsdp', axis=0, tiled=True)  133 us
    all_gather x1, waiting for transfers between devices, local(): lax.all_gather(w_qkv, 'fsdp', axis=0, tiled=True)  122 us
    unnamed x129, local copies, waits for them, and re-layouts  61.6 us
    psum x1, blocking collectives, local(): lax.psum((sum_ln1_gain, sum_ln1_shift, sum_q_bias, sum_v_bias, sum_out_bi...  49.2 us
    all_gather x1, waiting for transfers between devices, local(): lax.all_gather(w_down, 'fsdp', axis=0, tiled=True)  42.6 us
    dot_general x6, matrix products, block_scores(): jnp.einsum('qhd,khd->hqk', query_block, k_heads, preferred_element_type=j...  32.4 us
  transfers between devices with their start and end apart: 20, of which 13 were waited for; matrix products, arithmetic and copies ran while one was open for 37% of the time, Pallas kernels for 0%

commit v1 on v0

v1 whole, which is shorter than its diff:
```python
import functools
import math

import jax
import jax.numpy as jnp
from jax import lax
from jax.experimental import pallas as pl
from jax.experimental.pallas import tpu as pltpu
from jax.sharding import PartitionSpec as P

HEADS = 16
HD = 72
EPSILON = 1e-06
SCALING = HD ** (-0.5)
LOG2E = math.log2(math.e)
NEG = -1e30
BF = jnp.bfloat16
F32 = jnp.float32


def windows(heads, width):
    out = []
    for h in range(heads):
        lo = h * HD // 128 * 128
        out.append((lo, min(width, -(-(h * HD + HD) // 128) * 128)))
    return out


def head_lanes(lo, h, shape):
    lane = lax.broadcasted_iota(jnp.int32, shape, 1) + lo
    return (lane >= h * HD) & (lane < h * HD + HD)


def head_pieces(wins, outs):
    pieces = {}
    for (lo, hi), out in zip(wins, outs):
        for c in range(lo, hi, 128):
            part = out[:, c - lo : min(c + 128, hi) - lo]
            pieces[c] = part if c not in pieces else pieces[c] + part
    return pieces.items()


def lanes(width):
    return -(-width // 128) * 128


def load_blocks(blocks, target, slots, first, sems):
    rows = blocks[0].shape[0]
    copies = []
    for i, block in enumerate(blocks):
        start = pl.multiple_of(slots[first + i] * rows, 8)
        copies.append(pltpu.make_async_copy(block, target.at[pl.ds(start, rows)], sems.at[i]))
        copies[-1].start()
    for copy in copies:
        copy.wait()


def forward_kernel(heads, tile, bounds, q_ref, k_ref, v_ref, qid_ref, kid_ref, o_ref, lse_ref, s_ref):
    i = pl.program_id(0)
    lo, hi = bounds[0, i], bounds[1, i]
    wins = windows(heads, q_ref.shape[1])
    rel = lax.broadcasted_iota(jnp.int32, (tile, tile), 0) - lax.broadcasted_iota(jnp.int32, (tile, tile), 1)
    qid = jnp.concatenate([qid_ref[...]] * (tile // 128), axis=1)
    queries = []
    for h, (a, b) in enumerate(wins):
        w = q_ref[:, a:b]
        queries.append(jnp.where(head_lanes(a, h, w.shape), w, jnp.zeros_like(w)))

    def scores(t, tops):
        rows = pl.ds(pl.multiple_of(t * tile, tile), tile)
        allowed = (qid == kid_ref[:, rows]) | (rel == (t - i) * tile)
        new = []
        for h, (a, b) in enumerate(wins):
            s = lax.dot_general(queries[h], k_ref[rows, a:b], (((1,), (1,)), ((), ())), preferred_element_type=F32)
            s = jnp.where(allowed, s * (SCALING * LOG2E), NEG)
            s_ref[h, :, rows] = s
            top = tops[h]
            for c in range(0, tile, 128):
                top = jnp.maximum(top, s[:, c : c + 128])
            new.append(top)
        return tuple(new)

    tops = lax.fori_loop(lo, hi, scores, tuple(jnp.full((tile, 128), NEG, F32) for _ in range(heads)))
    tops = [jnp.broadcast_to(jnp.max(t, axis=1, keepdims=True), (tile, 128)) for t in tops]

    def attend(t, carry):
        rows = pl.ds(pl.multiple_of(t * tile, tile), tile)
        new = []
        for h, (a, b) in enumerate(wins):
            total, acc = carry[h]
            p = jnp.exp2(s_ref[h, :, rows] - jnp.concatenate([tops[h]] * (tile // 128), axis=1))
            for c in range(0, tile, 128):
                total = total + p[:, c : c + 128]
            acc = acc + jnp.dot(p.astype(BF), v_ref[rows, a:b], preferred_element_type=F32)
            new.append((total, acc))
        return tuple(new)

    start = tuple((jnp.zeros((tile, 128), F32), jnp.zeros((tile, b - a), F32)) for a, b in wins)
    carry = lax.fori_loop(lo, hi, attend, start)
    lane = lax.broadcasted_iota(jnp.int32, (tile, 128), 1)
    lse = jnp.zeros((tile, 128), F32)
    outs = []
    for h, (a, b) in enumerate(wins):
        total = jnp.sum(carry[h][0], axis=1, keepdims=True)
        out = carry[h][1] * (1.0 / total)
        outs.append(jnp.where(head_lanes(a, h, out.shape), out, 0.0))
        lse = jnp.where(lane == h, tops[h] + jnp.log2(total), lse)
    for c, part in head_pieces(wins, outs):
        o_ref[:, c : c + part.shape[1]] = part.astype(BF)
    lse_ref[...] = lse


def whole_block(shape):
    return pl.BlockSpec(shape, lambda *_: (0, 0))


def kept_block(shape):
    return pl.BlockSpec(shape, lambda *_: (0, 0), pipeline_mode=pl.Buffered(1))


def row_block(tile, width):
    return pl.BlockSpec((tile, width), lambda i, *_: (i, 0))


def slot_block(tile, width):
    return pl.BlockSpec((tile, width), lambda i, slots: (slots[i], 0))


def attention_forward(q, k, v, qid, kid, bounds, heads, tile):
    n, width = q.shape
    return pl.pallas_call(
        functools.partial(forward_kernel, heads, tile),
        out_shape=(jax.ShapeDtypeStruct((n, width), BF), jax.ShapeDtypeStruct((n, 128), F32)),
        grid_spec=pltpu.PrefetchScalarGridSpec(
            num_scalar_prefetch=1,
            grid=(n // tile,),
            in_specs=[
                row_block(tile, width),
                whole_block((n, width)),
                whole_block((n, width)),
                row_block(tile, 128),
                whole_block((1, n)),
            ],
            out_specs=[row_block(tile, width), row_block(tile, 128)],
            scratch_shapes=[pltpu.VMEM((heads, tile, n), F32)],
        ),
        compiler_params=pltpu.CompilerParams(vmem_limit_bytes=48 << 20),
        cost_estimate=pl.CostEstimate(flops=4 * n * n * 128 * heads, bytes_accessed=10 * n * width, transcendentals=n * n * heads),
        name="attention_forward",
    )(bounds, q, k, v, qid, kid)


def backward_kernel(
    heads, tile, count, bounds, slots, q_ref, k_ref, v_ref, o_ref, lse_ref, qid_ref, kid_ref, *refs
):
    blocks, (out_ref, go_ref, dk_acc, dv_acc, dq_acc, sems) = refs[:count], refs[count:]
    i = pl.program_id(0)
    lo, hi = bounds[0, i], bounds[1, i]
    width = q_ref.shape[1]
    wins = windows(heads, width)

    @pl.when(i == 0)
    def _():
        load_blocks(blocks, go_ref, slots, 0, sems)
        dk_acc[...] = jnp.zeros_like(dk_acc)
        dv_acc[...] = jnp.zeros_like(dv_acc)

    here = pl.ds(pl.multiple_of(i * tile, tile), tile)
    rel = lax.broadcasted_iota(jnp.int32, (tile, tile), 1) - lax.broadcasted_iota(jnp.int32, (tile, tile), 0)
    lane = lax.broadcasted_iota(jnp.int32, (tile, 128), 1)
    inner = jnp.zeros((tile, 128), F32)
    queries, grads = [], []
    for h, (a, b) in enumerate(wins):
        w, g = q_ref[:, a:b], go_ref[here, a:b]
        on = head_lanes(a, h, w.shape)
        queries.append(jnp.where(on, w, jnp.zeros_like(w)))
        g = jnp.where(on, g, jnp.zeros_like(g))
        grads.append(g)
        r = jnp.sum(o_ref[:, a:b].astype(F32) * g.astype(F32), axis=1, keepdims=True)
        inner = jnp.where(lane == h, r, inner)
        dq_acc[h, :, : b - a] = jnp.zeros((tile, b - a), F32)
    inner = inner.T
    lse = lse_ref[...].T
    qid = qid_ref[...]

    def step(t, carry):
        rows = pl.ds(pl.multiple_of(t * tile, tile), tile)
        allowed = (jnp.concatenate([kid_ref[rows, :]] * (tile // 128), axis=1) == qid) | (rel == (t - i) * tile)
        for h, (a, b) in enumerate(wins):
            key = k_ref[rows, a:b]
            s = lax.dot_general(key, queries[h], (((1,), (1,)), ((), ())), preferred_element_type=F32)
            p = jnp.exp2(jnp.where(allowed, s * (SCALING * LOG2E) - lse[h : h + 1, :], NEG))
            dp = lax.dot_general(v_ref[rows, a:b], grads[h], (((1,), (1,)), ((), ())), preferred_element_type=F32)
            ds = (p * (dp - inner[h : h + 1, :])).astype(BF)
            dv_acc[rows, a:b] += jnp.dot(p.astype(BF), grads[h], preferred_element_type=F32)
            dk_acc[rows, a:b] += jnp.dot(ds, queries[h], preferred_element_type=F32)
            dq_acc[h, :, : b - a] += lax.dot_general(ds, key, (((0,), (0,)), ((), ())), preferred_element_type=F32)
        return carry

    lax.fori_loop(lo, hi, step, 0)
    outs = []
    for h, (a, b) in enumerate(wins):
        outs.append(jnp.where(head_lanes(a, h, (tile, b - a)), dq_acc[h, :, : b - a] * SCALING, 0.0))
    for c, part in head_pieces(wins, outs):
        out_ref[here, c : c + part.shape[1]] = part.astype(BF)

    @pl.when(i == pl.num_programs(0) - 1)
    def _():
        out_ref[:, width : 2 * width] = (dk_acc[...] * SCALING).astype(BF)
        out_ref[:, 2 * width : 3 * width] = dv_acc[...].astype(BF)
        padding = out_ref.shape[1] - 3 * width
        if padding:
            out_ref[:, 3 * width :] = jnp.zeros((out_ref.shape[0], padding), BF)


def attention_backward(q, k, v, o, go_blocks, slots, lse, qid, kid, bounds, heads, tile):
    n, width = q.shape
    count = len(go_blocks)
    return pl.pallas_call(
        functools.partial(backward_kernel, heads, tile, count),
        out_shape=jax.ShapeDtypeStruct((n, lanes(3 * width)), BF),
        grid_spec=pltpu.PrefetchScalarGridSpec(
            num_scalar_prefetch=2,
            grid=(n // tile,),
            in_specs=[
                row_block(tile, width),
                whole_block((n, width)),
                whole_block((n, width)),
                row_block(tile, width),
                row_block(tile, 128),
                pl.BlockSpec((1, tile), lambda i, *_: (0, i)),
                whole_block((n, 128)),
            ]
            + [pl.BlockSpec(memory_space=pl.ANY)] * count,
            out_specs=whole_block((n, lanes(3 * width))),
            scratch_shapes=[
                pltpu.VMEM((n, width), BF),
                pltpu.VMEM((n, width), F32),
                pltpu.VMEM((n, width), F32),
                pltpu.VMEM((heads, tile, 256), F32),
                pltpu.SemaphoreType.DMA((count,)),
            ],
        ),
        compiler_params=pltpu.CompilerParams(vmem_limit_bytes=48 << 20),
        cost_estimate=pl.CostEstimate(flops=10 * n * n * 128 * heads, bytes_accessed=16 * n * width, transcendentals=n * n * heads),
        name="attention_backward",
    )(bounds, slots, q, k, v, o, lse, qid, kid, *go_blocks)


def tile_bounds(ids, tile):
    first, last = ids[::tile], ids[tile - 1 :: tile]
    lo = jnp.sum((last[None, :] < first[:, None]).astype(jnp.int32), axis=1)
    hi = jnp.sum((first[None, :] <= last[:, None]).astype(jnp.int32), axis=1)
    return jnp.stack([lo, hi])


def normalise(values):
    average = jnp.mean(values, axis=-1, keepdims=True)
    centred = values - average
    spread = jnp.mean(centred * centred, axis=-1, keepdims=True)
    inverse = lax.rsqrt(spread + EPSILON)
    return centred * inverse, inverse


def norm_back(normal, inverse, gain, grad):
    scaled = grad * gain
    first = jnp.mean(scaled, axis=-1, keepdims=True)
    second = jnp.mean(scaled * normal, axis=-1, keepdims=True)
    return (scaled - first - normal * second) * inverse


def gelu_both(u):
    root = math.sqrt(2.0 / math.pi)
    bent = jnp.tanh(root * (u + 0.044715 * u * u * u))
    half = 0.5 * (1.0 + bent)
    slope = half + 0.5 * u * (1.0 - bent * bent) * (root + 3 * 0.044715 * root * u * u)
    return u * half, slope


def dot(a, b):
    return jnp.dot(a, b, preferred_element_type=F32)


def dot_bt(a, b):
    return lax.dot_general(a, b, (((1,), (1,)), ((), ())), preferred_element_type=F32)


def dot_at(a, b):
    return lax.dot_general(a, b, (((0,), (0,)), ((), ())), preferred_element_type=F32)


def project_kernel(count, bands, slots, *refs):
    xs, pieces = refs[:count], refs[count : count + bands]
    gain, shift, q_bias, v_bias, x_out, h_out, q_out, k_out, v_out, w_out, x_now, sems = refs[count + bands :]
    j = pl.program_id(0)

    @pl.when(j == 0)
    def _():
        load_blocks(pieces, w_out, slots, count, sems)

    for i in range(count):

        @pl.when(j == i)
        def _(i=i):
            x_now[...] = xs[i][...]

    x = x_now[...]
    x_out[...] = x
    normal, _ = normalise(x.astype(F32))
    h = (normal * gain[...] + shift[...]).astype(BF)
    h_out[...] = h
    projected = dot(h, w_out[...])
    width = q_out.shape[1]
    q_out[...] = (projected[:, :width] + q_bias[...]).astype(BF)
    k_out[...] = projected[:, width : 2 * width].astype(BF)
    v_out[...] = (projected[:, 2 * width : 3 * width] + v_bias[...]).astype(BF)


def project(xs, pieces, slots, gain, shift, q_bias, v_bias):
    rows, width = xs[0].shape
    count, bands, cols = len(xs), len(pieces), q_bias.shape[1]
    n, columns = rows * count, pieces[0].shape[1]
    shape = jax.ShapeDtypeStruct
    return pl.pallas_call(
        functools.partial(project_kernel, count, bands),
        out_shape=[shape((n, width), BF)] * 2 + [shape((n, cols), BF)] * 3 + [shape((width, columns), BF)],
        grid_spec=pltpu.PrefetchScalarGridSpec(
            num_scalar_prefetch=1,
            grid=(count,),
            in_specs=[kept_block((rows, width))] * count
            + [pl.BlockSpec(memory_space=pl.ANY)] * bands
            + [kept_block((1, width))] * 2
            + [kept_block((1, cols))] * 2,
            out_specs=[slot_block(rows, width)] * 2
            + [slot_block(rows, cols)] * 3
            + [whole_block((width, columns))],
            scratch_shapes=[pltpu.VMEM((rows, width), BF), pltpu.SemaphoreType.DMA((bands,))],
        ),
        compiler_params=pltpu.CompilerParams(vmem_limit_bytes=48 << 20),
        cost_estimate=pl.CostEstimate(flops=2 * n * width * columns, bytes_accessed=8 * n * width, transcendentals=n),
        name="norm_project",
    )(slots, *xs, *pieces, gain, shift, q_bias, v_bias)


def widen_kernel(count, bands, slots, x_ref, *refs):
    os, pieces = refs[:count], refs[count : count + bands]
    (out_bias, gain, shift, w_up, up_bias, x_out, o_out, h_out, a_out, slope_out, w_out, o_now, sems) = refs[count + bands :]
    j = pl.program_id(0)
    cols = os[0].shape[1]

    @pl.when(j == 0)
    def _():
        load_blocks(pieces, w_out, slots, count, sems)

    for v in range(count):

        @pl.when(slots[0] == v)
        def _(v=v):
            for i in range(count):
                o_now[:, (v ^ i) * cols : (v ^ i) * cols + cols] = os[i][...]

    o = o_now[...]
    x = x_ref[...].astype(F32) + (dot(o, w_out[...]) + out_bias[...])

    @pl.when(j == 0)
    def _():
        x_out[...] = x
        o_out[...] = o

    normal, _ = normalise(x)
    h = (normal * gain[...] + shift[...]).astype(BF)
    h_out[...] = h
    value, slope = gelu_both(dot(h, w_up[...]) + up_bias[...])
    a_out[...] = value.astype(BF)
    slope_out[...] = slope


def widen(x_all, os, pieces, slots, out_bias, gain, shift, w_up, up_bias, rows):
    n, width = x_all.shape
    count, bands, cols, hidden = len(os), len(pieces), os[0].shape[1], w_up.shape[1]
    shape = jax.ShapeDtypeStruct
    return pl.pallas_call(
        functools.partial(widen_kernel, count, bands),
        out_shape=[
            shape((rows, width), F32),
            shape((rows, width), BF),
            shape((n, width), BF),
            shape((n, hidden), BF),
            shape((n, hidden), F32),
            shape((width, width), BF),
        ],
        grid_spec=pltpu.PrefetchScalarGridSpec(
            num_scalar_prefetch=1,
            grid=(count,),
            in_specs=[slot_block(rows, width)]
            + [slot_block(rows, cols)] * count
            + [pl.BlockSpec(memory_space=pl.ANY)] * bands
            + [kept_block((1, width))] * 3
            + [kept_block((width, hidden)), kept_block((1, hidden))],
            out_specs=[whole_block((rows, width))] * 2
            + [row_block(rows, width)]
            + [row_block(rows, hidden)] * 2
            + [whole_block((width, width))],
            scratch_shapes=[pltpu.VMEM((rows, width), BF), pltpu.SemaphoreType.DMA((bands,))],
        ),
        compiler_params=pltpu.CompilerParams(vmem_limit_bytes=56 << 20),
        cost_estimate=pl.CostEstimate(flops=2 * n * width * (width + hidden), bytes_accessed=16 * n * width, transcendentals=n * hidden),
        name="out_norm_up",
    )(slots, x_all, *os, *pieces, out_bias, gain, shift, w_up, up_bias)


def narrow_kernel(gy_ref, a_ref, slope_ref, w_up, w_down, gu_out, dh_out, y_out, sum_out):
    @pl.when(pl.program_id(0) == 0)
    def _():
        sum_out[...] = jnp.zeros_like(sum_out)

    gu = (dot(gy_ref[...], w_down[...]) * slope_ref[...]).astype(BF)
    gu_out[...] = gu
    dh_out[...] = dot_bt(gu, w_up[...]).astype(BF)
    y_out[...] = dot_bt(a_ref[...], w_down[...]).astype(BF)
    sum_out[...] += jnp.sum(gu.astype(F32), axis=0, keepdims=True)


def narrow(gy, active, slope, w_up, w_down, rows):
    n, width = gy.shape
    hidden = w_up.shape[1]
    shape = jax.ShapeDtypeStruct
    return pl.pallas_call(
        narrow_kernel,
        out_shape=[shape((n, hidden), BF), shape((n, width), BF), shape((n, width), BF), shape((1, hidden), F32)],
        grid_spec=pl.GridSpec(
            grid=(n // rows,),
            in_specs=[row_block(rows, width)] + [row_block(rows, hidden)] * 2 + [kept_block((width, hidden))] * 2,
            out_specs=[row_block(rows, hidden)] + [row_block(rows, width)] * 2 + [whole_block((1, hidden))],
        ),
        compiler_params=pltpu.CompilerParams(vmem_limit_bytes=56 << 20),
        cost_estimate=pl.CostEstimate(flops=6 * n * width * hidden, bytes_accessed=16 * n * width, transcendentals=0),
        name="down_and_back",
    )(gy, active, slope, w_up, w_down)


def middle_kernel(count, terms, slots, *refs):
    parts, (x_ref, gy_ref, gain, w_out, dx_out, sum_out) = refs[:terms], refs[terms : terms + 6]
    go_outs, ga_outs = refs[terms + 6 : terms + 6 + count], refs[terms + 6 + count :]
    grad = sum(part[...].astype(F32) for part in parts)
    normal, inverse = normalise(x_ref[...])
    dx = gy_ref[...].astype(F32) + norm_back(normal, inverse, gain[...], grad)
    dx_out[...] = dx
    ga = dx.astype(BF)
    sum_out[0:1, :] = jnp.sum(grad * normal, axis=0, keepdims=True)
    sum_out[1:2, :] = jnp.sum(grad, axis=0, keepdims=True)
    sum_out[2:3, :] = jnp.sum(ga.astype(F32), axis=0, keepdims=True)
    go = dot_bt(ga, w_out[...]).astype(BF)
    cols = go_outs[0].shape[1]
    for v in range(count):

        @pl.when(slots[0] == v)
        def _(v=v):
            for i in range(count):
                start = (v ^ i) * cols
                go_outs[i][...] = go[:, start : start + cols]
                ga_outs[i][...] = ga[:, start : start + cols]


def middle(parts, x_one, gy, gain, w_out, slots, count):
    rows, width = x_one.shape
    cols, terms = width // count, len(parts)
    shape = jax.ShapeDtypeStruct
    block = kept_block((rows, width))
    outs = pl.pallas_call(
        functools.partial(middle_kernel, count, terms),
        out_shape=[shape((rows, width), F32), shape((8, width), F32)] + [shape((rows, cols), BF)] * (2 * count),
        grid_spec=pltpu.PrefetchScalarGridSpec(
            num_scalar_prefetch=1,
            grid=(1,),
            in_specs=[block] * (terms + 2) + [kept_block((1, width)), kept_block((width, width))],
            out_specs=[whole_block((rows, width)), whole_block((8, width))] + [whole_block((rows, cols))] * (2 * count),
        ),
        compiler_params=pltpu.CompilerParams(vmem_limit_bytes=48 << 20),
        cost_estimate=pl.CostEstimate(flops=2 * rows * width * width, bytes_accessed=20 * rows * width, transcendentals=rows),
        name="norm_back_out",
    )(slots, *parts, x_one, gy, gain, w_out)
    return outs[0], outs[1], outs[2 : 2 + count], outs[2 + count :]


def swap(value, axis, bits):
    size = lax.axis_size(axis)
    return lax.ppermute(value, axis, [(i, i ^ bits) for i in range(size)])


def seq_gather(block):
    size = lax.axis_size("seq")
    got = [None] * size
    got[0] = block
    for far in range(2, size, 2):
        got[far] = swap(block, "seq", far)
    for j in range(0, size, 2):
        got[j + 1] = swap(got[j], "seq", 1)
    return got


def seq_scatter(part):
    size = lax.axis_size("seq")
    terms = []
    for j in [*range(2, size, 2), 0]:
        terms.append(swap(part(j + 1).astype(BF), "seq", 1))
    totals = []
    for j, got in zip(range(2, size, 2), terms):
        held = (part(j).astype(F32) + got.astype(F32)).astype(BF)
        totals.append(swap(held, "seq", j))
    return [part(0), terms[-1], *totals]


def add_up(terms):
    return sum(term.astype(F32) for term in terms)


def ring_order(size):
    half = size // 2
    return [2 * p if p < half else 2 * (size - 1 - p) + 1 for p in range(size)]


def ring_index(pos, size):
    pos = pos % size
    return jnp.where(pos < size // 2, 2 * pos, 2 * (size - 1 - pos) + 1)


def ring_perms(size):
    order = ring_order(size)
    ahead = [(order[p], order[(p + 1) % size]) for p in range(size)]
    return ahead, [(b, a) for a, b in ahead]


def ring_position(size):
    f = lax.axis_index("fsdp")
    return jnp.where(f % 2 == 0, f // 2, size - 1 - f // 2)


def ring_gather(block):
    size = lax.axis_size("fsdp")
    ahead, back = ring_perms(size)
    pos = ring_position(size)
    pieces, owners = [block], [ring_index(pos, size)]
    one, two = block, block
    for t in range(1, size // 2 + 1):
        one = lax.ppermute(one, "fsdp", ahead)
        pieces.append(one)
        owners.append(ring_index(pos - t, size))
        if t < size // 2:
            two = lax.ppermute(two, "fsdp", back)
            pieces.append(two)
            owners.append(ring_index(pos + t, size))
    return pieces, owners


def ring_scatter_sum(part):
    size = lax.axis_size("fsdp")
    ahead, back = ring_perms(size)
    pos = ring_position(size)
    half = size // 2
    one = part(ring_index(pos + half, size)).astype(BF)
    two = part(ring_index(pos - (half - 1), size)).astype(BF)
    for t in range(1, half):
        one = lax.ppermute(one, "fsdp", ahead)
        one = (one.astype(F32) + part(ring_index(pos + half - t, size))).astype(BF)
        two = lax.ppermute(two, "fsdp", back)
        if t < half - 1:
            two = (two.astype(F32) + part(ring_index(pos - (half - 1) + t, size))).astype(BF)
    one = lax.ppermute(one, "fsdp", ahead)
    return part(ring_index(pos, size)) + one.astype(F32) + two.astype(F32)


def total_sum(vector):
    for axis in ("seq", "fsdp"):
        bits = 1
        while bits < lax.axis_size(axis):
            vector = vector + swap(vector, axis, bits)
            bits *= 2
    return vector


def local(
    inputs, image_ids, pad_mask, cotangent, w_qkv, w_out, w_up, w_down, ln1_gain, ln1_shift,
    q_bias, v_bias, out_bias, ln2_gain, ln2_shift, up_bias, down_bias,
):
    ns, nf = lax.axis_size("seq"), lax.axis_size("fsdp")
    s, f = lax.axis_index("seq"), lax.axis_index("fsdp")
    rows, width = inputs.shape[1:]
    n = rows * ns
    hidden = w_up.shape[1]
    mine = hidden // ns
    wide = lanes(mine)
    cols = width // ns
    band = w_up.shape[0]
    ratio = nf // ns
    heads = HEADS // ns
    tile = 256
    order = [s ^ j for j in range(ns)]

    def pad_lanes(array, size):
        return jnp.pad(array, ((0, 0), (0, size - array.shape[1])))

    down_t = w_down.T
    both = ("seq", "fsdp")
    pieces = []
    for c in range(ratio):
        perm = []
        for ss in range(ns):
            for ff in range(nf):
                e = (ff % ratio - c) % ratio
                perm.append((ss * nf + ff, (ff // ratio) * nf + ratio * ss + e))
        e = (f % ratio - c) % ratio
        piece = lax.dynamic_slice_in_dim(down_t, (ratio * s + e) * band, band, axis=0)
        pieces.append(lax.ppermute(piece, both, perm))
    blocks = []
    for h in range(ratio):
        block = pieces[0]
        for c in range(1, ratio):
            block = jnp.where((f % ratio + c) % ratio == h, pieces[c], block)
        blocks.append(block)
    down_mine = pad_lanes(jnp.concatenate(blocks, axis=1), wide)

    x_own = inputs[0]
    x_blocks = seq_gather(x_own)
    code_blocks = seq_gather(image_ids * 2 + pad_mask)
    qkv_mine = pad_lanes(
        jnp.concatenate(
            [lax.dynamic_slice_in_dim(w_qkv, t * width + s * cols, cols, axis=1) for t in range(3)], axis=1
        ),
        lanes(3 * cols),
    )
    qkv_pieces, owners = ring_gather(qkv_mine)
    out_pieces, _ = ring_gather(w_out)
    slots = jnp.stack([jnp.asarray(i, jnp.int32) for i in order + owners])
    up_mine = pad_lanes(lax.dynamic_slice_in_dim(w_up, s * mine, mine, axis=1), wide)
    full_up = lax.all_gather(up_mine, "fsdp", axis=0, tiled=True)
    full_down = lax.all_gather(down_mine, "fsdp", axis=0, tiled=True)

    keep = (1 - pad_mask[0]).astype(F32)[:, None]
    gy_own = (cotangent[0].astype(F32) * keep).astype(BF)
    gy_rel = jnp.concatenate(seq_gather(gy_own), axis=0)

    codes = jnp.zeros((n,), jnp.int32)
    for j in range(ns):
        codes = lax.dynamic_update_slice(codes, code_blocks[j][0], (order[j] * rows,))
    ids = codes // 2
    key_ids = jnp.where(codes % 2 == 0, ids, -1)
    bounds = tile_bounds(ids, tile)
    ids_col = jnp.broadcast_to(ids[:, None], (n, 128))
    keys_col = jnp.broadcast_to(key_ids[:, None], (n, 128))

    def row(vector):
        return vector[None, :]

    q_part = row(lax.dynamic_slice_in_dim(q_bias, s * cols, cols))
    v_part = row(lax.dynamic_slice_in_dim(v_bias, s * cols, cols))
    x_all, h_one, q, k, v, full_qkv = project(x_blocks, qkv_pieces, slots, row(ln1_gain), row(ln1_shift), q_part, v_part)
    o, lse = attention_forward(q, k, v, ids_col, key_ids[None], bounds, heads, tile)

    up_part = pad_lanes(row(lax.dynamic_slice_in_dim(up_bias, s * mine, mine)), wide)
    x_one, o_own, h_two, active, slope, full_out = widen(
        x_all, seq_gather(o), out_pieces, slots, row(out_bias), row(ln2_gain), row(ln2_shift), full_up, up_part, rows
    )
    gu, dh_two, mixed, sum_up = narrow(gy_rel, active, slope, full_up, full_down, rows)

    def block_of(array):
        return lambda j: array[j * rows : (j + 1) * rows]

    dx_one, sums_two, go_parts, ga_parts = middle(
        seq_scatter(block_of(dh_two)), x_one, gy_own, row(ln2_gain), full_out, slots, ns
    )
    go_blocks = [part if j == 0 else swap(part, "seq", j) for j, part in enumerate(go_parts)]

    gqkv = attention_backward(q, k, v, o, go_blocks, slots, lse, ids[None], keys_col, bounds, heads, tile)
    grad_qkv_part = dot_at(h_one, gqkv).astype(BF)
    dh_one_part = dot_bt(gqkv, full_qkv).astype(BF)

    layer_out = (x_one + add_up(seq_scatter(block_of(mixed))) + down_bias).astype(BF)
    grad_up_part = dot_at(h_two, gu).astype(BF)
    grad_down_part = dot_at(gy_rel, active).astype(BF)
    sum_down_bias = jnp.sum(gy_own.astype(F32), axis=0)

    def bands(*arrays):
        return lambda owner: jnp.stack(
            [lax.dynamic_slice_in_dim(a, owner * band, band, axis=0).astype(F32) for a in arrays]
        )

    grad_up, grad_down_t = ring_scatter_sum(bands(grad_up_part, grad_down_part))
    grad_up = grad_up[:, :mine]
    grad_down_t = grad_down_t[:, :mine].astype(BF)
    grad_out_part = add_up(seq_scatter(lambda j: dot_at(o_own, ga_parts[j]))).astype(BF)
    grad_out = ring_scatter_sum(bands(grad_out_part))[0]

    got = []
    for c in range(ratio):
        perm = []
        for ss in range(ns):
            for ff in range(nf):
                h = (ff % ratio + c) % ratio
                perm.append((ss * nf + ff, (ff // ratio) * nf + ratio * ss + h))
        h = (f % ratio + c) % ratio
        piece = lax.dynamic_slice_in_dim(grad_down_t, h * w_down.shape[0], w_down.shape[0], axis=1)
        got.append(lax.ppermute(piece, both, perm))
    blocks = []
    for e in range(ratio):
        block = got[0]
        for c in range(1, ratio):
            block = jnp.where((e + c) % ratio == f % ratio, got[c], block)
        blocks.append(block)
    grad_down = jnp.concatenate(blocks, axis=0).T.astype(F32)

    def rows_of(array):
        return lambda j: lax.dynamic_slice_in_dim(array, order[j] * rows, rows, axis=0)

    dh_one = add_up(seq_scatter(rows_of(dh_one_part)))
    normal_x, inverse_x = normalise(x_own.astype(F32))
    sum_ln1_gain = jnp.sum(dh_one * normal_x, axis=0)
    sum_ln1_shift = jnp.sum(dh_one, axis=0)
    grad_inputs = (dx_one + norm_back(normal_x, inverse_x, ln1_gain, dh_one)).astype(BF)

    grad_qkv_mine = ring_scatter_sum(bands(grad_qkv_part))[0].astype(BF)
    thirds = [grad_qkv_mine[:, t * cols : (t + 1) * cols] for t in range(3)]
    got = []
    for p in range(3):
        perm = [((3 * d + p) % ns, d) for d in range(ns)]
        section = [0] * ns
        for d in range(ns):
            section[(3 * d + p) % ns] = (3 * d + p) // ns
        which = sum(jnp.where(s == i, t, 0) for i, t in enumerate(section))
        piece = jnp.where(which == 0, thirds[0], jnp.where(which == 1, thirds[1], thirds[2]))
        got.append(lax.ppermute(piece, "seq", perm))
    grad_qkv = jnp.concatenate(got, axis=1).astype(F32)

    def spread(vector, size, start):
        return lax.dynamic_update_slice(jnp.zeros((size,), F32), vector, (start,))

    sum_qkv = jnp.sum(gqkv.astype(F32), axis=0)
    sum_q = spread(sum_qkv[:cols], width, s * cols)
    sum_v = spread(sum_qkv[2 * cols : 3 * cols], width, s * cols)
    sum_hidden = spread(sum_up[0, :mine], hidden, s * mine)
    vectors = [sum_ln1_gain, sum_ln1_shift, sum_q, sum_v, sums_two[2], sums_two[0], sums_two[1], sum_hidden, sum_down_bias]
    totals = total_sum(jnp.concatenate(vectors))
    sums, start = [], 0
    for vector in vectors:
        sums.append(totals[start : start + vector.shape[0]])
        start += vector.shape[0]
    return (layer_out[None], grad_inputs[None], grad_qkv, grad_out, grad_up, grad_down, *sums)


def solution(mesh):
    tokens, weights, shared = P("fsdp", "seq", None), P("fsdp", None), P()
    marks, grads = P("fsdp", "seq"), P("fsdp", "seq")
    return jax.shard_map(
        local,
        mesh=mesh,
        in_specs=(tokens, marks, marks, tokens) + (weights,) * 4 + (shared,) * 9,
        out_specs=(tokens, tokens) + (grads,) * 4 + (shared,) * 9,
        check_vma=False,
    )
```

time: 1290 us -> 502 us (0.39)
  waiting for transfers between devices: 627 us -> 116 us
  blocking collectives: 217 us -> 0 us
  matrix products: 210 us -> 29.8 us
  Pallas kernels: 0 us -> 137 us
  starting transfers between devices: 31.8 us -> 116 us
  local copies, waits for them, and re-layouts: 124 us -> 42.1 us
  other arithmetic: 56.4 us -> 38.5 us
    all_gather x4 -> x2, waiting for transfers between devices: 298 us -> 0.02 us  [the longest x1 0.02 us: local(): full_up = lax.all_gather(up_mine, 'fsdp', axis=0, tiled=True)]
    unnamed x16 -> x2, waiting for transfers between devices: 234 us -> 0.03 us
    dot_general x33 -> x8, matrix products: 210 us -> 29.8 us  [the longest x7 23.8 us: dot_at(): lax.dot_general(a, b, (((0,), (0,)), ((), ())), preferred_element_type=F32)]
    unnamed x1 -> x0, blocking collectives: 148 us -> none
    pallas_call x0 -> x6, Pallas kernels: none -> 137 us  [the longest x1 41.1 us: attention_backward(): pl.pallas_call(functools.partial(backward_kernel, heads, tile, count), ou...]
    ppermute x0 -> x74, starting transfers between devices: none -> 116 us  [the longest x8 48.9 us: ring_gather(): one = lax.ppermute(one, 'fsdp', ahead)]
    ppermute x0 -> x74, waiting for transfers between devices: none -> 115 us  [the longest x12 41.2 us: ring_scatter_sum(): one = lax.ppermute(one, 'fsdp', ahead)]
    all_to_all x8 -> x0, waiting for transfers between devices: 95.7 us -> none  [the longest x1 20.1 us: local(): lax.all_to_all(o_heads, 'seq', split_axis=0, concat_axis=1, tiled=True)]
  transfers between devices with their start and end apart: 20 -> 76, of which waited for: 13 -> 30; matrix products, arithmetic and copies ran while one was open for 37% -> 19% of each run, Pallas kernels for 0% -> 24%
where the time goes in v1:
time: 502 us; the launch traced here: 495 us
  Pallas kernels  137 us (27%)
  starting transfers between devices  116 us (23%)
  waiting for transfers between devices  116 us (23%)
  local copies, waits for them, and re-layouts  42.1 us (8%)
  other arithmetic  38.5 us (8%)
  matrix products  29.8 us (6%)
  between operations  15.6 us (3%)
    ppermute x8, starting transfers between devices, ring_gather(): one = lax.ppermute(one, 'fsdp', ahead)  48.9 us
    ppermute x12, waiting for transfers between devices, ring_scatter_sum(): one = lax.ppermute(one, 'fsdp', ahead)  41.2 us
    pallas_call x1, Pallas kernels, attention_backward(): pl.pallas_call(functools.partial(backward_kernel, heads, tile, count), ou...  41.1 us
    ppermute x32, starting transfers between devices, swap(): return lax.ppermute(value, axis, [(i, i ^ bits) for i in range(size)])  33.5 us
    ppermute x32, waiting for transfers between devices, swap(): return lax.ppermute(value, axis, [(i, i ^ bits) for i in range(size)])  33 us
    pallas_call x1, Pallas kernels, attention_forward(): pl.pallas_call(functools.partial(forward_kernel, heads, tile), out_shape=...  27.4 us
    pallas_call x1, Pallas kernels, widen(): pl.pallas_call(functools.partial(widen_kernel, count, bands), out_shape=[...  25.6 us
    dot_general x7, matrix products, dot_at(): lax.dot_general(a, b, (((0,), (0,)), ((), ())), preferred_element_type=F32)  23.8 us
  transfers between devices with their start and end apart: 76, of which 30 were waited for; matrix products, arithmetic and copies ran while one was open for 19% of the time, Pallas kernels for 24%

profile of v1, /device:TPU:0, one launch (start us, length us, event | category | flops | bytes accessed | tf_op | source)
XLA Modules:
  0.0 495.1 jit_solution(9283486814336150412)
XLA Ops:
  9.5 3.0 collective-permute-start.1
  16.4 2.3 constant_dynamic-slice_fusion.4
  18.7 2.9 collective-permute-done.3.refs_5_
  29.8 2.6 collective-permute-done.11
  33.9 1.8 collective-permute-start.26
  36.2 3.4 collective-permute-start.7
  39.8 2.2 collective-permute-done.26
  43.8 15.8 %collective-permute-start.16 = (bf16[144,1152]{1,0:T(8,128)(2,1)}, bf16[144,1152]{1,0:T(8,128)(2,1)}, u32[]{:S(2)}, u32[]{:S(2)}) collective-permute-start(bf16[144,1152]{1,0:T(8,128)(2,1)} %refs_4_.1), channel_id=1, source_target_pairs={{0,2},{2,4},{4,6},{6,7},{7,5},{5,3},{3,1},{1,0},{8,10},{10,12},{12... | collective-permute-start | bytes 995336 | tf_op jit(solution)/shard_map/ppermute | solution.py:546
  59.6 19.2 %collective-permute-start.9 = (bf16[144,896]{1,0:T(8,128)(2,1)}, bf16[144,896]{1,0:T(8,128)(2,1)}, u32[]{:S(2)}, u32[]{:S(2)}) collective-permute-start(bf16[144,896]{1,0:T(8,128)(2,1)} %collective-permute-done.7.refs_9_), channel_id=1, source_target_pairs={{0,2},{2,4},{4,6},{6,7},{7,5},{5,3},{3,1},{1,0},{8,10},{10,12},{12... | collective-permute-start | bytes 774152 | tf_op jit(solution)/shard_map/ppermute | solution.py:546
  80.7 7.8 %collective-permute-done.8.refs_10_ = bf16[144,896]{1,0:T(8,128)(2,1)} collective-permute-done((bf16[144,896]{1,0:T(8,128)(2,1)}, bf16[144,896]{1,0:T(8,128)(2,1)}, u32[]{:S(2)}, u32[]{:S(2)}) %collective-permute-start.8) | collective-permute-done | bytes 258080 | tf_op jit(solution)/shard_map/ppermute | solution.py:550
  88.5 14.6 %norm_project.1 = (bf16[1536,1152]{1,0:T(8,128)(2,1)}, bf16[1536,1152]{1,0:T(8,128)(2,1)}, bf16[1536,288]{1,0:T(8,128)(2,1)}, bf16[1536,288]{1,0:T(8,128)(2,1)},...) custom-call(s32[12]{0:T(128)S(1)} %stack.244.slots, bf16[384,1152]{1,0:T(8,128)(2,1)S(1)} %bitcast.135, ...), custom_call_target="tpu_custom_call" | custom-call | flops 3170893824 | bytes 14155776 | tf_op jit(solution)/shard_map/norm_project/pallas_call | solution.py:324
  106.0 27.4 %attention_forward.1 = (bf16[1536,288]{1,0:T(8,128)(2,1)S(1)}, f32[1536,128]{1,0:T(8,128)S(1)}) custom-call(s32[2,6]{1,0:T(2,128)S(1)} %pad_add_fusion.bounds, bf16[1536,288]{1,0:T(8,128)(2,1)S(1)} %copy-done.7, bf16[1536,288]{1,0:T(8,128)(2,1)S(1)} %copy-done.9, bf16[1536,288]{1,0:T(8,128)(2,1)} %get-tuple-element.46.v_ref, ...), custom_call_target="tpu_custom_call" | custom-call | flops 4831838208 | bytes 4423680 | tf_op jit(solution)/shard_map/attention_forward/pallas_call | solution.py:131
  135.6 4.1 collective-permute-start.14
  143.5 2.0 collective-permute-start.18
  145.7 4.0 collective-permute-done.17.refs_6_
  149.7 4.0 collective-permute-done.18.refs_7_
  153.7 3.3 collective-permute-start.20
  157.4 3.4 collective-permute-done.19.refs_8_
  161.4 2.9 collective-permute-done.20.refs_9_
  164.3 2.0 collective-permute-start.22
  166.3 6.8 %pad_maximum_fusion.gy_ref = bf16[1536,1152]{1,0:T(8,128)(2,1)} fusion(bf16[384,1152]{1,0:T(8,128)(2,1)} %collective-permute-done.25, bf16[384,1152]{1,0:T(8,128)(2,1)} %collective-permute-done.24, bf16[384,1152]{1,0:T(8,128)(2,1)} %collective-permute-done.23, bf16[384,1152]{1,0:T(8,128)(2,1)S(1)} %get-tuple-element.126.refs_4_), kind=kLoop, calls=%fused_computation.5 | loop fusion | flops 14155776 | bytes 7077888 | tf_op jit(solution)/shard_map/concatenate | solution.py:641
  173.1 2.3 copy.46.refs_2_
  176.8 2.3 copy.47.refs_3_
  179.9 25.6 %out_norm_up.1 = (f32[384,1152]{1,0:T(8,128)}, bf16[384,1152]{1,0:T(8,128)(2,1)}, bf16[1536,1152]{1,0:T(8,128)(2,1)}, bf16[1536,1152]{1,0:T(8,128)(2,1)}, f32[15...) custom-call(s32[12]{0:T(128)} %copy-done.5, bf16[1536,1152]{1,0:T(8,128)(2,1)} %get-tuple-element.43.x_ref, ...), custom_call_target="tpu_custom_call" | custom-call | flops 8153726976 | bytes 28311552 | tf_op jit(solution)/shard_map/out_norm_up/pallas_call | solution.py:382
  205.5 7.6 %convolution_convert_fusion = bf16[1152,1152]{1,0:T(8,128)(2,1)S(1)} fusion(bf16[1536,1152]{1,0:T(8,128)(2,1)} %get-tuple-element.49.a_ref, bf16[384,1152]{1,0:T(8,128)(2,1)} %collective-permute-done.25, bf16[384,1152]{1,0:T(8,128)(2,1)} %collective-permute-done.24, bf16[384,1152]{1,0:T(8,128)(2,1)} %collective-permute-done.23, ...), kind=kOutput, calls=%fused_computation | convolution fusion | flops 4092346368 | bytes 9732096 | tf_op jit(solution)/shard_map/dot_general | solution.py:289
  214.6 20.9 %down_and_back.1 = (bf16[1536,1152]{1,0:T(8,128)(2,1)}, bf16[1536,1152]{1,0:T(8,128)(2,1)}, bf16[1536,1152]{1,0:T(8,128)(2,1)}, f32[1,1152]{1,0:T(1,128)}) custom-call(bf16[1536,1152]{1,0:T(8,128)(2,1)} %pad_maximum_fusion.gy_ref, bf16[1536,1152]{1,0:T(8,128)(2,1)} %get-tuple-element.49.a_ref, f32[1536,1152]{1,0:T(8,128)} %get-tuple-element.50.slope_ref, ...), custom_call_target="tpu_custom_call" | custom-call | flops 12230590464 | bytes 28311552 | tf_op jit(solution)/shard_map/down_and_back/pallas_call | solution.py:428
  235.5 3.3 fusion.48
  239.3 6.8 %convolution_convert_fusion.1 = bf16[1152,1152]{1,0:T(8,128)(2,1)S(1)} fusion(bf16[1536,1152]{1,0:T(8,128)(2,1)S(1)} %copy-done.39, bf16[1536,1152]{1,0:T(8,128)(2,1)} %get-tuple-element.68), kind=kOutput, calls=%fused_computation.1 | convolution fusion | flops 4078190592 | bytes 9732096 | tf_op jit(solution)/shard_map/dot_general | solution.py:289
  248.4 2.4 collective-permute-start.60
  253.5 12.0 %collective-permute-done.60 = bf16[2,144,1152]{2,1,0:T(8,128)(2,1)} collective-permute-done((bf16[2,144,1152]{2,1,0:T(8,128)(2,1)}, bf16[2,144,1152]{2,1,0:T(8,128)(2,1)}, u32[]{:S(2)}, u32[]{:S(2)}) %collective-permute-start.60) | collective-permute-done | bytes 663584 | tf_op jit(solution)/shard_map/ppermute | solution.py:564
  275.8 8.7 %collective-permute-done.61 = bf16[2,144,1152]{2,1,0:T(8,128)(2,1)S(1)} collective-permute-done((bf16[2,144,1152]{2,1,0:T(8,128)(2,1)S(1)}, bf16[2,144,1152]{2,1,0:T(8,128)(2,1)S(1)}, u32[]{:S(2)}, u32[]{:S(2)}) %collective-permute-start.61) | collective-permute-done | bytes 663584 | tf_op jit(solution)/shard_map/ppermute | solution.py:564
  285.9 2.4 collective-permute-done.65
  291.4 5.4 %collective-permute-done.33.refs_2_ = bf16[384,1152]{1,0:T(8,128)(2,1)S(1)} collective-permute-done((bf16[384,1152]{1,0:T(8,128)(2,1)S(1)}, bf16[384,1152]{1,0:T(8,128)(2,1)S(1)}, u32[]{:S(2)}, u32[]{:S(2)}) %collective-permute-start.33) | collective-permute-done | bytes 884768 | tf_op jit(solution)/shard_map/ppermute | solution.py:488
  296.8 7.9 %norm_back_out.1 = (f32[384,1152]{1,0:T(8,128)}, f32[8,1152]{1,0:T(8,128)S(1)}, bf16[384,288]{1,0:T(8,128)(2,1)S(1)}, bf16[384,288]{1,0:T(8,128)(2,1)S(1)}, bf16...) custom-call(s32[12]{0:T(128)S(1)} %copy-done.6, ...), custom_call_target="tpu_custom_call" | custom-call | flops 1019215872 | bytes 8847360 | tf_op jit(solution)/shard_map/norm_back_out/pallas_call | solution.py:470
  307.0 8.8 %collective-permute-done.30 = bf16[384,1152]{1,0:T(8,128)(2,1)} collective-permute-done((bf16[384,1152]{1,0:T(8,128)(2,1)S(1)}, bf16[384,1152]{1,0:T(8,128)(2,1)}, u32[]{:S(2)}, u32[]{:S(2)}) %collective-permute-start.30) | collective-permute-done | bytes 884768 | tf_op jit(solution)/shard_map/ppermute | solution.py:488
  315.9 2.9 fusion.16
  321.0 2.2 collective-permute-start.63
  323.2 2.0 collective-permute-done.36.refs_3_
  325.5 41.1 %attention_backward.1 = bf16[1536,896]{1,0:T(8,128)(2,1)} custom-call(s32[2,6]{1,0:T(2,128)S(1)} %pad_add_fusion.bounds, s32[12]{0:T(128)S(1)} %copy-done.6, bf16[1536,288]{1,0:T(8,128)(2,1)S(1)} %copy-done.8, bf16[1536,288]{1,0:T(8,128)(2,1)S(1)} %copy-done.10, bf16[1536,288]{1,0:T(8,128)(2,1)} %get-tuple-element.46.v_ref, bf16[1536,288]{1,0:T(8,128)(2,1)} %copy-done.3, ...), custom_call_target="tpu_custom_call" | custom-call | flops 12079595520 | bytes 7077888 | tf_op jit(solution)/shard_map/attention_backward/pallas_call | solution.py:219
  366.6 2.4 convert_reduce_fusion
  369.2 6.0 %convolution_convert_fusion.2 = bf16[1536,1152]{1,0:T(8,128)(2,1)S(1)} fusion(bf16[1536,896]{1,0:T(8,128)(2,1)S(1)} %copy-done.17, bf16[1152,896]{1,0:T(8,128)(2,1)} %get-tuple-element.60), kind=kOutput, calls=%fused_computation.2 | convolution fusion | flops 3172663296 | bytes 8355840 | tf_op jit(solution)/shard_map/dot_general | solution.py:285
  375.4 1.8 copy-done.40
  377.2 3.9 convolution_convert_fusion.3
  381.6 8.6 %collective-permute-done.40 = bf16[1,144,896]{2,1,0:T(8,128)(2,1)S(1)} collective-permute-done((bf16[1,144,896]{2,1,0:T(8,128)(2,1)S(1)}, bf16[1,144,896]{2,1,0:T(8,128)(2,1)S(1)}, u32[]{:S(2)}, u32[]{:S(2)}) %collective-permute-start.40) | collective-permute-done | bytes 258080 | tf_op jit(solution)/shard_map/ppermute | solution.py:564
  390.2 2.1 collective-permute-start.41
  394.0 4.4 collective-permute-done.44
  399.1 2.1 collective-permute-start.42
  404.6 2.8 collective-permute-done.42
  409.9 5.0 %collective-permute-done.67 = bf16[144,538]{1,0:T(8,128)(2,1)S(1)} collective-permute-done((bf16[144,538]{1,0:T(8,128)(2,1)S(1)}, bf16[144,538]{1,0:T(8,128)(2,1)S(1)}, u32[]{:S(2)}, u32[]{:S(2)}) %collective-permute-start.67) | collective-permute-done | bytes 154976 | tf_op jit(solution)/shard_map/ppermute | solution.py:703
  414.9 10.7 %collective-permute-start.52 = (bf16[1152,288]{0,1:T(8,128)(2,1)S(1)}, bf16[1152,288]{0,1:T(8,128)(2,1)S(1)}, u32[]{:S(2)}, u32[]{:S(2)}) collective-permute-start(bf16[1152,288]{0,1:T(8,128)(2,1)S(1)} %fusion.1), channel_id=1, source_target_pairs={{0,16},{8,24},{16,0},{24,8},{1,17},{9,25},{17,1},{25,9},{2,18},{10... | collective-permute-start | bytes 1990664 | tf_op jit(solution)/shard_map/ppermute | solution.py:488
  427.0 2.5 collective-permute-start.46
  429.7 4.3 collective-permute-start.39
  434.0 7.7 %collective-permute-done.52 = bf16[1152,288]{0,1:T(8,128)(2,1)S(1)} collective-permute-done((bf16[1152,288]{0,1:T(8,128)(2,1)S(1)}, bf16[1152,288]{0,1:T(8,128)(2,1)S(1)}, u32[]{:S(2)}, u32[]{:S(2)}) %collective-permute-start.52) | collective-permute-done | bytes 663584 | tf_op jit(solution)/shard_map/ppermute | solution.py:488
  444.0 1.9 collective-permute-start.57
  445.9 4.0 collective-permute-done.53
  451.0 4.2 collective-permute-done.54
  455.2 4.4 collective-permute-start.49
  459.9 2.0 collective-permute-start.58
  461.9 2.2 fusion.13
  469.8 2.0 collective-permute-done.70
  471.7 1.8 collective-permute-start.71
  477.4 2.8 collective-permute-done.72
  480.2 2.6 collective-permute-start.73
  482.9 3.7 fusion.17
  (292 shorter events, 83.5 us)
Async XLA Ops:
  7.2 172.0 %all-gather.3.cloned.1.call-start = ((), (), s32[]{:S(2)}) async-start(), calls=%async_computation | async-start | bytes 2985984 | tf_op jit(solution)/shard_map/all_gather | solution.py:636
  9.4 205.1 %all-gather.5.cloned.1.call-start = ((), (), s32[]{:S(2)}) async-start(), calls=%async_computation.1 | async-start | bytes 2985984 | tf_op jit(solution)/shard_map/all_gather | solution.py:637
  9.5 30.1 %collective-permute-start.1 = (bf16[384,1152]{1,0:T(8,128)(2,1)}, bf16[384,1152]{1,0:T(8,128)(2,1)S(1)}, u32[]{:S(2)}, u32[]{:S(2)}) collective-permute-start(bf16[384,1152]{1,0:T(8,128)(2,1)} %bitcast.133), channel_id=1, source_target_pairs={{0,16},{8,24},{16,0},{24,8},{1,17},{9,25},{17,1},{25,9},{2,18},{10... | collective-permute-start | bytes 2654216 | tf_op jit(solution)/shard_map/ppermute | solution.py:488
  13.9 7.7 %collective-permute-start.3 = (bf16[144,896]{1,0:T(8,128)(2,1)S(1)}, bf16[144,896]{1,0:T(8,128)(2,1)S(1)}, u32[]{:S(2)}, u32[]{:S(2)}) collective-permute-start(bf16[144,896]{1,0:T(8,128)(2,1)S(1)} %fusion.41.refs_4_), channel_id=1, source_target_pairs={{0,2},{2,4},{4,6},{6,7},{7,5},{5,3},{3,1},{1,0},{8,10},{10,12},{12... | collective-permute-start | bytes 774152 | tf_op jit(solution)/shard_map/ppermute | solution.py:546
  15.5 20.5 %collective-permute-start.4 = (bf16[144,896]{1,0:T(8,128)(2,1)S(1)}, bf16[144,896]{1,0:T(8,128)(2,1)S(1)}, u32[]{:S(2)}, u32[]{:S(2)}) collective-permute-start(bf16[144,896]{1,0:T(8,128)(2,1)S(1)} %fusion.41.refs_4_), channel_id=1, source_target_pairs={{2,0},{4,2},{6,4},{7,6},{5,7},{3,5},{1,3},{0,1},{10,8},{12,10},{14... | collective-permute-start | bytes 774152 | tf_op jit(solution)/shard_map/ppermute | solution.py:550
  16.0 16.8 %collective-permute-start.10 = (s32[1,384]{1,0:T(1,128)S(1)}, s32[1,384]{1,0:T(1,128)S(1)}, u32[]{:S(2)}, u32[]{:S(2)}) collective-permute-start(s32[1,384]{1,0:T(1,128)S(1)} %get-tuple-element.129), channel_id=1, source_target_pairs={{0,8},{8,0},{16,24},{24,16},{1,9},{9,1},{17,25},{25,17},{2,10},{10... | collective-permute-start | bytes 4616 | tf_op jit(solution)/shard_map/ppermute | solution.py:488
  16.1 16.3 %collective-permute-start.11 = (s32[1,384]{1,0:T(1,128)S(1)}, s32[1,384]{1,0:T(1,128)S(1)}, u32[]{:S(2)}, u32[]{:S(2)}) collective-permute-start(s32[1,384]{1,0:T(1,128)S(1)} %get-tuple-element.129), channel_id=1, source_target_pairs={{0,16},{8,24},{16,0},{24,8},{1,17},{9,25},{17,1},{25,9},{2,18},{10... | collective-permute-start | bytes 4616 | tf_op jit(solution)/shard_map/ppermute | solution.py:488
  21.6 14.6 %collective-permute-start.5 = (bf16[144,896]{1,0:T(8,128)(2,1)S(1)}, bf16[144,896]{1,0:T(8,128)(2,1)}, u32[]{:S(2)}, u32[]{:S(2)}) collective-permute-start(bf16[144,896]{1,0:T(8,128)(2,1)S(1)} %collective-permute-done.3.refs_5_), channel_id=1, source_target_pairs={{0,2},{2,4},{4,6},{6,7},{7,5},{5,3},{3,1},{1,0},{8,10},{10,12},{12... | collective-permute-start | bytes 774152 | tf_op jit(solution)/shard_map/ppermute | solution.py:546
  32.8 55.8 %collective-permute-start = (bf16[384,1152]{1,0:T(8,128)(2,1)S(1)}, bf16[384,1152]{1,0:T(8,128)(2,1)}, u32[]{:S(2)}, u32[]{:S(2)}) collective-permute-start(bf16[384,1152]{1,0:T(8,128)(2,1)S(1)} %bitcast.134), channel_id=1, source_target_pairs={{0,8},{8,0},{16,24},{24,16},{1,9},{9,1},{17,25},{25,17},{2,10},{10... | collective-permute-start | bytes 2654216 | tf_op jit(solution)/shard_map/ppermute | solution.py:488
  33.9 8.1 %collective-permute-start.26 = (bf16[144,538]{1,0:T(8,128)(2,1)}, bf16[144,538]{1,0:T(8,128)(2,1)}, u32[]{:S(2)}, u32[]{:S(2)}) collective-permute-start(bf16[144,538]{1,0:T(8,128)(2,1)} %bitcast.139), channel_id=1, source_target_pairs={{0,1},{1,0},{2,9},{3,8},{4,17},{5,16},{6,25},{7,24},{8,3},{9,2},{1... | collective-permute-start | bytes 464840 | tf_op jit(solution)/shard_map/ppermute | solution.py:614
  36.0 23.7 %collective-permute-start.6 = (bf16[144,896]{1,0:T(8,128)(2,1)S(1)}, bf16[144,896]{1,0:T(8,128)(2,1)}, u32[]{:S(2)}, u32[]{:S(2)}) collective-permute-start(bf16[144,896]{1,0:T(8,128)(2,1)S(1)} %collective-permute-done.4.refs_6_), channel_id=1, source_target_pairs={{2,0},{4,2},{6,4},{7,6},{5,7},{3,5},{1,3},{0,1},{10,8},{12,10},{14... | collective-permute-start | bytes 774152 | tf_op jit(solution)/shard_map/ppermute | solution.py:550
  36.2 23.4 %collective-permute-start.7 = (bf16[144,896]{1,0:T(8,128)(2,1)}, bf16[144,896]{1,0:T(8,128)(2,1)}, u32[]{:S(2)}, u32[]{:S(2)}) collective-permute-start(bf16[144,896]{1,0:T(8,128)(2,1)} %collective-permute-done.5.refs_7_), channel_id=1, source_target_pairs={{0,2},{2,4},{4,6},{6,7},{7,5},{5,3},{3,1},{1,0},{8,10},{10,12},{12... | collective-permute-start | bytes 774152 | tf_op jit(solution)/shard_map/ppermute | solution.py:546
  39.6 48.9 %collective-permute-start.2 = (bf16[384,1152]{1,0:T(8,128)(2,1)S(1)}, bf16[384,1152]{1,0:T(8,128)(2,1)}, u32[]{:S(2)}, u32[]{:S(2)}) collective-permute-start(bf16[384,1152]{1,0:T(8,128)(2,1)S(1)} %collective-permute-done.1.refs_2_), channel_id=1, source_target_pairs={{0,8},{8,0},{16,24},{24,16},{1,9},{9,1},{17,25},{25,17},{2,10},{10... | collective-permute-start | bytes 2654216 | tf_op jit(solution)/shard_map/ppermute | solution.py:488
  43.8 99.7 %collective-permute-start.16 = (bf16[144,1152]{1,0:T(8,128)(2,1)}, bf16[144,1152]{1,0:T(8,128)(2,1)}, u32[]{:S(2)}, u32[]{:S(2)}) collective-permute-start(bf16[144,1152]{1,0:T(8,128)(2,1)} %refs_4_.1), channel_id=1, source_target_pairs={{0,2},{2,4},{4,6},{6,7},{7,5},{5,3},{3,1},{1,0},{8,10},{10,12},{12... | collective-permute-start | bytes 995336 | tf_op jit(solution)/shard_map/ppermute | solution.py:546
  59.6 28.9 %collective-permute-start.8 = (bf16[144,896]{1,0:T(8,128)(2,1)}, bf16[144,896]{1,0:T(8,128)(2,1)}, u32[]{:S(2)}, u32[]{:S(2)}) collective-permute-start(bf16[144,896]{1,0:T(8,128)(2,1)} %collective-permute-done.6.refs_8_), channel_id=1, source_target_pairs={{2,0},{4,2},{6,4},{7,6},{5,7},{3,5},{1,3},{0,1},{10,8},{12,10},{14... | collective-permute-start | bytes 774152 | tf_op jit(solution)/shard_map/ppermute | solution.py:550
  59.6 28.9 %collective-permute-start.9 = (bf16[144,896]{1,0:T(8,128)(2,1)}, bf16[144,896]{1,0:T(8,128)(2,1)}, u32[]{:S(2)}, u32[]{:S(2)}) collective-permute-start(bf16[144,896]{1,0:T(8,128)(2,1)} %collective-permute-done.7.refs_9_), channel_id=1, source_target_pairs={{0,2},{2,4},{4,6},{6,7},{7,5},{5,3},{3,1},{1,0},{8,10},{10,12},{12... | collective-permute-start | bytes 774152 | tf_op jit(solution)/shard_map/ppermute | solution.py:546
  88.5 51.3 %collective-permute-start.24 = (bf16[384,1152]{1,0:T(8,128)(2,1)S(1)}, bf16[384,1152]{1,0:T(8,128)(2,1)}, u32[]{:S(2)}, u32[]{:S(2)}) collective-permute-start(bf16[384,1152]{1,0:T(8,128)(2,1)S(1)} %get-tuple-element.126.refs_4_), channel_id=1, source_target_pairs={{0,16},{8,24},{16,0},{24,8},{1,17},{9,25},{17,1},{25,9},{2,18},{10... | collective-permute-start | bytes 2654216 | tf_op jit(solution)/shard_map/ppermute | solution.py:488
  135.6 25.2 %collective-permute-start.14 = (bf16[1536,288]{0,1:T(8,128)(2,1)}, bf16[1536,288]{0,1:T(8,128)(2,1)}, u32[]{:S(2)}, u32[]{:S(2)}) collective-permute-start(bf16[1536,288]{0,1:T(8,128)(2,1)} %copy.43), channel_id=1, source_target_pairs={{0,16},{8,24},{16,0},{24,8},{1,17},{9,25},{17,1},{25,9},{2,18},{10... | collective-permute-start | bytes 2654216 | tf_op jit(solution)/shard_map/ppermute | solution.py:488
  139.8 10.0 %collective-permute-start.17 = (bf16[144,1152]{1,0:T(8,128)(2,1)}, bf16[144,1152]{1,0:T(8,128)(2,1)}, u32[]{:S(2)}, u32[]{:S(2)}) collective-permute-start(bf16[144,1152]{1,0:T(8,128)(2,1)} %refs_4_.1), channel_id=1, source_target_pairs={{2,0},{4,2},{6,4},{7,6},{5,7},{3,5},{1,3},{0,1},{10,8},{12,10},{14... | collective-permute-start | bytes 995336 | tf_op jit(solution)/shard_map/ppermute | solution.py:550
  139.8 21.5 %collective-permute-start.23 = (bf16[384,1152]{1,0:T(8,128)(2,1)S(1)}, bf16[384,1152]{1,0:T(8,128)(2,1)}, u32[]{:S(2)}, u32[]{:S(2)}) collective-permute-start(bf16[384,1152]{1,0:T(8,128)(2,1)S(1)} %get-tuple-element.126.refs_4_), channel_id=1, source_target_pairs={{0,8},{8,0},{16,24},{24,16},{1,9},{9,1},{17,25},{25,17},{2,10},{10... | collective-permute-start | bytes 2654216 | tf_op jit(solution)/shard_map/ppermute | solution.py:488
  139.8 26.5 %collective-permute-start.25 = (bf16[384,1152]{1,0:T(8,128)(2,1)}, bf16[384,1152]{1,0:T(8,128)(2,1)}, u32[]{:S(2)}, u32[]{:S(2)}) collective-permute-start(bf16[384,1152]{1,0:T(8,128)(2,1)} %collective-permute-done.24), channel_id=1, source_target_pairs={{0,8},{8,0},{16,24},{24,16},{1,9},{9,1},{17,25},{25,17},{2,10},{10... | collective-permute-start | bytes 2654216 | tf_op jit(solution)/shard_map/ppermute | solution.py:488
  143.5 10.3 %collective-permute-start.18 = (bf16[144,1152]{1,0:T(8,128)(2,1)}, bf16[144,1152]{1,0:T(8,128)(2,1)S(1)}, u32[]{:S(2)}, u32[]{:S(2)}) collective-permute-start(bf16[144,1152]{1,0:T(8,128)(2,1)} %collective-permute-done.16.refs_5_), channel_id=1, source_target_pairs={{0,2},{2,4},{4,6},{6,7},{7,5},{5,3},{3,1},{1,0},{8,10},{10,12},{12... | collective-permute-start | bytes 995336 | tf_op jit(solution)/shard_map/ppermute | solution.py:546
  149.7 11.0 %collective-permute-start.19 = (bf16[144,1152]{1,0:T(8,128)(2,1)}, bf16[144,1152]{1,0:T(8,128)(2,1)}, u32[]{:S(2)}, u32[]{:S(2)}) collective-permute-start(bf16[144,1152]{1,0:T(8,128)(2,1)} %collective-permute-done.17.refs_6_), channel_id=1, source_target_pairs={{2,0},{4,2},{6,4},{7,6},{5,7},{3,5},{1,3},{0,1},{10,8},{12,10},{14... | collective-permute-start | bytes 995336 | tf_op jit(solution)/shard_map/ppermute | solution.py:550
  153.7 10.6 %collective-permute-start.20 = (bf16[144,1152]{1,0:T(8,128)(2,1)S(1)}, bf16[144,1152]{1,0:T(8,128)(2,1)}, u32[]{:S(2)}, u32[]{:S(2)}) collective-permute-start(bf16[144,1152]{1,0:T(8,128)(2,1)S(1)} %collective-permute-done.18.refs_7_), channel_id=1, source_target_pairs={{0,2},{2,4},{4,6},{6,7},{7,5},{5,3},{3,1},{1,0},{8,10},{10,12},{12... | collective-permute-start | bytes 995336 | tf_op jit(solution)/shard_map/ppermute | solution.py:546
  160.8 14.7 %collective-permute-start.13 = (bf16[1536,288]{0,1:T(8,128)(2,1)}, bf16[1536,288]{0,1:T(8,128)(2,1)S(1)}, u32[]{:S(2)}, u32[]{:S(2)}) collective-permute-start(bf16[1536,288]{0,1:T(8,128)(2,1)} %copy.43), channel_id=1, source_target_pairs={{0,8},{8,0},{16,24},{24,16},{1,9},{9,1},{17,25},{25,17},{2,10},{10... | collective-permute-start | bytes 2654216 | tf_op jit(solution)/shard_map/ppermute | solution.py:488
  160.8 16.1 %collective-permute-start.15 = (bf16[1536,288]{0,1:T(8,128)(2,1)}, bf16[1536,288]{0,1:T(8,128)(2,1)}, u32[]{:S(2)}, u32[]{:S(2)}) collective-permute-start(bf16[1536,288]{0,1:T(8,128)(2,1)} %collective-permute-done.14), channel_id=1, source_target_pairs={{0,8},{8,0},{16,24},{24,16},{1,9},{9,1},{17,25},{25,17},{2,10},{10... | collective-permute-start | bytes 2654216 | tf_op jit(solution)/shard_map/ppermute | solution.py:488
  161.3 17.8 %collective-permute-start.21 = (bf16[144,1152]{1,0:T(8,128)(2,1)}, bf16[144,1152]{1,0:T(8,128)(2,1)S(1)}, u32[]{:S(2)}, u32[]{:S(2)}) collective-permute-start(bf16[144,1152]{1,0:T(8,128)(2,1)} %collective-permute-done.19.refs_8_), channel_id=1, source_target_pairs={{2,0},{4,2},{6,4},{7,6},{5,7},{3,5},{1,3},{0,1},{10,8},{12,10},{14... | collective-permute-start | bytes 995336 | tf_op jit(solution)/shard_map/ppermute | solution.py:550
  164.3 14.9 %collective-permute-start.22 = (bf16[144,1152]{1,0:T(8,128)(2,1)}, bf16[144,1152]{1,0:T(8,128)(2,1)}, u32[]{:S(2)}, u32[]{:S(2)}) collective-permute-start(bf16[144,1152]{1,0:T(8,128)(2,1)} %collective-permute-done.20.refs_9_), channel_id=1, source_target_pairs={{0,2},{2,4},{4,6},{6,7},{7,5},{5,3},{3,1},{1,0},{8,10},{10,12},{12... | collective-permute-start | bytes 995336 | tf_op jit(solution)/shard_map/ppermute | solution.py:546
  238.8 33.3 %collective-permute-start.32 = (bf16[384,1152]{1,0:T(8,128)(2,1)}, bf16[384,1152]{1,0:T(8,128)(2,1)}, u32[]{:S(2)}, u32[]{:S(2)}) collective-permute-start(bf16[384,1152]{1,0:T(8,128)(2,1)} %get-tuple-element.132), channel_id=1, source_target_pairs={{0,8},{8,0},{16,24},{24,16},{1,9},{9,1},{17,25},{25,17},{2,10},{10... | collective-permute-start | bytes 2654216 | tf_op jit(solution)/shard_map/ppermute | solution.py:488
  238.8 52.3 %collective-permute-start.31 = (bf16[384,1152]{1,0:T(8,128)(2,1)}, bf16[384,1152]{1,0:T(8,128)(2,1)}, u32[]{:S(2)}, u32[]{:S(2)}) collective-permute-start(bf16[384,1152]{1,0:T(8,128)(2,1)} %get-tuple-element.133), channel_id=1, source_target_pairs={{0,8},{8,0},{16,24},{24,16},{1,9},{9,1},{17,25},{25,17},{2,10},{10... | collective-permute-start | bytes 2654216 | tf_op jit(solution)/shard_map/ppermute | solution.py:488
  248.4 17.1 %collective-permute-start.60 = (bf16[2,144,1152]{2,1,0:T(8,128)(2,1)}, bf16[2,144,1152]{2,1,0:T(8,128)(2,1)}, u32[]{:S(2)}, u32[]{:S(2)}) collective-permute-start(bf16[2,144,1152]{2,1,0:T(8,128)(2,1)} %pad_maximum_fusion.1), channel_id=1, source_target_pairs={{0,2},{2,4},{4,6},{6,7},{7,5},{5,3},{3,1},{1,0},{8,10},{10,12},{12... | collective-permute-start | bytes 1990664 | tf_op jit(solution)/shard_map/ppermute | solution.py:564
  251.7 17.0 %collective-permute-start.64 = (bf16[2,144,1152]{2,1,0:T(8,128)(2,1)}, bf16[2,144,1152]{2,1,0:T(8,128)(2,1)}, u32[]{:S(2)}, u32[]{:S(2)}) collective-permute-start(bf16[2,144,1152]{2,1,0:T(8,128)(2,1)} %pad_maximum_fusion.2), channel_id=1, source_target_pairs={{2,0},{4,2},{6,4},{7,6},{5,7},{3,5},{1,3},{0,1},{10,8},{12,10},{14... | collective-permute-start | bytes 1990664 | tf_op jit(solution)/shard_map/ppermute | solution.py:566
  253.1 21.0 %collective-permute-start.29 = (bf16[384,1152]{1,0:T(8,128)(2,1)}, bf16[384,1152]{1,0:T(8,128)(2,1)}, u32[]{:S(2)}, u32[]{:S(2)}) collective-permute-start(bf16[384,1152]{1,0:T(8,128)(2,1)} %get-tuple-element.136), channel_id=1, source_target_pairs={{0,8},{8,0},{16,24},{24,16},{1,9},{9,1},{17,25},{25,17},{2,10},{10... | collective-permute-start | bytes 2654216 | tf_op jit(solution)/shard_map/ppermute | solution.py:488
  265.5 41.2 %collective-permute-start.28 = (bf16[384,1152]{1,0:T(8,128)(2,1)}, bf16[384,1152]{1,0:T(8,128)(2,1)}, u32[]{:S(2)}, u32[]{:S(2)}) collective-permute-start(bf16[384,1152]{1,0:T(8,128)(2,1)} %get-tuple-element.135), channel_id=1, source_target_pairs={{0,8},{8,0},{16,24},{24,16},{1,9},{9,1},{17,25},{25,17},{2,10},{10... | collective-permute-start | bytes 2654216 | tf_op jit(solution)/shard_map/ppermute | solution.py:488
  268.7 15.8 %collective-permute-start.61 = (bf16[2,144,1152]{2,1,0:T(8,128)(2,1)S(1)}, bf16[2,144,1152]{2,1,0:T(8,128)(2,1)S(1)}, u32[]{:S(2)}, u32[]{:S(2)}) collective-permute-start(bf16[2,144,1152]{2,1,0:T(8,128)(2,1)S(1)} %add_convert_fusion.8), channel_id=1, source_target_pairs={{0,2},{2,4},{4,6},{6,7},{7,5},{5,3},{3,1},{1,0},{8,10},{10,12},{12... | collective-permute-start | bytes 1990664 | tf_op jit(solution)/shard_map/ppermute | solution.py:564
  272.1 16.2 %collective-permute-start.65 = (bf16[2,144,1152]{2,1,0:T(8,128)(2,1)S(1)}, bf16[2,144,1152]{2,1,0:T(8,128)(2,1)S(1)}, u32[]{:S(2)}, u32[]{:S(2)}) collective-permute-start(bf16[2,144,1152]{2,1,0:T(8,128)(2,1)S(1)} %add_convert_fusion.5), channel_id=1, source_target_pairs={{2,0},{4,2},{6,4},{7,6},{5,7},{3,5},{1,3},{0,1},{10,8},{12,10},{14... | collective-permute-start | bytes 1990664 | tf_op jit(solution)/shard_map/ppermute | solution.py:566
  274.1 22.7 %collective-permute-start.33 = (bf16[384,1152]{1,0:T(8,128)(2,1)S(1)}, bf16[384,1152]{1,0:T(8,128)(2,1)S(1)}, u32[]{:S(2)}, u32[]{:S(2)}) collective-permute-start(bf16[384,1152]{1,0:T(8,128)(2,1)S(1)} %add_convert_fusion.1), channel_id=1, source_target_pairs={{0,16},{8,24},{16,0},{24,8},{1,17},{9,25},{17,1},{25,9},{2,18},{10... | collective-permute-start | bytes 2654216 | tf_op jit(solution)/shard_map/ppermute | solution.py:488
  284.5 31.3 %collective-permute-start.30 = (bf16[384,1152]{1,0:T(8,128)(2,1)S(1)}, bf16[384,1152]{1,0:T(8,128)(2,1)}, u32[]{:S(2)}, u32[]{:S(2)}) collective-permute-start(bf16[384,1152]{1,0:T(8,128)(2,1)S(1)} %add_convert_fusion.3), channel_id=1, source_target_pairs={{0,16},{8,24},{16,0},{24,8},{1,17},{9,25},{17,1},{25,9},{2,18},{10... | collective-permute-start | bytes 2654216 | tf_op jit(solution)/shard_map/ppermute | solution.py:488
  288.3 30.5 %collective-permute-start.62 = (bf16[2,144,1152]{2,1,0:T(8,128)(2,1)}, bf16[2,144,1152]{2,1,0:T(8,128)(2,1)}, u32[]{:S(2)}, u32[]{:S(2)}) collective-permute-start(bf16[2,144,1152]{2,1,0:T(8,128)(2,1)} %add_convert_fusion.7), channel_id=1, source_target_pairs={{0,2},{2,4},{4,6},{6,7},{7,5},{5,3},{3,1},{1,0},{8,10},{10,12},{12... | collective-permute-start | bytes 1990664 | tf_op jit(solution)/shard_map/ppermute | solution.py:564
  291.1 108.0 %collective-permute-start.66 = (bf16[2,144,1152]{2,1,0:T(8,128)(2,1)}, bf16[2,144,1152]{2,1,0:T(8,128)(2,1)}, u32[]{:S(2)}, u32[]{:S(2)}) collective-permute-start(bf16[2,144,1152]{2,1,0:T(8,128)(2,1)} %add_convert_fusion.4), channel_id=1, source_target_pairs={{2,0},{4,2},{6,4},{7,6},{5,7},{3,5},{1,3},{0,1},{10,8},{12,10},{14... | collective-permute-start | bytes 1990664 | tf_op jit(solution)/shard_map/ppermute | solution.py:566
  304.6 15.9 %collective-permute-start.34 = (bf16[384,288]{1,0:T(8,128)(2,1)S(1)}, bf16[384,288]{1,0:T(8,128)(2,1)S(1)}, u32[]{:S(2)}, u32[]{:S(2)}) collective-permute-start(bf16[384,288]{1,0:T(8,128)(2,1)S(1)} %get-tuple-element.57), channel_id=1, source_target_pairs={{0,8},{8,0},{16,24},{24,16},{1,9},{9,1},{17,25},{25,17},{2,10},{10... | collective-permute-start | bytes 663560 | tf_op jit(solution)/shard_map/ppermute | solution.py:488
  306.7 14.3 %collective-permute-start.35 = (bf16[384,288]{1,0:T(8,128)(2,1)S(1)}, bf16[384,288]{1,0:T(8,128)(2,1)S(1)}, u32[]{:S(2)}, u32[]{:S(2)}) collective-permute-start(bf16[384,288]{1,0:T(8,128)(2,1)S(1)} %get-tuple-element.58), channel_id=1, source_target_pairs={{0,16},{8,24},{16,0},{24,8},{1,17},{9,25},{17,1},{25,9},{2,18},{10... | collective-permute-start | bytes 663560 | tf_op jit(solution)/shard_map/ppermute | solution.py:488
  315.8 9.4 %collective-permute-start.36 = (bf16[384,288]{1,0:T(8,128)(2,1)S(1)}, bf16[384,288]{1,0:T(8,128)(2,1)S(1)}, u32[]{:S(2)}, u32[]{:S(2)}) collective-permute-start(bf16[384,288]{1,0:T(8,128)(2,1)S(1)} %get-tuple-element.59), channel_id=1, source_target_pairs={{0,24},{8,16},{16,8},{24,0},{1,25},{9,17},{17,9},{25,1},{2,26},{10... | collective-permute-start | bytes 663560 | tf_op jit(solution)/shard_map/ppermute | solution.py:488
  318.7 111.0 %collective-permute-start.50 = (bf16[1152,288]{0,1:T(8,128)(2,1)}, bf16[1152,288]{0,1:T(8,128)(2,1)}, u32[]{:S(2)}, u32[]{:S(2)}) collective-permute-start(bf16[1152,288]{0,1:T(8,128)(2,1)} %convolution_convert_fusion.5), channel_id=1, source_target_pairs={{0,8},{8,0},{16,24},{24,16},{1,9},{9,1},{17,25},{25,17},{2,10},{10... | collective-permute-start | bytes 1990664 | tf_op jit(solution)/shard_map/ppermute | solution.py:488
  320.5 69.7 %collective-permute-start.51 = (bf16[1152,288]{0,1:T(8,128)(2,1)S(1)}, bf16[1152,288]{0,1:T(8,128)(2,1)}, u32[]{:S(2)}, u32[]{:S(2)}) collective-permute-start(bf16[1152,288]{0,1:T(8,128)(2,1)S(1)} %convolution_convert_fusion.4), channel_id=1, source_target_pairs={{0,8},{8,0},{16,24},{24,16},{1,9},{9,1},{17,25},{25,17},{2,10},{10... | collective-permute-start | bytes 1990664 | tf_op jit(solution)/shard_map/ppermute | solution.py:488
  321.0 80.1 %collective-permute-start.63 = (bf16[2,144,1152]{2,1,0:T(8,128)(2,1)S(1)}, bf16[2,144,1152]{2,1,0:T(8,128)(2,1)S(1)}, u32[]{:S(2)}, u32[]{:S(2)}) collective-permute-start(bf16[2,144,1152]{2,1,0:T(8,128)(2,1)S(1)} %add_convert_fusion.6), channel_id=1, source_target_pairs={{0,2},{2,4},{4,6},{6,7},{7,5},{5,3},{3,1},{1,0},{8,10},{10,12},{12... | collective-permute-start | bytes 1990664 | tf_op jit(solution)/shard_map/ppermute | solution.py:569
  381.2 8.9 %collective-permute-start.40 = (bf16[1,144,896]{2,1,0:T(8,128)(2,1)S(1)}, bf16[1,144,896]{2,1,0:T(8,128)(2,1)S(1)}, u32[]{:S(2)}, u32[]{:S(2)}) collective-permute-start(bf16[1,144,896]{2,1,0:T(8,128)(2,1)S(1)} %get-tuple-element.157), channel_id=1, source_target_pairs={{0,2},{2,4},{4,6},{6,7},{7,5},{5,3},{3,1},{1,0},{8,10},{10,12},{12... | collective-permute-start | bytes 774152 | tf_op jit(solution)/shard_map/ppermute | solution.py:564
  390.2 8.2 %collective-permute-start.44 = (bf16[1,144,896]{2,1,0:T(8,128)(2,1)S(1)}, bf16[1,144,896]{2,1,0:T(8,128)(2,1)S(1)}, u32[]{:S(2)}, u32[]{:S(2)}) collective-permute-start(bf16[1,144,896]{2,1,0:T(8,128)(2,1)S(1)} %get-tuple-element.158), channel_id=1, source_target_pairs={{2,0},{4,2},{6,4},{7,6},{5,7},{3,5},{1,3},{0,1},{10,8},{12,10},{14... | collective-permute-start | bytes 774152 | tf_op jit(solution)/shard_map/ppermute | solution.py:566
  390.2 8.3 %collective-permute-start.41 = (bf16[1,144,896]{2,1,0:T(8,128)(2,1)S(1)}, bf16[1,144,896]{2,1,0:T(8,128)(2,1)S(1)}, u32[]{:S(2)}, u32[]{:S(2)}) collective-permute-start(bf16[1,144,896]{2,1,0:T(8,128)(2,1)S(1)} %fusion.27), channel_id=1, source_target_pairs={{0,2},{2,4},{4,6},{6,7},{7,5},{5,3},{3,1},{1,0},{8,10},{10,12},{12... | collective-permute-start | bytes 774152 | tf_op jit(solution)/shard_map/ppermute | solution.py:564
  398.4 28.6 %collective-permute-start.38 = (bf16[384,1152]{1,0:T(8,128)(2,1)S(1)}, bf16[384,1152]{1,0:T(8,128)(2,1)S(1)}, u32[]{:S(2)}, u32[]{:S(2)}) collective-permute-start(bf16[384,1152]{1,0:T(8,128)(2,1)S(1)} %get-tuple-element.131), channel_id=1, source_target_pairs={{0,8},{8,0},{16,24},{24,16},{1,9},{9,1},{17,25},{25,17},{2,10},{10... | collective-permute-start | bytes 2654216 | tf_op jit(solution)/shard_map/ppermute | solution.py:488
  398.5 61.2 %collective-permute-start.37 = (bf16[384,1152]{1,0:T(8,128)(2,1)S(1)}, bf16[384,1152]{1,0:T(8,128)(2,1)S(1)}, u32[]{:S(2)}, u32[]{:S(2)}) collective-permute-start(bf16[384,1152]{1,0:T(8,128)(2,1)S(1)} %get-tuple-element.130), channel_id=1, source_target_pairs={{0,8},{8,0},{16,24},{24,16},{1,9},{9,1},{17,25},{25,17},{2,10},{10... | collective-permute-start | bytes 2654216 | tf_op jit(solution)/shard_map/ppermute | solution.py:488
  399.1 8.3 %collective-permute-start.42 = (bf16[1,144,896]{2,1,0:T(8,128)(2,1)S(1)}, bf16[1,144,896]{2,1,0:T(8,128)(2,1)S(1)}, u32[]{:S(2)}, u32[]{:S(2)}) collective-permute-start(bf16[1,144,896]{2,1,0:T(8,128)(2,1)S(1)} %get-tuple-element.155), channel_id=1, source_target_pairs={{0,2},{2,4},{4,6},{6,7},{7,5},{5,3},{3,1},{1,0},{8,10},{10,12},{12... | collective-permute-start | bytes 774152 | tf_op jit(solution)/shard_map/ppermute | solution.py:564
  401.1 8.0 %collective-permute-start.45 = (bf16[1,144,896]{2,1,0:T(8,128)(2,1)S(1)}, bf16[1,144,896]{2,1,0:T(8,128)(2,1)S(1)}, u32[]{:S(2)}, u32[]{:S(2)}) collective-permute-start(bf16[1,144,896]{2,1,0:T(8,128)(2,1)S(1)} %get-tuple-element.156), channel_id=1, source_target_pairs={{2,0},{4,2},{6,4},{7,6},{5,7},{3,5},{1,3},{0,1},{10,8},{12,10},{14... | collective-permute-start | bytes 774152 | tf_op jit(solution)/shard_map/ppermute | solution.py:566
  407.4 7.5 %collective-permute-start.67 = (bf16[144,538]{1,0:T(8,128)(2,1)S(1)}, bf16[144,538]{1,0:T(8,128)(2,1)S(1)}, u32[]{:S(2)}, u32[]{:S(2)}) collective-permute-start(bf16[144,538]{1,0:T(8,128)(2,1)S(1)} %get-tuple-element.175), channel_id=1, source_target_pairs={{0,1},{1,0},{2,9},{3,8},{4,17},{5,16},{6,25},{7,24},{8,3},{9,2},{1... | collective-permute-start | bytes 464840 | tf_op jit(solution)/shard_map/ppermute | solution.py:703
  409.1 16.5 %collective-permute-start.68 = (bf16[144,538]{1,0:T(8,128)(2,1)S(1)}, bf16[144,538]{1,0:T(8,128)(2,1)S(1)}, u32[]{:S(2)}, u32[]{:S(2)}) collective-permute-start(bf16[144,538]{1,0:T(8,128)(2,1)S(1)} %get-tuple-element.174), channel_id=1, source_target_pairs={{0,0},{1,1},{2,8},{3,9},{4,16},{5,17},{6,24},{7,25},{8,2},{9,3},{1... | collective-permute-start | bytes 464840 | tf_op jit(solution)/shard_map/ppermute | solution.py:703
  414.9 26.8 %collective-permute-start.52 = (bf16[1152,288]{0,1:T(8,128)(2,1)S(1)}, bf16[1152,288]{0,1:T(8,128)(2,1)S(1)}, u32[]{:S(2)}, u32[]{:S(2)}) collective-permute-start(bf16[1152,288]{0,1:T(8,128)(2,1)S(1)} %fusion.1), channel_id=1, source_target_pairs={{0,16},{8,24},{16,0},{24,8},{1,17},{9,25},{17,1},{25,9},{2,18},{10... | collective-permute-start | bytes 1990664 | tf_op jit(solution)/shard_map/ppermute | solution.py:488
  425.6 18.4 %collective-permute-start.43 = (bf16[1,144,896]{2,1,0:T(8,128)(2,1)S(1)}, bf16[1,144,896]{2,1,0:T(8,128)(2,1)S(1)}, u32[]{:S(2)}, u32[]{:S(2)}) collective-permute-start(bf16[1,144,896]{2,1,0:T(8,128)(2,1)S(1)} %get-tuple-element.153), channel_id=1, source_target_pairs={{0,2},{2,4},{4,6},{6,7},{7,5},{5,3},{3,1},{1,0},{8,10},{10,12},{12... | collective-permute-start | bytes 774152 | tf_op jit(solution)/shard_map/ppermute | solution.py:569
  427.0 17.0 %collective-permute-start.46 = (bf16[1,144,896]{2,1,0:T(8,128)(2,1)S(1)}, bf16[1,144,896]{2,1,0:T(8,128)(2,1)S(1)}, u32[]{:S(2)}, u32[]{:S(2)}) collective-permute-start(bf16[1,144,896]{2,1,0:T(8,128)(2,1)S(1)} %get-tuple-element.154), channel_id=1, source_target_pairs={{2,0},{4,2},{6,4},{7,6},{5,7},{3,5},{1,3},{0,1},{10,8},{12,10},{14... | collective-permute-start | bytes 774152 | tf_op jit(solution)/shard_map/ppermute | solution.py:566
  429.7 30.1 %collective-permute-start.39 = (bf16[384,1152]{1,0:T(8,128)(2,1)S(1)}, bf16[384,1152]{1,0:T(8,128)(2,1)S(1)}, u32[]{:S(2)}, u32[]{:S(2)}) collective-permute-start(bf16[384,1152]{1,0:T(8,128)(2,1)S(1)} %add_convert_fusion), channel_id=1, source_target_pairs={{0,16},{8,24},{16,0},{24,8},{1,17},{9,25},{17,1},{25,9},{2,18},{10... | collective-permute-start | bytes 2654216 | tf_op jit(solution)/shard_map/ppermute | solution.py:488
  444.0 6.9 %collective-permute-start.57 = (bf16[1,144,288]{1,2,0:T(8,128)(2,1)S(1)}, bf16[1,144,288]{1,2,0:T(8,128)(2,1)S(1)}, u32[]{:S(2)}, u32[]{:S(2)}) collective-permute-start(bf16[1,144,288]{1,2,0:T(8,128)(2,1)S(1)} %get-tuple-element.169), channel_id=1, source_target_pairs={{2,0},{4,2},{6,4},{7,6},{5,7},{3,5},{1,3},{0,1},{10,8},{12,10},{14... | collective-permute-start | bytes 248840 | tf_op jit(solution)/shard_map/ppermute | solution.py:566
  450.2 17.3 %collective-permute-start.47 = (bf16[144,288]{1,0:T(8,128)(2,1)S(1)}, bf16[144,288]{1,0:T(8,128)(2,1)S(1)}, u32[]{:S(2)}, u32[]{:S(2)}) collective-permute-start(bf16[144,288]{1,0:T(8,128)(2,1)S(1)} %get-tuple-element.176), channel_id=1, source_target_pairs={{0,0},{24,8},{16,16},{8,24},{1,1},{25,9},{17,17},{9,25},{2,2},{26,... | collective-permute-start | bytes 248840 | tf_op jit(solution)/shard_map/ppermute | solution.py:731
  450.9 17.9 %collective-permute-start.48 = (bf16[144,288]{1,0:T(8,128)(2,1)S(1)}, bf16[144,288]{1,0:T(8,128)(2,1)S(1)}, u32[]{:S(2)}, u32[]{:S(2)}) collective-permute-start(bf16[144,288]{1,0:T(8,128)(2,1)S(1)} %get-tuple-element.177), channel_id=1, source_target_pairs={{8,0},{0,8},{24,16},{16,24},{9,1},{1,9},{25,17},{17,25},{10,2},{2,... | collective-permute-start | bytes 248840 | tf_op jit(solution)/shard_map/ppermute | solution.py:731
  455.2 13.6 %collective-permute-start.49 = (bf16[144,288]{1,0:T(8,128)(2,1)S(1)}, bf16[144,288]{1,0:T(8,128)(2,1)S(1)}, u32[]{:S(2)}, u32[]{:S(2)}) collective-permute-start(bf16[144,288]{1,0:T(8,128)(2,1)S(1)} %get-tuple-element.178), channel_id=1, source_target_pairs={{16,0},{8,8},{0,16},{24,24},{17,1},{9,9},{1,17},{25,25},{18,2},{10... | collective-permute-start | bytes 248840 | tf_op jit(solution)/shard_map/ppermute | solution.py:731
  465.2 8.4 %collective-permute-start.56 = (bf16[1,144,288]{1,2,0:T(8,128)(2,1)S(1)}, bf16[1,144,288]{1,2,0:T(8,128)(2,1)S(1)}, u32[]{:S(2)}, u32[]{:S(2)}) collective-permute-start(bf16[1,144,288]{1,2,0:T(8,128)(2,1)S(1)} %get-tuple-element.164), channel_id=1, source_target_pairs={{0,2},{2,4},{4,6},{6,7},{7,5},{5,3},{3,1},{1,0},{8,10},{10,12},{12... | collective-permute-start | bytes 248840 | tf_op jit(solution)/shard_map/ppermute | solution.py:569
  (53 other events, 418.2 us)
Sparse Core Ops, SparseCore 0:
  10.8 73.9 all-gather.2
  87.5 56.0 all-gather.4

commit v2 on v1

v2 whole, which is shorter than its diff:
```python
import functools
import math

import jax
import jax.numpy as jnp
from jax import lax
from jax.experimental import pallas as pl
from jax.experimental.pallas import tpu as pltpu
from jax.sharding import PartitionSpec as P

HEADS = 16
HD = 72
EPSILON = 1e-06
SCALING = HD ** (-0.5)
LOG2E = math.log2(math.e)
NEG = -1e30
BF = jnp.bfloat16
F32 = jnp.float32


def windows(heads, width):
    out = []
    for h in range(heads):
        lo = h * HD // 128 * 128
        out.append((lo, min(width, -(-(h * HD + HD) // 128) * 128)))
    return out


def head_lanes(lo, h, shape):
    lane = lax.broadcasted_iota(jnp.int32, shape, 1) + lo
    return (lane >= h * HD) & (lane < h * HD + HD)


def head_pieces(wins, outs):
    pieces = {}
    for (lo, hi), out in zip(wins, outs):
        for c in range(lo, hi, 128):
            part = out[:, c - lo : min(c + 128, hi) - lo]
            pieces[c] = part if c not in pieces else pieces[c] + part
    return pieces.items()


def lanes(width):
    return -(-width // 128) * 128


def load_blocks(blocks, target, slots, first, sems):
    rows = blocks[0].shape[0]
    copies = []
    for i, block in enumerate(blocks):
        start = pl.multiple_of(slots[first + i] * rows, 8)
        copies.append(pltpu.make_async_copy(block, target.at[pl.ds(start, rows)], sems.at[i]))
        copies[-1].start()
    for copy in copies:
        copy.wait()


def marks(code):
    ids = lax.shift_right_logical(code, 1)
    keys = jnp.where((code & 1) == 0, ids, -1)
    return ids.astype(F32), keys.astype(F32)


def key_tiles(mine, ids, tile):
    before = jnp.sum(jnp.where(ids < jnp.min(mine), 1.0, 0.0)).astype(jnp.int32)
    upto = jnp.sum(jnp.where(ids <= jnp.max(mine), 1.0, 0.0)).astype(jnp.int32)
    return before // tile, (upto + tile - 1) // tile


def column(row, width):
    return jnp.broadcast_to(row, (width, row.shape[1])).T


def forward_kernel(heads, tile, q_ref, k_ref, v_ref, code_ref, o_ref, lse_ref, s_ref):
    i = pl.program_id(0)
    mine, _ = marks(code_ref[0:1, pl.ds(pl.multiple_of(i * tile, tile), tile)])
    lo, hi = key_tiles(mine, marks(code_ref[0:1, :])[0], tile)
    wins = windows(heads, q_ref.shape[1])
    rel = lax.broadcasted_iota(jnp.int32, (tile, tile), 0) - lax.broadcasted_iota(jnp.int32, (tile, tile), 1)
    qid = jnp.concatenate([column(mine, 128)] * (tile // 128), axis=1)
    queries = []
    for h, (a, b) in enumerate(wins):
        w = q_ref[:, a:b]
        queries.append(jnp.where(head_lanes(a, h, w.shape), w, jnp.zeros_like(w)))

    def scores(t, tops):
        rows = pl.ds(pl.multiple_of(t * tile, tile), tile)
        allowed = (qid == marks(code_ref[0:1, rows])[1]) | (rel == (t - i) * tile)
        new = []
        for h, (a, b) in enumerate(wins):
            s = lax.dot_general(queries[h], k_ref[rows, a:b], (((1,), (1,)), ((), ())), preferred_element_type=F32)
            s = jnp.where(allowed, s * (SCALING * LOG2E), NEG)
            s_ref[h, :, rows] = s
            top = tops[h]
            for c in range(0, tile, 128):
                top = jnp.maximum(top, s[:, c : c + 128])
            new.append(top)
        return tuple(new)

    tops = lax.fori_loop(lo, hi, scores, tuple(jnp.full((tile, 128), NEG, F32) for _ in range(heads)))
    tops = [jnp.broadcast_to(jnp.max(t, axis=1, keepdims=True), (tile, 128)) for t in tops]

    def attend(t, carry):
        rows = pl.ds(pl.multiple_of(t * tile, tile), tile)
        new = []
        for h, (a, b) in enumerate(wins):
            total, acc = carry[h]
            p = jnp.exp2(s_ref[h, :, rows] - jnp.concatenate([tops[h]] * (tile // 128), axis=1))
            for c in range(0, tile, 128):
                total = total + p[:, c : c + 128]
            acc = acc + jnp.dot(p.astype(BF), v_ref[rows, a:b], preferred_element_type=F32)
            new.append((total, acc))
        return tuple(new)

    start = tuple((jnp.zeros((tile, 128), F32), jnp.zeros((tile, b - a), F32)) for a, b in wins)
    carry = lax.fori_loop(lo, hi, attend, start)
    lane = lax.broadcasted_iota(jnp.int32, (tile, 128), 1)
    lse = jnp.zeros((tile, 128), F32)
    outs = []
    for h, (a, b) in enumerate(wins):
        total = jnp.sum(carry[h][0], axis=1, keepdims=True)
        out = carry[h][1] * (1.0 / total)
        outs.append(jnp.where(head_lanes(a, h, out.shape), out, 0.0))
        lse = jnp.where(lane == h, tops[h] + jnp.log2(total), lse)
    for c, part in head_pieces(wins, outs):
        o_ref[c : c + part.shape[1], :] = part.T.astype(BF)
    lse_ref[...] = lse.T[: lse_ref.shape[0], :]


def whole_block(shape):
    return pl.BlockSpec(shape, lambda *_: (0, 0))


def kept_block(shape):
    return pl.BlockSpec(shape, lambda *_: (0, 0), pipeline_mode=pl.Buffered(1))


def row_block(tile, width):
    return pl.BlockSpec((tile, width), lambda i, *_: (i, 0))


def lane_block(height, tile):
    return pl.BlockSpec((height, tile), lambda i, *_: (0, i))


def slot_block(tile, width):
    return pl.BlockSpec((tile, width), lambda i, slots: (slots[i], 0))


def attention_forward(q, k, v, code, heads, tile):
    n, width = q.shape
    return pl.pallas_call(
        functools.partial(forward_kernel, heads, tile),
        out_shape=(jax.ShapeDtypeStruct((width, n), BF), jax.ShapeDtypeStruct((8, n), F32)),
        grid_spec=pl.GridSpec(
            grid=(n // tile,),
            in_specs=[row_block(tile, width), whole_block((n, width)), whole_block((n, width)), whole_block((8, n))],
            out_specs=[lane_block(width, tile), lane_block(8, tile)],
            scratch_shapes=[pltpu.VMEM((heads, tile, n), F32)],
        ),
        compiler_params=pltpu.CompilerParams(vmem_limit_bytes=56 << 20),
        cost_estimate=pl.CostEstimate(flops=4 * n * n * 128 * heads, bytes_accessed=10 * n * width, transcendentals=n * n * heads),
        name="attention_forward",
    )(q, k, v, code)


def backward_kernel(
    heads, tile, count, first, slots, q_ref, k_ref, v_ref, o_ref, lse_ref, code_ref, *refs
):
    blocks, (out_ref, go_ref, dk_acc, dv_acc, dq_acc, kid_ref, sems) = refs[:count], refs[count:]
    i = pl.program_id(0)
    qid, _ = marks(code_ref[0:1, pl.ds(pl.multiple_of(i * tile, tile), tile)])
    lo, hi = key_tiles(qid, marks(code_ref[0:1, :])[0], tile)
    width = q_ref.shape[1]
    wins = windows(heads, width)

    @pl.when(i == 0)
    def _():
        load_blocks(blocks, go_ref, slots, 0, sems)
        dk_acc[...] = jnp.zeros_like(dk_acc)
        dv_acc[...] = jnp.zeros_like(dv_acc)
        for t in range(0, kid_ref.shape[0], tile):
            kid_ref[t : t + tile, :] = column(marks(code_ref[0:1, t : t + tile])[1], 128)

    here = pl.ds(pl.multiple_of(i * tile, tile), tile)
    rel = lax.broadcasted_iota(jnp.int32, (tile, tile), 1) - lax.broadcasted_iota(jnp.int32, (tile, tile), 0)
    go = go_ref[here, first : first + width]
    product = go.astype(F32).T * o_ref[...].astype(F32)
    inner = [jnp.sum(product[h * HD : (h + 1) * HD, :], axis=0, keepdims=True) for h in range(heads)]
    queries, grads = [], []
    for h, (a, b) in enumerate(wins):
        w, g = q_ref[:, a:b], go[:, a:b]
        on = head_lanes(a, h, w.shape)
        queries.append(jnp.where(on, w, jnp.zeros_like(w)))
        g = jnp.where(on, g, jnp.zeros_like(g))
        grads.append(g)
        dq_acc[h, :, : b - a] = jnp.zeros((tile, b - a), F32)
    lse = lse_ref[...]

    def step(t, carry):
        rows = pl.ds(pl.multiple_of(t * tile, tile), tile)
        allowed = (jnp.concatenate([kid_ref[rows, :]] * (tile // 128), axis=1) == qid) | (rel == (t - i) * tile)
        for h, (a, b) in enumerate(wins):
            key = k_ref[rows, a:b]
            s = lax.dot_general(key, queries[h], (((1,), (1,)), ((), ())), preferred_element_type=F32)
            p = jnp.exp2(jnp.where(allowed, s * (SCALING * LOG2E) - lse[h : h + 1, :], NEG))
            dp = lax.dot_general(v_ref[rows, a:b], grads[h], (((1,), (1,)), ((), ())), preferred_element_type=F32)
            ds = (p * (dp - inner[h])).astype(BF)
            dv_acc[rows, a:b] += jnp.dot(p.astype(BF), grads[h], preferred_element_type=F32)
            dk_acc[rows, a:b] += jnp.dot(ds, queries[h], preferred_element_type=F32)
            dq_acc[h, :, : b - a] += lax.dot_general(ds, key, (((0,), (0,)), ((), ())), preferred_element_type=F32)
        return carry

    lax.fori_loop(lo, hi, step, 0)
    outs = []
    for h, (a, b) in enumerate(wins):
        outs.append(jnp.where(head_lanes(a, h, (tile, b - a)), dq_acc[h, :, : b - a] * SCALING, 0.0))
    for c, part in head_pieces(wins, outs):
        out_ref[here, c : c + part.shape[1]] = part.astype(BF)

    @pl.when(i == pl.num_programs(0) - 1)
    def _():
        out_ref[:, width : 2 * width] = (dk_acc[...] * SCALING).astype(BF)
        out_ref[:, 2 * width : 3 * width] = dv_acc[...].astype(BF)


def attention_backward(q, k, v, o, go_blocks, first, slots, lse, code, heads, tile):
    n, width = q.shape
    count = len(go_blocks)
    return pl.pallas_call(
        functools.partial(backward_kernel, heads, tile, count, first),
        out_shape=jax.ShapeDtypeStruct((n, 3 * width), BF),
        grid_spec=pltpu.PrefetchScalarGridSpec(
            num_scalar_prefetch=1,
            grid=(n // tile,),
            in_specs=[
                row_block(tile, width),
                whole_block((n, width)),
                whole_block((n, width)),
                lane_block(width, tile),
                lane_block(8, tile),
                whole_block((8, n)),
            ]
            + [pl.BlockSpec(memory_space=pl.ANY)] * count,
            out_specs=whole_block((n, 3 * width)),
            scratch_shapes=[
                pltpu.VMEM((n, go_blocks[0].shape[1]), BF),
                pltpu.VMEM((n, width), F32),
                pltpu.VMEM((n, width), F32),
                pltpu.VMEM((heads, tile, 256), F32),
                pltpu.VMEM((n, 128), F32),
                pltpu.SemaphoreType.DMA((count,)),
            ],
        ),
        compiler_params=pltpu.CompilerParams(vmem_limit_bytes=56 << 20),
        cost_estimate=pl.CostEstimate(flops=10 * n * n * 128 * heads, bytes_accessed=16 * n * width, transcendentals=n * n * heads),
        name="attention_backward",
    )(slots, q, k, v, o, lse, code, *go_blocks)


def normalise(values):
    average = jnp.mean(values, axis=-1, keepdims=True)
    centred = values - average
    spread = jnp.mean(centred * centred, axis=-1, keepdims=True)
    inverse = lax.rsqrt(spread + EPSILON)
    return centred * inverse, inverse


def norm_back(normal, inverse, gain, grad):
    scaled = grad * gain
    first = jnp.mean(scaled, axis=-1, keepdims=True)
    second = jnp.mean(scaled * normal, axis=-1, keepdims=True)
    return (scaled - first - normal * second) * inverse


def gelu_both(u):
    root = math.sqrt(2.0 / math.pi)
    bent = jnp.tanh(root * (u + 0.044715 * u * u * u))
    half = 0.5 * (1.0 + bent)
    slope = half + 0.5 * u * (1.0 - bent * bent) * (root + 3 * 0.044715 * root * u * u)
    return u * half, slope


def dot(a, b):
    return jnp.dot(a, b, preferred_element_type=F32)


def dot_bt(a, b):
    return lax.dot_general(a, b, (((1,), (1,)), ((), ())), preferred_element_type=F32)


def dot_at(a, b):
    return lax.dot_general(a, b, (((0,), (0,)), ((), ())), preferred_element_type=F32)


def project_kernel(counts, bands, slots, *refs):
    xs, pieces = refs[: sum(counts)], refs[sum(counts) : sum(counts) + bands]
    gain, shift, q_bias, v_bias, x_out, h_out, q_out, k_out, v_out, w_out, out_out, code_out, x_now, sems = refs[
        sum(counts) + bands :
    ]
    j = pl.program_id(0)
    rows, cols = q_out.shape

    @pl.when(j == 0)
    def _():
        load_blocks(pieces, w_out, slots, len(counts), sems)
        out_out[:, :cols] = w_out[:, 3 * cols :]

    at = 0
    for i, count in enumerate(counts):

        @pl.when(j == i)
        def _(parts=xs[at : at + count]):
            start = 0
            for part in parts:
                size = min(part.shape[0], rows - start)
                x_now[start : start + size, :] = part[:size, :]
                start += size
            last = parts[-1].shape[0] - 16
            code = parts[-1][last:, :rows].astype(F32)[0:1, :]
            code_out[...] = jnp.broadcast_to(code, code_out.shape).astype(jnp.int32)

        at += count
    x = x_now[...]
    x_out[...] = x
    normal, _ = normalise(x.astype(F32))
    h = (normal * gain[...] + shift[...]).astype(BF)
    h_out[...] = h
    projected = dot(h, w_out[...])
    q_out[...] = (projected[:, :cols] + q_bias[...]).astype(BF)
    k_out[...] = projected[:, cols : 2 * cols].astype(BF)
    v_out[...] = (projected[:, 2 * cols : 3 * cols] + v_bias[...]).astype(BF)


def project(xs, pieces, slots, gain, shift, q_bias, v_bias, rows):
    width, cols, bands = xs[0][0].shape[1], q_bias.shape[1], len(pieces)
    counts = tuple(len(parts) for parts in xs)
    xs = [part for parts in xs for part in parts]
    n, columns = rows * len(counts), pieces[0].shape[1]
    shape = jax.ShapeDtypeStruct
    return pl.pallas_call(
        functools.partial(project_kernel, counts, bands),
        out_shape=[shape((n, width), BF)] * 2
        + [shape((n, cols), BF)] * 3
        + [shape((width, columns), BF), shape((width, lanes(cols)), BF), shape((8, n), jnp.int32)],
        grid_spec=pltpu.PrefetchScalarGridSpec(
            num_scalar_prefetch=1,
            grid=(len(counts),),
            in_specs=[kept_block(part.shape) for part in xs]
            + [pl.BlockSpec(memory_space=pl.ANY)] * bands
            + [kept_block((1, width))] * 2
            + [kept_block((1, cols))] * 2,
            out_specs=[slot_block(rows, width)] * 2
            + [slot_block(rows, cols)] * 3
            + [
                whole_block((width, columns)),
                whole_block((width, lanes(cols))),
                pl.BlockSpec((8, rows), lambda i, slots: (0, slots[i])),
            ],
            scratch_shapes=[pltpu.VMEM((rows, width), BF), pltpu.SemaphoreType.DMA((bands,))],
        ),
        compiler_params=pltpu.CompilerParams(vmem_limit_bytes=56 << 20),
        cost_estimate=pl.CostEstimate(flops=2 * n * width * columns, bytes_accessed=8 * n * width, transcendentals=n),
        name="norm_project",
    )(slots, *xs, *pieces, gain, shift, q_bias, v_bias)


def widen_kernel(count, slots, x_ref, *refs):
    os, w_outs = refs[:count], refs[count : 2 * count]
    (out_bias, gain, shift, w_up, up_bias, x_out, o_out, h_out, a_out, slope_out, w_out) = refs[2 * count :]
    j = pl.program_id(0)
    cols = os[0].shape[0]
    for v in range(count):

        @pl.when((j == 0) & (slots[0] == v))
        def _(v=v):
            for i in range(count):
                start = (v ^ i) * cols
                w_out[:, start : start + cols] = w_outs[i][:, :cols]

    for i in range(count):
        o_out[pl.ds(pl.multiple_of(slots[i] * cols, 8), cols), :] = os[i][...]
    x = x_ref[...].astype(F32) + (dot_at(o_out[...], w_out[...]) + out_bias[...])

    @pl.when(j == 0)
    def _():
        x_out[...] = x

    normal, _ = normalise(x)
    h = (normal * gain[...] + shift[...]).astype(BF)
    h_out[...] = h
    value, slope = gelu_both(dot(h, w_up[...]) + up_bias[...])
    a_out[...] = value.astype(BF)
    slope_out[...] = slope


def widen(x_all, os, w_outs, slots, out_bias, gain, shift, w_up, up_bias, rows):
    n, width = x_all.shape
    count, cols, hidden = len(os), os[0].shape[0], up_bias.shape[1]
    shape = jax.ShapeDtypeStruct
    return pl.pallas_call(
        functools.partial(widen_kernel, count),
        out_shape=[
            shape((rows, width), F32),
            shape((width, n), BF),
            shape((n, width), BF),
            shape((n, hidden), BF),
            shape((n, hidden), F32),
            shape((width, width), BF),
        ],
        grid_spec=pltpu.PrefetchScalarGridSpec(
            num_scalar_prefetch=1,
            grid=(count,),
            in_specs=[slot_block(rows, width)]
            + [pl.BlockSpec((cols, rows), lambda i, slots: (0, slots[i]))] * count
            + [kept_block(w_outs[0].shape)] * count
            + [kept_block((1, width))] * 3
            + [kept_block((width, hidden)), kept_block((1, hidden))],
            out_specs=[whole_block((rows, width)), lane_block(width, rows), slot_block(rows, width)]
            + [slot_block(rows, hidden)] * 2
            + [whole_block((width, width))],
        ),
        compiler_params=pltpu.CompilerParams(vmem_limit_bytes=60 << 20),
        cost_estimate=pl.CostEstimate(flops=2 * n * width * (width + hidden), bytes_accessed=16 * n * width, transcendentals=n * hidden),
        name="out_norm_up",
    )(slots, x_all, *os, *w_outs, out_bias, gain, shift, w_up, up_bias)


def narrow_kernel(slots, gy_ref, a_ref, slope_ref, w_up, w_down, *refs):
    gu_out, y_out, dh_out, sum_out = refs[-4:]

    @pl.when(pl.program_id(0) == 0)
    def _():
        sum_out[...] = jnp.zeros_like(sum_out)

    gu = (dot_bt(gy_ref[...], w_down[...]) * slope_ref[...]).astype(BF)
    gu_out[...] = gu
    dh_out[...] = dot_bt(gu, w_up[...]).astype(BF)
    y_out[...] = dot(a_ref[...], w_down[...]).astype(BF)
    sum_out[...] += jnp.sum(gu.astype(F32), axis=0, keepdims=True)


def narrow(gy, active, slope, w_up, w_down, slots, rows, first, count, carried):
    n, width = gy.shape
    hidden = w_up.shape[1]
    shape = jax.ShapeDtypeStruct

    def block(size):
        return pl.BlockSpec((rows, size), lambda i, slots: (slots[first + i], 0))

    return pl.pallas_call(
        narrow_kernel,
        out_shape=[shape((n, hidden), BF), shape((n, width), BF), shape((rows * count, width), BF), shape((1, hidden), F32)],
        grid_spec=pltpu.PrefetchScalarGridSpec(
            num_scalar_prefetch=1,
            grid=(count,),
            in_specs=[block(width), block(hidden), block(hidden)]
            + [kept_block((width, hidden)), kept_block((hidden, width))]
            + [pl.BlockSpec(memory_space=pl.ANY)] * len(carried),
            out_specs=[block(hidden), block(width), row_block(rows, width), whole_block((1, hidden))],
        ),
        input_output_aliases={6 + i: i for i in range(len(carried))},
        compiler_params=pltpu.CompilerParams(vmem_limit_bytes=56 << 20),
        cost_estimate=pl.CostEstimate(flops=6 * rows * count * width * hidden, bytes_accessed=16 * rows * count * width, transcendentals=0),
        name="down_and_back",
    )(slots, gy, active, slope, w_up, w_down, *carried)


def finish_kernel(slots, g_ref, x_ref, w_qkv, dh_out, sum_out, bias_out):
    @pl.when(pl.program_id(0) == 0)
    def _():
        sum_out[...] = jnp.zeros_like(sum_out)
        bias_out[...] = jnp.zeros_like(bias_out)

    g = g_ref[...]
    dh = dot_bt(g, w_qkv[:, : g.shape[1]])
    dh_out[...] = dh.astype(BF)
    normal, _ = normalise(x_ref[...].astype(F32))
    sum_out[0:1, :] += jnp.sum(dh * normal, axis=0, keepdims=True)
    sum_out[1:2, :] += jnp.sum(dh, axis=0, keepdims=True)
    bias_out[...] += jnp.sum(g.astype(F32), axis=0, keepdims=True)


def finish(gqkv, x_all, w_qkv, slots, rows):
    n, width = x_all.shape
    columns = gqkv.shape[1]
    shape = jax.ShapeDtypeStruct
    return pl.pallas_call(
        finish_kernel,
        out_shape=[shape((n, width), BF), shape((8, width), F32), shape((1, columns), F32)],
        grid_spec=pltpu.PrefetchScalarGridSpec(
            num_scalar_prefetch=1,
            grid=(n // rows,),
            in_specs=[slot_block(rows, columns), slot_block(rows, width), kept_block(w_qkv.shape)],
            out_specs=[row_block(rows, width), whole_block((8, width)), whole_block((1, columns))],
        ),
        compiler_params=pltpu.CompilerParams(vmem_limit_bytes=56 << 20),
        cost_estimate=pl.CostEstimate(flops=2 * n * width * columns, bytes_accessed=8 * n * width, transcendentals=n),
        name="project_back",
    )(slots, gqkv, x_all, w_qkv)


def weigh_kernel(count, h_ref, g_ref, o_ref, *refs):
    gas, (out_ref, ga_now) = refs[:count], refs[count:]
    rows = gas[0].shape[0]

    @pl.when(pl.program_id(0) == 0)
    def _():
        for i in range(count):
            ga_now[i * rows : (i + 1) * rows, :] = gas[i][...]

    columns = g_ref.shape[1]
    out_ref[:, :columns] = dot_at(h_ref[...], g_ref[...]).astype(BF)
    out_ref[:, columns:] = dot(o_ref[...], ga_now[...]).astype(BF)


def weigh(h_one, gqkv, o_all, gas):
    n, width = h_one.shape
    rows, cols = gas[0].shape
    columns, tile = gqkv.shape[1], width // 3
    return pl.pallas_call(
        functools.partial(weigh_kernel, len(gas)),
        out_shape=jax.ShapeDtypeStruct((width, columns + cols), BF),
        grid_spec=pl.GridSpec(
            grid=(width // tile,),
            in_specs=[lane_block(n, tile), kept_block((n, columns)), row_block(tile, n)] + [kept_block((rows, cols))] * len(gas),
            out_specs=row_block(tile, columns + cols),
            scratch_shapes=[pltpu.VMEM((n, cols), BF)],
        ),
        compiler_params=pltpu.CompilerParams(vmem_limit_bytes=56 << 20),
        cost_estimate=pl.CostEstimate(flops=2 * n * width * (columns + cols), bytes_accessed=6 * n * width, transcendentals=0),
        name="grads_qkv_out",
    )(h_one, gqkv, o_all, *gas)


def middle_kernel(count, terms, slots, *refs):
    parts, (x_ref, gy_ref, gain, w_out, dx_out, sum_out) = refs[:terms], refs[terms : terms + 6]
    go_outs, ga_outs = refs[terms + 6 : terms + 6 + count], refs[terms + 6 + count :]
    grad = sum(part[...].astype(F32) for part in parts)
    normal, inverse = normalise(x_ref[...])
    dx = gy_ref[...].astype(F32) + norm_back(normal, inverse, gain[...], grad)
    dx_out[...] = dx
    ga = dx.astype(BF)
    sum_out[0:1, :] = jnp.sum(grad * normal, axis=0, keepdims=True)
    sum_out[1:2, :] = jnp.sum(grad, axis=0, keepdims=True)
    sum_out[2:3, :] = jnp.sum(ga.astype(F32), axis=0, keepdims=True)
    go = dot_bt(ga, w_out[...]).astype(BF)
    cols = go_outs[0].shape[1]
    for v in range(count):

        @pl.when(slots[0] == v)
        def _(v=v):
            for i in range(count):
                start = (v ^ i) * cols
                go_outs[i][...] = go[:, start : start + cols]
                ga_outs[i][...] = ga[:, start : start + cols]


def middle(parts, x_one, gy, gain, w_out, slots, count):
    rows, width = x_one.shape
    cols, terms = width // count, len(parts)
    shape = jax.ShapeDtypeStruct
    block = kept_block((rows, width))
    outs = pl.pallas_call(
        functools.partial(middle_kernel, count, terms),
        out_shape=[shape((rows, width), F32), shape((8, width), F32)] + [shape((rows, cols), BF)] * (2 * count),
        grid_spec=pltpu.PrefetchScalarGridSpec(
            num_scalar_prefetch=1,
            grid=(1,),
            in_specs=[block] * (terms + 2) + [kept_block((1, width)), kept_block((width, width))],
            out_specs=[whole_block((rows, width)), whole_block((8, width))] + [whole_block((rows, cols))] * (2 * count),
        ),
        compiler_params=pltpu.CompilerParams(vmem_limit_bytes=56 << 20),
        cost_estimate=pl.CostEstimate(flops=2 * rows * width * width, bytes_accessed=20 * rows * width, transcendentals=rows),
        name="norm_back_out",
    )(slots, *parts, x_one, gy, gain, w_out)
    return outs[0], outs[1], outs[2 : 2 + count], outs[2 + count :]


def swap(value, axis, bits):
    size = lax.axis_size(axis)
    return lax.ppermute(value, axis, [(i, i ^ bits) for i in range(size)])


def hold(values, *earlier):
    return lax.optimization_barrier((values, earlier))[0]


def far_swaps(block):
    return [swap(block, "seq", j) for j in range(2, lax.axis_size("seq"), 2)]


def near_swaps(blocks):
    return [swap(block, "seq", 1) for block in blocks]


def woven(own, near):
    return [block for pair in zip(own, near) for block in pair]


def add_up(terms):
    return sum(term.astype(F32) for term in terms)


def ring_order(size):
    half = size // 2
    return [2 * p if p < half else 2 * (size - 1 - p) + 1 for p in range(size)]


def ring_index(pos, size):
    pos = pos % size
    return jnp.where(pos < size // 2, 2 * pos, 2 * (size - 1 - pos) + 1)


def ring_perms(size):
    order = ring_order(size)
    ahead = [(order[p], order[(p + 1) % size]) for p in range(size)]
    return ahead, [(b, a) for a, b in ahead]


def ring_position(size):
    f = lax.axis_index("fsdp")
    return jnp.where(f % 2 == 0, f // 2, size - 1 - f // 2)


class RingGather:
    def __init__(self, block):
        self.size = lax.axis_size("fsdp")
        self.ahead, self.back = ring_perms(self.size)
        self.pos = ring_position(self.size)
        self.pieces = [block]
        self.one = self.two = block
        self.done = 0

    def indices(self):
        owners = [ring_index(self.pos, self.size)]
        for t in range(1, self.size // 2 + 1):
            owners.append(ring_index(self.pos - t, self.size))
            if t < self.size // 2:
                owners.append(ring_index(self.pos + t, self.size))
        return owners

    def hop(self, *earlier):
        one, two = hold((self.one, self.two), earlier)
        self.done += 1
        self.one = lax.ppermute(one, "fsdp", self.ahead)
        new = [self.one]
        self.pieces.append(self.one)
        if self.done < self.size // 2:
            self.two = lax.ppermute(two, "fsdp", self.back)
            new.append(self.two)
            self.pieces.append(self.two)
        return new


class RingSum:
    def __init__(self, part):
        self.part = part
        self.size = lax.axis_size("fsdp")
        self.half = self.size // 2
        self.ahead, self.back = ring_perms(self.size)
        self.pos = ring_position(self.size)
        self.done = 0
        self.one = self.term(self.half).astype(BF)
        self.two = self.term(1 - self.half).astype(BF)

    def term(self, away):
        return self.part(ring_index(self.pos + away, self.size))

    def hop(self, *earlier):
        one, two = hold((self.one, self.two), earlier)
        self.done += 1
        t, half = self.done, self.half
        one = lax.ppermute(one, "fsdp", self.ahead)
        if t < half:
            two = lax.ppermute(two, "fsdp", self.back)
        self.one, self.two = one, two
        return [one] if t == half else [one, two]

    def add(self, *earlier):
        one, two = hold((self.one, self.two), earlier)
        t, half = self.done, self.half
        self.one = (one.astype(F32) + self.term(half - t)).astype(BF)
        if t < half - 1:
            self.two = (two.astype(F32) + self.term(t + 1 - half)).astype(BF)
        return [self.one, self.two]

    def result(self):
        return self.term(0) + self.one.astype(F32) + self.two.astype(F32)


class TotalSum:
    def __init__(self, vector):
        self.vector = vector
        self.steps = []
        for axis in ("seq", "fsdp"):
            bits = 1
            while bits < lax.axis_size(axis):
                self.steps.append((axis, bits))
                bits *= 2

    def hop(self, *earlier):
        vector = hold(self.vector, earlier)
        axis, bits = self.steps.pop(0)
        self.vector = vector + swap(vector, axis, bits)
        return [self.vector]


def local(
    inputs, image_ids, pad_mask, cotangent, w_qkv, w_out, w_up, w_down, ln1_gain, ln1_shift,
    q_bias, v_bias, out_bias, ln2_gain, ln2_shift, up_bias, down_bias,
):
    ns, nf = lax.axis_size("seq"), lax.axis_size("fsdp")
    s = lax.axis_index("seq")
    rows, width = inputs.shape[1:]
    n = rows * ns
    cols = width // ns
    band = w_up.shape[0]
    strip = w_down.shape[0]
    wide = lanes(-(-strip // ns) * nf)
    sub = wide // nf
    heads = HEADS // ns
    tile = 256
    order = [s ^ j for j in range(ns)]
    slots = jnp.stack([jnp.asarray(i, jnp.int32) for i in order])
    hops = nf // 8

    def row(vector):
        return vector[None, :]

    def own(vector):
        return lax.dynamic_slice_in_dim(vector, s * cols, cols)

    def own_hidden(array):
        count = array.shape[0]
        array = array.reshape(count, nf, strip)
        array = jnp.pad(array, ((0, 0), (0, 0), (0, ns * sub - strip)))
        return lax.dynamic_slice_in_dim(array, s * sub, sub, axis=2).reshape(count, wide)

    first = [lax.dynamic_slice_in_dim(w_qkv, t * width + s * cols, cols, axis=1) for t in range(3)]
    first.append(lax.dynamic_slice_in_dim(w_out, s * cols, cols, axis=1))
    ring_one = RingGather(jnp.concatenate(first, axis=1))
    x_own = inputs[0]
    code = (image_ids * 2 + pad_mask).astype(BF)
    x_pack = jnp.concatenate([x_own, jnp.pad(code, ((0, 15), (0, width - rows)))], axis=0)
    split = rows // 2
    x_parts = hold([x_pack[:split], x_pack[split:]], ring_one.one)
    far_a = far_swaps(x_parts[0])
    done = [far_a, *[ring_one.hop(x_parts) for _ in range(hops)]]
    up_mine = own_hidden(w_up)
    keep = (1 - pad_mask[0]).astype(F32)[:, None]
    gy_own = (cotangent[0].astype(F32) * keep).astype(BF)
    gy_parts = [gy_own[:split], gy_own[split:]]
    down_mine = lax.dynamic_slice_in_dim(jnp.pad(w_down, ((0, ns * sub - strip), (0, 0))), s * sub, sub, axis=0)
    up_part = own_hidden(row(up_bias))
    q_part, v_part = row(own(q_bias)), row(own(v_bias))
    one_slots = jnp.stack([jnp.asarray(i, jnp.int32) for i in order + ring_one.indices()])
    done = [*done, up_mine]

    far_b, gy_parts, slots, one_slots = hold((x_parts[1], gy_parts, slots, one_slots), *done)
    far_b = far_swaps(far_b)
    done = [far_b, gy_parts, slots, one_slots, *[ring_one.hop(*done) for _ in range(hops)]]
    full_up = lax.all_gather(hold(up_mine, *done), "fsdp", axis=0, tiled=True)
    down_mine, up_part, q_part, v_part = hold((down_mine, up_part, q_part, v_part), *done)
    x_pack, far_a, far_b = hold((x_pack, far_a, far_b), *done)
    near, near_a, near_b = near_swaps([x_pack]), near_swaps(far_a), near_swaps(far_b)
    done = [near, near_a, near_b, down_mine, up_part, q_part, v_part, *[ring_one.hop(*done) for _ in range(hops)]]
    x_blocks = [[x_pack], [near[0]]]
    for i in range(ns // 2 - 1):
        x_blocks += [[far_a[i], far_b[i]], [near_a[i], near_b[i]]]
    gy_far_a = far_swaps(hold(gy_parts[0], *done))
    done = [gy_far_a, *[ring_one.hop(*done) for _ in range(hops)]]

    x_blocks, pieces, gy_parts = hold((x_blocks, ring_one.pieces, gy_parts), *done)
    gy_far_b = far_swaps(gy_parts[1])
    x_all, h_one, q, k, v, full_qkv, out_cols, code = project(
        x_blocks, pieces, one_slots, row(ln1_gain), row(ln1_shift), q_part, v_part, rows
    )
    done = [gy_far_b, q, out_cols]
    full_down = lax.all_gather(hold(down_mine, q), "fsdp", axis=0, tiled=True)

    q, k, v, out_cols, gy_parts, gy_far_a, gy_far_b = hold((q, k, v, out_cols, gy_parts, gy_far_a, gy_far_b), *done)
    out_far = far_swaps(out_cols)
    gy_near = [near_swaps([gy_parts[0], *gy_far_a]), near_swaps([gy_parts[1], *gy_far_b])]
    done = [out_far, gy_near]
    o, lse = attention_forward(q, k, v, code, heads, tile)
    o, out_row = hold((o, [out_cols, *out_far]), *done)
    o_row = [o, *far_swaps(o)]
    w_outs = woven(out_row, near_swaps(out_row))
    gy_all = jnp.zeros((n, width), BF)
    gy_rows = [woven([gy_parts[h], *far], near) for h, (far, near) in enumerate(zip((gy_far_a, gy_far_b), gy_near))]
    for h in range(2):
        for j in range(ns):
            gy_all = lax.dynamic_update_slice(gy_all, gy_rows[h][j], (order[j] * rows + h * split, 0))
    done = [o_row, w_outs, gy_all]
    o_row = hold(o_row, *done)
    os = woven(o_row, near_swaps(o_row))

    x_one, o_all, h_two, active, slope, full_out = widen(
        x_all, os, w_outs, slots, row(out_bias), row(ln2_gain), row(ln2_shift), full_up, up_part, rows
    )
    gu, mixed, far_dh, far_sum = narrow(gy_all, active, slope, full_up, full_down, slots, rows, 2, ns - 2, ())

    def cut(array, j):
        return array[j * rows : (j + 1) * rows]

    def summed(a, b):
        return (a.astype(F32) + b.astype(F32)).astype(BF)

    far_near = near_swaps([cut(far_dh, j + 1) for j in range(0, ns - 2, 2)])
    far_held = [summed(cut(far_dh, 2 * i), got) for i, got in enumerate(far_near)]
    gu, mixed, far_held = hold((gu, mixed, far_held))
    terms = [swap(held, "seq", 2 * i + 2) for i, held in enumerate(far_held)]
    gu, mixed, near_dh, near_sum = narrow(gy_all, active, slope, full_up, full_down, slots, rows, 0, 2, (gu, mixed))
    near_dh, gy_all, active = hold((near_dh, gy_all, active))
    terms += [cut(near_dh, 0), swap(cut(near_dh, 1), "seq", 1)]
    grad_down_part = dot_at(active, gy_all).astype(BF)
    down_sum = lax.psum_scatter(grad_down_part, "fsdp", scatter_dimension=0, tiled=True)
    terms = hold(terms, grad_down_part)
    dx_one, sums_two, go_parts, ga_parts = middle(terms, x_one, gy_own, row(ln2_gain), full_out, slots, ns)
    go_parts, h_two, gu, mixed = hold((go_parts, h_two, gu, mixed))
    go_blocks = [block if j == 0 else swap(block, "seq", j) for j, block in enumerate(go_parts)]
    grad_up_part = dot_at(h_two, gu).astype(BF)
    up_sum = lax.psum_scatter(grad_up_part, "fsdp", scatter_dimension=0, tiled=True)

    def mixed_block(j):
        return lax.dynamic_slice_in_dim(mixed, order[j] * rows, rows, axis=0)

    mixed_near = near_swaps([mixed_block(j + 1) for j in range(0, ns, 2)])
    mixed_held = [summed(mixed_block(2 * i), mixed_near[i]) for i in range(1, ns // 2)]
    done = [go_blocks, grad_up_part, mixed_near, mixed_held]
    q, k, v, go_blocks, ga_parts, mixed_held = hold((q, k, v, go_blocks, ga_parts, mixed_held), *done)
    ga_blocks = [block if j == 0 else swap(block, "seq", j) for j, block in enumerate(ga_parts)]
    mixed_far = [swap(block, "seq", 2 * i + 2) for i, block in enumerate(mixed_held)]
    gqkv = attention_backward(q, k, v, o, go_blocks, 0, slots, lse, code, heads, tile)

    gqkv, ga_blocks, mixed_far = hold((gqkv, ga_blocks, mixed_far))
    grad_part = weigh(h_one, gqkv, o_all, ga_blocks)

    def bands(owner):
        return lax.dynamic_slice_in_dim(grad_part, owner * band, band, axis=0).astype(F32)

    ring_sum = RingSum(bands)
    gqkv = hold(gqkv, ring_sum.one, ring_sum.two)

    def ring_round(*earlier):
        new = []
        for _ in range(hops):
            if ring_sum.done:
                ring_sum.add(*earlier)
            new.append(ring_sum.hop(*earlier))
        return new

    done = [ring_round(gqkv)]
    dh_one_part, sums_one, sum_qkv = finish(gqkv, x_all, full_qkv, slots, rows)

    def spread(vector):
        return lax.dynamic_update_slice(jnp.zeros((width,), F32), vector, (s * cols,))

    def spread_hidden(vector):
        shifted = lax.dynamic_update_slice(jnp.zeros((nf, ns * sub), F32), vector.reshape(nf, sub), (0, s * sub))
        return shifted[:, :strip].reshape(nf * strip)

    sum_down_bias = jnp.sum(gy_own.astype(F32), axis=0)
    sum_hidden = spread_hidden((far_sum + near_sum)[0])
    vectors = [
        sums_one[0], sums_one[1], spread(sum_qkv[0, :cols]), spread(sum_qkv[0, 2 * cols :]), sums_two[2],
        sums_two[0], sums_two[1], sum_hidden, sum_down_bias,
    ]
    totals = TotalSum(jnp.concatenate(vectors))
    done += [dh_one_part]
    dh_one_part = hold(dh_one_part, *done)
    dh_near = near_swaps([cut(dh_one_part, j + 1) for j in range(0, ns, 2)])
    done = [dh_near, ring_round(*done), totals.hop(*done)]
    dh_near = hold(dh_near, *done)
    dh_held = [summed(cut(dh_one_part, 2 * i), dh_near[i]) for i in range(1, ns // 2)]
    dh_far_a = [swap(block[:split], "seq", 2 * i + 2) for i, block in enumerate(dh_held)]
    done = [dh_far_a, ring_round(*done)]
    dh_held = hold(dh_held, *done)
    dh_far_b = [swap(block[split:], "seq", 2 * i + 2) for i, block in enumerate(dh_held)]
    done = [dh_far_b, ring_round(*done)]
    total = totals.hop(*done)

    mine = hold(ring_sum.result(), *done)
    grad_out = mine[:, 3 * cols :]
    thirds = [mine[:, t * cols : (t + 1) * cols].astype(BF) for t in range(3)]
    got = []
    for p in range(3):
        perm = [((3 * d + p) % ns, d) for d in range(ns)]
        section = [0] * ns
        for d in range(ns):
            section[(3 * d + p) % ns] = (3 * d + p) // ns
        which = sum(jnp.where(s == i, t, 0) for i, t in enumerate(section))
        piece = jnp.where(which == 0, thirds[0], jnp.where(which == 1, thirds[1], thirds[2]))
        got.append(lax.ppermute(piece, "seq", perm))
    grad_qkv = jnp.concatenate(got, axis=1).astype(F32)
    while totals.steps:
        total = totals.hop(total)

    ratio = nf // ns

    def up_piece(j):
        return lax.dynamic_slice_in_dim(up_sum, order[j] * (ratio * sub), ratio * sub, axis=1)

    def down_piece(j):
        return lax.dynamic_slice_in_dim(down_sum, order[j] * cols, cols, axis=1)

    ups = jnp.zeros((ns, band, ratio * sub), BF)
    downs = jnp.zeros((ns, sub, cols), BF)
    for j in range(ns):
        a, b = up_piece(j), down_piece(j)
        if j:
            a, b = swap(a, "seq", j), swap(b, "seq", j)
        ups = lax.dynamic_update_slice(ups, a[None], (order[j], 0, 0))
        downs = lax.dynamic_update_slice(downs, b[None], (order[j], 0, 0))
    grad_up = jnp.concatenate(
        [
            jnp.concatenate([ups[i, :, h * sub : (h + 1) * sub] for i in range(ns)], axis=1)[:, :strip]
            for h in range(ratio)
        ],
        axis=1,
    ).astype(F32)
    grad_down = downs.reshape(ns * sub, cols)[:strip].astype(F32)

    dh_far = [jnp.concatenate(pair, axis=0) for pair in zip(dh_far_a, dh_far_b)]
    dh_one = add_up([cut(dh_one_part, 0), dh_near[0], *dh_far])
    normal_x, inverse_x = normalise(x_own.astype(F32))
    grad_inputs = (dx_one + norm_back(normal_x, inverse_x, ln1_gain, dh_one)).astype(BF)
    layer_out = (x_one + add_up([mixed_block(0), mixed_near[0], *mixed_far]) + down_bias).astype(BF)
    sums, start = [], 0
    for vector in vectors:
        sums.append(totals.vector[start : start + vector.shape[0]])
        start += vector.shape[0]
    return (layer_out[None], grad_inputs[None], grad_qkv, grad_out, grad_up, grad_down, *sums)


def solution(mesh):
    tokens, weights, shared = P("fsdp", "seq", None), P("fsdp", None), P()
    marks, grads = P("fsdp", "seq"), P("fsdp", "seq")
    return jax.shard_map(
        local,
        mesh=mesh,
        in_specs=(tokens, marks, marks, tokens) + (weights,) * 4 + (shared,) * 9,
        out_specs=(tokens, tokens) + (grads,) * 4 + (shared,) * 9,
        check_vma=False,
    )
```

time: 502 us -> 453 us (0.902)
  starting transfers between devices: 116 us -> 51.3 us
  Pallas kernels: 137 us -> 172 us
  local copies, waits for them, and re-layouts: 42.1 us -> 57.8 us
  other arithmetic: 38.5 us -> 23.5 us
  matrix products: 29.8 us -> 17.8 us
  waiting for transfers between devices: 116 us -> 109 us
    ppermute x39 -> x14, starting transfers between devices: 77.4 us -> 16.6 us  [the longest x4 5.97 us: hop(): self.one = lax.ppermute(one, 'fsdp', self.ahead)]
    ppermute x39 -> x14, waiting for transfers between devices: 82.5 us -> 53.7 us  [the longest x4 25.9 us: hop(): one = lax.ppermute(one, 'fsdp', self.ahead)]
    pallas_call x3 -> x5, Pallas kernels: 81.4 us -> 103 us  [the longest x1 44.5 us: attention_backward(): pl.pallas_call(functools.partial(backward_kernel, heads, tile, count, fir...]
    ppermute x32 -> x44, waiting for transfers between devices: 33 us -> 51.8 us  [swap(): return lax.ppermute(value, axis, [(i, i ^ bits) for i in range(size)])]
    dynamic_update_slice x7 -> x19, local copies, waits for them, and re-layouts: 1.63 us -> 11.1 us  [the longest x8 4.61 us: local(): lax.dynamic_update_slice(gy_all, gy_rows[h][j], (order[j] * rows + h * sp...]
    unnamed x85 -> x93, local copies, waits for them, and re-layouts: 12.8 us -> 5.47 us
    pallas_call x1 -> x2, Pallas kernels: 20.9 us -> 28.2 us  [narrow(): pl.pallas_call(narrow_kernel, out_shape=[shape((n, hidden), BF), shape((n...]
    slice x7 -> x13, local copies, waits for them, and re-layouts: 6.18 us -> 12.9 us  [the longest x3 5.72 us: cut(): return array[j * rows:(j + 1) * rows]]
  transfers between devices with their start and end apart: 76 -> 65, of which waited for: 30 -> 26; matrix products, arithmetic and copies ran while one was open for 19% -> 19% of each run, Pallas kernels for 24% -> 35%
where the time goes in v2:
time: 453 us; the launch traced here: 446 us
  Pallas kernels  172 us (38%)
  waiting for transfers between devices  109 us (24%)
  local copies, waits for them, and re-layouts  57.8 us (13%)
  starting transfers between devices  51.3 us (11%)
  other arithmetic  23.5 us (5%)
  matrix products  17.8 us (4%)
  between operations  15.1 us (3%)
    ppermute x44, waiting for transfers between devices, swap(): return lax.ppermute(value, axis, [(i, i ^ bits) for i in range(size)])  51.8 us
    pallas_call x1, Pallas kernels, attention_backward(): pl.pallas_call(functools.partial(backward_kernel, heads, tile, count, fir...  44.5 us
    pallas_call x1, Pallas kernels, attention_forward(): pl.pallas_call(functools.partial(forward_kernel, heads, tile), out_shape=...  30.7 us
    ppermute x44, starting transfers between devices, swap(): return lax.ppermute(value, axis, [(i, i ^ bits) for i in range(size)])  30.2 us
    pallas_call x2, Pallas kernels, narrow(): pl.pallas_call(narrow_kernel, out_shape=[shape((n, hidden), BF), shape((n...  28.2 us
    ppermute x4, waiting for transfers between devices, hop(): one = lax.ppermute(one, 'fsdp', self.ahead)  25.9 us
    pallas_call x1, Pallas kernels, widen(): pl.pallas_call(functools.partial(widen_kernel, count), out_shape=[shape((...  24.5 us
    ppermute x4, waiting for transfers between devices, hop(): self.one = lax.ppermute(one, 'fsdp', self.ahead)  19.3 us
  transfers between devices with their start and end apart: 65, of which 26 were waited for; matrix products, arithmetic and copies ran while one was open for 19% of the time, Pallas kernels for 35%

profile of v2, /device:TPU:0, one launch (start us, length us, event | category | flops | bytes accessed | tf_op | source)
XLA Modules:
  0.0 446.5 jit_solution(16411386313681261363)
XLA Ops:
  7.2 1.8 slice_bitcast_fusion
  11.1 1.6 constant_dynamic-slice_fusion.11
  13.6 2.9 collective-permute-start
  16.6 1.6 collective-permute-start.1
  18.8 3.2 reshape.79
  23.7 1.5 convert_reduce_fusion.1
  28.8 1.6 collective-permute-start.4
  30.8 6.5 %collective-permute-done.4.refs_9_ = bf16[144,1152]{1,0:T(8,128)(2,1)S(1)} collective-permute-done((bf16[144,1152]{1,0:T(8,128)(2,1)}, bf16[144,1152]{1,0:T(8,128)(2,1)S(1)}, u32[]{:S(2)}, u32[]{:S(2)}) %collective-permute-start.4) | collective-permute-done | bytes 331808 | tf_op jit(solution)/shard_map/ppermute | solution.py:646
  40.8 1.6 collective-permute-start.9
  46.3 1.8 pad_dynamic-slice_fusion.1
  48.1 3.7 collective-permute-done.9.refs_11_
  51.8 3.9 collective-permute-done.10.refs_12_
  59.1 9.1 %collective-permute-done.11.refs_13_ = bf16[144,1152]{1,0:T(8,128)(2,1)S(1)} collective-permute-done((bf16[144,1152]{1,0:T(8,128)(2,1)}, bf16[144,1152]{1,0:T(8,128)(2,1)S(1)}, u32[]{:S(2)}, u32[]{:S(2)}) %collective-permute-start.11) | collective-permute-done | bytes 331808 | tf_op jit(solution)/shard_map/ppermute | solution.py:646
  68.9 14.2 %norm_project.1 = (bf16[1536,1152]{1,0:T(8,128)(2,1)}, bf16[1536,1152]{1,0:T(8,128)(2,1)}, bf16[1536,288]{1,0:T(8,128)(2,1)}, bf16[1536,288]{1,0:T(8,128)(2,1)},...) custom-call(s32[12]{0:T(128)} %stack.59.slots, ...), custom_call_target="tpu_custom_call" | custom-call | flops 4076863488 | bytes 14155776 | tf_op jit(solution)/shard_map/norm_project/pallas_call | solution.py:341
  84.7 9.7 %collective-permute-done.13 = bf16[192,1152]{1,0:T(8,128)(2,1)} collective-permute-done((bf16[192,1152]{1,0:T(8,128)(2,1)}, bf16[192,1152]{1,0:T(8,128)(2,1)}, u32[]{:S(2)}, u32[]{:S(2)}) %collective-permute-start.13) | collective-permute-done | bytes 442400 | tf_op jit(solution)/shard_map/ppermute | solution.py:582
  96.8 30.7 %attention_forward.1 = (bf16[288,1536]{1,0:T(8,128)(2,1)}, f32[8,1536]{1,0:T(8,128)}) custom-call(bf16[1536,288]{1,0:T(8,128)(2,1)} %get-tuple-element.255.q_ref, bf16[1536,288]{1,0:T(8,128)(2,1)} %get-tuple-element.256.k_ref, bf16[1536,288]{1,0:T(8,128)(2,1)} %get-tuple-element.257.v_ref, s32[8,1536]{1,0:T(8,128)} %get-tuple-element.206.code_ref), custom_call_target="tpu_custom_call" | custom-call | flops 4831838208 | bytes 4423680 | tf_op jit(solution)/shard_map/attention_forward/pallas_call | solution.py:152
  133.8 18.1 %collective-permute-done.19.refs_2_ = bf16[288,1536]{1,0:T(8,128)(2,1)S(1)} collective-permute-done((bf16[288,1536]{1,0:T(8,128)(2,1)S(1)}, bf16[288,1536]{1,0:T(8,128)(2,1)S(1)}, u32[]{:S(2)}, u32[]{:S(2)}) %collective-permute-start.19) | collective-permute-done | bytes 884768 | tf_op jit(solution)/shard_map/ppermute | solution.py:582
  155.9 24.5 %out_norm_up.1 = (f32[384,1152]{1,0:T(8,128)}, bf16[1152,1536]{1,0:T(8,128)(2,1)}, bf16[1536,1152]{1,0:T(8,128)(2,1)}, bf16[1536,1152]{1,0:T(8,128)(2,1)}, f32[1...) custom-call(s32[4]{0:T(128)} %pad_add_fusion.slots, bf16[1536,1152]{1,0:T(8,128)(2,1)} %get-tuple-element.196.x_ref, ...), custom_call_target="tpu_custom_call" | custom-call | flops 8153726976 | bytes 28311552 | tf_op jit(solution)/shard_map/out_norm_up/pallas_call | solution.py:401
  180.4 14.3 %down_and_back.2 = (bf16[1536,1152]{1,0:T(8,128)(2,1)}, bf16[1536,1152]{1,0:T(8,128)(2,1)}, bf16[768,1152]{1,0:T(8,128)(2,1)}, f32[1,1152]{1,0:T(1,128)}) custom-call(s32[4]{0:T(128)} %pad_add_fusion.slots, bf16[1536,1152]{1,0:T(8,128)(2,1)} %copy-done.1, bf16[1536,1152]{1,0:T(8,128)(2,1)} %get-tuple-element.231.a_ref, ...), custom_call_target="tpu_custom_call" | custom-call | flops 6115295232 | bytes 14155776 | tf_op jit(solution)/shard_map/down_and_back/pallas_call | solution.py:451
  194.7 1.4 slice.150
  197.1 1.6 collective-permute-done.24
  198.7 1.4 add_convert_fusion.3
  200.8 13.9 %down_and_back.3 = (bf16[1536,1152]{1,0:T(8,128)(2,1)}, bf16[1536,1152]{1,0:T(8,128)(2,1)}, bf16[768,1152]{1,0:T(8,128)(2,1)}, f32[1,1152]{1,0:T(1,128)}) custom-call(s32[4]{0:T(128)} %pad_add_fusion.slots, bf16[1536,1152]{1,0:T(8,128)(2,1)} %copy-done.1, bf16[1536,1152]{1,0:T(8,128)(2,1)} %get-tuple-element.231.a_ref, ...), custom_call_target="tpu_custom_call", output_to_operand_aliasing={{0}: (6, {}), {1}: (7, {})} | custom-call | flops 6115295232 | bytes 14155776 | tf_op jit(solution)/shard_map/down_and_back/pallas_call | solution.py:451
  214.7 2.5 fusion.22
  217.9 1.4 reshape_squeeze.3
  219.8 1.4 dynamic_update_slice.67
  221.2 1.4 reshape.82
  222.6 9.4 %convolution_convert_fusion.1 = bf16[1152,1152]{1,0:T(8,128)(2,1)} fusion(bf16[1536,1152]{1,0:T(8,128)(2,1)} %get-tuple-element.231.a_ref, bf16[1536,1152]{1,0:T(8,128)(2,1)} %copy-done.1), kind=kOutput, calls=%fused_computation.1 | convolution fusion | flops 4078190592 | bytes 9732096 | tf_op jit(solution)/shard_map/dot_general | solution.py:293
  233.2 9.9 %norm_back_out.1 = (f32[384,1152]{1,0:T(8,128)}, f32[8,1152]{1,0:T(8,128)}, bf16[384,288]{1,0:T(8,128)(2,1)}, bf16[384,288]{1,0:T(8,128)(2,1)}, bf16[384,288]{1,...) custom-call(s32[4]{0:T(128)} %pad_add_fusion.slots, ...), custom_call_target="tpu_custom_call" | custom-call | flops 1019215872 | bytes 8847360 | tf_op jit(solution)/shard_map/norm_back_out/pallas_call | solution.py:564
  246.2 8.4 %convolution_convert_fusion = bf16[1152,1152]{1,0:T(8,128)(2,1)} fusion(bf16[1536,1152]{1,0:T(8,128)(2,1)} %get-tuple-element.253, bf16[1536,1152]{1,0:T(8,128)(2,1)S(1)} %copy-done.6), kind=kOutput, calls=%fused_computation | convolution fusion | flops 4078190592 | bytes 9732096 | tf_op jit(solution)/shard_map/dot_general | solution.py:293
  254.6 1.5 add_convert_fusion.2
  256.1 2.4 collective-permute-done.30.refs_3_
  262.3 44.5 %attention_backward.1.g_ref = bf16[1536,864]{1,0:T(8,128)(2,1)} custom-call(s32[4]{0:T(128)} %pad_add_fusion.slots, bf16[1536,288]{1,0:T(8,128)(2,1)} %get-tuple-element.255.q_ref, bf16[1536,288]{1,0:T(8,128)(2,1)} %get-tuple-element.256.k_ref, bf16[1536,288]{1,0:T(8,128)(2,1)} %get-tuple-element.257.v_ref, ...), custom_call_target="tpu_custom_call" | custom-call | flops 12079595520 | bytes 7077888 | tf_op jit(solution)/shard_map/attention_backward/pallas_call | solution.py:230
  307.7 10.1 %grads_qkv_out.1 = bf16[1152,1152]{1,0:T(8,128)(2,1)} custom-call(bf16[1536,1152]{1,0:T(8,128)(2,1)} %get-tuple-element.271.h_ref, bf16[1536,864]{1,0:T(8,128)(2,1)} %attention_backward.1.g_ref, bf16[1152,1536]{1,0:T(8,128)(2,1)} %get-tuple-element.272.o_ref, bf16[384,288]{1,0:T(8,128)(2,1)} %get-tuple-element.273.refs_0_, bf16[384,288]{1,0:T(8,128)(2,1)} %copy-done.43, ...), custom_call_target="tpu_custom_call" | custom-call | flops 4076863488 | bytes 10616832 | tf_op jit(solution)/shard_map/grads_qkv_out/pallas_call | solution.py:521
  319.0 3.3 collective-permute-start.37
  322.3 1.5 slice_reduce_fusion
  323.8 9.9 %project_back.1 = (bf16[1536,1152]{1,0:T(8,128)(2,1)}, f32[8,1152]{1,0:T(8,128)}, f32[1,864]{1,0:T(1,128)}) custom-call(s32[4]{0:T(128)} %pad_add_fusion.slots, bf16[1536,864]{1,0:T(8,128)(2,1)} %attention_backward.1.g_ref, bf16[1536,1152]{1,0:T(8,128)(2,1)} %get-tuple-element.196.x_ref, bf16[1152,1152]{1,0:T(8,128)(2,1)} %get-tuple-element.278.w_qkv), custom_call_target="tpu_custom_call" | custom-call | flops 3057647616 | bytes 14155776 | tf_op jit(solution)/shard_map/project_back/pallas_call | solution.py:488
  333.7 1.8 fusion.21
  337.4 1.5 dynamic_update_slice.65
  339.5 1.5 dynamic_update_slice.66
  340.9 2.3 add_convert_fusion.7
  343.2 1.3 collective-permute-start.40
  345.2 1.5 slice_reduce_fusion.3
  346.7 1.5 concatenate.26
  350.7 2.8 collective-permute-done.40
  354.6 1.7 add_convert_fusion
  357.0 1.4 add_convert_fusion.5
  358.4 1.8 collective-permute-start.44
  360.9 13.6 %collective-permute-done.44 = bf16[144,1152]{1,0:T(8,128)(2,1)S(1)} collective-permute-done((bf16[144,1152]{1,0:T(8,128)(2,1)S(1)}, bf16[144,1152]{1,0:T(8,128)(2,1)S(1)}, u32[]{:S(2)}, u32[]{:S(2)}) %collective-permute-start.44) | collective-permute-done | bytes 331808 | tf_op jit(solution)/shard_map/ppermute | solution.py:674
  374.5 2.1 collective-permute-done.45
  376.7 1.8 collective-permute-start.47
  378.5 2.8 fusion.13
  381.4 9.5 %collective-permute-done.47 = bf16[144,1152]{1,0:T(8,128)(2,1)S(1)} collective-permute-done((bf16[144,1152]{1,0:T(8,128)(2,1)S(1)}, bf16[144,1152]{1,0:T(8,128)(2,1)S(1)}, u32[]{:S(2)}, u32[]{:S(2)}) %collective-permute-start.47) | collective-permute-done | bytes 331808 | tf_op jit(solution)/shard_map/ppermute | solution.py:674
  393.3 2.5 collective-permute-done.57
  395.8 3.7 collective-permute-start.58
  399.5 3.3 collective-permute-start.50
  404.2 1.8 fusion.14
  409.6 5.1 %collective-permute-done.60 = f32[13520]{0:T(1024)S(1)} collective-permute-done((f32[13520]{0:T(1024)S(1)}, f32[13520]{0:T(1024)S(1)}, u32[]{:S(2)}, u32[]{:S(2)}) %collective-permute-start.60) | collective-permute-done | bytes 54112 | tf_op jit(solution)/shard_map/ppermute | solution.py:582
  420.4 3.0 collective-permute-done.55
  423.3 1.4 collective-permute-done.56
  426.0 3.4 reduce-scatter.3.cloned.1.call-done
  430.7 2.0 collective-permute-start.52
  433.9 2.8 collective-permute-done.52
  436.7 1.7 collective-permute-done.53
  (272 shorter events, 73.4 us)
Async XLA Ops:
  7.2 148.7 %all-gather.3.cloned.1.call-start = ((), (), s32[]{:S(2)}) async-start(), calls=%async_computation.2 | async-start | bytes 2985984 | tf_op jit(solution)/shard_map/all_gather | solution.py:763
  13.6 13.8 %collective-permute-start = (bf16[192,1152]{1,0:T(8,128)(2,1)}, bf16[192,1152]{1,0:T(8,128)(2,1)}, u32[]{:S(2)}, u32[]{:S(2)}) collective-permute-start(bf16[192,1152]{1,0:T(8,128)(2,1)} %slice_bitcast_fusion), channel_id=1, source_target_pairs={{0,16},{8,24},{16,0},{24,8},{1,17},{9,25},{17,1},{25,9},{2,18},{10... | collective-permute-start | bytes 1327112 | tf_op jit(solution)/shard_map/ppermute | solution.py:582
  16.6 10.8 %collective-permute-start.1 = (bf16[144,1152]{1,0:T(8,128)(2,1)}, bf16[144,1152]{1,0:T(8,128)(2,1)}, u32[]{:S(2)}, u32[]{:S(2)}) collective-permute-start(bf16[144,1152]{1,0:T(8,128)(2,1)} %concatenate.25.refs_6_), channel_id=1, source_target_pairs={{0,2},{2,4},{4,6},{6,7},{7,5},{5,3},{3,1},{1,0},{8,10},{10,12},{12... | collective-permute-start | bytes 995336 | tf_op jit(solution)/shard_map/ppermute | solution.py:646
  18.2 9.3 %collective-permute-start.2 = (bf16[144,1152]{1,0:T(8,128)(2,1)}, bf16[144,1152]{1,0:T(8,128)(2,1)}, u32[]{:S(2)}, u32[]{:S(2)}) collective-permute-start(bf16[144,1152]{1,0:T(8,128)(2,1)} %concatenate.25.refs_6_), channel_id=1, source_target_pairs={{2,0},{4,2},{6,4},{7,6},{5,7},{3,5},{1,3},{0,1},{10,8},{12,10},{14... | collective-permute-start | bytes 995336 | tf_op jit(solution)/shard_map/ppermute | solution.py:650
  27.4 11.9 %collective-permute-start.3 = (bf16[208,1152]{1,0:T(8,128)(2,1)S(1)}, bf16[208,1152]{1,0:T(8,128)(2,1)S(1)}, u32[]{:S(2)}, u32[]{:S(2)}) collective-permute-start(bf16[208,1152]{1,0:T(8,128)(2,1)S(1)} %slice.191), channel_id=1, source_target_pairs={{0,16},{8,24},{16,0},{24,8},{1,17},{9,25},{17,1},{25,9},{2,18},{10... | collective-permute-start | bytes 1437704 | tf_op jit(solution)/shard_map/ppermute | solution.py:582
  28.8 8.6 %collective-permute-start.4 = (bf16[144,1152]{1,0:T(8,128)(2,1)}, bf16[144,1152]{1,0:T(8,128)(2,1)S(1)}, u32[]{:S(2)}, u32[]{:S(2)}) collective-permute-start(bf16[144,1152]{1,0:T(8,128)(2,1)} %collective-permute-done.1.refs_7_), channel_id=1, source_target_pairs={{0,2},{2,4},{4,6},{6,7},{7,5},{5,3},{3,1},{1,0},{8,10},{10,12},{12... | collective-permute-start | bytes 995336 | tf_op jit(solution)/shard_map/ppermute | solution.py:646
  30.4 8.3 %collective-permute-start.5 = (bf16[144,1152]{1,0:T(8,128)(2,1)}, bf16[144,1152]{1,0:T(8,128)(2,1)S(1)}, u32[]{:S(2)}, u32[]{:S(2)}) collective-permute-start(bf16[144,1152]{1,0:T(8,128)(2,1)} %collective-permute-done.2.refs_8_), channel_id=1, source_target_pairs={{2,0},{4,2},{6,4},{7,6},{5,7},{3,5},{1,3},{0,1},{10,8},{12,10},{14... | collective-permute-start | bytes 995336 | tf_op jit(solution)/shard_map/ppermute | solution.py:650
  40.1 140.3 %all-gather.5.cloned.1.call-start = ((), (), s32[]{:S(2)}) async-start(), calls=%async_computation.3 | async-start | bytes 2985984 | tf_op jit(solution)/shard_map/all_gather | solution.py:780
  40.1 15.6 %collective-permute-start.6 = (bf16[400,1152]{1,0:T(8,128)(2,1)S(1)}, bf16[400,1152]{1,0:T(8,128)(2,1)S(1)}, u32[]{:S(2)}, u32[]{:S(2)}) collective-permute-start(bf16[400,1152]{1,0:T(8,128)(2,1)S(1)} %fusion.12.refs_0_), channel_id=1, source_target_pairs={{0,8},{8,0},{16,24},{24,16},{1,9},{9,1},{17,25},{25,17},{2,10},{10... | collective-permute-start | bytes 2764808 | tf_op jit(solution)/shard_map/ppermute | solution.py:582
  40.1 15.6 %collective-permute-start.8 = (bf16[208,1152]{1,0:T(8,128)(2,1)}, bf16[208,1152]{1,0:T(8,128)(2,1)}, u32[]{:S(2)}, u32[]{:S(2)}) collective-permute-start(bf16[208,1152]{1,0:T(8,128)(2,1)} %copy-done.35), channel_id=1, source_target_pairs={{0,8},{8,0},{16,24},{24,16},{1,9},{9,1},{17,25},{25,17},{2,10},{10... | collective-permute-start | bytes 1437704 | tf_op jit(solution)/shard_map/ppermute | solution.py:582
  40.6 15.1 %collective-permute-start.7 = (bf16[192,1152]{1,0:T(8,128)(2,1)}, bf16[192,1152]{1,0:T(8,128)(2,1)S(1)}, u32[]{:S(2)}, u32[]{:S(2)}) collective-permute-start(bf16[192,1152]{1,0:T(8,128)(2,1)} %collective-permute-done.refs_2_), channel_id=1, source_target_pairs={{0,8},{8,0},{16,24},{24,16},{1,9},{9,1},{17,25},{25,17},{2,10},{10... | collective-permute-start | bytes 1327112 | tf_op jit(solution)/shard_map/ppermute | solution.py:582
  40.8 11.0 %collective-permute-start.9 = (bf16[144,1152]{1,0:T(8,128)(2,1)}, bf16[144,1152]{1,0:T(8,128)(2,1)}, u32[]{:S(2)}, u32[]{:S(2)}) collective-permute-start(bf16[144,1152]{1,0:T(8,128)(2,1)} %copy-done.37), channel_id=1, source_target_pairs={{0,2},{2,4},{4,6},{6,7},{7,5},{5,3},{3,1},{1,0},{8,10},{10,12},{12... | collective-permute-start | bytes 995336 | tf_op jit(solution)/shard_map/ppermute | solution.py:646
  42.4 13.3 %collective-permute-start.10 = (bf16[144,1152]{1,0:T(8,128)(2,1)}, bf16[144,1152]{1,0:T(8,128)(2,1)}, u32[]{:S(2)}, u32[]{:S(2)}) collective-permute-start(bf16[144,1152]{1,0:T(8,128)(2,1)} %copy-done.38), channel_id=1, source_target_pairs={{2,0},{4,2},{6,4},{7,6},{5,7},{3,5},{1,3},{0,1},{10,8},{12,10},{14... | collective-permute-start | bytes 995336 | tf_op jit(solution)/shard_map/ppermute | solution.py:650
  55.7 12.4 %collective-permute-start.12 = (bf16[192,1152]{1,0:T(8,128)(2,1)}, bf16[192,1152]{1,0:T(8,128)(2,1)}, u32[]{:S(2)}, u32[]{:S(2)}) collective-permute-start(bf16[192,1152]{1,0:T(8,128)(2,1)} %get-tuple-element.209), channel_id=1, source_target_pairs={{0,16},{8,24},{16,0},{24,8},{1,17},{9,25},{17,1},{25,9},{2,18},{10... | collective-permute-start | bytes 1327112 | tf_op jit(solution)/shard_map/ppermute | solution.py:582
  56.7 11.5 %collective-permute-start.11 = (bf16[144,1152]{1,0:T(8,128)(2,1)}, bf16[144,1152]{1,0:T(8,128)(2,1)S(1)}, u32[]{:S(2)}, u32[]{:S(2)}) collective-permute-start(bf16[144,1152]{1,0:T(8,128)(2,1)} %collective-permute-done.9.refs_11_), channel_id=1, source_target_pairs={{0,2},{2,4},{4,6},{6,7},{7,5},{5,3},{3,1},{1,0},{8,10},{10,12},{12... | collective-permute-start | bytes 995336 | tf_op jit(solution)/shard_map/ppermute | solution.py:646
  83.2 332.9 %reduce-scatter.5.cloned.1.call-start = ((), (), s32[]{:S(2)}) async-start(), calls=%async_computation.5 | async-start | bytes 2985984 | tf_op jit(solution)/shard_map/reduce_scatter | solution.py:818
  83.4 11.0 %collective-permute-start.13 = (bf16[192,1152]{1,0:T(8,128)(2,1)}, bf16[192,1152]{1,0:T(8,128)(2,1)}, u32[]{:S(2)}, u32[]{:S(2)}) collective-permute-start(bf16[192,1152]{1,0:T(8,128)(2,1)} %get-tuple-element.211), channel_id=1, source_target_pairs={{0,16},{8,24},{16,0},{24,8},{1,17},{9,25},{17,1},{25,9},{2,18},{10... | collective-permute-start | bytes 1327112 | tf_op jit(solution)/shard_map/ppermute | solution.py:582
  94.4 35.8 %collective-permute-start.14 = (bf16[1152,384]{1,0:T(8,128)(2,1)}, bf16[1152,384]{1,0:T(8,128)(2,1)S(1)}, u32[]{:S(2)}, u32[]{:S(2)}) collective-permute-start(bf16[1152,384]{1,0:T(8,128)(2,1)} %get-tuple-element.214.refs_4_), channel_id=1, source_target_pairs={{0,16},{8,24},{16,0},{24,8},{1,17},{9,25},{17,1},{25,9},{2,18},{10... | collective-permute-start | bytes 2654216 | tf_op jit(solution)/shard_map/ppermute | solution.py:582
  95.7 33.2 %collective-permute-start.15 = (bf16[192,1152]{1,0:T(8,128)(2,1)}, bf16[192,1152]{1,0:T(8,128)(2,1)S(1)}, u32[]{:S(2)}, u32[]{:S(2)}) collective-permute-start(bf16[192,1152]{1,0:T(8,128)(2,1)} %get-tuple-element.209), channel_id=1, source_target_pairs={{0,8},{8,0},{16,24},{24,16},{1,9},{9,1},{17,25},{25,17},{2,10},{10... | collective-permute-start | bytes 1327112 | tf_op jit(solution)/shard_map/ppermute | solution.py:582
  95.7 34.4 %collective-permute-start.16 = (bf16[192,1152]{1,0:T(8,128)(2,1)}, bf16[192,1152]{1,0:T(8,128)(2,1)S(1)}, u32[]{:S(2)}, u32[]{:S(2)}) collective-permute-start(bf16[192,1152]{1,0:T(8,128)(2,1)} %collective-permute-done.12), channel_id=1, source_target_pairs={{0,8},{8,0},{16,24},{24,16},{1,9},{9,1},{17,25},{25,17},{2,10},{10... | collective-permute-start | bytes 1327112 | tf_op jit(solution)/shard_map/ppermute | solution.py:582
  96.2 33.9 %collective-permute-start.17 = (bf16[192,1152]{1,0:T(8,128)(2,1)}, bf16[192,1152]{1,0:T(8,128)(2,1)S(1)}, u32[]{:S(2)}, u32[]{:S(2)}) collective-permute-start(bf16[192,1152]{1,0:T(8,128)(2,1)} %get-tuple-element.211), channel_id=1, source_target_pairs={{0,8},{8,0},{16,24},{24,16},{1,9},{9,1},{17,25},{25,17},{2,10},{10... | collective-permute-start | bytes 1327112 | tf_op jit(solution)/shard_map/ppermute | solution.py:582
  96.2 33.9 %collective-permute-start.18 = (bf16[192,1152]{1,0:T(8,128)(2,1)}, bf16[192,1152]{1,0:T(8,128)(2,1)S(1)}, u32[]{:S(2)}, u32[]{:S(2)}) collective-permute-start(bf16[192,1152]{1,0:T(8,128)(2,1)} %collective-permute-done.13), channel_id=1, source_target_pairs={{0,8},{8,0},{16,24},{24,16},{1,9},{9,1},{17,25},{25,17},{2,10},{10... | collective-permute-start | bytes 1327112 | tf_op jit(solution)/shard_map/ppermute | solution.py:582
  130.3 21.7 %collective-permute-start.19 = (bf16[288,1536]{1,0:T(8,128)(2,1)S(1)}, bf16[288,1536]{1,0:T(8,128)(2,1)S(1)}, u32[]{:S(2)}, u32[]{:S(2)}) collective-permute-start(bf16[288,1536]{1,0:T(8,128)(2,1)S(1)} %copy-done.28), channel_id=1, source_target_pairs={{0,16},{8,24},{16,0},{24,8},{1,17},{9,25},{17,1},{25,9},{2,18},{10... | collective-permute-start | bytes 2654216 | tf_op jit(solution)/shard_map/ppermute | solution.py:582
  131.0 20.9 %collective-permute-start.20 = (bf16[1152,384]{1,0:T(8,128)(2,1)S(1)}, bf16[1152,384]{1,0:T(8,128)(2,1)S(1)}, u32[]{:S(2)}, u32[]{:S(2)}) collective-permute-start(bf16[1152,384]{1,0:T(8,128)(2,1)S(1)} %copy-done.29), channel_id=1, source_target_pairs={{0,8},{8,0},{16,24},{24,16},{1,9},{9,1},{17,25},{25,17},{2,10},{10... | collective-permute-start | bytes 2654216 | tf_op jit(solution)/shard_map/ppermute | solution.py:582
  131.0 20.9 %collective-permute-start.21 = (bf16[1152,384]{1,0:T(8,128)(2,1)S(1)}, bf16[1152,384]{1,0:T(8,128)(2,1)S(1)}, u32[]{:S(2)}, u32[]{:S(2)}) collective-permute-start(bf16[1152,384]{1,0:T(8,128)(2,1)S(1)} %collective-permute-done.14.refs_6_), channel_id=1, source_target_pairs={{0,8},{8,0},{16,24},{24,16},{1,9},{9,1},{17,25},{25,17},{2,10},{10... | collective-permute-start | bytes 2654216 | tf_op jit(solution)/shard_map/ppermute | solution.py:582
  152.0 3.0 collective-permute-start.22
  152.1 3.8 collective-permute-start.23
  196.1 2.6 collective-permute-start.24
  200.1 32.2 %collective-permute-start.25 = (bf16[384,1152]{1,0:T(8,128)(2,1)S(1)}, bf16[384,1152]{1,0:T(8,128)(2,1)S(1)}, u32[]{:S(2)}, u32[]{:S(2)}) collective-permute-start(bf16[384,1152]{1,0:T(8,128)(2,1)S(1)} %add_convert_fusion.3), channel_id=1, source_target_pairs={{0,16},{8,24},{16,0},{24,8},{1,17},{9,25},{17,1},{25,9},{2,18},{10... | collective-permute-start | bytes 2654216 | tf_op jit(solution)/shard_map/ppermute | solution.py:582
  217.2 15.1 %collective-permute-start.26 = (bf16[384,1152]{1,0:T(8,128)(2,1)S(1)}, bf16[384,1152]{1,0:T(8,128)(2,1)}, u32[]{:S(2)}, u32[]{:S(2)}) collective-permute-start(bf16[384,1152]{1,0:T(8,128)(2,1)S(1)} %get-tuple-element.341), channel_id=1, source_target_pairs={{0,8},{8,0},{16,24},{24,16},{1,9},{9,1},{17,25},{25,17},{2,10},{10... | collective-permute-start | bytes 2654216 | tf_op jit(solution)/shard_map/ppermute | solution.py:582
  232.1 197.4 %reduce-scatter.3.cloned.1.call-start = ((), (), s32[]{:S(2)}) async-start(), calls=%async_computation.4 | async-start | bytes 2985984 | tf_op jit(solution)/shard_map/reduce_scatter | solution.py:824
  243.1 12.9 %collective-permute-start.28 = (bf16[384,288]{1,0:T(8,128)(2,1)}, bf16[384,288]{1,0:T(8,128)(2,1)}, u32[]{:S(2)}, u32[]{:S(2)}) collective-permute-start(bf16[384,288]{1,0:T(8,128)(2,1)} %get-tuple-element.246), channel_id=1, source_target_pairs={{0,8},{8,0},{16,24},{24,16},{1,9},{9,1},{17,25},{25,17},{2,10},{10... | collective-permute-start | bytes 663560 | tf_op jit(solution)/shard_map/ppermute | solution.py:582
  243.8 12.3 %collective-permute-start.29 = (bf16[384,288]{1,0:T(8,128)(2,1)}, bf16[384,288]{1,0:T(8,128)(2,1)}, u32[]{:S(2)}, u32[]{:S(2)}) collective-permute-start(bf16[384,288]{1,0:T(8,128)(2,1)} %get-tuple-element.247), channel_id=1, source_target_pairs={{0,16},{8,24},{16,0},{24,8},{1,17},{9,25},{17,1},{25,9},{2,18},{10... | collective-permute-start | bytes 663560 | tf_op jit(solution)/shard_map/ppermute | solution.py:582
  245.1 13.4 %collective-permute-start.30 = (bf16[384,288]{1,0:T(8,128)(2,1)}, bf16[384,288]{1,0:T(8,128)(2,1)}, u32[]{:S(2)}, u32[]{:S(2)}) collective-permute-start(bf16[384,288]{1,0:T(8,128)(2,1)} %get-tuple-element.248), channel_id=1, source_target_pairs={{0,24},{8,16},{16,8},{24,0},{1,25},{9,17},{17,9},{25,1},{2,26},{10... | collective-permute-start | bytes 663560 | tf_op jit(solution)/shard_map/ppermute | solution.py:582
  245.3 9.2 %collective-permute-start.31 = (bf16[384,1152]{1,0:T(8,128)(2,1)S(1)}, bf16[384,1152]{1,0:T(8,128)(2,1)S(1)}, u32[]{:S(2)}, u32[]{:S(2)}) collective-permute-start(bf16[384,1152]{1,0:T(8,128)(2,1)S(1)} %get-tuple-element.334), channel_id=1, source_target_pairs={{0,8},{8,0},{16,24},{24,16},{1,9},{9,1},{17,25},{25,17},{2,10},{10... | collective-permute-start | bytes 2654216 | tf_op jit(solution)/shard_map/ppermute | solution.py:582
  246.1 12.4 %collective-permute-start.27 = (bf16[384,1152]{1,0:T(8,128)(2,1)S(1)}, bf16[384,1152]{1,0:T(8,128)(2,1)}, u32[]{:S(2)}, u32[]{:S(2)}) collective-permute-start(bf16[384,1152]{1,0:T(8,128)(2,1)S(1)} %get-tuple-element.333), channel_id=1, source_target_pairs={{0,8},{8,0},{16,24},{24,16},{1,9},{9,1},{17,25},{25,17},{2,10},{10... | collective-permute-start | bytes 2654216 | tf_op jit(solution)/shard_map/ppermute | solution.py:582
  258.5 48.2 %collective-permute-start.32 = (bf16[384,288]{1,0:T(8,128)(2,1)S(1)}, bf16[384,288]{1,0:T(8,128)(2,1)S(1)}, u32[]{:S(2)}, u32[]{:S(2)}) collective-permute-start(bf16[384,288]{1,0:T(8,128)(2,1)S(1)} %copy-done.42), channel_id=1, source_target_pairs={{0,8},{8,0},{16,24},{24,16},{1,9},{9,1},{17,25},{25,17},{2,10},{10... | collective-permute-start | bytes 663560 | tf_op jit(solution)/shard_map/ppermute | solution.py:582
  259.5 47.3 %collective-permute-start.33 = (bf16[384,288]{1,0:T(8,128)(2,1)S(1)}, bf16[384,288]{1,0:T(8,128)(2,1)S(1)}, u32[]{:S(2)}, u32[]{:S(2)}) collective-permute-start(bf16[384,288]{1,0:T(8,128)(2,1)S(1)} %copy-done.41), channel_id=1, source_target_pairs={{0,16},{8,24},{16,0},{24,8},{1,17},{9,25},{17,1},{25,9},{2,18},{10... | collective-permute-start | bytes 663560 | tf_op jit(solution)/shard_map/ppermute | solution.py:582
  260.8 46.0 %collective-permute-start.34 = (bf16[384,288]{1,0:T(8,128)(2,1)S(1)}, bf16[384,288]{1,0:T(8,128)(2,1)S(1)}, u32[]{:S(2)}, u32[]{:S(2)}) collective-permute-start(bf16[384,288]{1,0:T(8,128)(2,1)S(1)} %copy-done.40), channel_id=1, source_target_pairs={{0,24},{8,16},{16,8},{24,0},{1,25},{9,17},{17,9},{25,1},{2,26},{10... | collective-permute-start | bytes 663560 | tf_op jit(solution)/shard_map/ppermute | solution.py:582
  260.9 45.9 %collective-permute-start.35 = (bf16[384,1152]{1,0:T(8,128)(2,1)S(1)}, bf16[384,1152]{1,0:T(8,128)(2,1)S(1)}, u32[]{:S(2)}, u32[]{:S(2)}) collective-permute-start(bf16[384,1152]{1,0:T(8,128)(2,1)S(1)} %add_convert_fusion.2), channel_id=1, source_target_pairs={{0,16},{8,24},{16,0},{24,8},{1,17},{9,25},{17,1},{25,9},{2,18},{10... | collective-permute-start | bytes 2654216 | tf_op jit(solution)/shard_map/ppermute | solution.py:582
  318.9 14.8 %collective-permute-start.36 = (bf16[144,1152]{1,0:T(8,128)(2,1)S(1)}, bf16[144,1152]{1,0:T(8,128)(2,1)S(1)}, u32[]{:S(2)}, u32[]{:S(2)}) collective-permute-start(bf16[144,1152]{1,0:T(8,128)(2,1)S(1)} %get-tuple-element.280), channel_id=1, source_target_pairs={{0,2},{2,4},{4,6},{6,7},{7,5},{5,3},{3,1},{1,0},{8,10},{10,12},{12... | collective-permute-start | bytes 995336 | tf_op jit(solution)/shard_map/ppermute | solution.py:674
  319.0 14.7 %collective-permute-start.37 = (bf16[144,1152]{1,0:T(8,128)(2,1)S(1)}, bf16[144,1152]{1,0:T(8,128)(2,1)S(1)}, u32[]{:S(2)}, u32[]{:S(2)}) collective-permute-start(bf16[144,1152]{1,0:T(8,128)(2,1)S(1)} %get-tuple-element.281), channel_id=1, source_target_pairs={{2,0},{4,2},{6,4},{7,6},{5,7},{3,5},{1,3},{0,1},{10,8},{12,10},{14... | collective-permute-start | bytes 995336 | tf_op jit(solution)/shard_map/ppermute | solution.py:676
  335.6 19.1 %collective-permute-start.38 = (bf16[384,1152]{1,0:T(8,128)(2,1)S(1)}, bf16[384,1152]{1,0:T(8,128)(2,1)S(1)}, u32[]{:S(2)}, u32[]{:S(2)}) collective-permute-start(bf16[384,1152]{1,0:T(8,128)(2,1)S(1)} %get-tuple-element.332), channel_id=1, source_target_pairs={{0,8},{8,0},{16,24},{24,16},{1,9},{9,1},{17,25},{25,17},{2,10},{10... | collective-permute-start | bytes 2654216 | tf_op jit(solution)/shard_map/ppermute | solution.py:582
  335.8 18.8 %collective-permute-start.39 = (bf16[384,1152]{1,0:T(8,128)(2,1)S(1)}, bf16[384,1152]{1,0:T(8,128)(2,1)}, u32[]{:S(2)}, u32[]{:S(2)}) collective-permute-start(bf16[384,1152]{1,0:T(8,128)(2,1)S(1)} %get-tuple-element.331), channel_id=1, source_target_pairs={{0,8},{8,0},{16,24},{24,16},{1,9},{9,1},{17,25},{25,17},{2,10},{10... | collective-permute-start | bytes 2654216 | tf_op jit(solution)/shard_map/ppermute | solution.py:582
  343.2 10.3 %collective-permute-start.40 = (bf16[144,1152]{1,0:T(8,128)(2,1)}, bf16[144,1152]{1,0:T(8,128)(2,1)}, u32[]{:S(2)}, u32[]{:S(2)}) collective-permute-start(bf16[144,1152]{1,0:T(8,128)(2,1)} %get-tuple-element.285), channel_id=1, source_target_pairs={{0,2},{2,4},{4,6},{6,7},{7,5},{5,3},{3,1},{1,0},{8,10},{10,12},{12... | collective-permute-start | bytes 995336 | tf_op jit(solution)/shard_map/ppermute | solution.py:674
  344.5 10.1 %collective-permute-start.41 = (bf16[144,1152]{1,0:T(8,128)(2,1)}, bf16[144,1152]{1,0:T(8,128)(2,1)}, u32[]{:S(2)}, u32[]{:S(2)}) collective-permute-start(bf16[144,1152]{1,0:T(8,128)(2,1)} %get-tuple-element.286), channel_id=1, source_target_pairs={{2,0},{4,2},{6,4},{7,6},{5,7},{3,5},{1,3},{0,1},{10,8},{12,10},{14... | collective-permute-start | bytes 995336 | tf_op jit(solution)/shard_map/ppermute | solution.py:676
  356.4 20.2 %collective-permute-start.43 = (bf16[192,1152]{1,0:T(8,128)(2,1)S(1)}, bf16[192,1152]{1,0:T(8,128)(2,1)S(1)}, u32[]{:S(2)}, u32[]{:S(2)}) collective-permute-start(bf16[192,1152]{1,0:T(8,128)(2,1)S(1)} %slice.195), channel_id=1, source_target_pairs={{0,16},{8,24},{16,0},{24,8},{1,17},{9,25},{17,1},{25,9},{2,18},{10... | collective-permute-start | bytes 1327112 | tf_op jit(solution)/shard_map/ppermute | solution.py:582
  358.4 16.0 %collective-permute-start.44 = (bf16[144,1152]{1,0:T(8,128)(2,1)S(1)}, bf16[144,1152]{1,0:T(8,128)(2,1)S(1)}, u32[]{:S(2)}, u32[]{:S(2)}) collective-permute-start(bf16[144,1152]{1,0:T(8,128)(2,1)S(1)} %get-tuple-element.297), channel_id=1, source_target_pairs={{0,2},{2,4},{4,6},{6,7},{7,5},{5,3},{3,1},{1,0},{8,10},{10,12},{12... | collective-permute-start | bytes 995336 | tf_op jit(solution)/shard_map/ppermute | solution.py:674
  360.2 16.3 %collective-permute-start.45 = (bf16[144,1152]{1,0:T(8,128)(2,1)S(1)}, bf16[144,1152]{1,0:T(8,128)(2,1)S(1)}, u32[]{:S(2)}, u32[]{:S(2)}) collective-permute-start(bf16[144,1152]{1,0:T(8,128)(2,1)S(1)} %get-tuple-element.298), channel_id=1, source_target_pairs={{2,0},{4,2},{6,4},{7,6},{5,7},{3,5},{1,3},{0,1},{10,8},{12,10},{14... | collective-permute-start | bytes 995336 | tf_op jit(solution)/shard_map/ppermute | solution.py:676
  376.7 14.3 %collective-permute-start.47 = (bf16[144,1152]{1,0:T(8,128)(2,1)S(1)}, bf16[144,1152]{1,0:T(8,128)(2,1)S(1)}, u32[]{:S(2)}, u32[]{:S(2)}) collective-permute-start(bf16[144,1152]{1,0:T(8,128)(2,1)S(1)} %add_convert_fusion.4), channel_id=1, source_target_pairs={{0,2},{2,4},{4,6},{6,7},{7,5},{5,3},{3,1},{1,0},{8,10},{10,12},{12... | collective-permute-start | bytes 995336 | tf_op jit(solution)/shard_map/ppermute | solution.py:674
  381.4 10.1 %collective-permute-start.46 = (bf16[192,1152]{1,0:T(8,128)(2,1)S(1)}, bf16[192,1152]{1,0:T(8,128)(2,1)S(1)}, u32[]{:S(2)}, u32[]{:S(2)}) collective-permute-start(bf16[192,1152]{1,0:T(8,128)(2,1)S(1)} %slice.166), channel_id=1, source_target_pairs={{0,16},{8,24},{16,0},{24,8},{1,17},{9,25},{17,1},{25,9},{2,18},{10... | collective-permute-start | bytes 1327112 | tf_op jit(solution)/shard_map/ppermute | solution.py:582
  391.5 4.2 collective-permute-start.57
  395.8 7.8 %collective-permute-start.58 = (f32[13520]{0:T(1024)S(1)}, f32[13520]{0:T(1024)S(1)}, u32[]{:S(2)}, u32[]{:S(2)}) collective-permute-start(f32[13520]{0:T(1024)S(1)} %add.427), channel_id=1, source_target_pairs={{0,1},{1,0},{2,3},{3,2},{4,5},{5,4},{6,7},{7,6},{8,9},{9,8},{10,11... | collective-permute-start | bytes 162248 | tf_op jit(solution)/shard_map/ppermute | solution.py:582
  399.5 9.2 %collective-permute-start.50 = (bf16[144,288]{1,0:T(8,128)(2,1)S(1)}, bf16[144,288]{1,0:T(8,128)(2,1)S(1)}, u32[]{:S(2)}, u32[]{:S(2)}) collective-permute-start(bf16[144,288]{1,0:T(8,128)(2,1)S(1)} %get-tuple-element.364), channel_id=1, source_target_pairs={{16,0},{8,8},{0,16},{24,24},{17,1},{9,9},{1,17},{25,25},{18,2},{10... | collective-permute-start | bytes 248840 | tf_op jit(solution)/shard_map/ppermute | solution.py:895
  402.8 5.9 %collective-permute-start.49 = (bf16[144,288]{1,0:T(8,128)(2,1)S(1)}, bf16[144,288]{1,0:T(8,128)(2,1)S(1)}, u32[]{:S(2)}, u32[]{:S(2)}) collective-permute-start(bf16[144,288]{1,0:T(8,128)(2,1)S(1)} %get-tuple-element.363), channel_id=1, source_target_pairs={{8,0},{0,8},{24,16},{16,24},{9,1},{1,9},{25,17},{17,25},{10,2},{2,... | collective-permute-start | bytes 248840 | tf_op jit(solution)/shard_map/ppermute | solution.py:895
  402.9 5.8 %collective-permute-start.48 = (bf16[144,288]{1,0:T(8,128)(2,1)S(1)}, bf16[144,288]{1,0:T(8,128)(2,1)S(1)}, u32[]{:S(2)}, u32[]{:S(2)}) collective-permute-start(bf16[144,288]{1,0:T(8,128)(2,1)S(1)} %get-tuple-element.362), channel_id=1, source_target_pairs={{0,0},{24,8},{16,16},{8,24},{1,1},{25,9},{17,17},{9,25},{2,2},{26,... | collective-permute-start | bytes 248840 | tf_op jit(solution)/shard_map/ppermute | solution.py:895
  403.6 4.2 collective-permute-start.59
  407.8 6.9 %collective-permute-start.60 = (f32[13520]{0:T(1024)S(1)}, f32[13520]{0:T(1024)S(1)}, u32[]{:S(2)}, u32[]{:S(2)}) collective-permute-start(f32[13520]{0:T(1024)S(1)} %add.429), channel_id=1, source_target_pairs={{0,4},{1,5},{2,6},{3,7},{4,0},{5,1},{6,2},{7,3},{8,12},{9,13},{10,... | collective-permute-start | bytes 162248 | tf_op jit(solution)/shard_map/ppermute | solution.py:582
  417.3 3.0 collective-permute-start.54
  417.4 5.9 %collective-permute-start.55 = (bf16[144,288]{1,0:T(8,128)(2,1)S(1)}, bf16[144,288]{1,0:T(8,128)(2,1)S(1)}, u32[]{:S(2)}, u32[]{:S(2)}) collective-permute-start(bf16[144,288]{1,0:T(8,128)(2,1)S(1)} %get-tuple-element.357), channel_id=1, source_target_pairs={{0,16},{8,24},{16,0},{24,8},{1,17},{9,25},{17,1},{25,9},{2,18},{10... | collective-permute-start | bytes 248840 | tf_op jit(solution)/shard_map/ppermute | solution.py:582
  418.1 6.7 %collective-permute-start.56 = (bf16[144,288]{1,0:T(8,128)(2,1)S(1)}, bf16[144,288]{1,0:T(8,128)(2,1)S(1)}, u32[]{:S(2)}, u32[]{:S(2)}) collective-permute-start(bf16[144,288]{1,0:T(8,128)(2,1)S(1)} %get-tuple-element.356), channel_id=1, source_target_pairs={{0,24},{8,16},{16,8},{24,0},{1,25},{9,17},{17,9},{25,1},{2,26},{10... | collective-permute-start | bytes 248840 | tf_op jit(solution)/shard_map/ppermute | solution.py:582
  430.6 3.3 collective-permute-start.51
  430.7 6.0 %collective-permute-start.52 = (bf16[144,288]{1,0:T(8,128)(2,1)S(1)}, bf16[144,288]{1,0:T(8,128)(2,1)S(1)}, u32[]{:S(2)}, u32[]{:S(2)}) collective-permute-start(bf16[144,288]{1,0:T(8,128)(2,1)S(1)} %get-tuple-element.360), channel_id=1, source_target_pairs={{0,16},{8,24},{16,0},{24,8},{1,17},{9,25},{17,1},{25,9},{2,18},{10... | collective-permute-start | bytes 248840 | tf_op jit(solution)/shard_map/ppermute | solution.py:582
  432.7 5.7 %collective-permute-start.53 = (bf16[144,288]{1,0:T(8,128)(2,1)S(1)}, bf16[144,288]{1,0:T(8,128)(2,1)S(1)}, u32[]{:S(2)}, u32[]{:S(2)}) collective-permute-start(bf16[144,288]{1,0:T(8,128)(2,1)S(1)} %get-tuple-element.359), channel_id=1, source_target_pairs={{0,24},{8,16},{16,8},{24,0},{1,25},{9,17},{17,9},{25,1},{2,26},{10... | collective-permute-start | bytes 248840 | tf_op jit(solution)/shard_map/ppermute | solution.py:582
  (47 other events, 462.9 us)
Sparse Core Ops, SparseCore 0:
  39.5 60.8 all-gather.2
  102.6 53.6 all-gather.4
  232.2 70.9 reduce-scatter.4
  349.1 80.3 reduce-scatter.2

commit v3 on v2

--- a/solution.py
+++ b/solution.py
@@ -10,6 +10,7 @@
 
 HEADS = 16
 HD = 72
+IMG_TOK = 729
 EPSILON = 1e-06
 SCALING = HD ** (-0.5)
 LOG2E = math.log2(math.e)
@@ -67,64 +68,52 @@
     return before // tile, (upto + tile - 1) // tile
 
 
+def most_tiles(tile, length):
+    return min(length // tile, -(-(tile + 2 * IMG_TOK) // tile) + 1)
+
+
 def column(row, width):
     return jnp.broadcast_to(row, (width, row.shape[1])).T
 
 
-def forward_kernel(heads, tile, q_ref, k_ref, v_ref, code_ref, o_ref, lse_ref, s_ref):
+def forward_kernel(heads, tile, q_ref, k_ref, v_ref, code_ref, o_ref, lse_ref):
     i = pl.program_id(0)
     mine, _ = marks(code_ref[0:1, pl.ds(pl.multiple_of(i * tile, tile), tile)])
     lo, hi = key_tiles(mine, marks(code_ref[0:1, :])[0], tile)
     wins = windows(heads, q_ref.shape[1])
-    rel = lax.broadcasted_iota(jnp.int32, (tile, tile), 0) - lax.broadcasted_iota(jnp.int32, (tile, tile), 1)
-    qid = jnp.concatenate([column(mine, 128)] * (tile // 128), axis=1)
-    queries = []
-    for h, (a, b) in enumerate(wins):
-        w = q_ref[:, a:b]
-        queries.append(jnp.where(head_lanes(a, h, w.shape), w, jnp.zeros_like(w)))
-
-    def scores(t, tops):
-        rows = pl.ds(pl.multiple_of(t * tile, tile), tile)
-        allowed = (qid == marks(code_ref[0:1, rows])[1]) | (rel == (t - i) * tile)
-        new = []
+
+    def attend(count):
+        size = count * tile
+        rows = pl.ds(pl.multiple_of(lo * tile, tile), size)
+        rel = lax.broadcasted_iota(jnp.int32, (tile, size), 0) - lax.broadcasted_iota(jnp.int32, (tile, size), 1)
+        allowed = (jnp.concatenate([column(mine, 128)] * (size // 128), axis=1) == marks(code_ref[0:1, rows])[1]) | (rel == (lo - i) * tile)
+        lane = lax.broadcasted_iota(jnp.int32, (tile, 128), 1)
+        lse = jnp.zeros((tile, 128), F32)
+        outs = []
+
+        def scores(h):
+            a, b = wins[h]
+            w = q_ref[:, a:b]
+            w = jnp.where(head_lanes(a, h, w.shape), w, jnp.zeros_like(w))
+            return dot_bt(w, k_ref[rows, a:b])
+
+        raw = scores(0)
         for h, (a, b) in enumerate(wins):
-            s = lax.dot_general(queries[h], k_ref[rows, a:b], (((1,), (1,)), ((), ())), preferred_element_type=F32)
-            s = jnp.where(allowed, s * (SCALING * LOG2E), NEG)
-            s_ref[h, :, rows] = s
-            top = tops[h]
-            for c in range(0, tile, 128):
-                top = jnp.maximum(top, s[:, c : c + 128])
-            new.append(top)
-        return tuple(new)
-
-    tops = lax.fori_loop(lo, hi, scores, tuple(jnp.full((tile, 128), NEG, F32) for _ in range(heads)))
-    tops = [jnp.broadcast_to(jnp.max(t, axis=1, keepdims=True), (tile, 128)) for t in tops]
-
-    def attend(t, carry):
-        rows = pl.ds(pl.multiple_of(t * tile, tile), tile)
-        new = []
-        for h, (a, b) in enumerate(wins):
-            total, acc = carry[h]
-            p = jnp.exp2(s_ref[h, :, rows] - jnp.concatenate([tops[h]] * (tile // 128), axis=1))
-            for c in range(0, tile, 128):
-                total = total + p[:, c : c + 128]
-            acc = acc + jnp.dot(p.astype(BF), v_ref[rows, a:b], preferred_element_type=F32)
-            new.append((total, acc))
-        return tuple(new)
-
-    start = tuple((jnp.zeros((tile, 128), F32), jnp.zeros((tile, b - a), F32)) for a, b in wins)
-    carry = lax.fori_loop(lo, hi, attend, start)
-    lane = lax.broadcasted_iota(jnp.int32, (tile, 128), 1)
-    lse = jnp.zeros((tile, 128), F32)
-    outs = []
-    for h, (a, b) in enumerate(wins):
-        total = jnp.sum(carry[h][0], axis=1, keepdims=True)
-        out = carry[h][1] * (1.0 / total)
-        outs.append(jnp.where(head_lanes(a, h, out.shape), out, 0.0))
-        lse = jnp.where(lane == h, tops[h] + jnp.log2(total), lse)
-    for c, part in head_pieces(wins, outs):
-        o_ref[c : c + part.shape[1], :] = part.T.astype(BF)
-    lse_ref[...] = lse.T[: lse_ref.shape[0], :]
+            s = jnp.where(allowed, raw * (SCALING * LOG2E), NEG)
+            if h + 1 < heads:
+                raw = scores(h + 1)
+            top = jnp.max(s, axis=1, keepdims=True)
+            p = jnp.exp2(s - top)
+            total = jnp.sum(p, axis=1, keepdims=True)
+            out = jnp.dot(p.astype(BF), v_ref[rows, a:b], preferred_element_type=F32) * (1.0 / total)
+            outs.append(jnp.where(head_lanes(a, h, out.shape), out, 0.0))
+            lse = jnp.where(lane == h, top + jnp.log2(total), lse)
+        for c, part in head_pieces(wins, outs):
+            o_ref[c : c + part.shape[1], :] = part.T.astype(BF)
+        lse_ref[...] = lse.T[: lse_ref.shape[0], :]
+
+    for count in range(1, most_tiles(tile, k_ref.shape[0]) + 1):
+        pl.when(hi - lo == count)(functools.partial(attend, count))
 
 
 def whole_block(shape):
@@ -156,7 +145,6 @@
             grid=(n // tile,),
             in_specs=[row_block(tile, width), whole_block((n, width)), whole_block((n, width)), whole_block((8, n))],
             out_specs=[lane_block(width, tile), lane_block(8, tile)],
-            scratch_shapes=[pltpu.VMEM((heads, tile, n), F32)],
         ),
         compiler_params=pltpu.CompilerParams(vmem_limit_bytes=56 << 20),
         cost_estimate=pl.CostEstimate(flops=4 * n * n * 128 * heads, bytes_accessed=10 * n * width, transcendentals=n * n * heads),
@@ -164,10 +152,8 @@
     )(q, k, v, code)
 
 
-def backward_kernel(
-    heads, tile, count, first, slots, q_ref, k_ref, v_ref, o_ref, lse_ref, code_ref, *refs
-):
-    blocks, (out_ref, go_ref, dk_acc, dv_acc, dq_acc, kid_ref, sems) = refs[:count], refs[count:]
+def backward_kernel(heads, tile, count, first, slots, q_ref, k_ref, v_ref, o_ref, lse_ref, code_ref, *refs):
+    blocks, (out_ref, go_ref, dk_acc, dv_acc, kid_ref, sems) = refs[:count], refs[count:]
     i = pl.program_id(0)
     qid, _ = marks(code_ref[0:1, pl.ds(pl.multiple_of(i * tile, tile), tile)])
     lo, hi = key_tiles(qid, marks(code_ref[0:1, :])[0], tile)
@@ -183,40 +169,41 @@
             kid_ref[t : t + tile, :] = column(marks(code_ref[0:1, t : t + tile])[1], 128)
 
     here = pl.ds(pl.multiple_of(i * tile, tile), tile)
-    rel = lax.broadcasted_iota(jnp.int32, (tile, tile), 1) - lax.broadcasted_iota(jnp.int32, (tile, tile), 0)
-    go = go_ref[here, first : first + width]
-    product = go.astype(F32).T * o_ref[...].astype(F32)
-    inner = [jnp.sum(product[h * HD : (h + 1) * HD, :], axis=0, keepdims=True) for h in range(heads)]
-    queries, grads = [], []
-    for h, (a, b) in enumerate(wins):
-        w, g = q_ref[:, a:b], go[:, a:b]
-        on = head_lanes(a, h, w.shape)
-        queries.append(jnp.where(on, w, jnp.zeros_like(w)))
-        g = jnp.where(on, g, jnp.zeros_like(g))
-        grads.append(g)
-        dq_acc[h, :, : b - a] = jnp.zeros((tile, b - a), F32)
-    lse = lse_ref[...]
-
-    def step(t, carry):
-        rows = pl.ds(pl.multiple_of(t * tile, tile), tile)
-        allowed = (jnp.concatenate([kid_ref[rows, :]] * (tile // 128), axis=1) == qid) | (rel == (t - i) * tile)
+
+    def attend(tiles):
+        size = tiles * tile
+        rows = pl.ds(pl.multiple_of(lo * tile, tile), size)
+        rel = lax.broadcasted_iota(jnp.int32, (size, tile), 1) - lax.broadcasted_iota(jnp.int32, (size, tile), 0)
+        allowed = (jnp.concatenate([kid_ref[rows, :]] * (tile // 128), axis=1) == qid) | (rel == (lo - i) * tile)
+        go = go_ref[here, first : first + width]
+        product = go.astype(F32).T * o_ref[...].astype(F32)
+        outs = []
+
+        def products(h):
+            a, b = wins[h]
+            on = head_lanes(a, h, (tile, b - a))
+            query = jnp.where(on, q_ref[:, a:b], jnp.zeros((tile, b - a), BF))
+            grad = jnp.where(on, go[:, a:b], jnp.zeros((tile, b - a), BF))
+            return query, grad, dot_bt(k_ref[rows, a:b], query), dot_bt(v_ref[rows, a:b], grad)
+
+        ready = products(0)
         for h, (a, b) in enumerate(wins):
+            query, grad, s, dp = ready
+            if h + 1 < heads:
+                ready = products(h + 1)
+            inner = jnp.sum(product[h * HD : (h + 1) * HD, :], axis=0, keepdims=True)
+            on = head_lanes(a, h, (tile, b - a))
             key = k_ref[rows, a:b]
-            s = lax.dot_general(key, queries[h], (((1,), (1,)), ((), ())), preferred_element_type=F32)
-            p = jnp.exp2(jnp.where(allowed, s * (SCALING * LOG2E) - lse[h : h + 1, :], NEG))
-            dp = lax.dot_general(v_ref[rows, a:b], grads[h], (((1,), (1,)), ((), ())), preferred_element_type=F32)
-            ds = (p * (dp - inner[h])).astype(BF)
-            dv_acc[rows, a:b] += jnp.dot(p.astype(BF), grads[h], preferred_element_type=F32)
-            dk_acc[rows, a:b] += jnp.dot(ds, queries[h], preferred_element_type=F32)
-            dq_acc[h, :, : b - a] += lax.dot_general(ds, key, (((0,), (0,)), ((), ())), preferred_element_type=F32)
-        return carry
-
-    lax.fori_loop(lo, hi, step, 0)
-    outs = []
-    for h, (a, b) in enumerate(wins):
-        outs.append(jnp.where(head_lanes(a, h, (tile, b - a)), dq_acc[h, :, : b - a] * SCALING, 0.0))
-    for c, part in head_pieces(wins, outs):
-        out_ref[here, c : c + part.shape[1]] = part.astype(BF)
+            p = jnp.exp2(jnp.where(allowed, s * (SCALING * LOG2E) - lse_ref[h : h + 1, :], NEG))
+            ds = (p * (dp - inner)).astype(BF)
+            dv_acc[rows, a:b] += dot(p.astype(BF), grad)
+            dk_acc[rows, a:b] += dot(ds, query)
+            outs.append(jnp.where(on, dot_at(ds, key) * SCALING, 0.0))
+        for c, part in head_pieces(wins, outs):
+            out_ref[here, c : c + part.shape[1]] = part.astype(BF)
+
+    for tiles in range(1, most_tiles(tile, k_ref.shape[0]) + 1):
+        pl.when(hi - lo == tiles)(functools.partial(attend, tiles))
 
     @pl.when(i == pl.num_programs(0) - 1)
     def _():
@@ -247,7 +234,6 @@
                 pltpu.VMEM((n, go_blocks[0].shape[1]), BF),
                 pltpu.VMEM((n, width), F32),
                 pltpu.VMEM((n, width), F32),
-                pltpu.VMEM((heads, tile, 256), F32),
                 pltpu.VMEM((n, 128), F32),
                 pltpu.SemaphoreType.DMA((count,)),
             ],
@@ -291,6 +277,10 @@
 
 def dot_at(a, b):
     return lax.dot_general(a, b, (((0,), (0,)), ((), ())), preferred_element_type=F32)
+
+
+def row_parts(rows):
+    return [slice(0, 256), slice(256, rows)]
 
 
 def project_kernel(counts, bands, slots, *refs):
@@ -380,18 +370,31 @@
 
     for i in range(count):
         o_out[pl.ds(pl.multiple_of(slots[i] * cols, 8), cols), :] = os[i][...]
-    x = x_ref[...].astype(F32) + (dot_at(o_out[...], w_out[...]) + out_bias[...])
-
-    @pl.when(j == 0)
-    def _():
-        x_out[...] = x
-
-    normal, _ = normalise(x)
-    h = (normal * gain[...] + shift[...]).astype(BF)
-    h_out[...] = h
-    value, slope = gelu_both(dot(h, w_up[...]) + up_bias[...])
-    a_out[...] = value.astype(BF)
-    slope_out[...] = slope
+    parts = row_parts(x_ref.shape[0])
+
+    def branch(part):
+        return dot_at(o_out[:, part], w_out[...])
+
+    def norm(part, product):
+        x = x_ref[part, :].astype(F32) + (product + out_bias[...])
+        x_out[part, :] = jnp.where(j == 0, x, x_out[part, :])
+        h = (normalise(x)[0] * gain[...] + shift[...]).astype(BF)
+        h_out[part, :] = h
+        return h
+
+    def bend(part, u):
+        value, slope = gelu_both(u + up_bias[...])
+        a_out[part, :] = value.astype(BF)
+        slope_out[part, :] = slope.astype(BF)
+
+    products, us = {}, {}
+    for t in range(len(parts) + 2):
+        if t < len(parts):
+            products[t] = branch(parts[t])
+        if 0 <= t - 1 < len(parts):
+            us[t - 1] = dot(norm(parts[t - 1], products[t - 1]), w_up[...])
+        if 0 <= t - 2 < len(parts):
+            bend(parts[t - 2], us[t - 2])
 
 
 def widen(x_all, os, w_outs, slots, out_bias, gain, shift, w_up, up_bias, rows):
@@ -405,7 +408,7 @@
             shape((width, n), BF),
             shape((n, width), BF),
             shape((n, hidden), BF),
-            shape((n, hidden), F32),
+            shape((n, hidden), BF),
             shape((width, width), BF),
         ],
         grid_spec=pltpu.PrefetchScalarGridSpec(
@@ -426,8 +429,10 @@
     )(slots, x_all, *os, *w_outs, out_bias, gain, shift, w_up, up_bias)
 
 
-def narrow_kernel(slots, gy_ref, a_ref, slope_ref, w_up, w_down, *refs):
-    gu_out, y_out, dh_out, sum_out = refs[-4:]
+def narrow_kernel(count, slots, gy_ref, a_ref, slope_ref, w_up, w_down, *refs):
+    dh_outs = refs[len(refs) - 1 - count : -1]
+    gu_out, y_out = refs[len(refs) - 3 - count : len(refs) - 1 - count]
+    sum_out = refs[-1]
 
     @pl.when(pl.program_id(0) == 0)
     def _():
@@ -435,7 +440,13 @@
 
     gu = (dot_bt(gy_ref[...], w_down[...]) * slope_ref[...]).astype(BF)
     gu_out[...] = gu
-    dh_out[...] = dot_bt(gu, w_up[...]).astype(BF)
+    dh = dot_bt(gu, w_up[...]).astype(BF)
+    for i in range(count):
+
+        @pl.when(pl.program_id(0) == i)
+        def _(i=i):
+            dh_outs[i][...] = dh
+
     y_out[...] = dot(a_ref[...], w_down[...]).astype(BF)
     sum_out[...] += jnp.sum(gu.astype(F32), axis=0, keepdims=True)
 
@@ -449,15 +460,17 @@
         return pl.BlockSpec((rows, size), lambda i, slots: (slots[first + i], 0))
 
     return pl.pallas_call(
-        narrow_kernel,
-        out_shape=[shape((n, hidden), BF), shape((n, width), BF), shape((rows * count, width), BF), shape((1, hidden), F32)],
+        functools.partial(narrow_kernel, count),
+        out_shape=[shape((n, hidden), BF), shape((n, width), BF)]
+        + [shape((rows, width), BF)] * count
+        + [shape((1, hidden), F32)],
         grid_spec=pltpu.PrefetchScalarGridSpec(
             num_scalar_prefetch=1,
             grid=(count,),
             in_specs=[block(width), block(hidden), block(hidden)]
             + [kept_block((width, hidden)), kept_block((hidden, width))]
             + [pl.BlockSpec(memory_space=pl.ANY)] * len(carried),
-            out_specs=[block(hidden), block(width), row_block(rows, width), whole_block((1, hidden))],
+            out_specs=[block(hidden), block(width)] + [whole_block((rows, width))] * count + [whole_block((1, hidden))],
         ),
         input_output_aliases={6 + i: i for i in range(len(carried))},
         compiler_params=pltpu.CompilerParams(vmem_limit_bytes=56 << 20),
@@ -466,11 +479,13 @@
     )(slots, gy, active, slope, w_up, w_down, *carried)
 
 
-def finish_kernel(slots, g_ref, x_ref, w_qkv, dh_out, sum_out, bias_out):
-    @pl.when(pl.program_id(0) == 0)
+def finish_kernel(count, slots, g_ref, x_ref, w_qkv, mid_ref, far_ref, near_ref, dh_out, sum_out, bias_acc):
+    j = pl.program_id(0)
+
+    @pl.when(j == 0)
     def _():
         sum_out[...] = jnp.zeros_like(sum_out)
-        bias_out[...] = jnp.zeros_like(bias_out)
+        bias_acc[...] = jnp.zeros_like(bias_acc)
 
     g = g_ref[...]
     dh = dot_bt(g, w_qkv[:, : g.shape[1]])
@@ -478,26 +493,80 @@
     normal, _ = normalise(x_ref[...].astype(F32))
     sum_out[0:1, :] += jnp.sum(dh * normal, axis=0, keepdims=True)
     sum_out[1:2, :] += jnp.sum(dh, axis=0, keepdims=True)
-    bias_out[...] += jnp.sum(g.astype(F32), axis=0, keepdims=True)
-
-
-def finish(gqkv, x_all, w_qkv, slots, rows):
+    bias_acc[...] += jnp.sum(g.astype(F32), axis=0, keepdims=True)
+    cols, wide = g.shape[1] // 3, far_ref.shape[1]
+
+    @pl.when(j == count - 1)
+    def _():
+        sum_out[4:5, :] = mid_ref[2:3, :]
+        sum_out[5:7, :] = mid_ref[0:2, :]
+        sum_out[7:8, :] = mid_ref[3:4, :]
+        for v in range(count):
+
+            @pl.when(slots[0] == v)
+            def _(v=v):
+                sum_out[2:3, v * cols : (v + 1) * cols] = bias_acc[:, :cols]
+                sum_out[3:4, v * cols : (v + 1) * cols] = bias_acc[:, 2 * cols :]
+                sum_out[8 + v : 9 + v, :wide] = far_ref[...] + near_ref[...]
+
+
+def finish(gqkv, x_all, w_qkv, mid, far_sum, near_sum, slots, rows):
     n, width = x_all.shape
-    columns = gqkv.shape[1]
+    columns, count, wide = gqkv.shape[1], n // rows, far_sum.shape[1]
+    height = -(-(8 + count) // 8) * 8
     shape = jax.ShapeDtypeStruct
     return pl.pallas_call(
-        finish_kernel,
-        out_shape=[shape((n, width), BF), shape((8, width), F32), shape((1, columns), F32)],
+        functools.partial(finish_kernel, count),
+        out_shape=[shape((n, width), BF), shape((height, width), F32)],
         grid_spec=pltpu.PrefetchScalarGridSpec(
             num_scalar_prefetch=1,
-            grid=(n // rows,),
-            in_specs=[slot_block(rows, columns), slot_block(rows, width), kept_block(w_qkv.shape)],
-            out_specs=[row_block(rows, width), whole_block((8, width)), whole_block((1, columns))],
+            grid=(count,),
+            in_specs=[slot_block(rows, columns), slot_block(rows, width), kept_block(w_qkv.shape)]
+            + [kept_block(mid.shape), kept_block((1, wide)), kept_block((1, wide))],
+            out_specs=[row_block(rows, width), whole_block((height, width))],
+            scratch_shapes=[pltpu.VMEM((1, columns), F32)],
         ),
         compiler_params=pltpu.CompilerParams(vmem_limit_bytes=56 << 20),
         cost_estimate=pl.CostEstimate(flops=2 * n * width * columns, bytes_accessed=8 * n * width, transcendentals=n),
         name="project_back",
-    )(slots, gqkv, x_all, w_qkv)
+    )(slots, gqkv, x_all, w_qkv, mid, far_sum, near_sum)
+
+
+def settle_kernel(count, slots, *refs):
+    ups, downs, (up_out, down_out) = refs[:count], refs[count : 2 * count], refs[2 * count :]
+    strip = down_out.shape[1]
+    sub = downs[0].shape[0]
+    ratio = ups[0].shape[1] // sub
+    for v in range(count):
+
+        @pl.when(slots[0] == v)
+        def _(v=v):
+            for i in range(count):
+                start = (v ^ i) * sub
+                size = min(sub, strip - start)
+                if size > 0:
+                    down_out[:, start : start + size] = downs[i][:size, :].astype(F32).T
+                    for h in range(ratio):
+                        piece = ups[i][:, h * sub : h * sub + size]
+                        up_out[:, h * strip + start : h * strip + start + size] = piece.astype(F32)
+
+
+def settle(ups, downs, slots, strip):
+    band, sub, cols = ups[0].shape[0], downs[0].shape[0], downs[0].shape[1]
+    ratio, count = ups[0].shape[1] // sub, len(ups)
+    shape = jax.ShapeDtypeStruct
+    return pl.pallas_call(
+        functools.partial(settle_kernel, count),
+        out_shape=[shape((band, ratio * strip), F32), shape((cols, strip), F32)],
+        grid_spec=pltpu.PrefetchScalarGridSpec(
+            num_scalar_prefetch=1,
+            grid=(1,),
+            in_specs=[kept_block(ups[0].shape)] * count + [kept_block(downs[0].shape)] * count,
+            out_specs=[whole_block((band, ratio * strip)), whole_block((cols, strip))],
+        ),
+        compiler_params=pltpu.CompilerParams(vmem_limit_bytes=56 << 20),
+        name="settle_hidden",
+    )(slots, *ups, *downs)
 
 
 def weigh_kernel(count, h_ref, g_ref, o_ref, *refs):
@@ -544,6 +613,7 @@
     sum_out[0:1, :] = jnp.sum(grad * normal, axis=0, keepdims=True)
     sum_out[1:2, :] = jnp.sum(grad, axis=0, keepdims=True)
     sum_out[2:3, :] = jnp.sum(ga.astype(F32), axis=0, keepdims=True)
+    sum_out[3:4, :] = jnp.sum(gy_ref[...].astype(F32), axis=0, keepdims=True)
     go = dot_bt(ga, w_out[...]).astype(BF)
     cols = go_outs[0].shape[1]
     for v in range(count):
@@ -744,9 +814,9 @@
     code = (image_ids * 2 + pad_mask).astype(BF)
     x_pack = jnp.concatenate([x_own, jnp.pad(code, ((0, 15), (0, width - rows)))], axis=0)
     split = rows // 2
-    x_parts = hold([x_pack[:split], x_pack[split:]], ring_one.one)
+    x_parts = [x_pack[:split], x_pack[split:]]
     far_a = far_swaps(x_parts[0])
-    done = [far_a, *[ring_one.hop(x_parts) for _ in range(hops)]]
+    done = [far_a, *[ring_one.hop() for _ in range(hops)]]
     up_mine = own_hidden(w_up)
     keep = (1 - pad_mask[0]).astype(F32)[:, None]
     gy_own = (cotangent[0].astype(F32) * keep).astype(BF)
@@ -776,16 +846,14 @@
     x_all, h_one, q, k, v, full_qkv, out_cols, code = project(
         x_blocks, pieces, one_slots, row(ln1_gain), row(ln1_shift), q_part, v_part, rows
     )
-    done = [gy_far_b, q, out_cols]
     full_down = lax.all_gather(hold(down_mine, q), "fsdp", axis=0, tiled=True)
 
-    q, k, v, out_cols, gy_parts, gy_far_a, gy_far_b = hold((q, k, v, out_cols, gy_parts, gy_far_a, gy_far_b), *done)
+    out_cols, gy_parts, gy_far_a, gy_far_b = hold((out_cols, gy_parts, gy_far_a, gy_far_b), q)
     out_far = far_swaps(out_cols)
+    o, lse = attention_forward(q, k, v, code, heads, 384 if rows % 384 == 0 else tile)
+    o, gy_parts, gy_far_a, gy_far_b, out_row = hold((o, gy_parts, gy_far_a, gy_far_b, [out_cols, *out_far]), o)
+    o_row = [o, *far_swaps(o)]
     gy_near = [near_swaps([gy_parts[0], *gy_far_a]), near_swaps([gy_parts[1], *gy_far_b])]
-    done = [out_far, gy_near]
-    o, lse = attention_forward(q, k, v, code, heads, tile)
-    o, out_row = hold((o, [out_cols, *out_far]), *done)
-    o_row = [o, *far_swaps(o)]
     w_outs = woven(out_row, near_swaps(out_row))
     gy_all = jnp.zeros((n, width), BF)
     gy_rows = [woven([gy_parts[h], *far], near) for h, (far, near) in enumerate(zip((gy_far_a, gy_far_b), gy_near))]
@@ -799,7 +867,7 @@
     x_one, o_all, h_two, active, slope, full_out = widen(
         x_all, os, w_outs, slots, row(out_bias), row(ln2_gain), row(ln2_shift), full_up, up_part, rows
     )
-    gu, mixed, far_dh, far_sum = narrow(gy_all, active, slope, full_up, full_down, slots, rows, 2, ns - 2, ())
+    gu, mixed, *far_dh, far_sum = narrow(gy_all, active, slope, full_up, full_down, slots, rows, 2, ns - 2, ())
 
     def cut(array, j):
         return array[j * rows : (j + 1) * rows]
@@ -807,16 +875,16 @@
     def summed(a, b):
         return (a.astype(F32) + b.astype(F32)).astype(BF)
 
-    far_near = near_swaps([cut(far_dh, j + 1) for j in range(0, ns - 2, 2)])
-    far_held = [summed(cut(far_dh, 2 * i), got) for i, got in enumerate(far_near)]
+    far_near = near_swaps(far_dh[1::2])
+    active, gy_all = hold((active, gy_all), far_dh)
+    grad_down_part = dot_at(active, gy_all).astype(BF)
+    down_sum = lax.psum_scatter(grad_down_part, "fsdp", scatter_dimension=0, tiled=True)
+    far_near, gy_all, active = hold((far_near, gy_all, active), grad_down_part)
+    far_held = [summed(far_dh[2 * i], got) for i, got in enumerate(far_near)]
     gu, mixed, far_held = hold((gu, mixed, far_held))
     terms = [swap(held, "seq", 2 * i + 2) for i, held in enumerate(far_held)]
-    gu, mixed, near_dh, near_sum = narrow(gy_all, active, slope, full_up, full_down, slots, rows, 0, 2, (gu, mixed))
-    near_dh, gy_all, active = hold((near_dh, gy_all, active))
-    terms += [cut(near_dh, 0), swap(cut(near_dh, 1), "seq", 1)]
-    grad_down_part = dot_at(active, gy_all).astype(BF)
-    down_sum = lax.psum_scatter(grad_down_part, "fsdp", scatter_dimension=0, tiled=True)
-    terms = hold(terms, grad_down_part)
+    gu, mixed, *near_dh, near_sum = narrow(gy_all, active, slope, full_up, full_down, slots, rows, 0, 2, (gu, mixed))
+    terms += [near_dh[0], swap(near_dh[1], "seq", 1)]
     dx_one, sums_two, go_parts, ga_parts = middle(terms, x_one, gy_own, row(ln2_gain), full_out, slots, ns)
     go_parts, h_two, gu, mixed = hold((go_parts, h_two, gu, mixed))
     go_blocks = [block if j == 0 else swap(block, "seq", j) for j, block in enumerate(go_parts)]
@@ -834,14 +902,18 @@
     mixed_far = [swap(block, "seq", 2 * i + 2) for i, block in enumerate(mixed_held)]
     gqkv = attention_backward(q, k, v, o, go_blocks, 0, slots, lse, code, heads, tile)
 
-    gqkv, ga_blocks, mixed_far = hold((gqkv, ga_blocks, mixed_far))
+    gqkv, ga_blocks, down_sum = hold((gqkv, ga_blocks, down_sum))
+
+    def exchanged(pieces):
+        return [piece if j == 0 else swap(piece, "seq", j) for j, piece in enumerate(pieces)]
+
+    downs = exchanged([lax.dynamic_slice_in_dim(down_sum, order[j] * cols, cols, axis=1) for j in range(ns)])
     grad_part = weigh(h_one, gqkv, o_all, ga_blocks)
 
     def bands(owner):
         return lax.dynamic_slice_in_dim(grad_part, owner * band, band, axis=0).astype(F32)
 
     ring_sum = RingSum(bands)
-    gqkv = hold(gqkv, ring_sum.one, ring_sum.two)
 
     def ring_round(*earlier):
         new = []
@@ -851,35 +923,21 @@
             new.append(ring_sum.hop(*earlier))
         return new
 
+    gqkv = hold(gqkv, ring_sum.one, ring_sum.two)
     done = [ring_round(gqkv)]
-    dh_one_part, sums_one, sum_qkv = finish(gqkv, x_all, full_qkv, slots, rows)
-
-    def spread(vector):
-        return lax.dynamic_update_slice(jnp.zeros((width,), F32), vector, (s * cols,))
-
-    def spread_hidden(vector):
-        shifted = lax.dynamic_update_slice(jnp.zeros((nf, ns * sub), F32), vector.reshape(nf, sub), (0, s * sub))
-        return shifted[:, :strip].reshape(nf * strip)
-
-    sum_down_bias = jnp.sum(gy_own.astype(F32), axis=0)
-    sum_hidden = spread_hidden((far_sum + near_sum)[0])
-    vectors = [
-        sums_one[0], sums_one[1], spread(sum_qkv[0, :cols]), spread(sum_qkv[0, 2 * cols :]), sums_two[2],
-        sums_two[0], sums_two[1], sum_hidden, sum_down_bias,
-    ]
-    totals = TotalSum(jnp.concatenate(vectors))
-    done += [dh_one_part]
+    dh_one_part, sums_one = finish(gqkv, x_all, full_qkv, sums_two, far_sum, near_sum, slots, rows)
+    totals = TotalSum(sums_one)
+    done += [dh_one_part, mixed_far, downs]
     dh_one_part = hold(dh_one_part, *done)
     dh_near = near_swaps([cut(dh_one_part, j + 1) for j in range(0, ns, 2)])
     done = [dh_near, ring_round(*done), totals.hop(*done)]
     dh_near = hold(dh_near, *done)
     dh_held = [summed(cut(dh_one_part, 2 * i), dh_near[i]) for i in range(1, ns // 2)]
     dh_far_a = [swap(block[:split], "seq", 2 * i + 2) for i, block in enumerate(dh_held)]
-    done = [dh_far_a, ring_round(*done)]
+    done = [dh_far_a, ring_round(*done), totals.hop(*done)]
     dh_held = hold(dh_held, *done)
     dh_far_b = [swap(block[split:], "seq", 2 * i + 2) for i, block in enumerate(dh_held)]
-    done = [dh_far_b, ring_round(*done)]
-    total = totals.hop(*done)
+    done = [dh_far_b, ring_round(*done), totals.hop(*done)]
 
     mine = hold(ring_sum.result(), *done)
     grad_out = mine[:, 3 * cols :]
@@ -894,44 +952,24 @@
         piece = jnp.where(which == 0, thirds[0], jnp.where(which == 1, thirds[1], thirds[2]))
         got.append(lax.ppermute(piece, "seq", perm))
     grad_qkv = jnp.concatenate(got, axis=1).astype(F32)
+    total = totals.hop(*done)
     while totals.steps:
         total = totals.hop(total)
 
-    ratio = nf // ns
-
-    def up_piece(j):
-        return lax.dynamic_slice_in_dim(up_sum, order[j] * (ratio * sub), ratio * sub, axis=1)
-
-    def down_piece(j):
-        return lax.dynamic_slice_in_dim(down_sum, order[j] * cols, cols, axis=1)
-
-    ups = jnp.zeros((ns, band, ratio * sub), BF)
-    downs = jnp.zeros((ns, sub, cols), BF)
-    for j in range(ns):
-        a, b = up_piece(j), down_piece(j)
-        if j:
-            a, b = swap(a, "seq", j), swap(b, "seq", j)
-        ups = lax.dynamic_update_slice(ups, a[None], (order[j], 0, 0))
-        downs = lax.dynamic_update_slice(downs, b[None], (order[j], 0, 0))
-    grad_up = jnp.concatenate(
-        [
-            jnp.concatenate([ups[i, :, h * sub : (h + 1) * sub] for i in range(ns)], axis=1)[:, :strip]
-            for h in range(ratio)
-        ],
-        axis=1,
-    ).astype(F32)
-    grad_down = downs.reshape(ns * sub, cols)[:strip].astype(F32)
+    share = nf // ns * sub
+    ups = exchanged([lax.dynamic_slice_in_dim(up_sum, order[j] * share, share, axis=1) for j in range(ns)])
+    grad_up, grad_down_t = settle(ups, downs, slots, strip)
 
     dh_far = [jnp.concatenate(pair, axis=0) for pair in zip(dh_far_a, dh_far_b)]
     dh_one = add_up([cut(dh_one_part, 0), dh_near[0], *dh_far])
     normal_x, inverse_x = normalise(x_own.astype(F32))
     grad_inputs = (dx_one + norm_back(normal_x, inverse_x, ln1_gain, dh_one)).astype(BF)
     layer_out = (x_one + add_up([mixed_block(0), mixed_near[0], *mixed_far]) + down_bias).astype(BF)
-    sums, start = [], 0
-    for vector in vectors:
-        sums.append(totals.vector[start : start + vector.shape[0]])
-        start += vector.shape[0]
-    return (layer_out[None], grad_inputs[None], grad_qkv, grad_out, grad_up, grad_down, *sums)
+    total = totals.vector
+    sum_hidden = jnp.swapaxes(total[8 : 8 + ns, :wide].reshape(ns, nf, sub), 0, 1).reshape(nf, ns * sub)
+    sums = [total[i] for i in range(8)]
+    sums.insert(7, sum_hidden[:, :strip].reshape(nf * strip))
+    return (layer_out[None], grad_inputs[None], grad_qkv, grad_out, grad_up, grad_down_t.T, *sums)
 
 
 def solution(mesh):

time: 453 us -> 387 us (0.85)
  Pallas kernels: 172 us -> 146 us
  waiting for transfers between devices: 109 us -> 88.8 us
  local copies, waits for them, and re-layouts: 57.8 us -> 45.8 us
  starting transfers between devices: 51.3 us -> 45.7 us
    pallas_call x1, Pallas kernels: 44.5 us -> 27.9 us  [attention_backward(): pl.pallas_call(functools.partial(backward_kernel, heads, tile, count, fir...]
    ppermute x4, waiting for transfers between devices: 25.9 us -> 10.6 us  [hop(): one = lax.ppermute(one, 'fsdp', self.ahead)]
    pallas_call x1, Pallas kernels: 30.7 us -> 17.3 us  [attention_forward(): pl.pallas_call(functools.partial(forward_kernel, heads, tile), out_shape=...]
    ppermute x44, waiting for transfers between devices: 51.8 us -> 44.9 us  [swap(): return lax.ppermute(value, axis, [(i, i ^ bits) for i in range(size)])]
    dynamic_update_slice x11 -> x0, local copies, waits for them, and re-layouts: 6.47 us -> none  [the longest x2 2.91 us: spread(): lax.dynamic_update_slice(jnp.zeros((width,), F32), vector, (s * cols,))]
    pallas_call x3 -> x4, Pallas kernels: 38 us -> 44.1 us  [the longest x2 30 us: narrow(): pl.pallas_call(functools.partial(narrow_kernel, count), out_shape=[shape(...]
  transfers between devices with their start and end apart: 65 -> 65, of which waited for: 26 -> 23; matrix products, arithmetic and copies ran while one was open for 19% -> 18% of each run, Pallas kernels for 35% -> 34%
where the time goes in v3:
time: 387 us; the launch traced here: 382 us
  Pallas kernels  146 us (38%)
  waiting for transfers between devices  88.8 us (23%)
  local copies, waits for them, and re-layouts  45.8 us (12%)
  starting transfers between devices  45.7 us (12%)
  other arithmetic  23.8 us (6%)
  matrix products  16.9 us (4%)
  between operations  14.9 us (4%)
    ppermute x44, waiting for transfers between devices, swap(): return lax.ppermute(value, axis, [(i, i ^ bits) for i in range(size)])  44.9 us
    pallas_call x2, Pallas kernels, narrow(): pl.pallas_call(functools.partial(narrow_kernel, count), out_shape=[shape(...  30 us
    pallas_call x1, Pallas kernels, attention_backward(): pl.pallas_call(functools.partial(backward_kernel, heads, tile, count, fir...  27.9 us
    ppermute x44, starting transfers between devices, swap(): return lax.ppermute(value, axis, [(i, i ^ bits) for i in range(size)])  27 us
    ppermute x4, waiting for transfers between devices, hop(): self.one = lax.ppermute(one, 'fsdp', self.ahead)  21.8 us
    pallas_call x1, Pallas kernels, widen(): pl.pallas_call(functools.partial(widen_kernel, count), out_shape=[shape((...  21.7 us
    pallas_call x1, Pallas kernels, attention_forward(): pl.pallas_call(functools.partial(forward_kernel, heads, tile), out_shape=...  17.3 us
    dot_general x2, matrix products, dot_at(): lax.dot_general(a, b, (((0,), (0,)), ((), ())), preferred_element_type=F32)  16.9 us
  transfers between devices with their start and end apart: 65, of which 23 were waited for; matrix products, arithmetic and copies ran while one was open for 18% of the time, Pallas kernels for 34%

profile of v3, /device:TPU:0, one launch (start us, length us, event | category | flops | bytes accessed | tf_op | source)
XLA Modules:
  0.0 381.5 jit_solution(1618375375795056367)
XLA Ops:
  7.3 1.9 slice_bitcast_fusion
  9.2 2.9 collective-permute-start
  14.4 1.6 collective-permute-start.1
  18.3 3.2 reshape.82
  21.9 1.3 reshape.83
  23.2 1.5 fusion.11.refs_4_
  27.0 2.0 collective-permute-start.4
  29.0 6.9 %collective-permute-done.4.refs_9_ = bf16[144,1152]{1,0:T(8,128)(2,1)S(1)} collective-permute-done((bf16[144,1152]{1,0:T(8,128)(2,1)}, bf16[144,1152]{1,0:T(8,128)(2,1)S(1)}, u32[]{:S(2)}, u32[]{:S(2)}) %collective-permute-start.4) | collective-permute-done | bytes 331808 | tf_op jit(solution)/shard_map/ppermute | solution.py:716
  35.9 1.6 collective-permute-done.5.refs_10_
  37.5 1.6 collective-permute-done.3.refs_3_
  39.9 1.6 collective-permute-start.9
  45.4 1.8 pad_dynamic-slice_fusion.1
  47.2 3.7 collective-permute-done.9.refs_11_
  51.0 4.0 %collective-permute-done.10.refs_12_ = bf16[144,1152]{1,0:T(8,128)(2,1)} collective-permute-done((bf16[144,1152]{1,0:T(8,128)(2,1)}, bf16[144,1152]{1,0:T(8,128)(2,1)}, u32[]{:S(2)}, u32[]{:S(2)}) %collective-permute-start.10) | collective-permute-done | bytes 331808 | tf_op jit(solution)/shard_map/ppermute | solution.py:720
  56.1 11.2 %collective-permute-done.11.refs_13_ = bf16[144,1152]{1,0:T(8,128)(2,1)S(1)} collective-permute-done((bf16[144,1152]{1,0:T(8,128)(2,1)}, bf16[144,1152]{1,0:T(8,128)(2,1)S(1)}, u32[]{:S(2)}, u32[]{:S(2)}) %collective-permute-start.11) | collective-permute-done | bytes 331808 | tf_op jit(solution)/shard_map/ppermute | solution.py:716
  69.7 14.2 %norm_project.1 = (bf16[1536,1152]{1,0:T(8,128)(2,1)}, bf16[1536,1152]{1,0:T(8,128)(2,1)}, bf16[1536,288]{1,0:T(8,128)(2,1)}, bf16[1536,288]{1,0:T(8,128)(2,1)},...) custom-call(s32[12]{0:T(128)} %stack.59.slots, ...), custom_call_target="tpu_custom_call" | custom-call | flops 4076863488 | bytes 14155776 | tf_op jit(solution)/shard_map/norm_project/pallas_call | solution.py:331
  85.3 17.3 %attention_forward.1 = (bf16[288,1536]{1,0:T(8,128)(2,1)}, f32[8,1536]{1,0:T(8,128)}) custom-call(bf16[1536,288]{1,0:T(8,128)(2,1)} %get-tuple-element.260.q_ref, bf16[1536,288]{1,0:T(8,128)(2,1)} %get-tuple-element.261.k_ref, bf16[1536,288]{1,0:T(8,128)(2,1)} %get-tuple-element.262.v_ref, s32[8,1536]{1,0:T(8,128)} %get-tuple-element.201.code_ref), custom_call_target="tpu_custom_call" | custom-call | flops 4831838208 | bytes 4423680 | tf_op jit(solution)/shard_map/attention_forward/pallas_call | solution.py:141
  102.6 1.5 collective-permute-done.14.refs_6_
  105.9 2.0 broadcast_in_dim.42
  114.9 11.5 %collective-permute-done.15.refs_2_ = bf16[288,1536]{1,0:T(8,128)(2,1)S(1)} collective-permute-done((bf16[288,1536]{1,0:T(8,128)(2,1)}, bf16[288,1536]{1,0:T(8,128)(2,1)S(1)}, u32[]{:S(2)}, u32[]{:S(2)}) %collective-permute-start.15) | collective-permute-done | bytes 884768 | tf_op jit(solution)/shard_map/ppermute | solution.py:652
  131.1 21.7 %out_norm_up.1 = (f32[384,1152]{1,0:T(8,128)}, bf16[1152,1536]{1,0:T(8,128)(2,1)}, bf16[1536,1152]{1,0:T(8,128)(2,1)}, bf16[1536,1152]{1,0:T(8,128)(2,1)}, bf16[...) custom-call(s32[4]{0:T(128)} %pad_add_fusion.slots, bf16[1536,1152]{1,0:T(8,128)(2,1)} %get-tuple-element.197.x_ref, ...), custom_call_target="tpu_custom_call" | custom-call | flops 8153726976 | bytes 28311552 | tf_op jit(solution)/shard_map/out_norm_up/pallas_call | solution.py:404
  152.8 2.4 all-gather.5.cloned.1.call-done.w_down
  155.2 15.0 %down_and_back.2 = (bf16[1536,1152]{1,0:T(8,128)(2,1)}, bf16[1536,1152]{1,0:T(8,128)(2,1)}, bf16[384,1152]{1,0:T(8,128)(2,1)}, bf16[384,1152]{1,0:T(8,128)(2,1)}, f32[1,1152]{1,0:T(1,128)}) custom-call(s32[4]{0:T(128)} %pad_add_fusion.slots, bf16[1536,1152]{1,0:T(8,128)(2,1)} %constant_dynamic-update-slice_fusion.gy_ref, ...), custom_call_target="tpu_custom_call" | custom-call | flops 6115295232 | bytes 14155776 | tf_op jit(solution)/shard_map/down_and_back/pallas_call | solution.py:462
  170.3 8.4 %convolution_convert_fusion.1 = bf16[1152,1152]{1,0:T(8,128)(2,1)} fusion(bf16[1536,1152]{1,0:T(8,128)(2,1)S(1)} %copy-done.9, bf16[1536,1152]{1,0:T(8,128)(2,1)} %constant_dynamic-update-slice_fusion.gy_ref), kind=kOutput, calls=%fused_computation.1 | convolution fusion | flops 4078190592 | bytes 9732096 | tf_op jit(solution)/shard_map/dot_general | solution.py:279
  179.8 2.4 collective-permute-done.24
  182.5 1.4 collective-permute-start.25
  183.9 15.0 %down_and_back.3 = (bf16[1536,1152]{1,0:T(8,128)(2,1)}, bf16[1536,1152]{1,0:T(8,128)(2,1)}, bf16[384,1152]{1,0:T(8,128)(2,1)}, bf16[384,1152]{1,0:T(8,128)(2,1)}, f32[1,1152]{1,0:T(1,128)}) custom-call(s32[4]{0:T(128)} %pad_add_fusion.slots, ...), custom_call_target="tpu_custom_call", output_to_operand_aliasing={{0}: (6, {}), {1}: (7, {})} | custom-call | flops 6115295232 | bytes 14155776 | tf_op jit(solution)/shard_map/down_and_back/pallas_call | solution.py:462
  199.0 5.2 %collective-permute-done.25.refs_0_ = bf16[384,1152]{1,0:T(8,128)(2,1)S(1)} collective-permute-done((bf16[384,1152]{1,0:T(8,128)(2,1)S(1)}, bf16[384,1152]{1,0:T(8,128)(2,1)S(1)}, u32[]{:S(2)}, u32[]{:S(2)}) %collective-permute-start.25) | collective-permute-done | bytes 884768 | tf_op jit(solution)/shard_map/ppermute | solution.py:652
  205.2 10.2 %norm_back_out.1 = (f32[384,1152]{1,0:T(8,128)}, f32[8,1152]{1,0:T(8,128)}, bf16[384,288]{1,0:T(8,128)(2,1)}, bf16[384,288]{1,0:T(8,128)(2,1)}, bf16[384,288]{1,...) custom-call(s32[4]{0:T(128)} %pad_add_fusion.slots, ...), custom_call_target="tpu_custom_call" | custom-call | flops 1019215872 | bytes 8847360 | tf_op jit(solution)/shard_map/norm_back_out/pallas_call | solution.py:634
  215.4 1.4 collective-permute-start.29
  218.8 8.4 %convolution_convert_fusion = bf16[1152,1152]{1,0:T(8,128)(2,1)} fusion(bf16[1536,1152]{1,0:T(8,128)(2,1)} %get-tuple-element.256, bf16[1536,1152]{1,0:T(8,128)(2,1)S(1)} %copy-done.10), kind=kOutput, calls=%fused_computation | convolution fusion | flops 4078190592 | bytes 9732096 | tf_op jit(solution)/shard_map/dot_general | solution.py:279
  227.3 1.5 add_convert_fusion.2
  228.8 2.1 collective-permute-done.30.refs_3_
  231.0 1.4 collective-permute-start.32
  234.2 27.9 %attention_backward.1.g_ref = bf16[1536,864]{1,0:T(8,128)(2,1)} custom-call(s32[4]{0:T(128)} %pad_add_fusion.slots, bf16[1536,288]{1,0:T(8,128)(2,1)} %get-tuple-element.260.q_ref, bf16[1536,288]{1,0:T(8,128)(2,1)} %get-tuple-element.261.k_ref, bf16[1536,288]{1,0:T(8,128)(2,1)} %get-tuple-element.262.v_ref, ...), custom_call_target="tpu_custom_call" | custom-call | flops 12079595520 | bytes 7077888 | tf_op jit(solution)/shard_map/attention_backward/pallas_call | solution.py:217
  263.6 1.3 collective-permute-done.35.refs_3_
  264.9 10.2 %grads_qkv_out.1 = bf16[1152,1152]{1,0:T(8,128)(2,1)} custom-call(bf16[1536,1152]{1,0:T(8,128)(2,1)} %get-tuple-element.273.h_ref, bf16[1536,864]{1,0:T(8,128)(2,1)} %attention_backward.1.g_ref, bf16[1152,1536]{1,0:T(8,128)(2,1)} %get-tuple-element.274.o_ref, bf16[384,288]{1,0:T(8,128)(2,1)} %get-tuple-element.275.refs_0_, bf16[384,288]{1,0:T(8,128)(2,1)} %copy-done.50, ...), custom_call_target="tpu_custom_call" | custom-call | flops 4076863488 | bytes 10616832 | tf_op jit(solution)/shard_map/grads_qkv_out/pallas_call | solution.py:590
  276.3 1.5 collective-permute-start.36
  279.2 1.3 collective-permute-start.39
  281.1 10.2 %project_back.1 = (bf16[1536,1152]{1,0:T(8,128)(2,1)}, f32[16,1152]{1,0:T(8,128)}) custom-call(s32[4]{0:T(128)} %pad_add_fusion.slots, bf16[1536,864]{1,0:T(8,128)(2,1)} %attention_backward.1.g_ref, bf16[1536,1152]{1,0:T(8,128)(2,1)} %get-tuple-element.197.x_ref, bf16[1152,1152]{1,0:T(8,128)(2,1)} %get-tuple-element.280.w_qkv, ...), custom_call_target="tpu_custom_call" | custom-call | flops 3057647616 | bytes 14155776 | tf_op jit(solution)/shard_map/project_back/pallas_call | solution.py:518
  291.8 2.5 fusion.16
  294.8 2.1 add_convert_fusion.7
  296.9 1.3 collective-permute-start.43
  299.2 1.4 collective-permute-done.45
  301.5 7.0 %collective-permute-done.43 = bf16[144,1152]{1,0:T(8,128)(2,1)S(1)} collective-permute-done((bf16[144,1152]{1,0:T(8,128)(2,1)}, bf16[144,1152]{1,0:T(8,128)(2,1)S(1)}, u32[]{:S(2)}, u32[]{:S(2)}) %collective-permute-start.43) | collective-permute-done | bytes 331808 | tf_op jit(solution)/shard_map/ppermute | solution.py:744
  308.5 2.2 add_convert_fusion
  311.6 1.6 collective-permute-start.46
  313.2 2.2 add_convert_fusion.5
  315.5 1.9 collective-permute-start.48
  318.3 7.0 %collective-permute-done.49 = f32[16,1152]{1,0:T(8,128)} collective-permute-done((f32[16,1152]{1,0:T(8,128)S(1)}, f32[16,1152]{1,0:T(8,128)}, u32[]{:S(2)}, u32[]{:S(2)}) %collective-permute-start.49) | collective-permute-done | bytes 73760 | tf_op jit(solution)/shard_map/ppermute | solution.py:652
  325.2 1.5 add.386
  326.8 3.6 collective-permute-done.47
  330.4 3.1 collective-permute-done.48
  336.7 2.0 constant_dynamic-slice_fusion
  340.5 3.1 fusion.13
  343.7 2.0 collective-permute-done.52
  348.3 3.9 %settle_hidden.1 = (f32[144,1076]{1,0:T(8,128)}, f32[288,538]{1,0:T(8,128)}) custom-call(s32[4]{0:T(128)} %pad_add_fusion.slots, bf16[144,288]{1,0:T(8,128)(2,1)} %get-tuple-element.339.refs_0_, bf16[144,288]{1,0:T(8,128)(2,1)} %copy-done.26, bf16[144,288]{1,0:T(8,128)(2,1)} %copy-done.27, bf16[144,288]{1,0:T(8,128)(2,1)} %copy-done.28, ...), custom_call_target="tpu_custom_call" | custom-call | tf_op jit(solution)/shard_map/settle_hidden/pallas_call | solution.py:558
  352.1 1.3 convert_add_fusion
  353.4 3.0 collective-permute-done.50
  356.6 3.0 collective-permute-start.55
  360.6 1.7 collective-permute-start.59
  363.2 1.8 fusion.14
  365.8 1.7 collective-permute-start.60
  368.5 4.7 %collective-permute-done.60 = f32[16,1152]{1,0:T(8,128)S(1)} collective-permute-done((f32[16,1152]{1,0:T(8,128)S(1)}, f32[16,1152]{1,0:T(8,128)S(1)}, u32[]{:S(2)}, u32[]{:S(2)}) %collective-permute-start.60) | collective-permute-done | bytes 73760 | tf_op jit(solution)/shard_map/ppermute | solution.py:652
  (260 shorter events, 58.7 us)
Async XLA Ops:
  7.2 123.0 %all-gather.3.cloned.1.call-start = ((), (), s32[]{:S(2)}) async-start(), calls=%async_computation.2 | async-start | bytes 2985984 | tf_op jit(solution)/shard_map/all_gather | solution.py:833
  9.2 17.7 %collective-permute-start = (bf16[192,1152]{1,0:T(8,128)(2,1)}, bf16[192,1152]{1,0:T(8,128)(2,1)}, u32[]{:S(2)}, u32[]{:S(2)}) collective-permute-start(bf16[192,1152]{1,0:T(8,128)(2,1)} %slice_bitcast_fusion), channel_id=1, source_target_pairs={{0,16},{8,24},{16,0},{24,8},{1,17},{9,25},{17,1},{25,9},{2,18},{10... | collective-permute-start | bytes 1327112 | tf_op jit(solution)/shard_map/ppermute | solution.py:652
  14.4 12.4 %collective-permute-start.1 = (bf16[144,1152]{1,0:T(8,128)(2,1)}, bf16[144,1152]{1,0:T(8,128)(2,1)}, u32[]{:S(2)}, u32[]{:S(2)}) collective-permute-start(bf16[144,1152]{1,0:T(8,128)(2,1)} %concatenate.13.refs_6_), channel_id=1, source_target_pairs={{0,2},{2,4},{4,6},{6,7},{7,5},{5,3},{3,1},{1,0},{8,10},{10,12},{12... | collective-permute-start | bytes 995336 | tf_op jit(solution)/shard_map/ppermute | solution.py:716
  16.0 10.9 %collective-permute-start.2 = (bf16[144,1152]{1,0:T(8,128)(2,1)}, bf16[144,1152]{1,0:T(8,128)(2,1)}, u32[]{:S(2)}, u32[]{:S(2)}) collective-permute-start(bf16[144,1152]{1,0:T(8,128)(2,1)} %concatenate.13.refs_6_), channel_id=1, source_target_pairs={{2,0},{4,2},{6,4},{7,6},{5,7},{3,5},{1,3},{0,1},{10,8},{12,10},{14... | collective-permute-start | bytes 995336 | tf_op jit(solution)/shard_map/ppermute | solution.py:720
  26.9 12.2 %collective-permute-start.3 = (bf16[208,1152]{1,0:T(8,128)(2,1)}, bf16[208,1152]{1,0:T(8,128)(2,1)}, u32[]{:S(2)}, u32[]{:S(2)}) collective-permute-start(bf16[208,1152]{1,0:T(8,128)(2,1)} %slice.103), channel_id=1, source_target_pairs={{0,16},{8,24},{16,0},{24,8},{1,17},{9,25},{17,1},{25,9},{2,18},{10... | collective-permute-start | bytes 1437704 | tf_op jit(solution)/shard_map/ppermute | solution.py:652
  27.0 8.9 %collective-permute-start.4 = (bf16[144,1152]{1,0:T(8,128)(2,1)}, bf16[144,1152]{1,0:T(8,128)(2,1)S(1)}, u32[]{:S(2)}, u32[]{:S(2)}) collective-permute-start(bf16[144,1152]{1,0:T(8,128)(2,1)} %collective-permute-done.1.refs_7_), channel_id=1, source_target_pairs={{0,2},{2,4},{4,6},{6,7},{7,5},{5,3},{3,1},{1,0},{8,10},{10,12},{12... | collective-permute-start | bytes 995336 | tf_op jit(solution)/shard_map/ppermute | solution.py:716
  29.0 8.4 %collective-permute-start.5 = (bf16[144,1152]{1,0:T(8,128)(2,1)}, bf16[144,1152]{1,0:T(8,128)(2,1)}, u32[]{:S(2)}, u32[]{:S(2)}) collective-permute-start(bf16[144,1152]{1,0:T(8,128)(2,1)} %collective-permute-done.2.refs_8_), channel_id=1, source_target_pairs={{2,0},{4,2},{6,4},{7,6},{5,7},{3,5},{1,3},{0,1},{10,8},{12,10},{14... | collective-permute-start | bytes 995336 | tf_op jit(solution)/shard_map/ppermute | solution.py:720
  39.1 116.1 %all-gather.5.cloned.1.call-start = ((), (), s32[]{:S(2)}) async-start(), calls=%async_computation.3 | async-start | bytes 2985984 | tf_op jit(solution)/shard_map/all_gather | solution.py:849
  39.2 15.9 %collective-permute-start.6 = (bf16[400,1152]{1,0:T(8,128)(2,1)S(1)}, bf16[400,1152]{1,0:T(8,128)(2,1)}, u32[]{:S(2)}, u32[]{:S(2)}) collective-permute-start(bf16[400,1152]{1,0:T(8,128)(2,1)S(1)} %copy-done.14), channel_id=1, source_target_pairs={{0,8},{8,0},{16,24},{24,16},{1,9},{9,1},{17,25},{25,17},{2,10},{10... | collective-permute-start | bytes 2764808 | tf_op jit(solution)/shard_map/ppermute | solution.py:652
  39.3 15.8 %collective-permute-start.8 = (bf16[208,1152]{1,0:T(8,128)(2,1)}, bf16[208,1152]{1,0:T(8,128)(2,1)}, u32[]{:S(2)}, u32[]{:S(2)}) collective-permute-start(bf16[208,1152]{1,0:T(8,128)(2,1)} %collective-permute-done.3.refs_3_), channel_id=1, source_target_pairs={{0,8},{8,0},{16,24},{24,16},{1,9},{9,1},{17,25},{25,17},{2,10},{10... | collective-permute-start | bytes 1437704 | tf_op jit(solution)/shard_map/ppermute | solution.py:652
  39.8 15.3 %collective-permute-start.7 = (bf16[192,1152]{1,0:T(8,128)(2,1)}, bf16[192,1152]{1,0:T(8,128)(2,1)}, u32[]{:S(2)}, u32[]{:S(2)}) collective-permute-start(bf16[192,1152]{1,0:T(8,128)(2,1)} %collective-permute-done.refs_2_), channel_id=1, source_target_pairs={{0,8},{8,0},{16,24},{24,16},{1,9},{9,1},{17,25},{25,17},{2,10},{10... | collective-permute-start | bytes 1327112 | tf_op jit(solution)/shard_map/ppermute | solution.py:652
  39.9 11.1 %collective-permute-start.9 = (bf16[144,1152]{1,0:T(8,128)(2,1)}, bf16[144,1152]{1,0:T(8,128)(2,1)}, u32[]{:S(2)}, u32[]{:S(2)}) collective-permute-start(bf16[144,1152]{1,0:T(8,128)(2,1)} %copy-done.45), channel_id=1, source_target_pairs={{0,2},{2,4},{4,6},{6,7},{7,5},{5,3},{3,1},{1,0},{8,10},{10,12},{12... | collective-permute-start | bytes 995336 | tf_op jit(solution)/shard_map/ppermute | solution.py:716
  41.6 13.5 %collective-permute-start.10 = (bf16[144,1152]{1,0:T(8,128)(2,1)}, bf16[144,1152]{1,0:T(8,128)(2,1)}, u32[]{:S(2)}, u32[]{:S(2)}) collective-permute-start(bf16[144,1152]{1,0:T(8,128)(2,1)} %collective-permute-done.5.refs_10_), channel_id=1, source_target_pairs={{2,0},{4,2},{6,4},{7,6},{5,7},{3,5},{1,3},{0,1},{10,8},{12,10},{14... | collective-permute-start | bytes 995336 | tf_op jit(solution)/shard_map/ppermute | solution.py:720
  55.0 12.3 %collective-permute-start.12 = (bf16[192,1152]{1,0:T(8,128)(2,1)}, bf16[192,1152]{1,0:T(8,128)(2,1)S(1)}, u32[]{:S(2)}, u32[]{:S(2)}) collective-permute-start(bf16[192,1152]{1,0:T(8,128)(2,1)} %get-tuple-element.214), channel_id=1, source_target_pairs={{0,16},{8,24},{16,0},{24,8},{1,17},{9,25},{17,1},{25,9},{2,18},{10... | collective-permute-start | bytes 1327112 | tf_op jit(solution)/shard_map/ppermute | solution.py:652
  55.1 12.2 %collective-permute-start.11 = (bf16[144,1152]{1,0:T(8,128)(2,1)}, bf16[144,1152]{1,0:T(8,128)(2,1)S(1)}, u32[]{:S(2)}, u32[]{:S(2)}) collective-permute-start(bf16[144,1152]{1,0:T(8,128)(2,1)} %collective-permute-done.9.refs_11_), channel_id=1, source_target_pairs={{0,2},{2,4},{4,6},{6,7},{7,5},{5,3},{3,1},{1,0},{8,10},{10,12},{12... | collective-permute-start | bytes 995336 | tf_op jit(solution)/shard_map/ppermute | solution.py:716
  67.3 16.6 %collective-permute-start.13 = (bf16[192,1152]{1,0:T(8,128)(2,1)S(1)}, bf16[192,1152]{1,0:T(8,128)(2,1)S(1)}, u32[]{:S(2)}, u32[]{:S(2)}) collective-permute-start(bf16[192,1152]{1,0:T(8,128)(2,1)S(1)} %get-tuple-element.216), channel_id=1, source_target_pairs={{0,16},{8,24},{16,0},{24,8},{1,17},{9,25},{17,1},{25,9},{2,18},{10... | collective-permute-start | bytes 1327112 | tf_op jit(solution)/shard_map/ppermute | solution.py:652
  83.9 20.2 %collective-permute-start.14 = (bf16[1152,384]{1,0:T(8,128)(2,1)}, bf16[1152,384]{1,0:T(8,128)(2,1)}, u32[]{:S(2)}, u32[]{:S(2)}) collective-permute-start(bf16[1152,384]{1,0:T(8,128)(2,1)} %get-tuple-element.212.refs_4_), channel_id=1, source_target_pairs={{0,16},{8,24},{16,0},{24,8},{1,17},{9,25},{17,1},{25,9},{2,18},{10... | collective-permute-start | bytes 2654216 | tf_op jit(solution)/shard_map/ppermute | solution.py:652
  85.2 179.7 %reduce-scatter.3.cloned.1.call-start = ((), (), s32[]{:S(2)}) async-start(), calls=%async_computation.4 | async-start | bytes 2985984 | tf_op jit(solution)/shard_map/reduce_scatter | solution.py:881
  104.1 4.6 %collective-permute-start.18 = (bf16[192,1152]{1,0:T(8,128)(2,1)S(1)}, bf16[192,1152]{1,0:T(8,128)(2,1)S(1)}, u32[]{:S(2)}, u32[]{:S(2)}) collective-permute-start(bf16[192,1152]{1,0:T(8,128)(2,1)S(1)} %copy-done.15), channel_id=1, source_target_pairs={{0,8},{8,0},{16,24},{24,16},{1,9},{9,1},{17,25},{25,17},{2,10},{10... | collective-permute-start | bytes 1327112 | tf_op jit(solution)/shard_map/ppermute | solution.py:652
  104.1 22.3 %collective-permute-start.15 = (bf16[288,1536]{1,0:T(8,128)(2,1)}, bf16[288,1536]{1,0:T(8,128)(2,1)S(1)}, u32[]{:S(2)}, u32[]{:S(2)}) collective-permute-start(bf16[288,1536]{1,0:T(8,128)(2,1)} %get-tuple-element.218.refs_0_.o_ref), channel_id=1, source_target_pairs={{0,16},{8,24},{16,0},{24,8},{1,17},{9,25},{17,1},{25,9},{2,18},{10... | collective-permute-start | bytes 2654216 | tf_op jit(solution)/shard_map/ppermute | solution.py:652
  105.2 21.3 %collective-permute-start.16 = (bf16[1152,384]{1,0:T(8,128)(2,1)}, bf16[1152,384]{1,0:T(8,128)(2,1)S(1)}, u32[]{:S(2)}, u32[]{:S(2)}) collective-permute-start(bf16[1152,384]{1,0:T(8,128)(2,1)} %get-tuple-element.212.refs_4_), channel_id=1, source_target_pairs={{0,8},{8,0},{16,24},{24,16},{1,9},{9,1},{17,25},{25,17},{2,10},{10... | collective-permute-start | bytes 2654216 | tf_op jit(solution)/shard_map/ppermute | solution.py:652
  105.4 21.0 %collective-permute-start.17 = (bf16[1152,384]{1,0:T(8,128)(2,1)}, bf16[1152,384]{1,0:T(8,128)(2,1)S(1)}, u32[]{:S(2)}, u32[]{:S(2)}) collective-permute-start(bf16[1152,384]{1,0:T(8,128)(2,1)} %collective-permute-done.14.refs_6_), channel_id=1, source_target_pairs={{0,8},{8,0},{16,24},{24,16},{1,9},{9,1},{17,25},{25,17},{2,10},{10... | collective-permute-start | bytes 2654216 | tf_op jit(solution)/shard_map/ppermute | solution.py:652
  105.7 4.9 %collective-permute-start.19 = (bf16[192,1152]{1,0:T(8,128)(2,1)S(1)}, bf16[192,1152]{1,0:T(8,128)(2,1)S(1)}, u32[]{:S(2)}, u32[]{:S(2)}) collective-permute-start(bf16[192,1152]{1,0:T(8,128)(2,1)S(1)} %collective-permute-done.12), channel_id=1, source_target_pairs={{0,8},{8,0},{16,24},{24,16},{1,9},{9,1},{17,25},{25,17},{2,10},{10... | collective-permute-start | bytes 1327112 | tf_op jit(solution)/shard_map/ppermute | solution.py:652
  108.7 3.8 collective-permute-start.20
  110.6 3.5 collective-permute-start.21
  126.4 2.6 collective-permute-start.22
  126.5 3.7 collective-permute-start.23
  178.7 158.0 %reduce-scatter.5.cloned.1.call-start = ((), (), s32[]{:S(2)}) async-start(), calls=%async_computation.5 | async-start | bytes 2985984 | tf_op jit(solution)/shard_map/reduce_scatter | solution.py:892
  179.8 2.4 collective-permute-start.24
  182.5 21.8 %collective-permute-start.25 = (bf16[384,1152]{1,0:T(8,128)(2,1)S(1)}, bf16[384,1152]{1,0:T(8,128)(2,1)S(1)}, u32[]{:S(2)}, u32[]{:S(2)}) collective-permute-start(bf16[384,1152]{1,0:T(8,128)(2,1)S(1)} %add_convert_fusion.3), channel_id=1, source_target_pairs={{0,16},{8,24},{16,0},{24,8},{1,17},{9,25},{17,1},{25,9},{2,18},{10... | collective-permute-start | bytes 2654216 | tf_op jit(solution)/shard_map/ppermute | solution.py:652
  198.9 5.4 %collective-permute-start.26 = (bf16[384,1152]{1,0:T(8,128)(2,1)}, bf16[384,1152]{1,0:T(8,128)(2,1)}, u32[]{:S(2)}, u32[]{:S(2)}) collective-permute-start(bf16[384,1152]{1,0:T(8,128)(2,1)} %get-tuple-element.238), channel_id=1, source_target_pairs={{0,8},{8,0},{16,24},{24,16},{1,9},{9,1},{17,25},{25,17},{2,10},{10... | collective-permute-start | bytes 2654216 | tf_op jit(solution)/shard_map/ppermute | solution.py:652
  215.3 13.5 %collective-permute-start.28 = (bf16[384,288]{1,0:T(8,128)(2,1)}, bf16[384,288]{1,0:T(8,128)(2,1)}, u32[]{:S(2)}, u32[]{:S(2)}) collective-permute-start(bf16[384,288]{1,0:T(8,128)(2,1)} %get-tuple-element.249), channel_id=1, source_target_pairs={{0,8},{8,0},{16,24},{24,16},{1,9},{9,1},{17,25},{25,17},{2,10},{10... | collective-permute-start | bytes 663560 | tf_op jit(solution)/shard_map/ppermute | solution.py:652
  215.4 13.4 %collective-permute-start.29 = (bf16[384,288]{1,0:T(8,128)(2,1)}, bf16[384,288]{1,0:T(8,128)(2,1)}, u32[]{:S(2)}, u32[]{:S(2)}) collective-permute-start(bf16[384,288]{1,0:T(8,128)(2,1)} %get-tuple-element.250), channel_id=1, source_target_pairs={{0,16},{8,24},{16,0},{24,8},{1,17},{9,25},{17,1},{25,9},{2,18},{10... | collective-permute-start | bytes 663560 | tf_op jit(solution)/shard_map/ppermute | solution.py:652
  216.8 14.2 %collective-permute-start.30 = (bf16[384,288]{1,0:T(8,128)(2,1)}, bf16[384,288]{1,0:T(8,128)(2,1)}, u32[]{:S(2)}, u32[]{:S(2)}) collective-permute-start(bf16[384,288]{1,0:T(8,128)(2,1)} %get-tuple-element.251), channel_id=1, source_target_pairs={{0,24},{8,16},{16,8},{24,0},{1,25},{9,17},{17,9},{25,1},{2,26},{10... | collective-permute-start | bytes 663560 | tf_op jit(solution)/shard_map/ppermute | solution.py:652
  218.3 9.0 %collective-permute-start.31 = (bf16[384,1152]{1,0:T(8,128)(2,1)S(1)}, bf16[384,1152]{1,0:T(8,128)(2,1)S(1)}, u32[]{:S(2)}, u32[]{:S(2)}) collective-permute-start(bf16[384,1152]{1,0:T(8,128)(2,1)S(1)} %get-tuple-element.324), channel_id=1, source_target_pairs={{0,8},{8,0},{16,24},{24,16},{1,9},{9,1},{17,25},{25,17},{2,10},{10... | collective-permute-start | bytes 2654216 | tf_op jit(solution)/shard_map/ppermute | solution.py:652
  218.6 12.3 %collective-permute-start.27 = (bf16[384,1152]{1,0:T(8,128)(2,1)}, bf16[384,1152]{1,0:T(8,128)(2,1)}, u32[]{:S(2)}, u32[]{:S(2)}) collective-permute-start(bf16[384,1152]{1,0:T(8,128)(2,1)} %get-tuple-element.323), channel_id=1, source_target_pairs={{0,8},{8,0},{16,24},{24,16},{1,9},{9,1},{17,25},{25,17},{2,10},{10... | collective-permute-start | bytes 2654216 | tf_op jit(solution)/shard_map/ppermute | solution.py:652
  231.0 49.6 %collective-permute-start.32 = (bf16[384,1152]{1,0:T(8,128)(2,1)S(1)}, bf16[384,1152]{1,0:T(8,128)(2,1)S(1)}, u32[]{:S(2)}, u32[]{:S(2)}) collective-permute-start(bf16[384,1152]{1,0:T(8,128)(2,1)S(1)} %add_convert_fusion.2), channel_id=1, source_target_pairs={{0,16},{8,24},{16,0},{24,8},{1,17},{9,25},{17,1},{25,9},{2,18},{10... | collective-permute-start | bytes 2654216 | tf_op jit(solution)/shard_map/ppermute | solution.py:652
  232.3 29.8 %collective-permute-start.33 = (bf16[384,288]{1,0:T(8,128)(2,1)S(1)}, bf16[384,288]{1,0:T(8,128)(2,1)S(1)}, u32[]{:S(2)}, u32[]{:S(2)}) collective-permute-start(bf16[384,288]{1,0:T(8,128)(2,1)S(1)} %copy-done.49), channel_id=1, source_target_pairs={{0,8},{8,0},{16,24},{24,16},{1,9},{9,1},{17,25},{25,17},{2,10},{10... | collective-permute-start | bytes 663560 | tf_op jit(solution)/shard_map/ppermute | solution.py:652
  232.4 29.8 %collective-permute-start.34 = (bf16[384,288]{1,0:T(8,128)(2,1)S(1)}, bf16[384,288]{1,0:T(8,128)(2,1)S(1)}, u32[]{:S(2)}, u32[]{:S(2)}) collective-permute-start(bf16[384,288]{1,0:T(8,128)(2,1)S(1)} %copy-done.48), channel_id=1, source_target_pairs={{0,16},{8,24},{16,0},{24,8},{1,17},{9,25},{17,1},{25,9},{2,18},{10... | collective-permute-start | bytes 663560 | tf_op jit(solution)/shard_map/ppermute | solution.py:652
  233.1 31.8 %collective-permute-start.35 = (bf16[384,288]{1,0:T(8,128)(2,1)S(1)}, bf16[384,288]{1,0:T(8,128)(2,1)}, u32[]{:S(2)}, u32[]{:S(2)}) collective-permute-start(bf16[384,288]{1,0:T(8,128)(2,1)S(1)} %copy-done.47), channel_id=1, source_target_pairs={{0,24},{8,16},{16,8},{24,0},{1,25},{9,17},{17,9},{25,1},{2,26},{10... | collective-permute-start | bytes 663560 | tf_op jit(solution)/shard_map/ppermute | solution.py:652
  276.3 15.1 %collective-permute-start.36 = (bf16[144,1152]{1,0:T(8,128)(2,1)S(1)}, bf16[144,1152]{1,0:T(8,128)(2,1)S(1)}, u32[]{:S(2)}, u32[]{:S(2)}) collective-permute-start(bf16[144,1152]{1,0:T(8,128)(2,1)S(1)} %get-tuple-element.285), channel_id=1, source_target_pairs={{0,2},{2,4},{4,6},{6,7},{7,5},{5,3},{3,1},{1,0},{8,10},{10,12},{12... | collective-permute-start | bytes 995336 | tf_op jit(solution)/shard_map/ppermute | solution.py:744
  277.8 13.9 %collective-permute-start.37 = (bf16[144,1152]{1,0:T(8,128)(2,1)S(1)}, bf16[144,1152]{1,0:T(8,128)(2,1)S(1)}, u32[]{:S(2)}, u32[]{:S(2)}) collective-permute-start(bf16[144,1152]{1,0:T(8,128)(2,1)S(1)} %get-tuple-element.286), channel_id=1, source_target_pairs={{2,0},{4,2},{6,4},{7,6},{5,7},{3,5},{1,3},{0,1},{10,8},{12,10},{14... | collective-permute-start | bytes 995336 | tf_op jit(solution)/shard_map/ppermute | solution.py:746
  279.2 12.1 %collective-permute-start.38 = (bf16[144,288]{1,0:T(8,128)(2,1)S(1)}, bf16[144,288]{1,0:T(8,128)(2,1)S(1)}, u32[]{:S(2)}, u32[]{:S(2)}) collective-permute-start(bf16[144,288]{1,0:T(8,128)(2,1)S(1)} %get-tuple-element.345), channel_id=1, source_target_pairs={{0,8},{8,0},{16,24},{24,16},{1,9},{9,1},{17,25},{25,17},{2,10},{10... | collective-permute-start | bytes 248840 | tf_op jit(solution)/shard_map/ppermute | solution.py:652
  279.2 12.1 %collective-permute-start.39 = (bf16[144,288]{1,0:T(8,128)(2,1)S(1)}, bf16[144,288]{1,0:T(8,128)(2,1)S(1)}, u32[]{:S(2)}, u32[]{:S(2)}) collective-permute-start(bf16[144,288]{1,0:T(8,128)(2,1)S(1)} %get-tuple-element.344), channel_id=1, source_target_pairs={{0,16},{8,24},{16,0},{24,8},{1,17},{9,25},{17,1},{25,9},{2,18},{10... | collective-permute-start | bytes 248840 | tf_op jit(solution)/shard_map/ppermute | solution.py:652
  280.6 10.8 %collective-permute-start.40 = (bf16[144,288]{1,0:T(8,128)(2,1)S(1)}, bf16[144,288]{1,0:T(8,128)(2,1)S(1)}, u32[]{:S(2)}, u32[]{:S(2)}) collective-permute-start(bf16[144,288]{1,0:T(8,128)(2,1)S(1)} %get-tuple-element.343), channel_id=1, source_target_pairs={{0,24},{8,16},{16,8},{24,0},{1,25},{9,17},{17,9},{25,1},{2,26},{10... | collective-permute-start | bytes 248840 | tf_op jit(solution)/shard_map/ppermute | solution.py:652
  294.2 14.3 %collective-permute-start.41 = (bf16[384,1152]{1,0:T(8,128)(2,1)}, bf16[384,1152]{1,0:T(8,128)(2,1)S(1)}, u32[]{:S(2)}, u32[]{:S(2)}) collective-permute-start(bf16[384,1152]{1,0:T(8,128)(2,1)} %get-tuple-element.322), channel_id=1, source_target_pairs={{0,8},{8,0},{16,24},{24,16},{1,9},{9,1},{17,25},{25,17},{2,10},{10... | collective-permute-start | bytes 2654216 | tf_op jit(solution)/shard_map/ppermute | solution.py:652
  294.3 14.3 %collective-permute-start.42 = (bf16[384,1152]{1,0:T(8,128)(2,1)S(1)}, bf16[384,1152]{1,0:T(8,128)(2,1)}, u32[]{:S(2)}, u32[]{:S(2)}) collective-permute-start(bf16[384,1152]{1,0:T(8,128)(2,1)S(1)} %get-tuple-element.321), channel_id=1, source_target_pairs={{0,8},{8,0},{16,24},{24,16},{1,9},{9,1},{17,25},{25,17},{2,10},{10... | collective-permute-start | bytes 2654216 | tf_op jit(solution)/shard_map/ppermute | solution.py:652
  296.9 11.6 %collective-permute-start.43 = (bf16[144,1152]{1,0:T(8,128)(2,1)}, bf16[144,1152]{1,0:T(8,128)(2,1)S(1)}, u32[]{:S(2)}, u32[]{:S(2)}) collective-permute-start(bf16[144,1152]{1,0:T(8,128)(2,1)} %get-tuple-element.291), channel_id=1, source_target_pairs={{0,2},{2,4},{4,6},{6,7},{7,5},{5,3},{3,1},{1,0},{8,10},{10,12},{12... | collective-permute-start | bytes 995336 | tf_op jit(solution)/shard_map/ppermute | solution.py:744
  298.1 10.4 %collective-permute-start.44 = (bf16[144,1152]{1,0:T(8,128)(2,1)}, bf16[144,1152]{1,0:T(8,128)(2,1)S(1)}, u32[]{:S(2)}, u32[]{:S(2)}) collective-permute-start(bf16[144,1152]{1,0:T(8,128)(2,1)} %get-tuple-element.292), channel_id=1, source_target_pairs={{2,0},{4,2},{6,4},{7,6},{5,7},{3,5},{1,3},{0,1},{10,8},{12,10},{14... | collective-permute-start | bytes 995336 | tf_op jit(solution)/shard_map/ppermute | solution.py:746
  311.6 21.9 %collective-permute-start.46 = (bf16[192,1152]{1,0:T(8,128)(2,1)}, bf16[192,1152]{1,0:T(8,128)(2,1)S(1)}, u32[]{:S(2)}, u32[]{:S(2)}) collective-permute-start(bf16[192,1152]{1,0:T(8,128)(2,1)} %slice.106), channel_id=1, source_target_pairs={{0,16},{8,24},{16,0},{24,8},{1,17},{9,25},{17,1},{25,9},{2,18},{10... | collective-permute-start | bytes 1327112 | tf_op jit(solution)/shard_map/ppermute | solution.py:652
  315.4 15.0 %collective-permute-start.47 = (bf16[144,1152]{1,0:T(8,128)(2,1)}, bf16[144,1152]{1,0:T(8,128)(2,1)}, u32[]{:S(2)}, u32[]{:S(2)}) collective-permute-start(bf16[144,1152]{1,0:T(8,128)(2,1)} %get-tuple-element.299), channel_id=1, source_target_pairs={{0,2},{2,4},{4,6},{6,7},{7,5},{5,3},{3,1},{1,0},{8,10},{10,12},{12... | collective-permute-start | bytes 995336 | tf_op jit(solution)/shard_map/ppermute | solution.py:744
  315.5 18.0 %collective-permute-start.48 = (bf16[144,1152]{1,0:T(8,128)(2,1)S(1)}, bf16[144,1152]{1,0:T(8,128)(2,1)}, u32[]{:S(2)}, u32[]{:S(2)}) collective-permute-start(bf16[144,1152]{1,0:T(8,128)(2,1)S(1)} %get-tuple-element.300), channel_id=1, source_target_pairs={{2,0},{4,2},{6,4},{7,6},{5,7},{3,5},{1,3},{0,1},{10,8},{12,10},{14... | collective-permute-start | bytes 995336 | tf_op jit(solution)/shard_map/ppermute | solution.py:746
  317.8 7.4 %collective-permute-start.49 = (f32[16,1152]{1,0:T(8,128)S(1)}, f32[16,1152]{1,0:T(8,128)}, u32[]{:S(2)}, u32[]{:S(2)}) collective-permute-start(f32[16,1152]{1,0:T(8,128)S(1)} %add.379), channel_id=1, source_target_pairs={{0,16},{8,24},{16,0},{24,8},{1,17},{9,25},{17,1},{25,9},{2,18},{10... | collective-permute-start | bytes 221192 | tf_op jit(solution)/shard_map/ppermute | solution.py:652
  334.6 17.5 %collective-permute-start.51 = (bf16[144,1152]{1,0:T(8,128)(2,1)S(1)}, bf16[144,1152]{1,0:T(8,128)(2,1)}, u32[]{:S(2)}, u32[]{:S(2)}) collective-permute-start(bf16[144,1152]{1,0:T(8,128)(2,1)S(1)} %add_convert_fusion.4), channel_id=1, source_target_pairs={{0,2},{2,4},{4,6},{6,7},{7,5},{5,3},{3,1},{1,0},{8,10},{10,12},{12... | collective-permute-start | bytes 995336 | tf_op jit(solution)/shard_map/ppermute | solution.py:744
  335.8 9.8 %collective-permute-start.52 = (f32[16,1152]{1,0:T(8,128)}, f32[16,1152]{1,0:T(8,128)}, u32[]{:S(2)}, u32[]{:S(2)}) collective-permute-start(f32[16,1152]{1,0:T(8,128)} %add.386), channel_id=1, source_target_pairs={{0,1},{1,0},{2,3},{3,2},{4,5},{5,4},{6,7},{7,6},{8,9},{9,8},{10,11... | collective-permute-start | bytes 221192 | tf_op jit(solution)/shard_map/ppermute | solution.py:652
  338.7 8.2 %collective-permute-start.56 = (bf16[144,288]{1,0:T(8,128)(2,1)S(1)}, bf16[144,288]{1,0:T(8,128)(2,1)S(1)}, u32[]{:S(2)}, u32[]{:S(2)}) collective-permute-start(bf16[144,288]{1,0:T(8,128)(2,1)S(1)} %get-tuple-element.338), channel_id=1, source_target_pairs={{0,8},{8,0},{16,24},{24,16},{1,9},{9,1},{17,25},{25,17},{2,10},{10... | collective-permute-start | bytes 248840 | tf_op jit(solution)/shard_map/ppermute | solution.py:652
  338.7 8.3 %collective-permute-start.57 = (bf16[144,288]{1,0:T(8,128)(2,1)S(1)}, bf16[144,288]{1,0:T(8,128)(2,1)S(1)}, u32[]{:S(2)}, u32[]{:S(2)}) collective-permute-start(bf16[144,288]{1,0:T(8,128)(2,1)S(1)} %get-tuple-element.337), channel_id=1, source_target_pairs={{0,16},{8,24},{16,0},{24,8},{1,17},{9,25},{17,1},{25,9},{2,18},{10... | collective-permute-start | bytes 248840 | tf_op jit(solution)/shard_map/ppermute | solution.py:652
  339.9 7.0 %collective-permute-start.58 = (bf16[144,288]{1,0:T(8,128)(2,1)S(1)}, bf16[144,288]{1,0:T(8,128)(2,1)S(1)}, u32[]{:S(2)}, u32[]{:S(2)}) collective-permute-start(bf16[144,288]{1,0:T(8,128)(2,1)S(1)} %get-tuple-element.336), channel_id=1, source_target_pairs={{0,24},{8,16},{16,8},{24,0},{1,25},{9,17},{17,9},{25,1},{2,26},{10... | collective-permute-start | bytes 248840 | tf_op jit(solution)/shard_map/ppermute | solution.py:652
  345.7 10.7 %collective-permute-start.50 = (bf16[192,1152]{1,0:T(8,128)(2,1)S(1)}, bf16[192,1152]{1,0:T(8,128)(2,1)S(1)}, u32[]{:S(2)}, u32[]{:S(2)}) collective-permute-start(bf16[192,1152]{1,0:T(8,128)(2,1)S(1)} %slice.88), channel_id=1, source_target_pairs={{0,16},{8,24},{16,0},{24,8},{1,17},{9,25},{17,1},{25,9},{2,18},{10... | collective-permute-start | bytes 1327112 | tf_op jit(solution)/shard_map/ppermute | solution.py:652
  356.6 10.9 %collective-permute-start.55 = (bf16[144,288]{1,0:T(8,128)(2,1)S(1)}, bf16[144,288]{1,0:T(8,128)(2,1)S(1)}, u32[]{:S(2)}, u32[]{:S(2)}) collective-permute-start(bf16[144,288]{1,0:T(8,128)(2,1)S(1)} %get-tuple-element.342), channel_id=1, source_target_pairs={{16,0},{8,8},{0,16},{24,24},{17,1},{9,9},{1,17},{25,25},{18,2},{10... | collective-permute-start | bytes 248840 | tf_op jit(solution)/shard_map/ppermute | solution.py:953
  359.6 7.9 %collective-permute-start.54 = (bf16[144,288]{1,0:T(8,128)(2,1)S(1)}, bf16[144,288]{1,0:T(8,128)(2,1)S(1)}, u32[]{:S(2)}, u32[]{:S(2)}) collective-permute-start(bf16[144,288]{1,0:T(8,128)(2,1)S(1)} %get-tuple-element.341), channel_id=1, source_target_pairs={{8,0},{0,8},{24,16},{16,24},{9,1},{1,9},{25,17},{17,25},{10,2},{2,... | collective-permute-start | bytes 248840 | tf_op jit(solution)/shard_map/ppermute | solution.py:953
  359.7 7.8 %collective-permute-start.53 = (bf16[144,288]{1,0:T(8,128)(2,1)S(1)}, bf16[144,288]{1,0:T(8,128)(2,1)S(1)}, u32[]{:S(2)}, u32[]{:S(2)}) collective-permute-start(bf16[144,288]{1,0:T(8,128)(2,1)S(1)} %get-tuple-element.340), channel_id=1, source_target_pairs={{0,0},{24,8},{16,16},{8,24},{1,1},{25,9},{17,17},{9,25},{2,2},{26,... | collective-permute-start | bytes 248840 | tf_op jit(solution)/shard_map/ppermute | solution.py:953
  360.6 5.2 %collective-permute-start.59 = (f32[16,1152]{1,0:T(8,128)S(1)}, f32[16,1152]{1,0:T(8,128)S(1)}, u32[]{:S(2)}, u32[]{:S(2)}) collective-permute-start(f32[16,1152]{1,0:T(8,128)S(1)} %add.397), channel_id=1, source_target_pairs={{0,2},{1,3},{2,0},{3,1},{4,6},{5,7},{6,4},{7,5},{8,10},{9,11},{10,... | collective-permute-start | bytes 221192 | tf_op jit(solution)/shard_map/ppermute | solution.py:652
  365.8 7.3 %collective-permute-start.60 = (f32[16,1152]{1,0:T(8,128)S(1)}, f32[16,1152]{1,0:T(8,128)S(1)}, u32[]{:S(2)}, u32[]{:S(2)}) collective-permute-start(f32[16,1152]{1,0:T(8,128)S(1)} %add.402), channel_id=1, source_target_pairs={{0,4},{1,5},{2,6},{3,7},{4,0},{5,1},{6,2},{7,3},{8,12},{9,13},{10,... | collective-permute-start | bytes 221192 | tf_op jit(solution)/shard_map/ppermute | solution.py:652
  (53 other events, 470.6 us)
Sparse Core Ops, SparseCore 0:
  39.2 60.1 all-gather.2
  101.6 53.5 all-gather.4
  178.8 70.0 reduce-scatter.2
  252.8 81.8 reduce-scatter.4

commit v4 on v3

--- a/solution.py
+++ b/solution.py
@@ -162,7 +162,14 @@
 
     @pl.when(i == 0)
     def _():
-        load_blocks(blocks, go_ref, slots, 0, sems)
+        copies = []
+        for t, block in enumerate(blocks):
+            size = block.shape[1]
+            there = go_ref.at[:, pl.ds(pl.multiple_of(slots[t] * size, 128), size)]
+            copies.append(pltpu.make_async_copy(block, there, sems.at[t]))
+            copies[-1].start()
+        for copy in copies:
+            copy.wait()
         dk_acc[...] = jnp.zeros_like(dk_acc)
         dv_acc[...] = jnp.zeros_like(dv_acc)
         for t in range(0, kid_ref.shape[0], tile):
@@ -175,16 +182,17 @@
         rows = pl.ds(pl.multiple_of(lo * tile, tile), size)
         rel = lax.broadcasted_iota(jnp.int32, (size, tile), 1) - lax.broadcasted_iota(jnp.int32, (size, tile), 0)
         allowed = (jnp.concatenate([kid_ref[rows, :]] * (tile // 128), axis=1) == qid) | (rel == (lo - i) * tile)
-        go = go_ref[here, first : first + width]
-        product = go.astype(F32).T * o_ref[...].astype(F32)
+        go = go_ref[:, here]
+        product = go.astype(F32) * o_ref[...].astype(F32)
         outs = []
 
         def products(h):
             a, b = wins[h]
             on = head_lanes(a, h, (tile, b - a))
             query = jnp.where(on, q_ref[:, a:b], jnp.zeros((tile, b - a), BF))
-            grad = jnp.where(on, go[:, a:b], jnp.zeros((tile, b - a), BF))
-            return query, grad, dot_bt(k_ref[rows, a:b], query), dot_bt(v_ref[rows, a:b], grad)
+            unit = lax.broadcasted_iota(jnp.int32, (b - a, tile), 0) + a
+            grad = jnp.where((unit >= h * HD) & (unit < h * HD + HD), go[a:b, :], jnp.zeros((b - a, tile), BF))
+            return query, grad, dot_bt(k_ref[rows, a:b], query), dot(v_ref[rows, a:b], grad)
 
         ready = products(0)
         for h, (a, b) in enumerate(wins):
@@ -196,7 +204,7 @@
             key = k_ref[rows, a:b]
             p = jnp.exp2(jnp.where(allowed, s * (SCALING * LOG2E) - lse_ref[h : h + 1, :], NEG))
             ds = (p * (dp - inner)).astype(BF)
-            dv_acc[rows, a:b] += dot(p.astype(BF), grad)
+            dv_acc[rows, a:b] += dot_bt(p.astype(BF), grad)
             dk_acc[rows, a:b] += dot(ds, query)
             outs.append(jnp.where(on, dot_at(ds, key) * SCALING, 0.0))
         for c, part in head_pieces(wins, outs):
@@ -231,7 +239,7 @@
             + [pl.BlockSpec(memory_space=pl.ANY)] * count,
             out_specs=whole_block((n, 3 * width)),
             scratch_shapes=[
-                pltpu.VMEM((n, go_blocks[0].shape[1]), BF),
+                pltpu.VMEM((go_blocks[0].shape[0], n), BF),
                 pltpu.VMEM((n, width), F32),
                 pltpu.VMEM((n, width), F32),
                 pltpu.VMEM((n, 128), F32),
@@ -614,15 +622,16 @@
     sum_out[1:2, :] = jnp.sum(grad, axis=0, keepdims=True)
     sum_out[2:3, :] = jnp.sum(ga.astype(F32), axis=0, keepdims=True)
     sum_out[3:4, :] = jnp.sum(gy_ref[...].astype(F32), axis=0, keepdims=True)
-    go = dot_bt(ga, w_out[...]).astype(BF)
-    cols = go_outs[0].shape[1]
+    cols = ga_outs[0].shape[1]
+    for i in range(count):
+        rows = pl.ds(pl.multiple_of(slots[i] * cols, 8), cols)
+        go_outs[i][...] = dot_bt(w_out[rows, :], ga).astype(BF)
     for v in range(count):
 
         @pl.when(slots[0] == v)
         def _(v=v):
             for i in range(count):
                 start = (v ^ i) * cols
-                go_outs[i][...] = go[:, start : start + cols]
                 ga_outs[i][...] = ga[:, start : start + cols]
 
 
@@ -633,12 +642,16 @@
     block = kept_block((rows, width))
     outs = pl.pallas_call(
         functools.partial(middle_kernel, count, terms),
-        out_shape=[shape((rows, width), F32), shape((8, width), F32)] + [shape((rows, cols), BF)] * (2 * count),
+        out_shape=[shape((rows, width), F32), shape((8, width), F32)]
+        + [shape((cols, rows), BF)] * count
+        + [shape((rows, cols), BF)] * count,
         grid_spec=pltpu.PrefetchScalarGridSpec(
             num_scalar_prefetch=1,
             grid=(1,),
             in_specs=[block] * (terms + 2) + [kept_block((1, width)), kept_block((width, width))],
-            out_specs=[whole_block((rows, width)), whole_block((8, width))] + [whole_block((rows, cols))] * (2 * count),
+            out_specs=[whole_block((rows, width)), whole_block((8, width))]
+            + [whole_block((cols, rows))] * count
+            + [whole_block((rows, cols))] * count,
         ),
         compiler_params=pltpu.CompilerParams(vmem_limit_bytes=56 << 20),
         cost_estimate=pl.CostEstimate(flops=2 * rows * width * width, bytes_accessed=20 * rows * width, transcendentals=rows),
@@ -764,10 +777,10 @@
         self.vector = vector
         self.steps = []
         for axis in ("seq", "fsdp"):
-            bits = 1
-            while bits < lax.axis_size(axis):
+            bits = lax.axis_size(axis) // 2
+            while bits:
                 self.steps.append((axis, bits))
-                bits *= 2
+                bits //= 2
 
     def hop(self, *earlier):
         vector = hold(self.vector, earlier)
@@ -814,7 +827,7 @@
     code = (image_ids * 2 + pad_mask).astype(BF)
     x_pack = jnp.concatenate([x_own, jnp.pad(code, ((0, 15), (0, width - rows)))], axis=0)
     split = rows // 2
-    x_parts = [x_pack[:split], x_pack[split:]]
+    x_parts = hold([x_pack[:split], x_pack[split:]], ring_one.one)
     far_a = far_swaps(x_parts[0])
     done = [far_a, *[ring_one.hop() for _ in range(hops)]]
     up_mine = own_hidden(w_up)
@@ -867,6 +880,9 @@
     x_one, o_all, h_two, active, slope, full_out = widen(
         x_all, os, w_outs, slots, row(out_bias), row(ln2_gain), row(ln2_shift), full_up, up_part, rows
     )
+    grad_down_part = dot_at(active, gy_all).astype(BF)
+    down_sum = lax.psum_scatter(grad_down_part, "fsdp", scatter_dimension=0, tiled=True)
+    active, gy_all = hold((active, gy_all), grad_down_part)
     gu, mixed, *far_dh, far_sum = narrow(gy_all, active, slope, full_up, full_down, slots, rows, 2, ns - 2, ())
 
     def cut(array, j):
@@ -876,14 +892,12 @@
         return (a.astype(F32) + b.astype(F32)).astype(BF)
 
     far_near = near_swaps(far_dh[1::2])
-    active, gy_all = hold((active, gy_all), far_dh)
-    grad_down_part = dot_at(active, gy_all).astype(BF)
-    down_sum = lax.psum_scatter(grad_down_part, "fsdp", scatter_dimension=0, tiled=True)
-    far_near, gy_all, active = hold((far_near, gy_all, active), grad_down_part)
+    far_near, gy_all, active = hold((far_near, gy_all, active), far_dh)
     far_held = [summed(far_dh[2 * i], got) for i, got in enumerate(far_near)]
     gu, mixed, far_held = hold((gu, mixed, far_held))
     terms = [swap(held, "seq", 2 * i + 2) for i, held in enumerate(far_held)]
     gu, mixed, *near_dh, near_sum = narrow(gy_all, active, slope, full_up, full_down, slots, rows, 0, 2, (gu, mixed))
+    near_dh, terms = hold((near_dh, terms))
     terms += [near_dh[0], swap(near_dh[1], "seq", 1)]
     dx_one, sums_two, go_parts, ga_parts = middle(terms, x_one, gy_own, row(ln2_gain), full_out, slots, ns)
     go_parts, h_two, gu, mixed = hold((go_parts, h_two, gu, mixed))
@@ -934,7 +948,7 @@
     dh_near = hold(dh_near, *done)
     dh_held = [summed(cut(dh_one_part, 2 * i), dh_near[i]) for i in range(1, ns // 2)]
     dh_far_a = [swap(block[:split], "seq", 2 * i + 2) for i, block in enumerate(dh_held)]
-    done = [dh_far_a, ring_round(*done), totals.hop(*done)]
+    done = [dh_far_a, up_sum, ring_round(*done), totals.hop(*done)]
     dh_held = hold(dh_held, *done)
     dh_far_b = [swap(block[split:], "seq", 2 * i + 2) for i, block in enumerate(dh_held)]
     done = [dh_far_b, ring_round(*done), totals.hop(*done)]

time: 387 us -> 386 us (level)
  waiting for transfers between devices: 88.8 us -> 82.8 us
  starting transfers between devices: 45.7 us -> 49.9 us
    ppermute x4, starting transfers between devices: 4.12 us -> 8.08 us  [hop(): one = lax.ppermute(one, 'fsdp', self.ahead)]
  transfers between devices with their start and end apart: 65 -> 65, of which waited for: 23 -> 22; matrix products, arithmetic and copies ran while one was open for 18% -> 20% of each run, Pallas kernels for 34% -> 38%
where the time goes in v4:
time: 386 us; the launch traced here: 380 us
  Pallas kernels  143 us (37%)
  waiting for transfers between devices  82.8 us (21%)
  starting transfers between devices  49.9 us (13%)
  local copies, waits for them, and re-layouts  44.7 us (12%)
  other arithmetic  27.3 us (7%)
  matrix products  17.7 us (5%)
  between operations  14.8 us (4%)
    ppermute x44, waiting for transfers between devices, swap(): return lax.ppermute(value, axis, [(i, i ^ bits) for i in range(size)])  41 us
    pallas_call x2, Pallas kernels, narrow(): pl.pallas_call(functools.partial(narrow_kernel, count), out_shape=[shape(...  29.9 us
    ppermute x44, starting transfers between devices, swap(): return lax.ppermute(value, axis, [(i, i ^ bits) for i in range(size)])  27.6 us
    pallas_call x1, Pallas kernels, attention_backward(): pl.pallas_call(functools.partial(backward_kernel, heads, tile, count, fir...  26.1 us
    ppermute x4, waiting for transfers between devices, hop(): self.one = lax.ppermute(one, 'fsdp', self.ahead)  22.1 us
    pallas_call x1, Pallas kernels, widen(): pl.pallas_call(functools.partial(widen_kernel, count), out_shape=[shape((...  22 us
    dot_general x2, matrix products, dot_at(): lax.dot_general(a, b, (((0,), (0,)), ((), ())), preferred_element_type=F32)  17.7 us
    pallas_call x1, Pallas kernels, attention_forward(): pl.pallas_call(functools.partial(forward_kernel, heads, tile), out_shape=...  16.7 us
  transfers between devices with their start and end apart: 65, of which 22 were waited for; matrix products, arithmetic and copies ran while one was open for 20% of the time, Pallas kernels for 38%

profile of v4, /device:TPU:0, one launch (start us, length us, event | category | flops | bytes accessed | tf_op | source)
XLA Modules:
  0.0 379.9 jit_solution(12278955369515146614)
XLA Ops:
  7.3 1.4 constant_dynamic-slice_fusion.13
  8.9 3.1 collective-permute-start.1
  14.7 1.9 collective-permute-start
  16.7 3.2 reshape.82
  21.5 1.5 fusion.11.refs_4_
  25.2 1.4 collective-permute-done.refs_2_
  26.6 1.6 collective-permute-start.3
  28.2 1.6 collective-permute-start.4
  30.3 5.9 %collective-permute-done.4.refs_9_ = bf16[144,1152]{1,0:T(8,128)(2,1)S(1)} collective-permute-done((bf16[144,1152]{1,0:T(8,128)(2,1)}, bf16[144,1152]{1,0:T(8,128)(2,1)S(1)}, u32[]{:S(2)}, u32[]{:S(2)}) %collective-permute-start.4) | collective-permute-done | bytes 331808 | tf_op jit(solution)/shard_map/ppermute | solution.py:729
  36.2 1.4 collective-permute-done.5.refs_10_
  41.9 1.5 collective-permute-start.9
  44.8 1.8 pad_dynamic-slice_fusion.1
  46.6 8.2 %collective-permute-done.9.refs_11_ = bf16[144,1152]{1,0:T(8,128)(2,1)} collective-permute-done((bf16[144,1152]{1,0:T(8,128)(2,1)}, bf16[144,1152]{1,0:T(8,128)(2,1)}, u32[]{:S(2)}, u32[]{:S(2)}) %collective-permute-start.9) | collective-permute-done | bytes 331808 | tf_op jit(solution)/shard_map/ppermute | solution.py:729
  54.8 3.9 %collective-permute-done.10.refs_12_ = bf16[144,1152]{1,0:T(8,128)(2,1)} collective-permute-done((bf16[144,1152]{1,0:T(8,128)(2,1)}, bf16[144,1152]{1,0:T(8,128)(2,1)}, u32[]{:S(2)}, u32[]{:S(2)}) %collective-permute-start.10) | collective-permute-done | bytes 331808 | tf_op jit(solution)/shard_map/ppermute | solution.py:733
  58.7 1.5 collective-permute-start.12
  61.1 8.0 %collective-permute-done.11.refs_13_ = bf16[144,1152]{1,0:T(8,128)(2,1)S(1)} collective-permute-done((bf16[144,1152]{1,0:T(8,128)(2,1)}, bf16[144,1152]{1,0:T(8,128)(2,1)S(1)}, u32[]{:S(2)}, u32[]{:S(2)}) %collective-permute-start.11) | collective-permute-done | bytes 331808 | tf_op jit(solution)/shard_map/ppermute | solution.py:729
  69.2 1.4 collective-permute-start.13
  71.8 14.2 %norm_project.1 = (bf16[1536,1152]{1,0:T(8,128)(2,1)}, bf16[1536,1152]{1,0:T(8,128)(2,1)}, bf16[1536,288]{1,0:T(8,128)(2,1)}, bf16[1536,288]{1,0:T(8,128)(2,1)},...) custom-call(s32[12]{0:T(128)} %stack.59.slots, ...), custom_call_target="tpu_custom_call" | custom-call | flops 4076863488 | bytes 14155776 | tf_op jit(solution)/shard_map/norm_project/pallas_call | solution.py:339
  87.0 16.7 %attention_forward.1 = (bf16[288,1536]{1,0:T(8,128)(2,1)}, f32[8,1536]{1,0:T(8,128)}) custom-call(bf16[1536,288]{1,0:T(8,128)(2,1)} %get-tuple-element.270.q_ref, bf16[1536,288]{1,0:T(8,128)(2,1)} %get-tuple-element.271.k_ref, bf16[1536,288]{1,0:T(8,128)(2,1)} %get-tuple-element.272.v_ref, s32[8,1536]{1,0:T(8,128)} %get-tuple-element.208.code_ref), custom_call_target="tpu_custom_call" | custom-call | flops 4831838208 | bytes 4423680 | tf_op jit(solution)/shard_map/attention_forward/pallas_call | solution.py:141
  103.7 3.3 collective-permute-done.14.refs_6_
  109.4 2.0 broadcast_in_dim.42
  118.4 12.5 %collective-permute-done.15.refs_2_ = bf16[288,1536]{1,0:T(8,128)(2,1)S(1)} collective-permute-done((bf16[288,1536]{1,0:T(8,128)(2,1)}, bf16[288,1536]{1,0:T(8,128)(2,1)S(1)}, u32[]{:S(2)}, u32[]{:S(2)}) %collective-permute-start.15) | collective-permute-done | bytes 884768 | tf_op jit(solution)/shard_map/ppermute | solution.py:665
  134.9 22.0 %out_norm_up.1 = (f32[384,1152]{1,0:T(8,128)}, bf16[1152,1536]{1,0:T(8,128)(2,1)}, bf16[1536,1152]{1,0:T(8,128)(2,1)}, bf16[1536,1152]{1,0:T(8,128)(2,1)}, bf16[...) custom-call(s32[4]{0:T(128)} %pad_add_fusion.slots, bf16[1536,1152]{1,0:T(8,128)(2,1)} %get-tuple-element.204.x_ref, ...), custom_call_target="tpu_custom_call" | custom-call | flops 8153726976 | bytes 28311552 | tf_op jit(solution)/shard_map/out_norm_up/pallas_call | solution.py:412
  156.9 9.4 %convolution_convert_fusion.1 = bf16[1152,1152]{1,0:T(8,128)(2,1)} fusion(bf16[1536,1152]{1,0:T(8,128)(2,1)} %get-tuple-element.237.a_ref, bf16[1536,1152]{1,0:T(8,128)(2,1)} %constant_dynamic-update-slice_fusion.gy_ref), kind=kOutput, calls=%fused_computation.1 | convolution fusion | flops 4078190592 | bytes 9732096 | tf_op jit(solution)/shard_map/dot_general | solution.py:287
  166.4 14.9 %down_and_back.2 = (bf16[1536,1152]{1,0:T(8,128)(2,1)}, bf16[1536,1152]{1,0:T(8,128)(2,1)}, bf16[384,1152]{1,0:T(8,128)(2,1)}, bf16[384,1152]{1,0:T(8,128)(2,1)}, f32[1,1152]{1,0:T(1,128)}) custom-call(s32[4]{0:T(128)} %pad_add_fusion.slots, bf16[1536,1152]{1,0:T(8,128)(2,1)} %constant_dynamic-update-slice_fusion.gy_ref, ...), custom_call_target="tpu_custom_call" | custom-call | flops 6115295232 | bytes 14155776 | tf_op jit(solution)/shard_map/down_and_back/pallas_call | solution.py:470
  181.4 2.5 collective-permute-done.24
  183.9 1.4 add_convert_fusion.3
  185.6 15.0 %down_and_back.3 = (bf16[1536,1152]{1,0:T(8,128)(2,1)}, bf16[1536,1152]{1,0:T(8,128)(2,1)}, bf16[384,1152]{1,0:T(8,128)(2,1)}, bf16[384,1152]{1,0:T(8,128)(2,1)}, f32[1,1152]{1,0:T(1,128)}) custom-call(s32[4]{0:T(128)} %pad_add_fusion.slots, ...), custom_call_target="tpu_custom_call", output_to_operand_aliasing={{0}: (6, {}), {1}: (7, {})} | custom-call | flops 6115295232 | bytes 14155776 | tf_op jit(solution)/shard_map/down_and_back/pallas_call | solution.py:470
  200.6 6.5 %collective-permute-done.25.refs_0_ = bf16[384,1152]{1,0:T(8,128)(2,1)S(1)} collective-permute-done((bf16[384,1152]{1,0:T(8,128)(2,1)S(1)}, bf16[384,1152]{1,0:T(8,128)(2,1)S(1)}, u32[]{:S(2)}, u32[]{:S(2)}) %collective-permute-start.25) | collective-permute-done | bytes 884768 | tf_op jit(solution)/shard_map/ppermute | solution.py:665
  207.1 2.6 collective-permute-done.26.refs_2_
  210.7 10.1 %norm_back_out.1 = (f32[384,1152]{1,0:T(8,128)}, f32[8,1152]{1,0:T(8,128)}, bf16[288,384]{1,0:T(8,128)(2,1)}, bf16[288,384]{1,0:T(8,128)(2,1)}, bf16[288,384]{1,...) custom-call(s32[4]{0:T(128)} %pad_add_fusion.slots, ...), custom_call_target="tpu_custom_call" | custom-call | flops 1019215872 | bytes 8847360 | tf_op jit(solution)/shard_map/norm_back_out/pallas_call | solution.py:643
  221.2 1.4 collective-permute-start.30
  223.3 8.3 %convolution_convert_fusion = bf16[1152,1152]{1,0:T(8,128)(2,1)} fusion(bf16[1536,1152]{1,0:T(8,128)(2,1)} %get-tuple-element.266, bf16[1536,1152]{1,0:T(8,128)(2,1)S(1)} %copy-done.5), kind=kOutput, calls=%fused_computation | convolution fusion | flops 4078190592 | bytes 9732096 | tf_op jit(solution)/shard_map/dot_general | solution.py:287
  231.7 1.5 add_convert_fusion.2
  235.9 26.1 %attention_backward.1.g_ref = bf16[1536,864]{1,0:T(8,128)(2,1)} custom-call(s32[4]{0:T(128)} %pad_add_fusion.slots, bf16[1536,288]{1,0:T(8,128)(2,1)} %get-tuple-element.270.q_ref, bf16[1536,288]{1,0:T(8,128)(2,1)} %get-tuple-element.271.k_ref, bf16[1536,288]{1,0:T(8,128)(2,1)} %get-tuple-element.272.v_ref, ...), custom_call_target="tpu_custom_call" | custom-call | flops 12079595520 | bytes 7077888 | tf_op jit(solution)/shard_map/attention_backward/pallas_call | solution.py:225
  262.8 2.1 constant_dynamic-slice_fusion.4
  264.9 1.4 collective-permute-start.40
  266.3 10.2 %grads_qkv_out.1 = bf16[1152,1152]{1,0:T(8,128)(2,1)} custom-call(bf16[1536,1152]{1,0:T(8,128)(2,1)} %get-tuple-element.283.h_ref, bf16[1536,864]{1,0:T(8,128)(2,1)} %attention_backward.1.g_ref, bf16[1152,1536]{1,0:T(8,128)(2,1)} %get-tuple-element.284.o_ref, bf16[384,288]{1,0:T(8,128)(2,1)} %get-tuple-element.285.refs_0_, bf16[384,288]{1,0:T(8,128)(2,1)} %copy-done.50, ...), custom_call_target="tpu_custom_call" | custom-call | flops 4076863488 | bytes 10616832 | tf_op jit(solution)/shard_map/grads_qkv_out/pallas_call | solution.py:598
  276.4 2.0 constant_dynamic-slice_fusion.8
  278.4 5.1 %collective-permute-start.36 = (bf16[144,1152]{1,0:T(8,128)(2,1)}, bf16[144,1152]{1,0:T(8,128)(2,1)S(1)}, u32[]{:S(2)}, u32[]{:S(2)}) collective-permute-start(bf16[144,1152]{1,0:T(8,128)(2,1)} %get-tuple-element.295), channel_id=1, source_target_pairs={{0,2},{2,4},{4,6},{6,7},{7,5},{5,3},{3,1},{1,0},{8,10},{10,12},{12... | collective-permute-start | bytes 995336 | tf_op jit(solution)/shard_map/ppermute | solution.py:757
  284.8 10.2 %project_back.1 = (bf16[1536,1152]{1,0:T(8,128)(2,1)}, f32[16,1152]{1,0:T(8,128)}) custom-call(s32[4]{0:T(128)} %pad_add_fusion.slots, bf16[1536,864]{1,0:T(8,128)(2,1)} %attention_backward.1.g_ref, bf16[1536,1152]{1,0:T(8,128)(2,1)} %get-tuple-element.204.x_ref, bf16[1152,1152]{1,0:T(8,128)(2,1)} %get-tuple-element.290.w_qkv, ...), custom_call_target="tpu_custom_call" | custom-call | flops 3057647616 | bytes 14155776 | tf_op jit(solution)/shard_map/project_back/pallas_call | solution.py:526
  296.2 1.6 fusion.16
  298.4 2.2 add_convert_fusion.7
  300.6 2.1 collective-permute-start.43
  304.6 2.7 collective-permute-done.45
  307.4 1.6 add.379
  308.9 8.4 %collective-permute-done.43 = bf16[144,1152]{1,0:T(8,128)(2,1)} collective-permute-done((bf16[144,1152]{1,0:T(8,128)(2,1)}, bf16[144,1152]{1,0:T(8,128)(2,1)}, u32[]{:S(2)}, u32[]{:S(2)}) %collective-permute-start.43) | collective-permute-done | bytes 331808 | tf_op jit(solution)/shard_map/ppermute | solution.py:757
  317.4 2.1 collective-permute-done.44
  319.5 1.6 add_convert_fusion
  322.8 1.5 collective-permute-start.46
  324.3 2.3 add_convert_fusion.5
  327.0 1.6 collective-permute-start.48
  328.6 1.6 add.386
  330.1 2.0 constant_dynamic-slice_fusion
  333.5 3.3 collective-permute-done.47
  336.9 2.4 collective-permute-start.52
  339.4 1.9 add_convert_fusion.4
  341.7 2.8 fusion.13
  346.6 3.5 settle_hidden.1
  351.6 4.9 %collective-permute-done.50 = bf16[192,1152]{1,0:T(8,128)(2,1)S(1)} collective-permute-done((bf16[192,1152]{1,0:T(8,128)(2,1)S(1)}, bf16[192,1152]{1,0:T(8,128)(2,1)S(1)}, u32[]{:S(2)}, u32[]{:S(2)}) %collective-permute-start.50) | collective-permute-done | bytes 442400 | tf_op jit(solution)/shard_map/ppermute | solution.py:665
  356.5 1.8 fusion.15
  360.1 3.3 collective-permute-start.55
  363.5 2.8 fusion.14
  369.1 2.4 collective-permute-done.60
  (262 shorter events, 54.0 us)
Async XLA Ops:
  7.2 127.6 %all-gather.3.cloned.1.call-start = ((), (), s32[]{:S(2)}) async-start(), calls=%async_computation.2 | async-start | bytes 2985984 | tf_op jit(solution)/shard_map/all_gather | solution.py:846
  8.9 16.3 %collective-permute-start.1 = (bf16[144,1152]{1,0:T(8,128)(2,1)S(1)}, bf16[144,1152]{1,0:T(8,128)(2,1)}, u32[]{:S(2)}, u32[]{:S(2)}) collective-permute-start(bf16[144,1152]{1,0:T(8,128)(2,1)S(1)} %concatenate.13.refs_6_), channel_id=1, source_target_pairs={{0,2},{2,4},{4,6},{6,7},{7,5},{5,3},{3,1},{1,0},{8,10},{10,12},{12... | collective-permute-start | bytes 995336 | tf_op jit(solution)/shard_map/ppermute | solution.py:729
  12.0 13.2 %collective-permute-start.2 = (bf16[144,1152]{1,0:T(8,128)(2,1)S(1)}, bf16[144,1152]{1,0:T(8,128)(2,1)}, u32[]{:S(2)}, u32[]{:S(2)}) collective-permute-start(bf16[144,1152]{1,0:T(8,128)(2,1)S(1)} %concatenate.13.refs_6_), channel_id=1, source_target_pairs={{2,0},{4,2},{6,4},{7,6},{5,7},{3,5},{1,3},{0,1},{10,8},{12,10},{14... | collective-permute-start | bytes 995336 | tf_op jit(solution)/shard_map/ppermute | solution.py:733
  14.7 11.9 %collective-permute-start = (bf16[192,1152]{1,0:T(8,128)(2,1)}, bf16[192,1152]{1,0:T(8,128)(2,1)}, u32[]{:S(2)}, u32[]{:S(2)}) collective-permute-start(bf16[192,1152]{1,0:T(8,128)(2,1)} %slice_bitcast_fusion), channel_id=1, source_target_pairs={{0,16},{8,24},{16,0},{24,8},{1,17},{9,25},{17,1},{25,9},{2,18},{10... | collective-permute-start | bytes 1327112 | tf_op jit(solution)/shard_map/ppermute | solution.py:665
  26.6 11.8 %collective-permute-start.3 = (bf16[208,1152]{1,0:T(8,128)(2,1)}, bf16[208,1152]{1,0:T(8,128)(2,1)}, u32[]{:S(2)}, u32[]{:S(2)}) collective-permute-start(bf16[208,1152]{1,0:T(8,128)(2,1)} %slice.103), channel_id=1, source_target_pairs={{0,16},{8,24},{16,0},{24,8},{1,17},{9,25},{17,1},{25,9},{2,18},{10... | collective-permute-start | bytes 1437704 | tf_op jit(solution)/shard_map/ppermute | solution.py:665
  28.2 8.0 %collective-permute-start.4 = (bf16[144,1152]{1,0:T(8,128)(2,1)}, bf16[144,1152]{1,0:T(8,128)(2,1)S(1)}, u32[]{:S(2)}, u32[]{:S(2)}) collective-permute-start(bf16[144,1152]{1,0:T(8,128)(2,1)} %collective-permute-done.1.refs_7_), channel_id=1, source_target_pairs={{0,2},{2,4},{4,6},{6,7},{7,5},{5,3},{3,1},{1,0},{8,10},{10,12},{12... | collective-permute-start | bytes 995336 | tf_op jit(solution)/shard_map/ppermute | solution.py:729
  29.8 7.8 %collective-permute-start.5 = (bf16[144,1152]{1,0:T(8,128)(2,1)}, bf16[144,1152]{1,0:T(8,128)(2,1)}, u32[]{:S(2)}, u32[]{:S(2)}) collective-permute-start(bf16[144,1152]{1,0:T(8,128)(2,1)} %collective-permute-done.2.refs_8_), channel_id=1, source_target_pairs={{2,0},{4,2},{6,4},{7,6},{5,7},{3,5},{1,3},{0,1},{10,8},{12,10},{14... | collective-permute-start | bytes 995336 | tf_op jit(solution)/shard_map/ppermute | solution.py:733
  38.5 127.9 %all-gather.5.cloned.1.call-start = ((), (), s32[]{:S(2)}) async-start(), calls=%async_computation.3 | async-start | bytes 2985984 | tf_op jit(solution)/shard_map/all_gather | solution.py:862
  38.5 20.1 %collective-permute-start.6 = (bf16[400,1152]{1,0:T(8,128)(2,1)S(1)}, bf16[400,1152]{1,0:T(8,128)(2,1)}, u32[]{:S(2)}, u32[]{:S(2)}) collective-permute-start(bf16[400,1152]{1,0:T(8,128)(2,1)S(1)} %copy-done.9), channel_id=1, source_target_pairs={{0,8},{8,0},{16,24},{24,16},{1,9},{9,1},{17,25},{25,17},{2,10},{10... | collective-permute-start | bytes 2764808 | tf_op jit(solution)/shard_map/ppermute | solution.py:665
  38.6 20.1 %collective-permute-start.8 = (bf16[208,1152]{1,0:T(8,128)(2,1)}, bf16[208,1152]{1,0:T(8,128)(2,1)}, u32[]{:S(2)}, u32[]{:S(2)}) collective-permute-start(bf16[208,1152]{1,0:T(8,128)(2,1)} %collective-permute-done.3.refs_3_), channel_id=1, source_target_pairs={{0,8},{8,0},{16,24},{24,16},{1,9},{9,1},{17,25},{25,17},{2,10},{10... | collective-permute-start | bytes 1437704 | tf_op jit(solution)/shard_map/ppermute | solution.py:665
  39.1 19.6 %collective-permute-start.7 = (bf16[192,1152]{1,0:T(8,128)(2,1)}, bf16[192,1152]{1,0:T(8,128)(2,1)}, u32[]{:S(2)}, u32[]{:S(2)}) collective-permute-start(bf16[192,1152]{1,0:T(8,128)(2,1)} %collective-permute-done.refs_2_), channel_id=1, source_target_pairs={{0,8},{8,0},{16,24},{24,16},{1,9},{9,1},{17,25},{25,17},{2,10},{10... | collective-permute-start | bytes 1327112 | tf_op jit(solution)/shard_map/ppermute | solution.py:665
  41.9 12.8 %collective-permute-start.9 = (bf16[144,1152]{1,0:T(8,128)(2,1)}, bf16[144,1152]{1,0:T(8,128)(2,1)}, u32[]{:S(2)}, u32[]{:S(2)}) collective-permute-start(bf16[144,1152]{1,0:T(8,128)(2,1)} %copy-done.45), channel_id=1, source_target_pairs={{0,2},{2,4},{4,6},{6,7},{7,5},{5,3},{3,1},{1,0},{8,10},{10,12},{12... | collective-permute-start | bytes 995336 | tf_op jit(solution)/shard_map/ppermute | solution.py:729
  43.4 15.2 %collective-permute-start.10 = (bf16[144,1152]{1,0:T(8,128)(2,1)}, bf16[144,1152]{1,0:T(8,128)(2,1)}, u32[]{:S(2)}, u32[]{:S(2)}) collective-permute-start(bf16[144,1152]{1,0:T(8,128)(2,1)} %collective-permute-done.5.refs_10_), channel_id=1, source_target_pairs={{2,0},{4,2},{6,4},{7,6},{5,7},{3,5},{1,3},{0,1},{10,8},{12,10},{14... | collective-permute-start | bytes 995336 | tf_op jit(solution)/shard_map/ppermute | solution.py:733
  58.7 10.5 %collective-permute-start.12 = (bf16[192,1152]{1,0:T(8,128)(2,1)}, bf16[192,1152]{1,0:T(8,128)(2,1)S(1)}, u32[]{:S(2)}, u32[]{:S(2)}) collective-permute-start(bf16[192,1152]{1,0:T(8,128)(2,1)} %get-tuple-element.221), channel_id=1, source_target_pairs={{0,16},{8,24},{16,0},{24,8},{1,17},{9,25},{17,1},{25,9},{2,18},{10... | collective-permute-start | bytes 1327112 | tf_op jit(solution)/shard_map/ppermute | solution.py:665
  60.1 9.1 %collective-permute-start.11 = (bf16[144,1152]{1,0:T(8,128)(2,1)}, bf16[144,1152]{1,0:T(8,128)(2,1)S(1)}, u32[]{:S(2)}, u32[]{:S(2)}) collective-permute-start(bf16[144,1152]{1,0:T(8,128)(2,1)} %collective-permute-done.9.refs_11_), channel_id=1, source_target_pairs={{0,2},{2,4},{4,6},{6,7},{7,5},{5,3},{3,1},{1,0},{8,10},{10,12},{12... | collective-permute-start | bytes 995336 | tf_op jit(solution)/shard_map/ppermute | solution.py:729
  69.2 16.9 %collective-permute-start.13 = (bf16[192,1152]{1,0:T(8,128)(2,1)S(1)}, bf16[192,1152]{1,0:T(8,128)(2,1)S(1)}, u32[]{:S(2)}, u32[]{:S(2)}) collective-permute-start(bf16[192,1152]{1,0:T(8,128)(2,1)S(1)} %get-tuple-element.223), channel_id=1, source_target_pairs={{0,16},{8,24},{16,0},{24,8},{1,17},{9,25},{17,1},{25,9},{2,18},{10... | collective-permute-start | bytes 1327112 | tf_op jit(solution)/shard_map/ppermute | solution.py:665
  86.1 20.9 %collective-permute-start.14 = (bf16[1152,384]{1,0:T(8,128)(2,1)}, bf16[1152,384]{1,0:T(8,128)(2,1)S(1)}, u32[]{:S(2)}, u32[]{:S(2)}) collective-permute-start(bf16[1152,384]{1,0:T(8,128)(2,1)} %get-tuple-element.219.refs_4_), channel_id=1, source_target_pairs={{0,16},{8,24},{16,0},{24,8},{1,17},{9,25},{17,1},{25,9},{2,18},{10... | collective-permute-start | bytes 2654216 | tf_op jit(solution)/shard_map/ppermute | solution.py:665
  107.9 4.4 %collective-permute-start.18 = (bf16[192,1152]{1,0:T(8,128)(2,1)S(1)}, bf16[192,1152]{1,0:T(8,128)(2,1)S(1)}, u32[]{:S(2)}, u32[]{:S(2)}) collective-permute-start(bf16[192,1152]{1,0:T(8,128)(2,1)S(1)} %copy-done.10), channel_id=1, source_target_pairs={{0,8},{8,0},{16,24},{24,16},{1,9},{9,1},{17,25},{25,17},{2,10},{10... | collective-permute-start | bytes 1327112 | tf_op jit(solution)/shard_map/ppermute | solution.py:665
  107.9 154.9 %reduce-scatter.3.cloned.1.call-start = ((), (), s32[]{:S(2)}) async-start(), calls=%async_computation.4 | async-start | bytes 2985984 | tf_op jit(solution)/shard_map/reduce_scatter | solution.py:884
  108.0 5.8 %collective-permute-start.19 = (bf16[192,1152]{1,0:T(8,128)(2,1)S(1)}, bf16[192,1152]{1,0:T(8,128)(2,1)S(1)}, u32[]{:S(2)}, u32[]{:S(2)}) collective-permute-start(bf16[192,1152]{1,0:T(8,128)(2,1)S(1)} %collective-permute-done.12), channel_id=1, source_target_pairs={{0,8},{8,0},{16,24},{24,16},{1,9},{9,1},{17,25},{25,17},{2,10},{10... | collective-permute-start | bytes 1327112 | tf_op jit(solution)/shard_map/ppermute | solution.py:665
  108.6 7.4 %collective-permute-start.20 = (bf16[192,1152]{1,0:T(8,128)(2,1)S(1)}, bf16[192,1152]{1,0:T(8,128)(2,1)S(1)}, u32[]{:S(2)}, u32[]{:S(2)}) collective-permute-start(bf16[192,1152]{1,0:T(8,128)(2,1)S(1)} %get-tuple-element.223), channel_id=1, source_target_pairs={{0,8},{8,0},{16,24},{24,16},{1,9},{9,1},{17,25},{25,17},{2,10},{10... | collective-permute-start | bytes 1327112 | tf_op jit(solution)/shard_map/ppermute | solution.py:665
  108.7 8.9 %collective-permute-start.21 = (bf16[192,1152]{1,0:T(8,128)(2,1)S(1)}, bf16[192,1152]{1,0:T(8,128)(2,1)S(1)}, u32[]{:S(2)}, u32[]{:S(2)}) collective-permute-start(bf16[192,1152]{1,0:T(8,128)(2,1)S(1)} %collective-permute-done.13), channel_id=1, source_target_pairs={{0,8},{8,0},{16,24},{24,16},{1,9},{9,1},{17,25},{25,17},{2,10},{10... | collective-permute-start | bytes 1327112 | tf_op jit(solution)/shard_map/ppermute | solution.py:665
  109.1 21.8 %collective-permute-start.15 = (bf16[288,1536]{1,0:T(8,128)(2,1)}, bf16[288,1536]{1,0:T(8,128)(2,1)S(1)}, u32[]{:S(2)}, u32[]{:S(2)}) collective-permute-start(bf16[288,1536]{1,0:T(8,128)(2,1)} %get-tuple-element.225.refs_0_.o_ref), channel_id=1, source_target_pairs={{0,16},{8,24},{16,0},{24,8},{1,17},{9,25},{17,1},{25,9},{2,18},{10... | collective-permute-start | bytes 2654216 | tf_op jit(solution)/shard_map/ppermute | solution.py:665
  112.2 18.7 %collective-permute-start.16 = (bf16[1152,384]{1,0:T(8,128)(2,1)S(1)}, bf16[1152,384]{1,0:T(8,128)(2,1)S(1)}, u32[]{:S(2)}, u32[]{:S(2)}) collective-permute-start(bf16[1152,384]{1,0:T(8,128)(2,1)S(1)} %copy-done.38), channel_id=1, source_target_pairs={{0,8},{8,0},{16,24},{24,16},{1,9},{9,1},{17,25},{25,17},{2,10},{10... | collective-permute-start | bytes 2654216 | tf_op jit(solution)/shard_map/ppermute | solution.py:665
  113.8 17.1 %collective-permute-start.17 = (bf16[1152,384]{1,0:T(8,128)(2,1)S(1)}, bf16[1152,384]{1,0:T(8,128)(2,1)S(1)}, u32[]{:S(2)}, u32[]{:S(2)}) collective-permute-start(bf16[1152,384]{1,0:T(8,128)(2,1)S(1)} %copy-done.40), channel_id=1, source_target_pairs={{0,8},{8,0},{16,24},{24,16},{1,9},{9,1},{17,25},{25,17},{2,10},{10... | collective-permute-start | bytes 2654216 | tf_op jit(solution)/shard_map/ppermute | solution.py:665
  131.0 3.0 collective-permute-start.22
  131.0 3.8 %collective-permute-start.23 = (bf16[288,1536]{1,0:T(8,128)(2,1)S(1)}, bf16[288,1536]{1,0:T(8,128)(2,1)}, u32[]{:S(2)}, u32[]{:S(2)}) collective-permute-start(bf16[288,1536]{1,0:T(8,128)(2,1)S(1)} %collective-permute-done.15.refs_2_), channel_id=1, source_target_pairs={{0,8},{8,0},{16,24},{24,16},{1,9},{9,1},{17,25},{25,17},{2,10},{10... | collective-permute-start | bytes 2654216 | tf_op jit(solution)/shard_map/ppermute | solution.py:665
  166.3 163.8 %reduce-scatter.5.cloned.1.call-start = ((), (), s32[]{:S(2)}) async-start(), calls=%async_computation.5 | async-start | bytes 2985984 | tf_op jit(solution)/shard_map/reduce_scatter | solution.py:906
  181.3 2.6 collective-permute-start.24
  185.3 21.8 %collective-permute-start.25 = (bf16[384,1152]{1,0:T(8,128)(2,1)S(1)}, bf16[384,1152]{1,0:T(8,128)(2,1)S(1)}, u32[]{:S(2)}, u32[]{:S(2)}) collective-permute-start(bf16[384,1152]{1,0:T(8,128)(2,1)S(1)} %add_convert_fusion.3), channel_id=1, source_target_pairs={{0,16},{8,24},{16,0},{24,8},{1,17},{9,25},{17,1},{25,9},{2,18},{10... | collective-permute-start | bytes 2654216 | tf_op jit(solution)/shard_map/ppermute | solution.py:665
  220.7 12.4 %collective-permute-start.28 = (bf16[288,384]{1,0:T(8,128)(2,1)}, bf16[288,384]{1,0:T(8,128)(2,1)}, u32[]{:S(2)}, u32[]{:S(2)}) collective-permute-start(bf16[288,384]{1,0:T(8,128)(2,1)} %get-tuple-element.259), channel_id=1, source_target_pairs={{0,8},{8,0},{16,24},{24,16},{1,9},{9,1},{17,25},{25,17},{2,10},{10... | collective-permute-start | bytes 663560 | tf_op jit(solution)/shard_map/ppermute | solution.py:665
  220.8 12.3 %collective-permute-start.29 = (bf16[288,384]{1,0:T(8,128)(2,1)}, bf16[288,384]{1,0:T(8,128)(2,1)}, u32[]{:S(2)}, u32[]{:S(2)}) collective-permute-start(bf16[288,384]{1,0:T(8,128)(2,1)} %get-tuple-element.260), channel_id=1, source_target_pairs={{0,16},{8,24},{16,0},{24,8},{1,17},{9,25},{17,1},{25,9},{2,18},{10... | collective-permute-start | bytes 663560 | tf_op jit(solution)/shard_map/ppermute | solution.py:665
  221.2 12.0 %collective-permute-start.30 = (bf16[288,384]{1,0:T(8,128)(2,1)}, bf16[288,384]{1,0:T(8,128)(2,1)}, u32[]{:S(2)}, u32[]{:S(2)}) collective-permute-start(bf16[288,384]{1,0:T(8,128)(2,1)} %get-tuple-element.261), channel_id=1, source_target_pairs={{0,24},{8,16},{16,8},{24,0},{1,25},{9,17},{17,9},{25,1},{2,26},{10... | collective-permute-start | bytes 663560 | tf_op jit(solution)/shard_map/ppermute | solution.py:665
  222.8 10.4 %collective-permute-start.27 = (bf16[384,1152]{1,0:T(8,128)(2,1)S(1)}, bf16[384,1152]{1,0:T(8,128)(2,1)}, u32[]{:S(2)}, u32[]{:S(2)}) collective-permute-start(bf16[384,1152]{1,0:T(8,128)(2,1)S(1)} %get-tuple-element.333), channel_id=1, source_target_pairs={{0,8},{8,0},{16,24},{24,16},{1,9},{9,1},{17,25},{25,17},{2,10},{10... | collective-permute-start | bytes 2654216 | tf_op jit(solution)/shard_map/ppermute | solution.py:665
  223.2 8.5 %collective-permute-start.31 = (bf16[384,1152]{1,0:T(8,128)(2,1)S(1)}, bf16[384,1152]{1,0:T(8,128)(2,1)S(1)}, u32[]{:S(2)}, u32[]{:S(2)}) collective-permute-start(bf16[384,1152]{1,0:T(8,128)(2,1)S(1)} %get-tuple-element.334), channel_id=1, source_target_pairs={{0,8},{8,0},{16,24},{24,16},{1,9},{9,1},{17,25},{25,17},{2,10},{10... | collective-permute-start | bytes 2654216 | tf_op jit(solution)/shard_map/ppermute | solution.py:665
  233.2 28.7 %collective-permute-start.33 = (bf16[384,288]{1,0:T(8,128)(2,1)S(1)}, bf16[384,288]{1,0:T(8,128)(2,1)S(1)}, u32[]{:S(2)}, u32[]{:S(2)}) collective-permute-start(bf16[384,288]{1,0:T(8,128)(2,1)S(1)} %copy-done.49), channel_id=1, source_target_pairs={{0,8},{8,0},{16,24},{24,16},{1,9},{9,1},{17,25},{25,17},{2,10},{10... | collective-permute-start | bytes 663560 | tf_op jit(solution)/shard_map/ppermute | solution.py:665
  233.8 28.2 %collective-permute-start.34 = (bf16[384,288]{1,0:T(8,128)(2,1)S(1)}, bf16[384,288]{1,0:T(8,128)(2,1)S(1)}, u32[]{:S(2)}, u32[]{:S(2)}) collective-permute-start(bf16[384,288]{1,0:T(8,128)(2,1)S(1)} %copy-done.48), channel_id=1, source_target_pairs={{0,16},{8,24},{16,0},{24,8},{1,17},{9,25},{17,1},{25,9},{2,18},{10... | collective-permute-start | bytes 663560 | tf_op jit(solution)/shard_map/ppermute | solution.py:665
  234.1 27.9 %collective-permute-start.35 = (bf16[384,288]{1,0:T(8,128)(2,1)S(1)}, bf16[384,288]{1,0:T(8,128)(2,1)S(1)}, u32[]{:S(2)}, u32[]{:S(2)}) collective-permute-start(bf16[384,288]{1,0:T(8,128)(2,1)S(1)} %copy-done.47), channel_id=1, source_target_pairs={{0,24},{8,16},{16,8},{24,0},{1,25},{9,17},{17,9},{25,1},{2,26},{10... | collective-permute-start | bytes 663560 | tf_op jit(solution)/shard_map/ppermute | solution.py:665
  235.2 59.8 %collective-permute-start.32 = (bf16[384,1152]{1,0:T(8,128)(2,1)S(1)}, bf16[384,1152]{1,0:T(8,128)(2,1)S(1)}, u32[]{:S(2)}, u32[]{:S(2)}) collective-permute-start(bf16[384,1152]{1,0:T(8,128)(2,1)S(1)} %add_convert_fusion.2), channel_id=1, source_target_pairs={{0,16},{8,24},{16,0},{24,8},{1,17},{9,25},{17,1},{25,9},{2,18},{10... | collective-permute-start | bytes 2654216 | tf_op jit(solution)/shard_map/ppermute | solution.py:665
  264.9 19.9 %collective-permute-start.40 = (bf16[144,288]{1,0:T(8,128)(2,1)}, bf16[144,288]{1,0:T(8,128)(2,1)S(1)}, u32[]{:S(2)}, u32[]{:S(2)}) collective-permute-start(bf16[144,288]{1,0:T(8,128)(2,1)} %get-tuple-element.353), channel_id=1, source_target_pairs={{0,24},{8,16},{16,8},{24,0},{1,25},{9,17},{17,9},{25,1},{2,26},{10... | collective-permute-start | bytes 248840 | tf_op jit(solution)/shard_map/ppermute | solution.py:665
  278.4 16.6 %collective-permute-start.36 = (bf16[144,1152]{1,0:T(8,128)(2,1)}, bf16[144,1152]{1,0:T(8,128)(2,1)S(1)}, u32[]{:S(2)}, u32[]{:S(2)}) collective-permute-start(bf16[144,1152]{1,0:T(8,128)(2,1)} %get-tuple-element.295), channel_id=1, source_target_pairs={{0,2},{2,4},{4,6},{6,7},{7,5},{5,3},{3,1},{1,0},{8,10},{10,12},{12... | collective-permute-start | bytes 995336 | tf_op jit(solution)/shard_map/ppermute | solution.py:757
  283.6 11.4 %collective-permute-start.37 = (bf16[144,1152]{1,0:T(8,128)(2,1)}, bf16[144,1152]{1,0:T(8,128)(2,1)S(1)}, u32[]{:S(2)}, u32[]{:S(2)}) collective-permute-start(bf16[144,1152]{1,0:T(8,128)(2,1)} %get-tuple-element.296), channel_id=1, source_target_pairs={{2,0},{4,2},{6,4},{7,6},{5,7},{3,5},{1,3},{0,1},{10,8},{12,10},{14... | collective-permute-start | bytes 995336 | tf_op jit(solution)/shard_map/ppermute | solution.py:759
  283.8 11.2 %collective-permute-start.39 = (bf16[144,288]{1,0:T(8,128)(2,1)}, bf16[144,288]{1,0:T(8,128)(2,1)S(1)}, u32[]{:S(2)}, u32[]{:S(2)}) collective-permute-start(bf16[144,288]{1,0:T(8,128)(2,1)} %get-tuple-element.354), channel_id=1, source_target_pairs={{0,16},{8,24},{16,0},{24,8},{1,17},{9,25},{17,1},{25,9},{2,18},{10... | collective-permute-start | bytes 248840 | tf_op jit(solution)/shard_map/ppermute | solution.py:665
  284.8 10.2 %collective-permute-start.38 = (bf16[144,288]{1,0:T(8,128)(2,1)S(1)}, bf16[144,288]{1,0:T(8,128)(2,1)S(1)}, u32[]{:S(2)}, u32[]{:S(2)}) collective-permute-start(bf16[144,288]{1,0:T(8,128)(2,1)S(1)} %get-tuple-element.355), channel_id=1, source_target_pairs={{0,8},{8,0},{16,24},{24,16},{1,9},{9,1},{17,25},{25,17},{2,10},{10... | collective-permute-start | bytes 248840 | tf_op jit(solution)/shard_map/ppermute | solution.py:665
  297.8 21.6 %collective-permute-start.42 = (bf16[384,1152]{1,0:T(8,128)(2,1)S(1)}, bf16[384,1152]{1,0:T(8,128)(2,1)}, u32[]{:S(2)}, u32[]{:S(2)}) collective-permute-start(bf16[384,1152]{1,0:T(8,128)(2,1)S(1)} %get-tuple-element.331), channel_id=1, source_target_pairs={{0,8},{8,0},{16,24},{24,16},{1,9},{9,1},{17,25},{25,17},{2,10},{10... | collective-permute-start | bytes 2654216 | tf_op jit(solution)/shard_map/ppermute | solution.py:665
  298.4 21.1 %collective-permute-start.41 = (bf16[384,1152]{1,0:T(8,128)(2,1)S(1)}, bf16[384,1152]{1,0:T(8,128)(2,1)S(1)}, u32[]{:S(2)}, u32[]{:S(2)}) collective-permute-start(bf16[384,1152]{1,0:T(8,128)(2,1)S(1)} %get-tuple-element.332), channel_id=1, source_target_pairs={{0,8},{8,0},{16,24},{24,16},{1,9},{9,1},{17,25},{25,17},{2,10},{10... | collective-permute-start | bytes 2654216 | tf_op jit(solution)/shard_map/ppermute | solution.py:665
  300.6 16.8 %collective-permute-start.43 = (bf16[144,1152]{1,0:T(8,128)(2,1)}, bf16[144,1152]{1,0:T(8,128)(2,1)}, u32[]{:S(2)}, u32[]{:S(2)}) collective-permute-start(bf16[144,1152]{1,0:T(8,128)(2,1)} %get-tuple-element.301), channel_id=1, source_target_pairs={{0,2},{2,4},{4,6},{6,7},{7,5},{5,3},{3,1},{1,0},{8,10},{10,12},{12... | collective-permute-start | bytes 995336 | tf_op jit(solution)/shard_map/ppermute | solution.py:757
  302.7 16.8 %collective-permute-start.44 = (bf16[144,1152]{1,0:T(8,128)(2,1)}, bf16[144,1152]{1,0:T(8,128)(2,1)}, u32[]{:S(2)}, u32[]{:S(2)}) collective-permute-start(bf16[144,1152]{1,0:T(8,128)(2,1)} %get-tuple-element.302), channel_id=1, source_target_pairs={{2,0},{4,2},{6,4},{7,6},{5,7},{3,5},{1,3},{0,1},{10,8},{12,10},{14... | collective-permute-start | bytes 995336 | tf_op jit(solution)/shard_map/ppermute | solution.py:759
  302.7 4.7 %collective-permute-start.45 = (f32[16,1152]{1,0:T(8,128)}, f32[16,1152]{1,0:T(8,128)}, u32[]{:S(2)}, u32[]{:S(2)}) collective-permute-start(f32[16,1152]{1,0:T(8,128)} %get-tuple-element.304), channel_id=1, source_target_pairs={{0,16},{8,24},{16,0},{24,8},{1,17},{9,25},{17,1},{25,9},{2,18},{10... | collective-permute-start | bytes 221192 | tf_op jit(solution)/shard_map/ppermute | solution.py:665
  319.4 9.1 %collective-permute-start.49 = (f32[16,1152]{1,0:T(8,128)}, f32[16,1152]{1,0:T(8,128)}, u32[]{:S(2)}, u32[]{:S(2)}) collective-permute-start(f32[16,1152]{1,0:T(8,128)} %add.379), channel_id=1, source_target_pairs={{0,8},{8,0},{16,24},{24,16},{1,9},{9,1},{17,25},{25,17},{2,10},{10... | collective-permute-start | bytes 221192 | tf_op jit(solution)/shard_map/ppermute | solution.py:665
  322.8 14.1 %collective-permute-start.46 = (bf16[192,1152]{1,0:T(8,128)(2,1)}, bf16[192,1152]{1,0:T(8,128)(2,1)}, u32[]{:S(2)}, u32[]{:S(2)}) collective-permute-start(bf16[192,1152]{1,0:T(8,128)(2,1)} %slice.106), channel_id=1, source_target_pairs={{0,16},{8,24},{16,0},{24,8},{1,17},{9,25},{17,1},{25,9},{2,18},{10... | collective-permute-start | bytes 1327112 | tf_op jit(solution)/shard_map/ppermute | solution.py:665
  326.5 10.2 %collective-permute-start.47 = (bf16[144,1152]{1,0:T(8,128)(2,1)}, bf16[144,1152]{1,0:T(8,128)(2,1)}, u32[]{:S(2)}, u32[]{:S(2)}) collective-permute-start(bf16[144,1152]{1,0:T(8,128)(2,1)} %get-tuple-element.309), channel_id=1, source_target_pairs={{0,2},{2,4},{4,6},{6,7},{7,5},{5,3},{3,1},{1,0},{8,10},{10,12},{12... | collective-permute-start | bytes 995336 | tf_op jit(solution)/shard_map/ppermute | solution.py:757
  327.0 10.0 %collective-permute-start.48 = (bf16[144,1152]{1,0:T(8,128)(2,1)}, bf16[144,1152]{1,0:T(8,128)(2,1)}, u32[]{:S(2)}, u32[]{:S(2)}) collective-permute-start(bf16[144,1152]{1,0:T(8,128)(2,1)} %get-tuple-element.310), channel_id=1, source_target_pairs={{2,0},{4,2},{6,4},{7,6},{5,7},{3,5},{1,3},{0,1},{10,8},{12,10},{14... | collective-permute-start | bytes 995336 | tf_op jit(solution)/shard_map/ppermute | solution.py:759
  332.2 13.1 %collective-permute-start.58 = (bf16[144,288]{1,0:T(8,128)(2,1)S(1)}, bf16[144,288]{1,0:T(8,128)(2,1)}, u32[]{:S(2)}, u32[]{:S(2)}) collective-permute-start(bf16[144,288]{1,0:T(8,128)(2,1)S(1)} %get-tuple-element.346), channel_id=1, source_target_pairs={{0,24},{8,16},{16,8},{24,0},{1,25},{9,17},{17,9},{25,1},{2,26},{10... | collective-permute-start | bytes 248840 | tf_op jit(solution)/shard_map/ppermute | solution.py:665
  332.2 13.1 %collective-permute-start.57 = (bf16[144,288]{1,0:T(8,128)(2,1)S(1)}, bf16[144,288]{1,0:T(8,128)(2,1)S(1)}, u32[]{:S(2)}, u32[]{:S(2)}) collective-permute-start(bf16[144,288]{1,0:T(8,128)(2,1)S(1)} %get-tuple-element.347), channel_id=1, source_target_pairs={{0,16},{8,24},{16,0},{24,8},{1,17},{9,25},{17,1},{25,9},{2,18},{10... | collective-permute-start | bytes 248840 | tf_op jit(solution)/shard_map/ppermute | solution.py:665
  336.8 8.6 %collective-permute-start.56 = (bf16[144,288]{1,0:T(8,128)(2,1)S(1)}, bf16[144,288]{1,0:T(8,128)(2,1)S(1)}, u32[]{:S(2)}, u32[]{:S(2)}) collective-permute-start(bf16[144,288]{1,0:T(8,128)(2,1)S(1)} %get-tuple-element.348), channel_id=1, source_target_pairs={{0,8},{8,0},{16,24},{24,16},{1,9},{9,1},{17,25},{25,17},{2,10},{10... | collective-permute-start | bytes 248840 | tf_op jit(solution)/shard_map/ppermute | solution.py:665
  336.9 7.6 %collective-permute-start.52 = (f32[16,1152]{1,0:T(8,128)}, f32[16,1152]{1,0:T(8,128)S(1)}, u32[]{:S(2)}, u32[]{:S(2)}) collective-permute-start(f32[16,1152]{1,0:T(8,128)} %add.386), channel_id=1, source_target_pairs={{0,4},{1,5},{2,6},{3,7},{4,0},{5,1},{6,2},{7,3},{8,12},{9,13},{10,... | collective-permute-start | bytes 221192 | tf_op jit(solution)/shard_map/ppermute | solution.py:665
  341.3 9.0 %collective-permute-start.51 = (bf16[144,1152]{1,0:T(8,128)(2,1)}, bf16[144,1152]{1,0:T(8,128)(2,1)}, u32[]{:S(2)}, u32[]{:S(2)}) collective-permute-start(bf16[144,1152]{1,0:T(8,128)(2,1)} %add_convert_fusion.4), channel_id=1, source_target_pairs={{0,2},{2,4},{4,6},{6,7},{7,5},{5,3},{3,1},{1,0},{8,10},{10,12},{12... | collective-permute-start | bytes 995336 | tf_op jit(solution)/shard_map/ppermute | solution.py:757
  344.6 11.9 %collective-permute-start.50 = (bf16[192,1152]{1,0:T(8,128)(2,1)S(1)}, bf16[192,1152]{1,0:T(8,128)(2,1)S(1)}, u32[]{:S(2)}, u32[]{:S(2)}) collective-permute-start(bf16[192,1152]{1,0:T(8,128)(2,1)S(1)} %slice.88), channel_id=1, source_target_pairs={{0,16},{8,24},{16,0},{24,8},{1,17},{9,25},{17,1},{25,9},{2,18},{10... | collective-permute-start | bytes 1327112 | tf_op jit(solution)/shard_map/ppermute | solution.py:665
  358.3 8.7 %collective-permute-start.59 = (f32[16,1152]{1,0:T(8,128)S(1)}, f32[16,1152]{1,0:T(8,128)S(1)}, u32[]{:S(2)}, u32[]{:S(2)}) collective-permute-start(f32[16,1152]{1,0:T(8,128)S(1)} %add.397), channel_id=1, source_target_pairs={{0,2},{1,3},{2,0},{3,1},{4,6},{5,7},{6,4},{7,5},{8,10},{9,11},{10,... | collective-permute-start | bytes 221192 | tf_op jit(solution)/shard_map/ppermute | solution.py:665
  359.2 9.0 %collective-permute-start.53 = (bf16[144,288]{1,0:T(8,128)(2,1)S(1)}, bf16[144,288]{1,0:T(8,128)(2,1)S(1)}, u32[]{:S(2)}, u32[]{:S(2)}) collective-permute-start(bf16[144,288]{1,0:T(8,128)(2,1)S(1)} %get-tuple-element.350), channel_id=1, source_target_pairs={{0,0},{24,8},{16,16},{8,24},{1,1},{25,9},{17,17},{9,25},{2,2},{26,... | collective-permute-start | bytes 248840 | tf_op jit(solution)/shard_map/ppermute | solution.py:967
  359.9 8.3 %collective-permute-start.54 = (bf16[144,288]{1,0:T(8,128)(2,1)S(1)}, bf16[144,288]{1,0:T(8,128)(2,1)S(1)}, u32[]{:S(2)}, u32[]{:S(2)}) collective-permute-start(bf16[144,288]{1,0:T(8,128)(2,1)S(1)} %get-tuple-element.351), channel_id=1, source_target_pairs={{8,0},{0,8},{24,16},{16,24},{9,1},{1,9},{25,17},{17,25},{10,2},{2,... | collective-permute-start | bytes 248840 | tf_op jit(solution)/shard_map/ppermute | solution.py:967
  360.1 8.0 %collective-permute-start.55 = (bf16[144,288]{1,0:T(8,128)(2,1)S(1)}, bf16[144,288]{1,0:T(8,128)(2,1)S(1)}, u32[]{:S(2)}, u32[]{:S(2)}) collective-permute-start(bf16[144,288]{1,0:T(8,128)(2,1)S(1)} %get-tuple-element.352), channel_id=1, source_target_pairs={{16,0},{8,8},{0,16},{24,24},{17,1},{9,9},{1,17},{25,25},{18,2},{10... | collective-permute-start | bytes 248840 | tf_op jit(solution)/shard_map/ppermute | solution.py:967
  367.1 4.4 %collective-permute-start.60 = (f32[16,1152]{1,0:T(8,128)S(1)}, f32[16,1152]{1,0:T(8,128)S(1)}, u32[]{:S(2)}, u32[]{:S(2)}) collective-permute-start(f32[16,1152]{1,0:T(8,128)S(1)} %add.402), channel_id=1, source_target_pairs={{0,1},{1,0},{2,3},{3,2},{4,5},{5,4},{6,7},{7,6},{8,9},{9,8},{10,11... | collective-permute-start | bytes 221192 | tf_op jit(solution)/shard_map/ppermute | solution.py:665
  (54 other events, 439.1 us)
Sparse Core Ops, SparseCore 0:
  38.6 60.3 all-gather.2
  108.0 55.8 all-gather.4
  167.6 70.2 reduce-scatter.2
  241.8 78.9 reduce-scatter.4

commit v5 on v4

--- a/solution.py
+++ b/solution.py
@@ -291,6 +291,36 @@
     return [slice(0, 256), slice(256, rows)]
 
 
+def deal_kernel(count, strips, slots, w_ref, out_ref):
+    strip, sub = w_ref.shape[1] // strips, out_ref.shape[1] // strips
+    out_ref[...] = jnp.zeros_like(out_ref)
+    for v in range(count):
+        size = min(sub, strip - v * sub)
+        if size > 0:
+
+            @pl.when(slots[0] == v)
+            def _(v=v, size=size):
+                for f in range(strips):
+                    start = f * strip + v * sub
+                    out_ref[:, f * sub : f * sub + size] = w_ref[:, start : start + size]
+
+
+def deal(w_up, slots, count, strips, wide):
+    band, hidden = w_up.shape
+    return pl.pallas_call(
+        functools.partial(deal_kernel, count, strips),
+        out_shape=jax.ShapeDtypeStruct((band, wide), BF),
+        grid_spec=pltpu.PrefetchScalarGridSpec(
+            num_scalar_prefetch=1,
+            grid=(1,),
+            in_specs=[kept_block((band, hidden))],
+            out_specs=whole_block((band, wide)),
+        ),
+        cost_estimate=pl.CostEstimate(flops=0, bytes_accessed=2 * band * (hidden + wide), transcendentals=0),
+        name="deal_hidden",
+    )(slots, w_up)
+
+
 def project_kernel(counts, bands, slots, *refs):
     xs, pieces = refs[: sum(counts)], refs[sum(counts) : sum(counts) + bands]
     gain, shift, q_bias, v_bias, x_out, h_out, q_out, k_out, v_out, w_out, out_out, code_out, x_now, sems = refs[
@@ -830,7 +860,7 @@
     x_parts = hold([x_pack[:split], x_pack[split:]], ring_one.one)
     far_a = far_swaps(x_parts[0])
     done = [far_a, *[ring_one.hop() for _ in range(hops)]]
-    up_mine = own_hidden(w_up)
+    up_mine = deal(w_up, slots, ns, nf, wide)
     keep = (1 - pad_mask[0]).astype(F32)[:, None]
     gy_own = (cotangent[0].astype(F32) * keep).astype(BF)
     gy_parts = [gy_own[:split], gy_own[split:]]

time: 386 us -> 385 us (level)
  local copies, waits for them, and re-layouts: 44.7 us -> 39.1 us
  Pallas kernels: 143 us -> 148 us
  transfers between devices with their start and end apart: 65 -> 65, of which waited for: 22 -> 22; matrix products, arithmetic and copies ran while one was open for 20% -> 19% of each run, Pallas kernels for 38% -> 39%
where the time goes in v5:
time: 385 us; the launch traced here: 379 us
  Pallas kernels  148 us (38%)
  waiting for transfers between devices  82.3 us (21%)
  starting transfers between devices  49.7 us (13%)
  local copies, waits for them, and re-layouts  39.1 us (10%)
  other arithmetic  26.9 us (7%)
  matrix products  17.7 us (5%)
  between operations  14.8 us (4%)
    ppermute x44, waiting for transfers between devices, swap(): return lax.ppermute(value, axis, [(i, i ^ bits) for i in range(size)])  38.1 us
    pallas_call x2, Pallas kernels, narrow(): pl.pallas_call(functools.partial(narrow_kernel, count), out_shape=[shape(...  29.9 us
    ppermute x44, starting transfers between devices, swap(): return lax.ppermute(value, axis, [(i, i ^ bits) for i in range(size)])  28.2 us
    pallas_call x1, Pallas kernels, attention_backward(): pl.pallas_call(functools.partial(backward_kernel, heads, tile, count, fir...  26.1 us
    ppermute x4, waiting for transfers between devices, hop(): self.one = lax.ppermute(one, 'fsdp', self.ahead)  22.1 us
    pallas_call x1, Pallas kernels, widen(): pl.pallas_call(functools.partial(widen_kernel, count), out_shape=[shape((...  22 us
    pallas_call x1, Pallas kernels, attention_forward(): pl.pallas_call(functools.partial(forward_kernel, heads, tile), out_shape=...  19 us
    dot_general x2, matrix products, dot_at(): lax.dot_general(a, b, (((0,), (0,)), ((), ())), preferred_element_type=F32)  17.7 us
  transfers between devices with their start and end apart: 65, of which 22 were waited for; matrix products, arithmetic and copies ran while one was open for 19% of the time, Pallas kernels for 39%

profile of v5, /device:TPU:0, one launch (start us, length us, event | category | flops | bytes accessed | tf_op | source)
XLA Modules:
  0.0 378.8 jit_solution(3292332755161600482)
XLA Ops:
  7.3 1.4 constant_dynamic-slice_fusion.13
  8.9 3.1 collective-permute-start.1
  13.8 1.9 collective-permute-start
  16.4 2.9 deal_hidden.1
  22.5 3.3 collective-permute-done.refs_2_
  25.7 1.6 collective-permute-start.3
  27.4 1.6 collective-permute-start.4
  29.4 5.9 %collective-permute-done.4.refs_9_ = bf16[144,1152]{1,0:T(8,128)(2,1)S(1)} collective-permute-done((bf16[144,1152]{1,0:T(8,128)(2,1)}, bf16[144,1152]{1,0:T(8,128)(2,1)S(1)}, u32[]{:S(2)}, u32[]{:S(2)}) %collective-permute-start.4) | collective-permute-done | bytes 331808 | tf_op jit(solution)/shard_map/ppermute | solution.py:759
  35.3 1.4 collective-permute-done.5.refs_10_
  41.1 1.5 collective-permute-start.9
  43.9 1.8 pad_dynamic-slice_fusion
  45.7 8.2 %collective-permute-done.9.refs_11_ = bf16[144,1152]{1,0:T(8,128)(2,1)} collective-permute-done((bf16[144,1152]{1,0:T(8,128)(2,1)}, bf16[144,1152]{1,0:T(8,128)(2,1)}, u32[]{:S(2)}, u32[]{:S(2)}) %collective-permute-start.9) | collective-permute-done | bytes 331808 | tf_op jit(solution)/shard_map/ppermute | solution.py:759
  53.9 3.9 %collective-permute-done.10.refs_12_ = bf16[144,1152]{1,0:T(8,128)(2,1)} collective-permute-done((bf16[144,1152]{1,0:T(8,128)(2,1)}, bf16[144,1152]{1,0:T(8,128)(2,1)}, u32[]{:S(2)}, u32[]{:S(2)}) %collective-permute-start.10) | collective-permute-done | bytes 331808 | tf_op jit(solution)/shard_map/ppermute | solution.py:763
  57.8 1.5 collective-permute-start.12
  60.3 8.0 %collective-permute-done.11.refs_13_ = bf16[144,1152]{1,0:T(8,128)(2,1)S(1)} collective-permute-done((bf16[144,1152]{1,0:T(8,128)(2,1)}, bf16[144,1152]{1,0:T(8,128)(2,1)S(1)}, u32[]{:S(2)}, u32[]{:S(2)}) %collective-permute-start.11) | collective-permute-done | bytes 331808 | tf_op jit(solution)/shard_map/ppermute | solution.py:759
  68.3 1.4 collective-permute-start.13
  71.0 14.2 %norm_project.1 = (bf16[1536,1152]{1,0:T(8,128)(2,1)}, bf16[1536,1152]{1,0:T(8,128)(2,1)}, bf16[1536,288]{1,0:T(8,128)(2,1)}, bf16[1536,288]{1,0:T(8,128)(2,1)},...) custom-call(s32[12]{0:T(128)} %stack.59.slots, ...), custom_call_target="tpu_custom_call" | custom-call | flops 4076863488 | bytes 14155776 | tf_op jit(solution)/shard_map/norm_project/pallas_call | solution.py:369
  86.1 19.0 %attention_forward.1 = (bf16[288,1536]{1,0:T(8,128)(2,1)}, f32[8,1536]{1,0:T(8,128)}) custom-call(bf16[1536,288]{1,0:T(8,128)(2,1)} %get-tuple-element.270.q_ref, bf16[1536,288]{1,0:T(8,128)(2,1)} %get-tuple-element.271.k_ref, bf16[1536,288]{1,0:T(8,128)(2,1)} %get-tuple-element.272.v_ref, s32[8,1536]{1,0:T(8,128)} %get-tuple-element.208.code_ref), custom_call_target="tpu_custom_call" | custom-call | flops 4831838208 | bytes 4423680 | tf_op jit(solution)/shard_map/attention_forward/pallas_call | solution.py:141
  108.6 2.0 broadcast_in_dim.42
  117.7 12.5 %collective-permute-done.15.refs_2_ = bf16[288,1536]{1,0:T(8,128)(2,1)S(1)} collective-permute-done((bf16[288,1536]{1,0:T(8,128)(2,1)}, bf16[288,1536]{1,0:T(8,128)(2,1)S(1)}, u32[]{:S(2)}, u32[]{:S(2)}) %collective-permute-start.15) | collective-permute-done | bytes 884768 | tf_op jit(solution)/shard_map/ppermute | solution.py:695
  134.1 22.0 %out_norm_up.1 = (f32[384,1152]{1,0:T(8,128)}, bf16[1152,1536]{1,0:T(8,128)(2,1)}, bf16[1536,1152]{1,0:T(8,128)(2,1)}, bf16[1536,1152]{1,0:T(8,128)(2,1)}, bf16[...) custom-call(s32[4]{0:T(128)} %pad_add_fusion.slots, bf16[1536,1152]{1,0:T(8,128)(2,1)} %get-tuple-element.204.x_ref, ...), custom_call_target="tpu_custom_call" | custom-call | flops 8153726976 | bytes 28311552 | tf_op jit(solution)/shard_map/out_norm_up/pallas_call | solution.py:442
  156.2 9.4 %convolution_convert_fusion.1 = bf16[1152,1152]{1,0:T(8,128)(2,1)} fusion(bf16[1536,1152]{1,0:T(8,128)(2,1)} %get-tuple-element.237.a_ref, bf16[1536,1152]{1,0:T(8,128)(2,1)} %constant_dynamic-update-slice_fusion.gy_ref), kind=kOutput, calls=%fused_computation.1 | convolution fusion | flops 4078190592 | bytes 9732096 | tf_op jit(solution)/shard_map/dot_general | solution.py:287
  165.6 14.9 %down_and_back.2 = (bf16[1536,1152]{1,0:T(8,128)(2,1)}, bf16[1536,1152]{1,0:T(8,128)(2,1)}, bf16[384,1152]{1,0:T(8,128)(2,1)}, bf16[384,1152]{1,0:T(8,128)(2,1)}, f32[1,1152]{1,0:T(1,128)}) custom-call(s32[4]{0:T(128)} %pad_add_fusion.slots, bf16[1536,1152]{1,0:T(8,128)(2,1)} %constant_dynamic-update-slice_fusion.gy_ref, ...), custom_call_target="tpu_custom_call" | custom-call | flops 6115295232 | bytes 14155776 | tf_op jit(solution)/shard_map/down_and_back/pallas_call | solution.py:500
  180.6 2.5 collective-permute-done.24
  184.8 15.0 %down_and_back.3 = (bf16[1536,1152]{1,0:T(8,128)(2,1)}, bf16[1536,1152]{1,0:T(8,128)(2,1)}, bf16[384,1152]{1,0:T(8,128)(2,1)}, bf16[384,1152]{1,0:T(8,128)(2,1)}, f32[1,1152]{1,0:T(1,128)}) custom-call(s32[4]{0:T(128)} %pad_add_fusion.slots, ...), custom_call_target="tpu_custom_call", output_to_operand_aliasing={{0}: (6, {}), {1}: (7, {})} | custom-call | flops 6115295232 | bytes 14155776 | tf_op jit(solution)/shard_map/down_and_back/pallas_call | solution.py:500
  199.8 6.5 %collective-permute-done.25.refs_0_ = bf16[384,1152]{1,0:T(8,128)(2,1)S(1)} collective-permute-done((bf16[384,1152]{1,0:T(8,128)(2,1)S(1)}, bf16[384,1152]{1,0:T(8,128)(2,1)S(1)}, u32[]{:S(2)}, u32[]{:S(2)}) %collective-permute-start.25) | collective-permute-done | bytes 884768 | tf_op jit(solution)/shard_map/ppermute | solution.py:695
  206.3 2.6 collective-permute-done.26.refs_2_
  209.9 10.1 %norm_back_out.1 = (f32[384,1152]{1,0:T(8,128)}, f32[8,1152]{1,0:T(8,128)}, bf16[288,384]{1,0:T(8,128)(2,1)}, bf16[288,384]{1,0:T(8,128)(2,1)}, bf16[288,384]{1,...) custom-call(s32[4]{0:T(128)} %pad_add_fusion.slots, ...), custom_call_target="tpu_custom_call" | custom-call | flops 1019215872 | bytes 8847360 | tf_op jit(solution)/shard_map/norm_back_out/pallas_call | solution.py:673
  220.4 1.5 collective-permute-start.30
  222.6 8.3 %convolution_convert_fusion = bf16[1152,1152]{1,0:T(8,128)(2,1)} fusion(bf16[1536,1152]{1,0:T(8,128)(2,1)} %get-tuple-element.266, bf16[1536,1152]{1,0:T(8,128)(2,1)S(1)} %copy-done.5), kind=kOutput, calls=%fused_computation | convolution fusion | flops 4078190592 | bytes 9732096 | tf_op jit(solution)/shard_map/dot_general | solution.py:287
  231.0 1.5 add_convert_fusion.2
  235.1 26.1 %attention_backward.1.g_ref = bf16[1536,864]{1,0:T(8,128)(2,1)} custom-call(s32[4]{0:T(128)} %pad_add_fusion.slots, bf16[1536,288]{1,0:T(8,128)(2,1)} %get-tuple-element.270.q_ref, bf16[1536,288]{1,0:T(8,128)(2,1)} %get-tuple-element.271.k_ref, bf16[1536,288]{1,0:T(8,128)(2,1)} %get-tuple-element.272.v_ref, ...), custom_call_target="tpu_custom_call" | custom-call | flops 12079595520 | bytes 7077888 | tf_op jit(solution)/shard_map/attention_backward/pallas_call | solution.py:225
  262.1 2.1 constant_dynamic-slice_fusion.4
  264.2 1.4 collective-permute-start.40
  265.6 10.2 %grads_qkv_out.1 = bf16[1152,1152]{1,0:T(8,128)(2,1)} custom-call(bf16[1536,1152]{1,0:T(8,128)(2,1)} %get-tuple-element.283.h_ref, bf16[1536,864]{1,0:T(8,128)(2,1)} %attention_backward.1.g_ref, bf16[1152,1536]{1,0:T(8,128)(2,1)} %get-tuple-element.284.o_ref, bf16[384,288]{1,0:T(8,128)(2,1)} %get-tuple-element.285.refs_0_, bf16[384,288]{1,0:T(8,128)(2,1)} %copy-done.49, ...), custom_call_target="tpu_custom_call" | custom-call | flops 4076863488 | bytes 10616832 | tf_op jit(solution)/shard_map/grads_qkv_out/pallas_call | solution.py:628
  275.8 2.0 constant_dynamic-slice_fusion.8
  277.8 1.9 collective-permute-start.36
  281.5 10.2 %project_back.1 = (bf16[1536,1152]{1,0:T(8,128)(2,1)}, f32[16,1152]{1,0:T(8,128)}) custom-call(s32[4]{0:T(128)} %pad_add_fusion.slots, bf16[1536,864]{1,0:T(8,128)(2,1)} %attention_backward.1.g_ref, bf16[1536,1152]{1,0:T(8,128)(2,1)} %get-tuple-element.204.x_ref, bf16[1152,1152]{1,0:T(8,128)(2,1)} %get-tuple-element.290.w_qkv, ...), custom_call_target="tpu_custom_call" | custom-call | flops 3057647616 | bytes 14155776 | tf_op jit(solution)/shard_map/project_back/pallas_call | solution.py:556
  293.9 1.6 fusion.16
  296.1 2.1 add_convert_fusion.7
  298.2 3.4 collective-permute-start.43
  301.6 1.5 collective-permute-start.45
  304.0 2.3 collective-permute-done.45
  306.2 1.6 add.376
  307.8 8.3 %collective-permute-done.43 = bf16[144,1152]{1,0:T(8,128)(2,1)} collective-permute-done((bf16[144,1152]{1,0:T(8,128)(2,1)}, bf16[144,1152]{1,0:T(8,128)(2,1)}, u32[]{:S(2)}, u32[]{:S(2)}) %collective-permute-start.43) | collective-permute-done | bytes 331808 | tf_op jit(solution)/shard_map/ppermute | solution.py:787
  316.1 2.6 collective-permute-done.44
  318.7 1.6 add_convert_fusion
  322.1 1.5 collective-permute-start.46
  323.6 2.3 add_convert_fusion.5
  325.9 1.7 collective-permute-start.47
  327.9 1.6 add.383
  329.5 2.0 constant_dynamic-slice_fusion
  332.8 3.3 collective-permute-done.47
  336.1 1.4 collective-permute-done.48
  338.2 1.9 add_convert_fusion.4
  340.1 1.6 collective-permute-start.51
  341.8 2.8 fusion.13
  346.8 3.5 settle_hidden.1
  351.6 3.8 collective-permute-done.50
  355.4 1.8 fusion.15
  359.3 2.7 collective-permute-start.55
  362.0 2.8 fusion.14
  365.7 2.4 collective-permute-start.60
  369.0 1.4 collective-permute-done.60
  (258 shorter events, 55.3 us)
Async XLA Ops:
  7.2 126.9 %all-gather.3.cloned.1.call-start = ((), (), s32[]{:S(2)}) async-start(), calls=%async_computation.2 | async-start | bytes 2985984 | tf_op jit(solution)/shard_map/all_gather | solution.py:876
  8.9 13.5 %collective-permute-start.1 = (bf16[144,1152]{1,0:T(8,128)(2,1)S(1)}, bf16[144,1152]{1,0:T(8,128)(2,1)}, u32[]{:S(2)}, u32[]{:S(2)}) collective-permute-start(bf16[144,1152]{1,0:T(8,128)(2,1)S(1)} %concatenate.13.refs_6_), channel_id=1, source_target_pairs={{0,2},{2,4},{4,6},{6,7},{7,5},{5,3},{3,1},{1,0},{8,10},{10,12},{12... | collective-permute-start | bytes 995336 | tf_op jit(solution)/shard_map/ppermute | solution.py:759
  12.0 10.4 %collective-permute-start.2 = (bf16[144,1152]{1,0:T(8,128)(2,1)S(1)}, bf16[144,1152]{1,0:T(8,128)(2,1)}, u32[]{:S(2)}, u32[]{:S(2)}) collective-permute-start(bf16[144,1152]{1,0:T(8,128)(2,1)S(1)} %concatenate.13.refs_6_), channel_id=1, source_target_pairs={{2,0},{4,2},{6,4},{7,6},{5,7},{3,5},{1,3},{0,1},{10,8},{12,10},{14... | collective-permute-start | bytes 995336 | tf_op jit(solution)/shard_map/ppermute | solution.py:763
  13.8 11.9 %collective-permute-start = (bf16[192,1152]{1,0:T(8,128)(2,1)}, bf16[192,1152]{1,0:T(8,128)(2,1)}, u32[]{:S(2)}, u32[]{:S(2)}) collective-permute-start(bf16[192,1152]{1,0:T(8,128)(2,1)} %slice_bitcast_fusion), channel_id=1, source_target_pairs={{0,16},{8,24},{16,0},{24,8},{1,17},{9,25},{17,1},{25,9},{2,18},{10... | collective-permute-start | bytes 1327112 | tf_op jit(solution)/shard_map/ppermute | solution.py:695
  25.7 11.8 %collective-permute-start.3 = (bf16[208,1152]{1,0:T(8,128)(2,1)}, bf16[208,1152]{1,0:T(8,128)(2,1)}, u32[]{:S(2)}, u32[]{:S(2)}) collective-permute-start(bf16[208,1152]{1,0:T(8,128)(2,1)} %slice.103), channel_id=1, source_target_pairs={{0,16},{8,24},{16,0},{24,8},{1,17},{9,25},{17,1},{25,9},{2,18},{10... | collective-permute-start | bytes 1437704 | tf_op jit(solution)/shard_map/ppermute | solution.py:695
  27.4 8.0 %collective-permute-start.4 = (bf16[144,1152]{1,0:T(8,128)(2,1)}, bf16[144,1152]{1,0:T(8,128)(2,1)S(1)}, u32[]{:S(2)}, u32[]{:S(2)}) collective-permute-start(bf16[144,1152]{1,0:T(8,128)(2,1)} %collective-permute-done.1.refs_7_), channel_id=1, source_target_pairs={{0,2},{2,4},{4,6},{6,7},{7,5},{5,3},{3,1},{1,0},{8,10},{10,12},{12... | collective-permute-start | bytes 995336 | tf_op jit(solution)/shard_map/ppermute | solution.py:759
  28.9 7.8 %collective-permute-start.5 = (bf16[144,1152]{1,0:T(8,128)(2,1)}, bf16[144,1152]{1,0:T(8,128)(2,1)}, u32[]{:S(2)}, u32[]{:S(2)}) collective-permute-start(bf16[144,1152]{1,0:T(8,128)(2,1)} %collective-permute-done.2.refs_8_), channel_id=1, source_target_pairs={{2,0},{4,2},{6,4},{7,6},{5,7},{3,5},{1,3},{0,1},{10,8},{12,10},{14... | collective-permute-start | bytes 995336 | tf_op jit(solution)/shard_map/ppermute | solution.py:763
  37.6 128.0 %all-gather.5.cloned.1.call-start = ((), (), s32[]{:S(2)}) async-start(), calls=%async_computation.3 | async-start | bytes 2985984 | tf_op jit(solution)/shard_map/all_gather | solution.py:892
  37.7 20.1 %collective-permute-start.6 = (bf16[400,1152]{1,0:T(8,128)(2,1)S(1)}, bf16[400,1152]{1,0:T(8,128)(2,1)}, u32[]{:S(2)}, u32[]{:S(2)}) collective-permute-start(bf16[400,1152]{1,0:T(8,128)(2,1)S(1)} %fusion.12.refs_0_), channel_id=1, source_target_pairs={{0,8},{8,0},{16,24},{24,16},{1,9},{9,1},{17,25},{25,17},{2,10},{10... | collective-permute-start | bytes 2764808 | tf_op jit(solution)/shard_map/ppermute | solution.py:695
  37.7 20.1 %collective-permute-start.8 = (bf16[208,1152]{1,0:T(8,128)(2,1)}, bf16[208,1152]{1,0:T(8,128)(2,1)}, u32[]{:S(2)}, u32[]{:S(2)}) collective-permute-start(bf16[208,1152]{1,0:T(8,128)(2,1)} %collective-permute-done.3.refs_3_), channel_id=1, source_target_pairs={{0,8},{8,0},{16,24},{24,16},{1,9},{9,1},{17,25},{25,17},{2,10},{10... | collective-permute-start | bytes 1437704 | tf_op jit(solution)/shard_map/ppermute | solution.py:695
  38.2 19.6 %collective-permute-start.7 = (bf16[192,1152]{1,0:T(8,128)(2,1)}, bf16[192,1152]{1,0:T(8,128)(2,1)}, u32[]{:S(2)}, u32[]{:S(2)}) collective-permute-start(bf16[192,1152]{1,0:T(8,128)(2,1)} %collective-permute-done.refs_2_), channel_id=1, source_target_pairs={{0,8},{8,0},{16,24},{24,16},{1,9},{9,1},{17,25},{25,17},{2,10},{10... | collective-permute-start | bytes 1327112 | tf_op jit(solution)/shard_map/ppermute | solution.py:695
  41.1 12.8 %collective-permute-start.9 = (bf16[144,1152]{1,0:T(8,128)(2,1)}, bf16[144,1152]{1,0:T(8,128)(2,1)}, u32[]{:S(2)}, u32[]{:S(2)}) collective-permute-start(bf16[144,1152]{1,0:T(8,128)(2,1)} %copy-done.44), channel_id=1, source_target_pairs={{0,2},{2,4},{4,6},{6,7},{7,5},{5,3},{3,1},{1,0},{8,10},{10,12},{12... | collective-permute-start | bytes 995336 | tf_op jit(solution)/shard_map/ppermute | solution.py:759
  42.6 15.2 %collective-permute-start.10 = (bf16[144,1152]{1,0:T(8,128)(2,1)}, bf16[144,1152]{1,0:T(8,128)(2,1)}, u32[]{:S(2)}, u32[]{:S(2)}) collective-permute-start(bf16[144,1152]{1,0:T(8,128)(2,1)} %collective-permute-done.5.refs_10_), channel_id=1, source_target_pairs={{2,0},{4,2},{6,4},{7,6},{5,7},{3,5},{1,3},{0,1},{10,8},{12,10},{14... | collective-permute-start | bytes 995336 | tf_op jit(solution)/shard_map/ppermute | solution.py:763
  57.8 10.5 %collective-permute-start.12 = (bf16[192,1152]{1,0:T(8,128)(2,1)}, bf16[192,1152]{1,0:T(8,128)(2,1)S(1)}, u32[]{:S(2)}, u32[]{:S(2)}) collective-permute-start(bf16[192,1152]{1,0:T(8,128)(2,1)} %get-tuple-element.221), channel_id=1, source_target_pairs={{0,16},{8,24},{16,0},{24,8},{1,17},{9,25},{17,1},{25,9},{2,18},{10... | collective-permute-start | bytes 1327112 | tf_op jit(solution)/shard_map/ppermute | solution.py:695
  59.3 9.1 %collective-permute-start.11 = (bf16[144,1152]{1,0:T(8,128)(2,1)}, bf16[144,1152]{1,0:T(8,128)(2,1)S(1)}, u32[]{:S(2)}, u32[]{:S(2)}) collective-permute-start(bf16[144,1152]{1,0:T(8,128)(2,1)} %collective-permute-done.9.refs_11_), channel_id=1, source_target_pairs={{0,2},{2,4},{4,6},{6,7},{7,5},{5,3},{3,1},{1,0},{8,10},{10,12},{12... | collective-permute-start | bytes 995336 | tf_op jit(solution)/shard_map/ppermute | solution.py:759
  68.3 16.9 %collective-permute-start.13 = (bf16[192,1152]{1,0:T(8,128)(2,1)S(1)}, bf16[192,1152]{1,0:T(8,128)(2,1)S(1)}, u32[]{:S(2)}, u32[]{:S(2)}) collective-permute-start(bf16[192,1152]{1,0:T(8,128)(2,1)S(1)} %get-tuple-element.223), channel_id=1, source_target_pairs={{0,16},{8,24},{16,0},{24,8},{1,17},{9,25},{17,1},{25,9},{2,18},{10... | collective-permute-start | bytes 1327112 | tf_op jit(solution)/shard_map/ppermute | solution.py:695
  85.2 21.0 %collective-permute-start.14 = (bf16[1152,384]{1,0:T(8,128)(2,1)}, bf16[1152,384]{1,0:T(8,128)(2,1)S(1)}, u32[]{:S(2)}, u32[]{:S(2)}) collective-permute-start(bf16[1152,384]{1,0:T(8,128)(2,1)} %get-tuple-element.219.refs_4_), channel_id=1, source_target_pairs={{0,16},{8,24},{16,0},{24,8},{1,17},{9,25},{17,1},{25,9},{2,18},{10... | collective-permute-start | bytes 2654216 | tf_op jit(solution)/shard_map/ppermute | solution.py:695
  107.1 4.4 %collective-permute-start.18 = (bf16[192,1152]{1,0:T(8,128)(2,1)S(1)}, bf16[192,1152]{1,0:T(8,128)(2,1)S(1)}, u32[]{:S(2)}, u32[]{:S(2)}) collective-permute-start(bf16[192,1152]{1,0:T(8,128)(2,1)S(1)} %copy-done.9), channel_id=1, source_target_pairs={{0,8},{8,0},{16,24},{24,16},{1,9},{9,1},{17,25},{25,17},{2,10},{10... | collective-permute-start | bytes 1327112 | tf_op jit(solution)/shard_map/ppermute | solution.py:695
  107.1 155.0 %reduce-scatter.3.cloned.1.call-start = ((), (), s32[]{:S(2)}) async-start(), calls=%async_computation.4 | async-start | bytes 2985984 | tf_op jit(solution)/shard_map/reduce_scatter | solution.py:914
  107.2 5.9 %collective-permute-start.19 = (bf16[192,1152]{1,0:T(8,128)(2,1)S(1)}, bf16[192,1152]{1,0:T(8,128)(2,1)S(1)}, u32[]{:S(2)}, u32[]{:S(2)}) collective-permute-start(bf16[192,1152]{1,0:T(8,128)(2,1)S(1)} %collective-permute-done.12), channel_id=1, source_target_pairs={{0,8},{8,0},{16,24},{24,16},{1,9},{9,1},{17,25},{25,17},{2,10},{10... | collective-permute-start | bytes 1327112 | tf_op jit(solution)/shard_map/ppermute | solution.py:695
  107.8 7.5 %collective-permute-start.20 = (bf16[192,1152]{1,0:T(8,128)(2,1)S(1)}, bf16[192,1152]{1,0:T(8,128)(2,1)S(1)}, u32[]{:S(2)}, u32[]{:S(2)}) collective-permute-start(bf16[192,1152]{1,0:T(8,128)(2,1)S(1)} %get-tuple-element.223), channel_id=1, source_target_pairs={{0,8},{8,0},{16,24},{24,16},{1,9},{9,1},{17,25},{25,17},{2,10},{10... | collective-permute-start | bytes 1327112 | tf_op jit(solution)/shard_map/ppermute | solution.py:695
  107.9 9.0 %collective-permute-start.21 = (bf16[192,1152]{1,0:T(8,128)(2,1)S(1)}, bf16[192,1152]{1,0:T(8,128)(2,1)S(1)}, u32[]{:S(2)}, u32[]{:S(2)}) collective-permute-start(bf16[192,1152]{1,0:T(8,128)(2,1)S(1)} %collective-permute-done.13), channel_id=1, source_target_pairs={{0,8},{8,0},{16,24},{24,16},{1,9},{9,1},{17,25},{25,17},{2,10},{10... | collective-permute-start | bytes 1327112 | tf_op jit(solution)/shard_map/ppermute | solution.py:695
  108.3 21.8 %collective-permute-start.15 = (bf16[288,1536]{1,0:T(8,128)(2,1)}, bf16[288,1536]{1,0:T(8,128)(2,1)S(1)}, u32[]{:S(2)}, u32[]{:S(2)}) collective-permute-start(bf16[288,1536]{1,0:T(8,128)(2,1)} %get-tuple-element.225.refs_0_.o_ref), channel_id=1, source_target_pairs={{0,16},{8,24},{16,0},{24,8},{1,17},{9,25},{17,1},{25,9},{2,18},{10... | collective-permute-start | bytes 2654216 | tf_op jit(solution)/shard_map/ppermute | solution.py:695
  111.5 18.7 %collective-permute-start.16 = (bf16[1152,384]{1,0:T(8,128)(2,1)S(1)}, bf16[1152,384]{1,0:T(8,128)(2,1)S(1)}, u32[]{:S(2)}, u32[]{:S(2)}) collective-permute-start(bf16[1152,384]{1,0:T(8,128)(2,1)S(1)} %copy-done.37), channel_id=1, source_target_pairs={{0,8},{8,0},{16,24},{24,16},{1,9},{9,1},{17,25},{25,17},{2,10},{10... | collective-permute-start | bytes 2654216 | tf_op jit(solution)/shard_map/ppermute | solution.py:695
  113.1 17.1 %collective-permute-start.17 = (bf16[1152,384]{1,0:T(8,128)(2,1)S(1)}, bf16[1152,384]{1,0:T(8,128)(2,1)S(1)}, u32[]{:S(2)}, u32[]{:S(2)}) collective-permute-start(bf16[1152,384]{1,0:T(8,128)(2,1)S(1)} %copy-done.39), channel_id=1, source_target_pairs={{0,8},{8,0},{16,24},{24,16},{1,9},{9,1},{17,25},{25,17},{2,10},{10... | collective-permute-start | bytes 2654216 | tf_op jit(solution)/shard_map/ppermute | solution.py:695
  130.2 3.0 collective-permute-start.22
  130.3 3.8 %collective-permute-start.23 = (bf16[288,1536]{1,0:T(8,128)(2,1)S(1)}, bf16[288,1536]{1,0:T(8,128)(2,1)}, u32[]{:S(2)}, u32[]{:S(2)}) collective-permute-start(bf16[288,1536]{1,0:T(8,128)(2,1)S(1)} %collective-permute-done.15.refs_2_), channel_id=1, source_target_pairs={{0,8},{8,0},{16,24},{24,16},{1,9},{9,1},{17,25},{25,17},{2,10},{10... | collective-permute-start | bytes 2654216 | tf_op jit(solution)/shard_map/ppermute | solution.py:695
  165.6 163.9 %reduce-scatter.5.cloned.1.call-start = ((), (), s32[]{:S(2)}) async-start(), calls=%async_computation.5 | async-start | bytes 2985984 | tf_op jit(solution)/shard_map/reduce_scatter | solution.py:936
  180.5 2.6 collective-permute-start.24
  184.5 21.8 %collective-permute-start.25 = (bf16[384,1152]{1,0:T(8,128)(2,1)S(1)}, bf16[384,1152]{1,0:T(8,128)(2,1)S(1)}, u32[]{:S(2)}, u32[]{:S(2)}) collective-permute-start(bf16[384,1152]{1,0:T(8,128)(2,1)S(1)} %add_convert_fusion.3), channel_id=1, source_target_pairs={{0,16},{8,24},{16,0},{24,8},{1,17},{9,25},{17,1},{25,9},{2,18},{10... | collective-permute-start | bytes 2654216 | tf_op jit(solution)/shard_map/ppermute | solution.py:695
  220.0 12.4 %collective-permute-start.28 = (bf16[288,384]{1,0:T(8,128)(2,1)}, bf16[288,384]{1,0:T(8,128)(2,1)}, u32[]{:S(2)}, u32[]{:S(2)}) collective-permute-start(bf16[288,384]{1,0:T(8,128)(2,1)} %get-tuple-element.259), channel_id=1, source_target_pairs={{0,8},{8,0},{16,24},{24,16},{1,9},{9,1},{17,25},{25,17},{2,10},{10... | collective-permute-start | bytes 663560 | tf_op jit(solution)/shard_map/ppermute | solution.py:695
  220.1 12.3 %collective-permute-start.29 = (bf16[288,384]{1,0:T(8,128)(2,1)}, bf16[288,384]{1,0:T(8,128)(2,1)}, u32[]{:S(2)}, u32[]{:S(2)}) collective-permute-start(bf16[288,384]{1,0:T(8,128)(2,1)} %get-tuple-element.260), channel_id=1, source_target_pairs={{0,16},{8,24},{16,0},{24,8},{1,17},{9,25},{17,1},{25,9},{2,18},{10... | collective-permute-start | bytes 663560 | tf_op jit(solution)/shard_map/ppermute | solution.py:695
  220.4 12.0 %collective-permute-start.30 = (bf16[288,384]{1,0:T(8,128)(2,1)}, bf16[288,384]{1,0:T(8,128)(2,1)}, u32[]{:S(2)}, u32[]{:S(2)}) collective-permute-start(bf16[288,384]{1,0:T(8,128)(2,1)} %get-tuple-element.261), channel_id=1, source_target_pairs={{0,24},{8,16},{16,8},{24,0},{1,25},{9,17},{17,9},{25,1},{2,26},{10... | collective-permute-start | bytes 663560 | tf_op jit(solution)/shard_map/ppermute | solution.py:695
  222.0 10.4 %collective-permute-start.27 = (bf16[384,1152]{1,0:T(8,128)(2,1)S(1)}, bf16[384,1152]{1,0:T(8,128)(2,1)}, u32[]{:S(2)}, u32[]{:S(2)}) collective-permute-start(bf16[384,1152]{1,0:T(8,128)(2,1)S(1)} %get-tuple-element.333), channel_id=1, source_target_pairs={{0,8},{8,0},{16,24},{24,16},{1,9},{9,1},{17,25},{25,17},{2,10},{10... | collective-permute-start | bytes 2654216 | tf_op jit(solution)/shard_map/ppermute | solution.py:695
  222.4 8.5 %collective-permute-start.31 = (bf16[384,1152]{1,0:T(8,128)(2,1)S(1)}, bf16[384,1152]{1,0:T(8,128)(2,1)S(1)}, u32[]{:S(2)}, u32[]{:S(2)}) collective-permute-start(bf16[384,1152]{1,0:T(8,128)(2,1)S(1)} %get-tuple-element.334), channel_id=1, source_target_pairs={{0,8},{8,0},{16,24},{24,16},{1,9},{9,1},{17,25},{25,17},{2,10},{10... | collective-permute-start | bytes 2654216 | tf_op jit(solution)/shard_map/ppermute | solution.py:695
  232.5 28.8 %collective-permute-start.33 = (bf16[384,288]{1,0:T(8,128)(2,1)S(1)}, bf16[384,288]{1,0:T(8,128)(2,1)S(1)}, u32[]{:S(2)}, u32[]{:S(2)}) collective-permute-start(bf16[384,288]{1,0:T(8,128)(2,1)S(1)} %copy-done.48), channel_id=1, source_target_pairs={{0,8},{8,0},{16,24},{24,16},{1,9},{9,1},{17,25},{25,17},{2,10},{10... | collective-permute-start | bytes 663560 | tf_op jit(solution)/shard_map/ppermute | solution.py:695
  233.1 28.2 %collective-permute-start.34 = (bf16[384,288]{1,0:T(8,128)(2,1)S(1)}, bf16[384,288]{1,0:T(8,128)(2,1)S(1)}, u32[]{:S(2)}, u32[]{:S(2)}) collective-permute-start(bf16[384,288]{1,0:T(8,128)(2,1)S(1)} %copy-done.47), channel_id=1, source_target_pairs={{0,16},{8,24},{16,0},{24,8},{1,17},{9,25},{17,1},{25,9},{2,18},{10... | collective-permute-start | bytes 663560 | tf_op jit(solution)/shard_map/ppermute | solution.py:695
  233.4 27.9 %collective-permute-start.35 = (bf16[384,288]{1,0:T(8,128)(2,1)S(1)}, bf16[384,288]{1,0:T(8,128)(2,1)S(1)}, u32[]{:S(2)}, u32[]{:S(2)}) collective-permute-start(bf16[384,288]{1,0:T(8,128)(2,1)S(1)} %copy-done.46), channel_id=1, source_target_pairs={{0,24},{8,16},{16,8},{24,0},{1,25},{9,17},{17,9},{25,1},{2,26},{10... | collective-permute-start | bytes 663560 | tf_op jit(solution)/shard_map/ppermute | solution.py:695
  234.5 58.4 %collective-permute-start.32 = (bf16[384,1152]{1,0:T(8,128)(2,1)S(1)}, bf16[384,1152]{1,0:T(8,128)(2,1)S(1)}, u32[]{:S(2)}, u32[]{:S(2)}) collective-permute-start(bf16[384,1152]{1,0:T(8,128)(2,1)S(1)} %add_convert_fusion.2), channel_id=1, source_target_pairs={{0,16},{8,24},{16,0},{24,8},{1,17},{9,25},{17,1},{25,9},{2,18},{10... | collective-permute-start | bytes 2654216 | tf_op jit(solution)/shard_map/ppermute | solution.py:695
  264.2 17.3 %collective-permute-start.40 = (bf16[144,288]{1,0:T(8,128)(2,1)}, bf16[144,288]{1,0:T(8,128)(2,1)S(1)}, u32[]{:S(2)}, u32[]{:S(2)}) collective-permute-start(bf16[144,288]{1,0:T(8,128)(2,1)} %get-tuple-element.353), channel_id=1, source_target_pairs={{0,24},{8,16},{16,8},{24,0},{1,25},{9,17},{17,9},{25,1},{2,26},{10... | collective-permute-start | bytes 248840 | tf_op jit(solution)/shard_map/ppermute | solution.py:695
  277.8 14.0 %collective-permute-start.36 = (bf16[144,1152]{1,0:T(8,128)(2,1)}, bf16[144,1152]{1,0:T(8,128)(2,1)S(1)}, u32[]{:S(2)}, u32[]{:S(2)}) collective-permute-start(bf16[144,1152]{1,0:T(8,128)(2,1)} %get-tuple-element.295), channel_id=1, source_target_pairs={{0,2},{2,4},{4,6},{6,7},{7,5},{5,3},{3,1},{1,0},{8,10},{10,12},{12... | collective-permute-start | bytes 995336 | tf_op jit(solution)/shard_map/ppermute | solution.py:787
  279.6 13.2 %collective-permute-start.37 = (bf16[144,1152]{1,0:T(8,128)(2,1)}, bf16[144,1152]{1,0:T(8,128)(2,1)S(1)}, u32[]{:S(2)}, u32[]{:S(2)}) collective-permute-start(bf16[144,1152]{1,0:T(8,128)(2,1)} %get-tuple-element.296), channel_id=1, source_target_pairs={{2,0},{4,2},{6,4},{7,6},{5,7},{3,5},{1,3},{0,1},{10,8},{12,10},{14... | collective-permute-start | bytes 995336 | tf_op jit(solution)/shard_map/ppermute | solution.py:789
  280.6 11.1 %collective-permute-start.39 = (bf16[144,288]{1,0:T(8,128)(2,1)}, bf16[144,288]{1,0:T(8,128)(2,1)S(1)}, u32[]{:S(2)}, u32[]{:S(2)}) collective-permute-start(bf16[144,288]{1,0:T(8,128)(2,1)} %get-tuple-element.354), channel_id=1, source_target_pairs={{0,16},{8,24},{16,0},{24,8},{1,17},{9,25},{17,1},{25,9},{2,18},{10... | collective-permute-start | bytes 248840 | tf_op jit(solution)/shard_map/ppermute | solution.py:695
  281.5 10.3 %collective-permute-start.38 = (bf16[144,288]{1,0:T(8,128)(2,1)S(1)}, bf16[144,288]{1,0:T(8,128)(2,1)S(1)}, u32[]{:S(2)}, u32[]{:S(2)}) collective-permute-start(bf16[144,288]{1,0:T(8,128)(2,1)S(1)} %get-tuple-element.355), channel_id=1, source_target_pairs={{0,8},{8,0},{16,24},{24,16},{1,9},{9,1},{17,25},{25,17},{2,10},{10... | collective-permute-start | bytes 248840 | tf_op jit(solution)/shard_map/ppermute | solution.py:695
  295.5 23.2 %collective-permute-start.42 = (bf16[384,1152]{1,0:T(8,128)(2,1)S(1)}, bf16[384,1152]{1,0:T(8,128)(2,1)}, u32[]{:S(2)}, u32[]{:S(2)}) collective-permute-start(bf16[384,1152]{1,0:T(8,128)(2,1)S(1)} %get-tuple-element.331), channel_id=1, source_target_pairs={{0,8},{8,0},{16,24},{24,16},{1,9},{9,1},{17,25},{25,17},{2,10},{10... | collective-permute-start | bytes 2654216 | tf_op jit(solution)/shard_map/ppermute | solution.py:695
  295.6 23.1 %collective-permute-start.41 = (bf16[384,1152]{1,0:T(8,128)(2,1)S(1)}, bf16[384,1152]{1,0:T(8,128)(2,1)S(1)}, u32[]{:S(2)}, u32[]{:S(2)}) collective-permute-start(bf16[384,1152]{1,0:T(8,128)(2,1)S(1)} %get-tuple-element.332), channel_id=1, source_target_pairs={{0,8},{8,0},{16,24},{24,16},{1,9},{9,1},{17,25},{25,17},{2,10},{10... | collective-permute-start | bytes 2654216 | tf_op jit(solution)/shard_map/ppermute | solution.py:695
  298.2 17.9 %collective-permute-start.43 = (bf16[144,1152]{1,0:T(8,128)(2,1)}, bf16[144,1152]{1,0:T(8,128)(2,1)}, u32[]{:S(2)}, u32[]{:S(2)}) collective-permute-start(bf16[144,1152]{1,0:T(8,128)(2,1)} %get-tuple-element.301), channel_id=1, source_target_pairs={{0,2},{2,4},{4,6},{6,7},{7,5},{5,3},{3,1},{1,0},{8,10},{10,12},{12... | collective-permute-start | bytes 995336 | tf_op jit(solution)/shard_map/ppermute | solution.py:787
  301.6 17.2 %collective-permute-start.44 = (bf16[144,1152]{1,0:T(8,128)(2,1)}, bf16[144,1152]{1,0:T(8,128)(2,1)}, u32[]{:S(2)}, u32[]{:S(2)}) collective-permute-start(bf16[144,1152]{1,0:T(8,128)(2,1)} %get-tuple-element.302), channel_id=1, source_target_pairs={{2,0},{4,2},{6,4},{7,6},{5,7},{3,5},{1,3},{0,1},{10,8},{12,10},{14... | collective-permute-start | bytes 995336 | tf_op jit(solution)/shard_map/ppermute | solution.py:789
  301.6 4.7 %collective-permute-start.45 = (f32[16,1152]{1,0:T(8,128)}, f32[16,1152]{1,0:T(8,128)}, u32[]{:S(2)}, u32[]{:S(2)}) collective-permute-start(f32[16,1152]{1,0:T(8,128)} %get-tuple-element.304), channel_id=1, source_target_pairs={{0,16},{8,24},{16,0},{24,8},{1,17},{9,25},{17,1},{25,9},{2,18},{10... | collective-permute-start | bytes 221192 | tf_op jit(solution)/shard_map/ppermute | solution.py:695
  318.7 9.2 %collective-permute-start.49 = (f32[16,1152]{1,0:T(8,128)}, f32[16,1152]{1,0:T(8,128)}, u32[]{:S(2)}, u32[]{:S(2)}) collective-permute-start(f32[16,1152]{1,0:T(8,128)} %add.376), channel_id=1, source_target_pairs={{0,8},{8,0},{16,24},{24,16},{1,9},{9,1},{17,25},{25,17},{2,10},{10... | collective-permute-start | bytes 221192 | tf_op jit(solution)/shard_map/ppermute | solution.py:695
  322.1 15.4 %collective-permute-start.46 = (bf16[192,1152]{1,0:T(8,128)(2,1)}, bf16[192,1152]{1,0:T(8,128)(2,1)}, u32[]{:S(2)}, u32[]{:S(2)}) collective-permute-start(bf16[192,1152]{1,0:T(8,128)(2,1)} %slice.106), channel_id=1, source_target_pairs={{0,16},{8,24},{16,0},{24,8},{1,17},{9,25},{17,1},{25,9},{2,18},{10... | collective-permute-start | bytes 1327112 | tf_op jit(solution)/shard_map/ppermute | solution.py:695
  325.9 10.2 %collective-permute-start.47 = (bf16[144,1152]{1,0:T(8,128)(2,1)}, bf16[144,1152]{1,0:T(8,128)(2,1)}, u32[]{:S(2)}, u32[]{:S(2)}) collective-permute-start(bf16[144,1152]{1,0:T(8,128)(2,1)} %get-tuple-element.309), channel_id=1, source_target_pairs={{0,2},{2,4},{4,6},{6,7},{7,5},{5,3},{3,1},{1,0},{8,10},{10,12},{12... | collective-permute-start | bytes 995336 | tf_op jit(solution)/shard_map/ppermute | solution.py:787
  327.6 9.9 %collective-permute-start.48 = (bf16[144,1152]{1,0:T(8,128)(2,1)}, bf16[144,1152]{1,0:T(8,128)(2,1)}, u32[]{:S(2)}, u32[]{:S(2)}) collective-permute-start(bf16[144,1152]{1,0:T(8,128)(2,1)} %get-tuple-element.310), channel_id=1, source_target_pairs={{2,0},{4,2},{6,4},{7,6},{5,7},{3,5},{1,3},{0,1},{10,8},{12,10},{14... | collective-permute-start | bytes 995336 | tf_op jit(solution)/shard_map/ppermute | solution.py:789
  331.5 14.0 %collective-permute-start.58 = (bf16[144,288]{1,0:T(8,128)(2,1)S(1)}, bf16[144,288]{1,0:T(8,128)(2,1)}, u32[]{:S(2)}, u32[]{:S(2)}) collective-permute-start(bf16[144,288]{1,0:T(8,128)(2,1)S(1)} %get-tuple-element.346), channel_id=1, source_target_pairs={{0,24},{8,16},{16,8},{24,0},{1,25},{9,17},{17,9},{25,1},{2,26},{10... | collective-permute-start | bytes 248840 | tf_op jit(solution)/shard_map/ppermute | solution.py:695
  331.5 14.0 %collective-permute-start.57 = (bf16[144,288]{1,0:T(8,128)(2,1)S(1)}, bf16[144,288]{1,0:T(8,128)(2,1)S(1)}, u32[]{:S(2)}, u32[]{:S(2)}) collective-permute-start(bf16[144,288]{1,0:T(8,128)(2,1)S(1)} %get-tuple-element.347), channel_id=1, source_target_pairs={{0,16},{8,24},{16,0},{24,8},{1,17},{9,25},{17,1},{25,9},{2,18},{10... | collective-permute-start | bytes 248840 | tf_op jit(solution)/shard_map/ppermute | solution.py:695
  336.1 9.4 %collective-permute-start.56 = (bf16[144,288]{1,0:T(8,128)(2,1)S(1)}, bf16[144,288]{1,0:T(8,128)(2,1)S(1)}, u32[]{:S(2)}, u32[]{:S(2)}) collective-permute-start(bf16[144,288]{1,0:T(8,128)(2,1)S(1)} %get-tuple-element.348), channel_id=1, source_target_pairs={{0,8},{8,0},{16,24},{24,16},{1,9},{9,1},{17,25},{25,17},{2,10},{10... | collective-permute-start | bytes 248840 | tf_op jit(solution)/shard_map/ppermute | solution.py:695
  337.5 7.1 %collective-permute-start.52 = (f32[16,1152]{1,0:T(8,128)}, f32[16,1152]{1,0:T(8,128)S(1)}, u32[]{:S(2)}, u32[]{:S(2)}) collective-permute-start(f32[16,1152]{1,0:T(8,128)} %add.383), channel_id=1, source_target_pairs={{0,4},{1,5},{2,6},{3,7},{4,0},{5,1},{6,2},{7,3},{8,12},{9,13},{10,... | collective-permute-start | bytes 221192 | tf_op jit(solution)/shard_map/ppermute | solution.py:695
  340.1 10.2 %collective-permute-start.51 = (bf16[144,1152]{1,0:T(8,128)(2,1)}, bf16[144,1152]{1,0:T(8,128)(2,1)}, u32[]{:S(2)}, u32[]{:S(2)}) collective-permute-start(bf16[144,1152]{1,0:T(8,128)(2,1)} %add_convert_fusion.4), channel_id=1, source_target_pairs={{0,2},{2,4},{4,6},{6,7},{7,5},{5,3},{3,1},{1,0},{8,10},{10,12},{12... | collective-permute-start | bytes 995336 | tf_op jit(solution)/shard_map/ppermute | solution.py:787
  344.6 10.7 %collective-permute-start.50 = (bf16[192,1152]{1,0:T(8,128)(2,1)S(1)}, bf16[192,1152]{1,0:T(8,128)(2,1)S(1)}, u32[]{:S(2)}, u32[]{:S(2)}) collective-permute-start(bf16[192,1152]{1,0:T(8,128)(2,1)S(1)} %slice.88), channel_id=1, source_target_pairs={{0,16},{8,24},{16,0},{24,8},{1,17},{9,25},{17,1},{25,9},{2,18},{10... | collective-permute-start | bytes 1327112 | tf_op jit(solution)/shard_map/ppermute | solution.py:695
  357.2 8.4 %collective-permute-start.59 = (f32[16,1152]{1,0:T(8,128)S(1)}, f32[16,1152]{1,0:T(8,128)S(1)}, u32[]{:S(2)}, u32[]{:S(2)}) collective-permute-start(f32[16,1152]{1,0:T(8,128)S(1)} %add.394), channel_id=1, source_target_pairs={{0,2},{1,3},{2,0},{3,1},{4,6},{5,7},{6,4},{7,5},{8,10},{9,11},{10,... | collective-permute-start | bytes 221192 | tf_op jit(solution)/shard_map/ppermute | solution.py:695
  358.5 9.6 %collective-permute-start.53 = (bf16[144,288]{1,0:T(8,128)(2,1)S(1)}, bf16[144,288]{1,0:T(8,128)(2,1)S(1)}, u32[]{:S(2)}, u32[]{:S(2)}) collective-permute-start(bf16[144,288]{1,0:T(8,128)(2,1)S(1)} %get-tuple-element.350), channel_id=1, source_target_pairs={{0,0},{24,8},{16,16},{8,24},{1,1},{25,9},{17,17},{9,25},{2,2},{26,... | collective-permute-start | bytes 248840 | tf_op jit(solution)/shard_map/ppermute | solution.py:997
  359.2 8.9 %collective-permute-start.54 = (bf16[144,288]{1,0:T(8,128)(2,1)S(1)}, bf16[144,288]{1,0:T(8,128)(2,1)S(1)}, u32[]{:S(2)}, u32[]{:S(2)}) collective-permute-start(bf16[144,288]{1,0:T(8,128)(2,1)S(1)} %get-tuple-element.351), channel_id=1, source_target_pairs={{8,0},{0,8},{24,16},{16,24},{9,1},{1,9},{25,17},{17,25},{10,2},{2,... | collective-permute-start | bytes 248840 | tf_op jit(solution)/shard_map/ppermute | solution.py:997
  359.3 8.8 %collective-permute-start.55 = (bf16[144,288]{1,0:T(8,128)(2,1)S(1)}, bf16[144,288]{1,0:T(8,128)(2,1)S(1)}, u32[]{:S(2)}, u32[]{:S(2)}) collective-permute-start(bf16[144,288]{1,0:T(8,128)(2,1)S(1)} %get-tuple-element.352), channel_id=1, source_target_pairs={{16,0},{8,8},{0,16},{24,24},{17,1},{9,9},{1,17},{25,25},{18,2},{10... | collective-permute-start | bytes 248840 | tf_op jit(solution)/shard_map/ppermute | solution.py:997
  365.7 4.8 %collective-permute-start.60 = (f32[16,1152]{1,0:T(8,128)S(1)}, f32[16,1152]{1,0:T(8,128)S(1)}, u32[]{:S(2)}, u32[]{:S(2)}) collective-permute-start(f32[16,1152]{1,0:T(8,128)S(1)} %add.399), channel_id=1, source_target_pairs={{0,1},{1,0},{2,3},{3,2},{4,5},{5,4},{6,7},{7,6},{8,9},{9,8},{10,11... | collective-permute-start | bytes 221192 | tf_op jit(solution)/shard_map/ppermute | solution.py:695
  (53 other events, 455.3 us)
Sparse Core Ops, SparseCore 0:
  37.7 60.3 all-gather.2
  107.3 55.8 all-gather.4
  166.8 70.2 reduce-scatter.2
  241.0 77.7 reduce-scatter.4
